TPU v7x, 32 devices: a whole 2x2x4 slice. The times are simulated.
32 devices in a mesh: dp: 16 (over z, y, core), head: 2 (over x).
Axes of the slice: x: 2, y: 2, z: 4, core: 2. Of those that a mesh axis runs over, the one named last changes fastest.
Arguments:
- tokens: bfloat16 [49152, 512], P(('dp', 'head')), may hold values from -6 to 6
- ln1_gain: float32 [512], replicated, may hold values from 0.5 to 1.5
- qkv_weight: bfloat16 [3, 512, 512], P(None, 'dp', 'head'), may hold values from -0.25 to 0.25
- out_weight: bfloat16 [512, 512], P('head', 'dp'), may hold values from -0.75 to 0.75
- blend: float32 [3, 8], replicated, may hold values from 0.5 to 4
- ln2_gain: float32 [512], replicated, may hold values from 0.5 to 1.5
- in_weight: bfloat16 [2048, 512], P(('dp', 'head')), may hold values from -0.25 to 0.25
- down_weight: bfloat16 [2048, 512], P(('dp', 'head')), may hold values from -0.125 to 0.125
- cotangent: bfloat16 [49152, 512], P(('dp', 'head')), may hold values from -6 to 6
- lengths: int32 [16, 10], P('dp'), may hold values from 0 to 3072, as said below
Outputs:
- layer_out: bfloat16 [49152, 512], P(('dp', 'head'))
- input_grad: float32 [49152, 512], P(('dp', 'head'))
- ln1_gain_grad: float32 [512], replicated
- qkv_grad: float32 [3, 512, 512], P(None, 'dp', 'head')
- out_weight_grad: float32 [512, 512], P('head', 'dp')
- blend_grad: float32 [3, 8], replicated
- ln2_gain_grad: float32 [512], replicated
- in_weight_grad: float32 [2048, 512], P(('dp', 'head'))
- down_weight_grad: float32 [2048, 512], P(('dp', 'head'))
Inputs may be any that keep to these rules, and one draw needn't show every extreme that they name: In each row of lengths the used slots come first and are followed by zeros; every nonzero length is at least 1; a row sums to at most 3072; in every draw some row sums to exactly 3072 and begins with an item of exactly 3072 tokens.
All inputs are finite; a program needn't handle non-finite values.
Results may differ from a plain program's by a relative error of at most 0.018.
Values may be sent and summed in bfloat16 or wider, within the bound.
No kernel may reach another device: no remote copies, remote signals or barrier semaphores. Data moves between devices by JAX's collectives and lax.ppermute only.
A program may use at most 192 MiB of HBM per device.

v0:
```python
import jax
import jax.numpy as jnp
from jax import lax
from jax.sharding import PartitionSpec as P

HEAD_DIM = 64
BAND = 30
BLOCK = 512
TAIL = 32


EXACT = lax.Precision.HIGHEST


def layer_norm(source, gain_vec):
    centered = source - jnp.mean(source, axis=-1, keepdims=True)
    spread = jnp.mean(centered * centered, axis=-1, keepdims=True)
    return centered * lax.rsqrt(spread + 1e-05) * gain_vec


def smooth(values_in):
    return jax.nn.gelu(values_in, approximate=True)


def layout(item_lengths, slot_count):
    places = jnp.arange(slot_count, dtype=jnp.int32)
    item_ends = jnp.cumsum(item_lengths)
    passed = item_ends[None, :] <= places[:, None]
    segment = jnp.sum(passed.astype(jnp.int32), axis=1)
    item_start = jnp.sum(jnp.where(passed, item_lengths[None, :], 0), axis=1)
    inside = places < item_ends[-1]
    segment = jnp.where(inside, segment, item_lengths.shape[0] + places)
    counted = jnp.where(inside, places - item_start + 1, 1).astype(jnp.float32)
    return (segment, places, counted, inside.astype(jnp.float32))


def blocked(source, block_rows, tail_rows, filler):
    pieces = source.reshape((source.shape[0] // block_rows, block_rows) + source.shape[1:])
    leading = jnp.full((1, tail_rows) + source.shape[1:], filler, source.dtype)
    return (pieces, jnp.concatenate([leading, pieces[:-1, block_rows - tail_rows :]], axis=0))


def block_mix(
    queries,
    key_rows,
    value_rows,
    key_tail,
    value_tail,
    blend_here,
    states,
    seg_rows,
    seg_tail,
    pos_rows,
    pos_tail,
    counted,
    inside,
    seg_before,
):
    elu_state, elu_total, tanh_state = states
    key_all = jnp.concatenate([key_tail, key_rows], axis=0)
    value_all = jnp.concatenate([value_tail, value_rows], axis=0)
    seg_keys = jnp.concatenate([seg_tail, seg_rows])
    pos_keys = jnp.concatenate([pos_tail, pos_rows])
    distance = pos_rows[:, None] - pos_keys[None, :]
    near_mask = (seg_rows[:, None] == seg_keys[None, :]) & (distance >= 0) & (distance < BAND)
    scores = jnp.einsum(
        "ihd,jhd->hij",
        queries.astype(jnp.bfloat16),
        key_all.astype(jnp.bfloat16),
        preferred_element_type=jnp.float32,
    ) * queries.shape[-1] ** (-0.5)
    scores = jnp.where(near_mask[None], scores, -1e30)
    highest = jnp.max(scores, axis=-1, keepdims=True)
    weights = jnp.exp(scores - highest)
    weights = weights / jnp.sum(weights, axis=-1, keepdims=True)
    near = jnp.einsum("hij,jhd->ihd", weights, value_all, precision=EXACT)
    order = pos_rows[:, None] - pos_rows[None, :]
    far_mask = ((seg_rows[:, None] == seg_rows[None, :]) & (order >= 0)).astype(queries.dtype)
    carried = (seg_rows == seg_before).astype(queries.dtype)
    lift_q = jax.nn.elu(queries) + 1.0
    lift_k = jax.nn.elu(key_rows) + 1.0
    pair_weight = jnp.einsum("ihd,jhd->hij", lift_q, lift_k, precision=EXACT) * far_mask[None]
    numerator = jnp.einsum("hij,jhd->ihd", pair_weight, value_rows, precision=EXACT) + carried[
        :, None, None
    ] * jnp.einsum("ihd,hde->ihe", lift_q, elu_state, precision=EXACT)
    denominator = jnp.transpose(jnp.sum(pair_weight, axis=-1)) + carried[:, None] * jnp.einsum(
        "ihd,hd->ih", lift_q, elu_total, precision=EXACT
    )
    far_elu = numerator / denominator[:, :, None]
    bend_q = jnp.tanh(queries)
    bend_k = jnp.tanh(key_rows)
    pair_bend = jnp.einsum("ihd,jhd->hij", bend_q, bend_k, precision=EXACT) * far_mask[None]
    far_tanh = (
        jnp.einsum("hij,jhd->ihd", pair_bend, value_rows, precision=EXACT)
        + carried[:, None, None] * jnp.einsum("ihd,hde->ihe", bend_q, tanh_state, precision=EXACT)
    ) / counted[:, None, None]
    mixed = (
        blend_here[0][None, :, None] * near
        + blend_here[1][None, :, None] * far_elu
        + blend_here[2][None, :, None] * far_tanh
    ) * inside[:, None, None]
    closing_seg = seg_rows[-1]
    continues = (seg_before == closing_seg).astype(queries.dtype)
    closing = (seg_rows == closing_seg).astype(queries.dtype)[:, None, None]
    elu_state = continues * elu_state + jnp.einsum(
        "jhd,jhe->hde", lift_k * closing, value_rows, precision=EXACT
    )
    elu_total = continues * elu_total + jnp.sum(lift_k * closing, axis=0)
    tanh_state = continues * tanh_state + jnp.einsum(
        "jhd,jhe->hde", bend_k * closing, value_rows, precision=EXACT
    )
    return (mixed, (elu_state, elu_total, tanh_state))


def per_device(
    tokens,
    ln1_gain,
    qkv_weight,
    out_weight,
    blend,
    ln2_gain,
    in_weight,
    down_weight,
    cotangent,
    lengths,
):
    row_count = tokens.shape[0]
    heads_here = qkv_weight.shape[2] // HEAD_DIM
    slot_count = row_count * lax.axis_size("head")
    block_count = slot_count // BLOCK
    segment, places, counted, inside = layout(lengths[0], slot_count)
    own_blend = lax.dynamic_slice_in_dim(blend, lax.axis_index("head") * heads_here, heads_here, 1)
    residual = tokens.astype(jnp.float32)
    normed_one, pull_one = jax.vjp(layer_norm, residual, ln1_gain)
    normed_one = normed_one.astype(jnp.bfloat16)
    qkv_cols, out_rows = (
        lax.all_gather(qkv_weight, "dp", axis=1, tiled=True),
        lax.all_gather(out_weight, "dp", axis=1, tiled=True),
    )
    normed_all = lax.all_gather(normed_one, "head", axis=0, tiled=True)
    projected = jnp.einsum(
        "td,cde->tce", normed_all, qkv_cols, preferred_element_type=jnp.float32
    ).astype(jnp.bfloat16)
    shaped = projected.reshape(slot_count, 3, heads_here, HEAD_DIM)
    q_pieces, q_tails = blocked(shaped[:, 0], BLOCK, TAIL, 0.0)
    k_pieces, k_tails = blocked(shaped[:, 1], BLOCK, TAIL, 0.0)
    v_pieces, v_tails = blocked(shaped[:, 2], BLOCK, TAIL, 0.0)
    s_pieces, s_tails = blocked(segment, BLOCK, TAIL, -2)
    p_pieces, p_tails = blocked(places, BLOCK, TAIL, -4 * BAND)
    c_pieces, c_tails = blocked(counted, BLOCK, TAIL, 1.0)
    i_pieces, i_tails = blocked(inside, BLOCK, TAIL, 0.0)
    before = jnp.concatenate([jnp.full((1,), -1, jnp.int32), s_pieces[:-1, -1]])
    block_inputs = (
        q_pieces,
        k_pieces,
        v_pieces,
        k_tails,
        v_tails,
        s_pieces,
        s_tails,
        p_pieces,
        p_tails,
        c_pieces,
        i_pieces,
        before,
    )
    zero_states = (
        jnp.zeros((heads_here, HEAD_DIM, HEAD_DIM), jnp.float32),
        jnp.zeros((heads_here, HEAD_DIM), jnp.float32),
        jnp.zeros((heads_here, HEAD_DIM, HEAD_DIM), jnp.float32),
    )

    def forward_step(states, inputs):
        qb, kb, vb, ktb, vtb, sb, stb, pb, ptb, cb, ib, seg_prev = inputs
        mixed, after = block_mix(
            qb.astype(jnp.float32),
            kb.astype(jnp.float32),
            vb.astype(jnp.float32),
            ktb.astype(jnp.float32),
            vtb.astype(jnp.float32),
            own_blend,
            states,
            sb,
            stb,
            pb,
            ptb,
            cb,
            ib,
            seg_prev,
        )
        return (after, (mixed.astype(jnp.bfloat16), states))

    _, (mixed_pieces, states_before) = lax.scan(forward_step, zero_states, block_inputs)
    mixed_flat = mixed_pieces.reshape(slot_count, heads_here * HEAD_DIM)
    selected = mixed_flat
    branch = lax.psum_scatter(
        jnp.dot(selected, out_rows, preferred_element_type=jnp.float32).astype(jnp.bfloat16),
        "head",
        scatter_dimension=0,
        tiled=True,
    ).astype(jnp.float32)
    hidden = residual + branch
    normed_two, pull_two = jax.vjp(layer_norm, hidden, ln2_gain)
    normed_two = normed_two.astype(jnp.bfloat16)
    in_full, down_full = (
        lax.all_gather(in_weight, ("dp", "head"), axis=0, tiled=True),
        lax.all_gather(down_weight, ("dp", "head"), axis=0, tiled=True),
    )
    inner = lax.dot_general(
        normed_two, in_full, (((1,), (1,)), ((), ())), preferred_element_type=jnp.float32
    )
    active, pull_gelu = jax.vjp(smooth, inner)
    active = active.astype(jnp.bfloat16)
    layer_out = (hidden + jnp.dot(active, down_full, preferred_element_type=jnp.float32)).astype(
        jnp.bfloat16
    )
    d_active = lax.dot_general(
        cotangent, down_full, (((1,), (1,)), ((), ())), preferred_element_type=jnp.float32
    )
    down_grad = lax.dot_general(
        active, cotangent, (((0,), (0,)), ((), ())), preferred_element_type=jnp.float32
    )
    d_inner = pull_gelu(d_active)[0].astype(jnp.bfloat16)
    in_grad = lax.dot_general(
        d_inner, normed_two, (((0,), (0,)), ((), ())), preferred_element_type=jnp.float32
    )
    d_normed_two = jnp.dot(d_inner, in_full, preferred_element_type=jnp.float32)
    d_hidden_part, gain_two_grad = pull_two(d_normed_two)
    d_hidden = cotangent.astype(jnp.float32) + d_hidden_part
    d_hidden_low = d_hidden.astype(jnp.bfloat16)
    d_branch = lax.all_gather(d_hidden_low, "head", axis=0, tiled=True)
    d_mixed = lax.dot_general(
        d_branch, out_rows, (((1,), (1,)), ((), ())), preferred_element_type=jnp.float32
    ).astype(jnp.bfloat16)
    out_grad = lax.dot_general(
        mixed_flat, d_branch, (((0,), (0,)), ((), ())), preferred_element_type=jnp.float32
    )
    grad_pieces = d_mixed.reshape(block_count, BLOCK, heads_here, HEAD_DIM)

    def backward_step(running, inputs):
        d_states, d_blend = running
        qb, kb, vb, ktb, vtb, sb, stb, pb, ptb, cb, ib, seg_prev, states_in, grad_block = inputs

        def local_mix(query_in, key_in, value_in, key_tail_in, value_tail_in, blend_in, states_arg):
            return block_mix(
                query_in,
                key_in,
                value_in,
                key_tail_in,
                value_tail_in,
                blend_in,
                states_arg,
                sb,
                stb,
                pb,
                ptb,
                cb,
                ib,
                seg_prev,
            )

        _, pull_block = jax.vjp(
            local_mix,
            qb.astype(jnp.float32),
            kb.astype(jnp.float32),
            vb.astype(jnp.float32),
            ktb.astype(jnp.float32),
            vtb.astype(jnp.float32),
            own_blend,
            states_in,
        )
        d_query, d_key, d_value, d_key_tail, d_value_tail, d_blend_here, d_states_in = pull_block(
            (grad_block.astype(jnp.float32), d_states)
        )
        return (
            (d_states_in, d_blend + d_blend_here),
            (d_query, d_key, d_value, d_key_tail, d_value_tail),
        )

    (_, blend_part), (d_query, d_key, d_value, d_key_tail, d_value_tail) = lax.scan(
        backward_step,
        (zero_states, jnp.zeros_like(own_blend)),
        block_inputs + (states_before, grad_pieces),
        reverse=True,
    )
    d_key = d_key.at[:-1, BLOCK - TAIL :].add(d_key_tail[1:])
    d_value = d_value.at[:-1, BLOCK - TAIL :].add(d_value_tail[1:])
    d_projected = (
        jnp.stack([d_query, d_key, d_value], axis=2)
        .reshape(slot_count, 3, heads_here * HEAD_DIM)
        .astype(jnp.bfloat16)
    )
    qkv_grad = jnp.einsum(
        "td,tce->cde", normed_all, d_projected, preferred_element_type=jnp.float32
    )
    selected = d_projected
    d_normed_one = lax.psum_scatter(
        jnp.einsum("tce,cde->td", selected, qkv_cols, preferred_element_type=jnp.float32).astype(
            jnp.bfloat16
        ),
        "head",
        scatter_dimension=0,
        tiled=True,
    ).astype(jnp.float32)
    d_residual_part, gain_one_grad = pull_one(d_normed_one)
    input_grad = d_hidden + d_residual_part
    qkv_share, out_share = (
        lax.psum_scatter(
            qkv_grad.astype(jnp.bfloat16), "dp", scatter_dimension=1, tiled=True
        ).astype(jnp.float32),
        lax.psum_scatter(
            out_grad.astype(jnp.bfloat16), "dp", scatter_dimension=1, tiled=True
        ).astype(jnp.float32),
    )
    in_share, down_share = (
        lax.psum_scatter(in_grad, ("dp", "head"), scatter_dimension=0, tiled=True),
        lax.psum_scatter(down_grad, ("dp", "head"), scatter_dimension=0, tiled=True),
    )
    blend_full = lax.dynamic_update_slice(
        jnp.zeros(blend.shape, jnp.float32),
        blend_part,
        (jnp.int32(0), lax.axis_index("head") * heads_here),
    )
    gain_one, gain_two, blend_sum = lax.psum(
        (gain_one_grad, gain_two_grad, blend_full), ("dp", "head")
    )
    return (
        layer_out,
        input_grad,
        gain_one,
        qkv_share,
        out_share,
        blend_sum,
        gain_two,
        in_share,
        down_share,
    )


def solution(mesh):
    return jax.shard_map(
        per_device,
        mesh=mesh,
        in_specs=(
            P(("dp", "head"), None),
            P(),
            P(None, "dp", "head"),
            P("head", "dp"),
            P(),
            P(),
            P(("dp", "head"), None),
            P(("dp", "head"), None),
            P(("dp", "head"), None),
            P("dp", None),
        ),
        out_specs=(
            P(("dp", "head"), None),
            P(("dp", "head"), None),
            P(),
            P(None, "dp", "head"),
            P("head", "dp"),
            P(),
            P(),
            P(("dp", "head"), None),
            P(("dp", "head"), None),
        ),
        check_vma=False,
    )
```

profile of v0, /device:TPU:0, one launch (start us, length us, event | category | flops | bytes accessed | tf_op | source)
XLA Modules:
  0.0 1572.5 jit_solution(3423338426514947390)
XLA Ops:
  16.8 25.2 %all_gather.20 = bf16[256,512]{0,1:T(8,128)(2,1)} all-gather(bf16[256,32]{0,1:T(8,128)(2,1)S(1)} %copy-done.37), channel_id=1, replica_groups=mesh['dp'=16,'head'=2] {'dp'}, dimensions={1}, use_global_device_ids=true | all-gather | bytes 278528 | tf_op jit(solution)/shard_map/all_gather | solution.py:138
  42.1 19.6 %all_gather.19 = bf16[3,512,256]{2,1,0:T(8,128)(2,1)S(1)} all-gather(bf16[3,32,256]{2,1,0:T(8,128)(2,1)S(1)} %copy-done.32), channel_id=1, replica_groups=mesh['dp'=16,'head'=2] {'dp'}, dimensions={1}, use_global_device_ids=true | all-gather | bytes 835584 | tf_op jit(solution)/shard_map/all_gather | solution.py:137
  95.0 189.5 %while.56 = (s32[]{:T(128)}, f32[4,64,64]{2,1,0:T(8,128)S(1)}, f32[4,64]{1,0:T(4,128)S(1)}, f32[4,64,64]{2,1,0:T(8,128)S(1)}, bf16[6,512,4,64]{1,3,2,0:T(8,128)(...) while((s32[]{:T(128)}, f32[4,64,64]{2,1,0:T(8,128)S(1)}, ...), condition=%wide.region_10.11_spmd.clone, body=%wide.region_5.10_spmd.clone.sunk | while | flops 4651091456 | bytes 46382844 | solution.py:193
  292.8 42.3 %reduce-scatter.6.cloned.1.call-done = bf16[1536,512]{1,0:T(8,128)(2,1)} async-done(((bf16[3072,512]{1,0:T(8,128)(2,1)}), bf16[1536,512]{1,0:T(8,128)(2,1)}) %reduce-scatter.6.cloned.1.call-update) | async-done | bytes 1572880 | tf_op jit(solution)/shard_map/reduce_scatter | solution.py:196
  337.9 40.1 %all-gather.7.cloned.1.call-done = bf16[2048,512]{1,0:T(8,128)(2,1)} async-done(((bf16[64,512]{1,0:T(8,128)(2,1)}), bf16[2048,512]{1,0:T(8,128)(2,1)}) %all-gather.7.cloned.1.call-update) | async-done | bytes 2097168 | tf_op jit(solution)/shard_map/all_gather | solution.py:206
  378.0 11.2 multiply_convert_fusion
  389.2 47.0 %all-gather.9.cloned.1.call-done = bf16[2048,512]{1,0:T(8,128)(2,1)} async-done(((bf16[64,512]{1,0:T(8,128)(2,1)}), bf16[2048,512]{1,0:T(8,128)(2,1)}) %all-gather.9.cloned.1.call-update) | async-done | bytes 2097168 | tf_op jit(solution)/shard_map/all_gather | solution.py:207
  436.2 13.9 fusion.469
  462.6 41.2 %all-gather.11.cloned.1.call-done = bf16[3072,512]{1,0:T(8,128)(2,1)} async-done(((bf16[1536,512]{1,0:T(8,128)(2,1)}), bf16[3072,512]{1,0:T(8,128)(2,1)}) %all-gather.11.cloned.1.call-update) | async-done | bytes 3145744 | tf_op jit(solution)/shard_map/all_gather | solution.py:231
  519.8 494.9 %while.57 = (s32[]{:T(128)}, f32[4,64,64]{2,1,0:T(8,128)S(1)}, f32[4,64]{1,0:T(4,128)S(1)}, f32[4,64,64]{2,1,0:T(8,128)S(1)}, f32[3,4]{1,0:T(4,128)S(1)}, /*inde...) while((s32[]{:T(128)}, f32[4,64,64]{2,1,0:T(8,128)S(1)}, ...), condition=%wide.region_27.28_spmd.clone, body=%wide.region_16.27_spmd.clone.sunk | while | flops 13751126016 | bytes 146586576 | solution.py:280
  595.3 5.2 fusion.731
  652.9 5.1 fusion.735
  676.3 5.2 fusion.731
  757.6 5.2 fusion.731
  838.8 5.2 fusion.731
  896.4 5.1 fusion.735
  919.8 5.2 fusion.731
  1001.0 5.2 fusion.731
  1018.2 8.0 scatter-add.6
  1031.6 7.9 scatter-add.9
  1053.5 5.8 reshape.611
  1062.9 5.8 reshape.610
  1082.1 6.5 bitcast_convert_fusion
  1090.0 8.3 fusion.508
  1100.2 8.4 fusion.500
  1110.5 8.2 fusion.483
  1118.8 52.4 %all-reduce.11.cloned.1.call-done = bf16[3,512,256]{2,0,1:T(4,128)(2,1)} async-done(((bf16[3,512,256]{2,0,1:T(4,128)(2,1)}), bf16[3,512,256]{2,0,1:T(4,128)(2,1)}) %all-reduce.11.cloned.1.call-update) | async-done | bytes 786448
  1172.8 57.1 %reduce-scatter.10.cloned.1.call-done = bf16[256,32]{0,1:T(8,128)(2,1)} async-done(((bf16[256,512]{0,1:T(8,128)(2,1)}), bf16[256,32]{0,1:T(8,128)(2,1)}) %reduce-scatter.10.cloned.1.call-update) | async-done | bytes 16400 | tf_op jit(solution)/shard_map/reduce_scatter | solution.py:311
  1231.2 44.0 %reduce-scatter.8.cloned.1.call-done = bf16[1536,512]{1,0:T(8,128)(2,1)} async-done(((bf16[3072,512]{1,0:T(8,128)(2,1)}), bf16[1536,512]{1,0:T(8,128)(2,1)}) %reduce-scatter.8.cloned.1.call-update) | async-done | bytes 1572880 | tf_op jit(solution)/shard_map/reduce_scatter | solution.py:297
  1279.8 40.4 %all-reduce.8 = (f32[512]{0:T(512)}, f32[3,8]{1,0:T(4,128)}, f32[512]{0:T(512)}) all-reduce(f32[512]{0:T(512)S(1)} %get-tuple-element.1040, f32[3,8]{1,0:T(4,128)S(1)} %dynamic_update_slice.65, f32[512]{0:T(512)S(1)} %copy-done.38), channel_id=1, replica_groups=mesh['dp'=16,'head'=2] {'dp','head'}, use_global_device_ids=true, to_apply=%region_33.34 | all-reduce | flops 1048 | bytes 8384 | tf_op jit(solution)/shard_map/psum | solution.py:324
  1325.0 96.9 %reduce-scatter.14.cloned.1.call-done = f32[64,512]{1,0:T(8,128)} async-done(((f32[2048,512]{1,0:T(8,128)}), f32[64,512]{1,0:T(8,128)}) %reduce-scatter.14.cloned.1.call-update) | async-done | bytes 131088 | tf_op jit(solution)/shard_map/reduce_scatter | solution.py:317
  1421.9 143.3 %reduce-scatter.12.cloned.1.call-done = f32[64,512]{1,0:T(8,128)} async-done(((f32[2048,512]{1,0:T(8,128)}), f32[64,512]{1,0:T(8,128)}) %reduce-scatter.12.cloned.1.call-update) | async-done | bytes 131088 | tf_op jit(solution)/shard_map/reduce_scatter | solution.py:316
  (728 shorter events, 740.2 us)
Async XLA Ops:
  8.0 8.1 copy-start
  8.0 53.6 %all-gather.5.cloned.1.call-start = ((), (), s32[]{:S(2)}) async-start(), calls=%async_computation.5 | async-start | bytes 4718592 | tf_op jit(solution)/shard_map/all_gather | solution.py:140
  9.9 6.9 copy-start.37
  9.9 32.1 %copy-start.32 = (bf16[3,32,256]{2,1,0:T(8,128)(2,1)S(1)}, bf16[3,32,256]{2,1,0:T(8,128)(2,1)}, u32[]{:S(2)}) copy-start(bf16[3,32,256]{2,1,0:T(8,128)(2,1)} %param.20) | copy-start | bytes 147460
  12.1 4.7 copy-start.26
  12.1 4.7 copy-start.24
  13.9 321.2 %reduce-scatter.6.cloned.1.call-start = ((), (), s32[]{:S(2)}) async-start(), calls=%async_computation.6 | async-start | bytes 4718592 | tf_op jit(solution)/shard_map/reduce_scatter | solution.py:196
  61.6 5.1 copy-start.19
  291.5 86.4 %all-gather.7.cloned.1.call-start = ((), (), s32[]{:S(2)}) async-start(), calls=%async_computation.7 | async-start | bytes 2162688 | tf_op jit(solution)/shard_map/all_gather | solution.py:206
  292.1 144.1 %all-gather.9.cloned.1.call-start = ((), (), s32[]{:S(2)}) async-start(), calls=%async_computation.8 | async-start | bytes 2162688 | tf_op jit(solution)/shard_map/all_gather | solution.py:207
  292.7 85.3 %copy-start.39 = (f32[512]{0:T(512)S(1)}, f32[512]{0:T(512)}, u32[]{:S(2)}) copy-start(f32[512]{0:T(512)} %param.23) | copy-start | bytes 6148
  292.7 211.1 %all-gather.11.cloned.1.call-start = ((), (), s32[]{:S(2)}) async-start(), calls=%async_computation.9 | async-start | bytes 4718592 | tf_op jit(solution)/shard_map/all_gather | solution.py:231
  337.1 117.7 %copy-start.30 = (f32[1536]{0:T(1024)}, f32[1536]{0:T(1024)S(1)}, u32[]{:S(2)}) copy-start(f32[1536]{0:T(1024)S(1)} %broadcast_multiply_fusion.1) | copy-start | bytes 18436
  337.9 116.9 %copy-start.33 = (f32[1536]{0:T(1024)}, f32[1536]{0:T(1024)S(1)}, u32[]{:S(2)}) copy-start(f32[1536]{0:T(1024)S(1)} %fusion.499) | copy-start | bytes 18436
  436.2 13.9 copy-start.6
  436.2 13.9 copy-start.44
  450.2 4.6 copy-start.46
  459.9 711.3 %all-reduce.11.cloned.1.call-start = ((), (), s32[]{:S(2)}) async-start(), calls=%async_computation.14 | async-start | bytes 2097152
  1018.2 10.1 copy-start.15
  1053.5 5.8 copy-start.11
  1062.9 7.3 copy-start.12
  1078.0 151.9 %reduce-scatter.10.cloned.1.call-start = ((), (), s32[]{:S(2)}) async-start(), calls=%async_computation.11 | async-start | bytes 278528 | tf_op jit(solution)/shard_map/reduce_scatter | solution.py:311
  1082.0 193.1 %reduce-scatter.8.cloned.1.call-start = ((), (), s32[]{:S(2)}) async-start(), calls=%async_computation.10 | async-start | bytes 4718592 | tf_op jit(solution)/shard_map/reduce_scatter | solution.py:297
  1088.6 333.3 %reduce-scatter.14.cloned.1.call-start = ((), (), s32[]{:S(2)}) async-start(), calls=%async_computation.13 | async-start | bytes 4325376 | tf_op jit(solution)/shard_map/reduce_scatter | solution.py:317
  1098.3 466.9 %reduce-scatter.12.cloned.1.call-start = ((), (), s32[]{:S(2)}) async-start(), calls=%async_computation.12 | async-start | bytes 4325376 | tf_op jit(solution)/shard_map/reduce_scatter | solution.py:316
  1110.5 164.7 %copy-start.23 = (f32[1536]{0:T(1024)S(1)}, f32[1536]{0:T(1024)}, u32[]{:S(2)}) copy-start(f32[1536]{0:T(1024)} %copy-done.22) | copy-start | bytes 18436
  1110.5 164.7 %copy-start.36 = (f32[512]{0:T(512)S(1)}, f32[512]{0:T(512)}, u32[]{:S(2)}) copy-start(f32[512]{0:T(512)} %param.19) | copy-start | bytes 6148
  1118.7 159.0 %copy-start.27 = (f32[1536]{0:T(1024)S(1)}, f32[1536]{0:T(1024)}, u32[]{:S(2)}) copy-start(f32[1536]{0:T(1024)} %copy-done.26) | copy-start | bytes 18436
  1118.7 159.0 %copy-start.25 = (f32[1536]{0:T(1024)S(1)}, f32[1536]{0:T(1024)}, u32[]{:S(2)}) copy-start(f32[1536]{0:T(1024)} %copy-done.24) | copy-start | bytes 18436
  1231.2 48.6 %copy-start.38 = (f32[512]{0:T(512)S(1)}, f32[512]{0:T(512)}, u32[]{:S(2)}) copy-start(f32[512]{0:T(512)} %get-tuple-element.1038) | copy-start | bytes 6148
  1231.2 89.1 %copy-start.29 = (f32[1536]{0:T(1024)S(1)}, f32[1536]{0:T(1024)}, u32[]{:S(2)}) copy-start(f32[1536]{0:T(1024)} %copy-done.28) | copy-start | bytes 18436
  1320.2 245.0 %copy-start.1 = (f32[3,8]{1,0:T(4,128)S(1)}, f32[3,8]{1,0:T(4,128)}, u32[]{:S(2)}) copy-start(f32[3,8]{1,0:T(4,128)} %param.22) | copy-start | bytes 292
  (25 other events, 65.2 us)
Sparse Core Ops, SparseCore 0:
  14.0 47.6 all-gather.4
  291.6 43.3 reduce-scatter.5
  460.0 43.7 all-gather.10
Sparse Core Ops, SparseCore 1:
  295.1 82.8 all-gather.6
  380.9 55.2 all-gather.8
  1078.0 93.2 all-reduce.10
  1174.8 55.0 reduce-scatter.9
  1232.7 42.4 reduce-scatter.7
  1278.0 143.8 reduce-scatter.13
  1424.6 140.6 reduce-scatter.11
where the time goes:
time: 1580 us; the launch traced here: 1570 us
  matrix products  620 us (39%)
  waiting for transfers between devices  565 us (36%)
  local copies, waits for them, and re-layouts  149 us (9%)
  other arithmetic  95 us (6%)
  blocking collectives  85.3 us (5%)
  loops' own time  40.7 us (3%)
  between operations  16.9 us (1%)
    reduce_scatter x1, waiting for transfers between devices, per_device(): lax.psum_scatter(in_grad, ('dp', 'head'), scatter_dimension=0, tiled=True)  143 us
    dot_general x24, matrix products, block_mix(): near = jnp.einsum('hij,jhd->ihd', weights, value_all, precision=EXACT)  98.1 us
    reduce_scatter x1, waiting for transfers between devices, per_device(): lax.psum_scatter(down_grad, ('dp', 'head'), scatter_dimension=0, tiled=True)  96.9 us
    dot_general x24, matrix products, block_mix(): jnp.einsum('ihd,jhd->hij', bend_q, bend_k, precision=EXACT) * far_mask[None]  95.6 us
    dot_general x24, matrix products, block_mix(): jnp.einsum('ihd,jhd->hij', lift_q, lift_k, precision=EXACT) * far_mask[None]  92.6 us
    dot_general x24, matrix products, block_mix(): jnp.einsum('hij,jhd->ihd', pair_bend, value_rows, precision=EXACT)  64.8 us
    dot_general x24, matrix products, block_mix(): jnp.einsum('hij,jhd->ihd', pair_weight, value_rows, precision=EXACT)  64 us
    reduce_scatter x1, waiting for transfers between devices, per_device(): lax.psum_scatter(out_grad.astype(jnp.bfloat16), 'dp', scatter_dimension=1...  57.1 us
  transfers between devices with their start and end apart: 10, of which 9 were waited for; matrix products, arithmetic and copies ran while one was open for 4% of the time, Pallas kernels for 0%

commit v1 on v0

v1 whole, which is shorter than its diff:
```python
import functools
import math

import jax
import jax.numpy as jnp
from jax import lax
from jax.experimental import pallas as pl
from jax.experimental.pallas import tpu as pltpu
from jax.sharding import PartitionSpec as P

HEAD_DIM = 64
BAND = 30
ROWS = 96
TAIL = 32
WIN = ROWS + TAIL
PAIR = 2 * HEAD_DIM
EPS = 1e-05
NEG = -1e30
F32 = jnp.float32
BF16 = jnp.bfloat16
NT = (((1,), (1,)), ((), ()))
TN = (((0,), (0,)), ((), ()))
NN = (((1,), (0,)), ((), ()))


def mm(left, right, dims=NN):
    return lax.dot_general(left, right, dims, preferred_element_type=F32)


def iota(shape, axis):
    return lax.broadcasted_iota(jnp.int32, shape, axis)


def lift(values):
    return jnp.where(values > 0, values + 1.0, jnp.exp(jnp.minimum(values, 0.0)))


def head_lanes(dtype):
    first = (iota((1, PAIR), 1) < HEAD_DIM).astype(F32)
    return first.astype(dtype), (1.0 - first).astype(dtype)


def split_heads(block):
    first, second = head_lanes(block.dtype)
    return jnp.concatenate([block * first, block * second], axis=0)


def same_head():
    return (iota((PAIR, PAIR), 0) < HEAD_DIM) == (iota((PAIR, PAIR), 1) < HEAD_DIM)


def block_only(wide):
    keep = same_head()
    parts = [
        jnp.where(keep, wide[:, p * PAIR : (p + 1) * PAIR], 0.0)
        for p in range(wide.shape[1] // PAIR)
    ]
    return jnp.concatenate(parts, axis=1)


def fold(tall):
    half = tall.shape[0] // 2
    lanes = iota((half, PAIR), 1) < HEAD_DIM
    return jnp.where(lanes, tall[:half], tall[half:])


def two(half):
    return jnp.concatenate([half, half], axis=1)


def masks(step, start):
    row = iota((ROWS, WIN), 0) + step * ROWS
    first = step * ROWS - TAIL
    key = iota((ROWS, WIN), 1) + first
    floor = jnp.maximum(first, 0)
    causal = key <= row
    near = causal & (key >= jnp.maximum(start, row - (BAND - 1)))
    far = causal & (key >= jnp.maximum(start, floor))
    return near, far, start < floor, row, floor, first


def near_weights(query, key_heads, near):
    scores = mm(query, key_heads, NT) * (HEAD_DIM**-0.5)
    parts = []
    for h in range(2):
        part = jnp.where(near, scores[:, h * WIN : (h + 1) * WIN], NEG)
        parts.append(jnp.exp(part - jnp.max(part, axis=1, keepdims=True)))
    return jnp.concatenate(parts, axis=1)


def spread(product):
    high = product.astype(BF16)
    low = (product - high.astype(F32)).astype(BF16)
    table = (
        ((iota((2 * PAIR, 2 * WIN), 0) % PAIR) < HEAD_DIM) == (iota((2 * PAIR, 2 * WIN), 1) < WIN)
    ).astype(F32)
    return mm(jnp.concatenate([high, low], axis=1), table.astype(BF16))


def load_keys(qkv_ref, tail_ref, keys, values):
    rows = qkv_ref.shape[1]
    keys[pl.ds(0, TAIL), :] = tail_ref[0]
    keys[pl.ds(TAIL, rows), :] = qkv_ref[1]
    values[pl.ds(0, TAIL), :] = tail_ref[1]
    values[pl.ds(TAIL, rows), :] = qkv_ref[2]


def ends_kernel(scalars, qkv_ref, out_ref):
    rows = qkv_ref.shape[1]
    step_rows = rows // 4
    last = jnp.maximum(scalars[scalars.shape[0] - 2], 0)
    out_ref[0] = jnp.zeros(out_ref.shape[1:], F32)

    def body(step, carry):
        at = pl.multiple_of(step * step_rows, 16)
        key = qkv_ref[1, pl.ds(at, step_rows), :].astype(F32)
        value = qkv_ref[2, pl.ds(at, step_rows), :]
        live = iota((step_rows, PAIR), 0) + at >= last
        lifted = jnp.where(live, lift(key), 0.0).astype(BF16)
        bent = jnp.where(live, jnp.tanh(key), 0.0).astype(BF16)
        ones = jnp.ones((step_rows, PAIR), BF16)
        out_ref[0, :, : 2 * PAIR] += mm(lifted, jnp.concatenate([value, ones], axis=1), TN)
        out_ref[0, :, 2 * PAIR :] += mm(bent, value, TN)
        return carry

    lax.fori_loop(0, 4, body, 0)
    out_ref[0] = block_only(out_ref[0])


def forward_kernel(
    scalars,
    qkv_ref,
    tail_ref,
    start_ref,
    blend_ref,
    state_in_ref,
    att_ref,
    near_ref,
    far1_ref,
    far2_ref,
    invl_ref,
    invd_ref,
    states_ref,
    keys,
    values,
    state,
):
    rows = qkv_ref.shape[1]
    load_keys(qkv_ref, tail_ref, keys, values)
    state[...] = state_in_ref[0].astype(F32)
    count_valid = scalars[scalars.shape[0] - 1]
    b0, b1, b2 = (blend_ref[pl.ds(f, 1), :] for f in range(3))

    def body(step, carry):
        at = pl.multiple_of(step * ROWS, 32)
        query = qkv_ref[0, pl.ds(at, ROWS), :]
        key = keys[pl.ds(at, WIN), :]
        value = values[pl.ds(at, WIN), :]
        start = start_ref[pl.ds(at, ROWS), :]
        near_mask, far_mask, carried, row, floor, first = masks(step, start)
        query_f = query.astype(F32)
        key_f = key.astype(F32)
        lift_q = lift(query_f).astype(BF16)
        bend_q = jnp.tanh(query_f).astype(BF16)
        lift_k = lift(key_f)
        bend_k = jnp.tanh(key_f)
        ones = jnp.ones((WIN, PAIR), BF16)
        value_heads = jnp.concatenate([split_heads(value), split_heads(ones)], axis=1)
        weights = near_weights(query, split_heads(key), near_mask).astype(BF16)
        near_out = mm(weights, value_heads)
        inv_l = 1.0 / near_out[:, PAIR:]
        near = near_out[:, :PAIR] * inv_l
        before = state[...]
        before_low = before.astype(BF16)
        states_ref[0, pl.ds(pl.multiple_of(step * PAIR, PAIR), PAIR), :] = before_low
        far_two = two(far_mask)
        pair_weight = jnp.where(far_two, mm(lift_q, split_heads(lift_k.astype(BF16)), NT), 0.0)
        elu_out = mm(pair_weight.astype(BF16), value_heads)
        elu_state = mm(lift_q, before_low[:, : 2 * PAIR])
        numerator = elu_out[:, :PAIR] + jnp.where(carried, elu_state[:, :PAIR], 0.0)
        inv_d = 1.0 / (elu_out[:, PAIR:] + jnp.where(carried, elu_state[:, PAIR:], 0.0))
        far1 = numerator * inv_d
        pair_bend = jnp.where(far_two, mm(bend_q, split_heads(bend_k.astype(BF16)), NT), 0.0)
        tanh_out = mm(pair_bend.astype(BF16), value_heads[:, :PAIR]) + jnp.where(
            carried, mm(bend_q, before_low[:, 2 * PAIR :]), 0.0
        )
        far2 = tanh_out / (row - start + 1).astype(F32)
        mixed = jnp.where(row < count_valid, b0 * near + b1 * far1 + b2 * far2, 0.0)
        att_ref[pl.ds(at, ROWS), :] = mixed.astype(BF16)
        near_ref[pl.ds(at, ROWS), :] = near
        far1_ref[pl.ds(at, ROWS), :] = far1
        far2_ref[pl.ds(at, ROWS), :] = far2
        invl_ref[pl.ds(at, ROWS), :] = inv_l
        invd_ref[pl.ds(at, ROWS), :] = inv_d
        closing = scalars[step]
        live = iota((ROWS, PAIR), 0) + first >= jnp.maximum(closing, floor)
        lifted = jnp.where(live, lift_k[:ROWS], 0.0).astype(BF16)
        bent = jnp.where(live, bend_k[:ROWS], 0.0).astype(BF16)
        with_ones = jnp.concatenate([value[:ROWS], ones[:ROWS]], axis=1)
        added = jnp.concatenate([mm(lifted, with_ones, TN), mm(bent, value[:ROWS], TN)], axis=1)
        keep = (closing < floor).astype(F32)
        state[...] = keep * before + block_only(added)
        return carry

    lax.fori_loop(0, rows // ROWS, body, 0, unroll=2)


def near_back(query, key_heads, grad_pair, near_mask, spread_near, scale_q, rows_q, rows_g):
    weights = near_weights(query, key_heads, near_mask)
    shifted = (weights * (grad_pair - spread_near)).astype(BF16)
    d_query = mm(shifted, key_heads) * scale_q
    d_key = fold(mm(shifted, rows_q, TN))
    return weights.astype(BF16), d_query, d_key


def prologue_kernel(
    scalars,
    qkv_ref,
    tail_ref,
    start_ref,
    blend_ref,
    grad_ref,
    near_ref,
    far1_ref,
    far2_ref,
    invl_ref,
    invd_ref,
    adjoint_ref,
    tail_grad_ref,
    sums_ref,
):
    rows = qkv_ref.shape[1]
    count_valid = scalars[scalars.shape[0] - 1]
    b0, b1, b2 = (blend_ref[pl.ds(f, 1), :] for f in range(3))
    adjoint_ref[0] = jnp.zeros(adjoint_ref.shape[1:], F32)
    sums_ref[...] = jnp.zeros(sums_ref.shape, F32)
    lanes = iota((ROWS, PAIR), 1) < HEAD_DIM

    key = jnp.concatenate([tail_ref[0], qkv_ref[1, pl.ds(0, ROWS), :]], axis=0)
    value = jnp.concatenate([tail_ref[1], qkv_ref[2, pl.ds(0, ROWS), :]], axis=0)
    start = start_ref[pl.ds(0, ROWS), :]
    near_mask, _, _, row, _, _ = masks(0, start)
    query = qkv_ref[0, pl.ds(0, ROWS), :]
    grad_f = jnp.where(row < count_valid, grad_ref[pl.ds(0, ROWS), :].astype(F32), 0.0)
    grad = grad_f.astype(BF16)
    scale = b0 * invl_ref[pl.ds(0, ROWS), :]
    rows_q = (query.astype(F32) * (scale * HEAD_DIM**-0.5)).astype(BF16)
    rows_g = (grad_f * scale).astype(BF16)
    weights, _, d_key = near_back(
        query,
        split_heads(key),
        mm(grad, split_heads(value), NT),
        near_mask,
        spread(grad_f * near_ref[pl.ds(0, ROWS), :]),
        scale * HEAD_DIM**-0.5,
        rows_q,
        rows_g,
    )
    tail_grad_ref[0] = d_key[:TAIL]
    tail_grad_ref[1] = fold(mm(weights, rows_g, TN))[:TAIL]

    def body(step, carry):
        at = pl.multiple_of(step * ROWS, 32)
        row = iota((ROWS, PAIR), 0) + at
        start = start_ref[pl.ds(at, ROWS), :]
        grad_f = jnp.where(row < count_valid, grad_ref[pl.ds(at, ROWS), :].astype(F32), 0.0)
        grad = grad_f.astype(BF16)
        far1 = grad_f * far1_ref[pl.ds(at, ROWS), :]
        sums_ref[pl.ds(0, 8), :] += jnp.sum(
            (grad_f * near_ref[pl.ds(at, ROWS), :]).reshape(ROWS // 8, 8, PAIR), axis=0
        )
        sums_ref[pl.ds(8, 8), :] += jnp.sum(far1.reshape(ROWS // 8, 8, PAIR), axis=0)
        sums_ref[pl.ds(16, 8), :] += jnp.sum(
            (grad_f * far2_ref[pl.ds(at, ROWS), :]).reshape(ROWS // 8, 8, PAIR), axis=0
        )

        @pl.when(scalars[scalars.shape[0] - 3] > at)
        def _():
            wide = spread(far1)
            along = jnp.where(lanes, wide[:, :WIN], wide[:, WIN:]).astype(BF16)
            query_f = qkv_ref[0, pl.ds(at, ROWS), :].astype(F32)
            live = start < 0
            scaled = jnp.where(live, lift(query_f) * (b1 * invd_ref[pl.ds(at, ROWS), :]), 0.0)
            bent = jnp.where(
                live, jnp.tanh(query_f) * (b2 / (row - start + 1).astype(F32)), 0.0
            )
            adjoint_ref[0, :, : 2 * PAIR] += mm(
                scaled.astype(BF16), jnp.concatenate([grad, along], axis=1), TN
            )
            adjoint_ref[0, :, 2 * PAIR :] += mm(bent.astype(BF16), grad, TN)

        return carry

    lax.fori_loop(0, rows // ROWS, body, 0)
    adjoint_ref[0] = block_only(adjoint_ref[0])


def key_side(adjoint_low, lift_k, bend_k, value):
    ones = jnp.full(value.shape, -1.0 / HEAD_DIM, BF16)
    d_lift = mm(jnp.concatenate([value, ones], axis=1), adjoint_low[:, : 2 * PAIR], NT)
    d_bend = mm(value, adjoint_low[:, 2 * PAIR :], NT)
    both = jnp.concatenate([adjoint_low[:, :PAIR], adjoint_low[:, 2 * PAIR :]], axis=0)
    d_value = mm(jnp.concatenate([lift_k, bend_k], axis=1), both)
    return d_lift, d_bend, d_value


def backward_kernel(
    scalars,
    qkv_ref,
    tail_ref,
    start_ref,
    blend_ref,
    grad_ref,
    near_ref,
    far1_ref,
    invl_ref,
    invd_ref,
    states_ref,
    adjoint_in_ref,
    tail_grad_ref,
    out_ref,
    keys,
    values,
    adjoint,
    key_carry,
    value_carry,
):
    rows = qkv_ref.shape[1]
    steps = rows // ROWS
    load_keys(qkv_ref, tail_ref, keys, values)
    count_valid = scalars[scalars.shape[0] - 1]
    last = scalars[scalars.shape[0] - 2]
    b0, b1, b2 = (blend_ref[pl.ds(f, 1), :] for f in range(3))
    lanes = iota((ROWS, PAIR), 1) < HEAD_DIM

    arrived = adjoint_in_ref[0].astype(F32)
    end_key = keys[pl.ds(rows, TAIL), :].astype(F32)
    end_lift, end_bend = lift(end_key), jnp.tanh(end_key)
    end_parts = key_side(
        arrived.astype(BF16), end_lift.astype(BF16), end_bend.astype(BF16), values[pl.ds(rows, TAIL), :]
    )
    live = iota((TAIL, PAIR), 0) + (rows - TAIL) >= last
    key_carry[...] = tail_grad_ref[0] + jnp.where(
        live,
        end_parts[0] * jnp.minimum(end_lift, 1.0) + end_parts[1] * (1.0 - end_bend * end_bend),
        0.0,
    )
    value_carry[...] = tail_grad_ref[1] + jnp.where(live, end_parts[2], 0.0)
    adjoint[...] = jnp.where(last < rows - TAIL, 1.0, 0.0) * arrived

    def body(back, carry):
        step = steps - 1 - back
        at = pl.multiple_of(step * ROWS, 32)
        query = qkv_ref[0, pl.ds(at, ROWS), :]
        key = keys[pl.ds(at, WIN), :]
        value = values[pl.ds(at, WIN), :]
        start = start_ref[pl.ds(at, ROWS), :]
        near_mask, far_mask, carried, row, floor, first = masks(step, start)
        far_two = two(far_mask)
        grad_f = jnp.where(row < count_valid, grad_ref[pl.ds(at, ROWS), :].astype(F32), 0.0)
        grad = grad_f.astype(BF16)
        query_f = query.astype(F32)
        key_f = key.astype(F32)
        lift_qf, bend_qf = lift(query_f), jnp.tanh(query_f)
        lift_kf, bend_kf = lift(key_f), jnp.tanh(key_f)
        lift_q, bend_q = lift_qf.astype(BF16), bend_qf.astype(BF16)
        lift_k, bend_k = lift_kf.astype(BF16), bend_kf.astype(BF16)
        lift_heads, bend_heads = split_heads(lift_k), split_heads(bend_k)
        r0 = b0 * invl_ref[pl.ds(at, ROWS), :]
        r1 = b1 * invd_ref[pl.ds(at, ROWS), :]
        r2 = b2 / (row - start + 1).astype(F32)
        grad_pair = mm(grad, split_heads(value), NT)
        rows_q = (query_f * (r0 * HEAD_DIM**-0.5)).astype(BF16)
        weights, d_query, d_key = near_back(
            query,
            split_heads(key),
            grad_pair,
            near_mask,
            spread(grad_f * near_ref[pl.ds(at, ROWS), :]),
            r0 * HEAD_DIM**-0.5,
            rows_q,
            None,
        )
        spread_far = spread(grad_f * far1_ref[pl.ds(at, ROWS), :])
        along = jnp.where(lanes, spread_far[:, :WIN], spread_far[:, WIN:])
        shifted = jnp.where(far_two, grad_pair - spread_far, 0.0).astype(BF16)
        plain = jnp.where(far_two, grad_pair, 0.0).astype(BF16)
        pair_weight = jnp.where(far_two, mm(lift_q, lift_heads, NT), 0.0).astype(BF16)
        pair_bend = jnp.where(far_two, mm(bend_q, bend_heads, NT), 0.0).astype(BF16)
        before = states_ref[0, pl.ds(pl.multiple_of(step * PAIR, PAIR), PAIR), :]
        scaled_along = (along * (-1.0 / HEAD_DIM)).astype(BF16)
        state_lift = mm(jnp.concatenate([grad, scaled_along], axis=1), before[:, : 2 * PAIR], NT)
        state_bend = mm(grad, before[:, 2 * PAIR :], NT)
        d_query = (
            d_query
            + (mm(shifted, lift_heads) + jnp.where(carried, state_lift, 0.0))
            * (r1 * jnp.minimum(lift_qf, 1.0))
            + (mm(plain, bend_heads) + jnp.where(carried, state_bend, 0.0))
            * (r2 * (1.0 - bend_qf * bend_qf))
        )
        out_ref[0, pl.ds(at, ROWS), :] = d_query.astype(BF16)
        rows_a = lift_qf * r1
        rows_t = bend_qf * r2
        d_lift = fold(mm(shifted, rows_a.astype(BF16), TN))
        d_bend = fold(mm(plain, rows_t.astype(BF16), TN))
        d_value = fold(
            mm(
                jnp.concatenate([weights, pair_weight, pair_bend], axis=0),
                jnp.concatenate([grad_f * r0, grad_f * r1, grad_f * r2], axis=0).astype(BF16),
                TN,
            )
        )
        after = adjoint[...]
        parts = key_side(after.astype(BF16), lift_k[:ROWS], bend_k[:ROWS], value[:ROWS])
        closing = scalars[step]
        live = iota((ROWS, PAIR), 0) + first >= jnp.maximum(closing, floor)
        pad = jnp.zeros((TAIL, PAIR), F32)
        d_lift = d_lift + jnp.concatenate([jnp.where(live, parts[0], 0.0), pad], axis=0)
        d_bend = d_bend + jnp.concatenate([jnp.where(live, parts[1], 0.0), pad], axis=0)
        d_value = d_value + jnp.concatenate([jnp.where(live, parts[2], 0.0), pad], axis=0)
        d_key = d_key + d_lift * jnp.minimum(lift_kf, 1.0) + d_bend * (1.0 - bend_kf * bend_kf)
        out_ref[1, pl.ds(at, ROWS), :] = jnp.concatenate(
            [d_key[TAIL:ROWS], d_key[ROWS:] + key_carry[...]], axis=0
        ).astype(BF16)
        out_ref[2, pl.ds(at, ROWS), :] = jnp.concatenate(
            [d_value[TAIL:ROWS], d_value[ROWS:] + value_carry[...]], axis=0
        ).astype(BF16)
        key_carry[...] = d_key[:TAIL]
        value_carry[...] = d_value[:TAIL]
        from_lift = mm(
            jnp.where(carried, rows_a, 0.0).astype(BF16),
            jnp.concatenate([grad, along.astype(BF16)], axis=1),
            TN,
        )
        from_bend = mm(jnp.where(carried, rows_t, 0.0).astype(BF16), grad, TN)
        keep = (closing < floor).astype(F32)
        adjoint[...] = keep * after + block_only(jnp.concatenate([from_lift, from_bend], axis=1))
        return carry

    lax.fori_loop(0, steps, body, 0)


def pair_specs(rows):
    column = pl.BlockSpec((rows, PAIR), lambda p, s: (0, p))
    return {
        "qkv": pl.BlockSpec((3, rows, PAIR), lambda p, s: (0, 0, p)),
        "tail": pl.BlockSpec((2, TAIL, PAIR), lambda p, s: (0, 0, p)),
        "start": pl.BlockSpec((rows, PAIR), lambda p, s: (0, 0)),
        "blend": pl.BlockSpec((3, PAIR), lambda p, s: (0, p)),
        "column": column,
        "state": pl.BlockSpec((1, PAIR, 3 * PAIR), lambda p, s: (p, 0, 0)),
        "states": pl.BlockSpec((1, rows // ROWS * PAIR, 3 * PAIR), lambda p, s: (p, 0, 0)),
        "sums": pl.BlockSpec((24, PAIR), lambda p, s: (0, p)),
    }


def call(kernel, ins, outs, out_shapes, scratch, pairs, name, flops, moved):
    return pl.pallas_call(
        kernel,
        out_shape=out_shapes,
        grid_spec=pltpu.PrefetchScalarGridSpec(
            num_scalar_prefetch=1,
            grid=(pairs,),
            in_specs=ins,
            out_specs=outs,
            scratch_shapes=scratch,
        ),
        compiler_params=pltpu.CompilerParams(
            dimension_semantics=("arbitrary",), vmem_limit_bytes=56 * 1024 * 1024
        ),
        cost_estimate=pl.CostEstimate(flops=flops, bytes_accessed=moved, transcendentals=0),
        name=name,
    )


def norm_parts(source):
    centered = source - jnp.mean(source, axis=-1, keepdims=True)
    spread_of = jnp.mean(centered * centered, axis=-1, keepdims=True)
    scale = lax.rsqrt(spread_of + EPS)
    return centered * scale, scale


def norm_back(d_out, gain, normal, scale):
    e = d_out * gain
    inner = jnp.mean(e, axis=-1, keepdims=True)
    along = jnp.mean(e * normal, axis=-1, keepdims=True)
    return scale * (e - inner - normal * along), jnp.sum(d_out * normal, axis=0)


def bits(size):
    return [1 << b for b in range(int(math.log2(size)))]


def swap(array, axis, mask):
    size = lax.axis_size(axis)
    return lax.ppermute(array, axis, [(i, i ^ mask) for i in range(size)])


def orders():
    dp = bits(lax.axis_size("dp"))
    core, rest = dp[:1], dp[1:]
    mid = len(rest) // 2
    y = [("dp", m) for m in rest[:mid]]
    z = [("dp", m) for m in reversed(rest[mid:])]
    x = [("head", m) for m in bits(lax.axis_size("head"))]
    core = [("dp", m) for m in core]
    return z + y + x + core, z + x + y + core


def my_bit(axis, mask):
    return (lax.axis_index(axis) & mask) > 0


def slot(order, axis, mask):
    main = orders()[0]
    here = main.index((axis, mask))
    return sum(1 for pair in order if main.index(pair) < here)


def gather_relative(shard, order):
    block = shard[None]
    for step, (axis, mask) in enumerate(order):
        inner = 1 << slot(order[:step], axis, mask)
        other = swap(block, axis, mask)
        shape = (block.shape[0] // inner, 1, inner) + shard.shape
        block = jnp.concatenate([block.reshape(shape), other.reshape(shape)], axis=1)
        block = block.reshape((-1,) + shard.shape)
    return block.reshape((-1,) + shard.shape[1:])


def scatter_relative(total, order):
    block = total.reshape((1 << len(order), -1) + total.shape[1:])
    for step in reversed(range(len(order))):
        axis, mask = order[step]
        inner = 1 << slot(order[:step], axis, mask)
        block = block.reshape((-1, 2, inner) + block.shape[1:])
        give = block[:, 1].astype(BF16)
        block = block[:, 0] + swap(give, axis, mask).astype(F32)
        block = block.reshape((-1,) + block.shape[2:])
    return block[0]


def gather_absolute(shard, order):
    block = shard[None]
    for axis, mask in order:
        other = swap(block, axis, mask)
        mine = my_bit(axis, mask)
        block = jnp.stack([jnp.where(mine, other, block), jnp.where(mine, block, other)])
        block = block.reshape((-1,) + shard.shape)
    sizes = (2,) * len(order)
    block = block.reshape(sizes + shard.shape)
    stacked = list(reversed(order))
    dp = [stacked.index(("dp", m)) for m in reversed(bits(lax.axis_size("dp")))]
    head = [stacked.index(("head", m)) for m in reversed(bits(lax.axis_size("head")))]
    rest = [len(order) + d for d in range(shard.ndim)]
    block = jnp.transpose(block, dp + head + rest)
    return block.reshape((lax.axis_size("dp"), lax.axis_size("head")) + shard.shape)


def scatter_absolute(total, order):
    n_dp, n_head = lax.axis_size("dp"), lax.axis_size("head")
    dp_bits = list(reversed(bits(n_dp)))
    head_bits = list(reversed(bits(n_head)))
    shard = total.shape[2:]
    block = total.reshape((2,) * (len(dp_bits) + len(head_bits)) + shard)
    left = [("dp", m) for m in dp_bits] + [("head", m) for m in head_bits]
    for axis, mask in reversed(order):
        at = left.index((axis, mask))
        mine = my_bit(axis, mask).astype(jnp.int32)
        keep = lax.dynamic_index_in_dim(block, mine, at, keepdims=False)
        give = lax.dynamic_index_in_dim(block, 1 - mine, at, keepdims=False)
        block = keep + swap(give.astype(BF16), axis, mask).astype(F32)
        left.pop(at)
    return block


def sum_everywhere(array, order):
    for axis, mask in order:
        array = array + swap(array, axis, mask)
    return array


def pass_along(local, keep, shift):
    size = lax.axis_size("head")
    pairs = [(i, i + shift) for i in range(size) if 0 <= i + shift < size]
    arrived = None
    for _ in range(size - 1):
        total = local if arrived is None else local + keep * arrived.astype(F32)
        arrived = lax.ppermute(total.astype(BF16), "head", pairs)
    return arrived


def per_device(
    tokens,
    ln1_gain,
    qkv_weight,
    out_weight,
    blend,
    ln2_gain,
    in_weight,
    down_weight,
    cotangent,
    lengths,
):
    rows, width = tokens.shape
    n_head = lax.axis_size("head")
    pairs = width // PAIR
    steps = rows // ROWS
    order_a, order_b = orders()
    shift_next = [(i, i + 1) for i in range(n_head - 1)]
    shift_back = [(i + 1, i) for i in range(n_head - 1)]

    qkv_all = gather_absolute(qkv_weight, order_a)
    qkv_all = jnp.transpose(qkv_all, (2, 0, 3, 1, 4)).reshape(3, width, width)
    out_all = gather_absolute(out_weight.T, order_b)
    out_all = jnp.transpose(out_all, (1, 3, 0, 2)).reshape(width, width)
    in_all = gather_relative(in_weight, order_a)
    down_all = gather_relative(down_weight, order_b)

    item_lengths = lengths[0]
    slots = item_lengths.shape[0]
    ends = jnp.sum(
        jnp.where(iota((slots, slots), 1) <= iota((slots, slots), 0), item_lengths[None, :], 0),
        axis=1,
    )
    offset = lax.axis_index("head") * rows
    local = jnp.arange(rows, dtype=jnp.int32)
    place = local + offset
    total = ends[slots - 1]
    item_start = jnp.max(
        jnp.where(ends[None, :] <= place[:, None], ends[None, :], 0), axis=1
    )
    start = jnp.where(place < total, item_start - offset, local)
    carried_rows = jnp.sum((start < 0).astype(jnp.int32))
    scalars = jnp.concatenate(
        [
            start.reshape(steps, ROWS)[:, ROWS - TAIL - 1],
            carried_rows[None],
            start[rows - 1 :],
            (total - offset)[None],
        ]
    )
    start_wide = jnp.broadcast_to(start[:, None], (rows, PAIR))
    keep_all = (start[rows - 1] < 0).astype(F32)
    blend_wide = jnp.repeat(blend, HEAD_DIM, axis=1)

    residual = tokens.astype(F32)
    normal_one, scale_one = norm_parts(residual)
    normed_one = (normal_one * ln1_gain).astype(BF16)
    qkv = jnp.einsum("td,cde->cte", normed_one, qkv_all, preferred_element_type=F32).astype(BF16)

    spec = pair_specs(rows)
    wide = jax.ShapeDtypeStruct((rows, width), F32)
    state_shape = jax.ShapeDtypeStruct((pairs, PAIR, 3 * PAIR), F32)
    states_shape = jax.ShapeDtypeStruct((pairs, steps * PAIR, 3 * PAIR), BF16)
    tail_shape = jax.ShapeDtypeStruct((2, TAIL, width), F32)
    big = rows * width

    ends_state = call(
        ends_kernel, [spec["qkv"]], spec["state"], state_shape, [], pairs, "ends", 400 * big, 6 * big
    )(scalars, qkv)
    tails = lax.ppermute(qkv[1:, rows - TAIL :], "head", shift_next)
    state_in = pass_along(ends_state, keep_all, 1)

    key_scratch = pltpu.VMEM((rows + TAIL, PAIR), BF16)
    state_scratch = pltpu.VMEM((PAIR, 3 * PAIR), F32)
    tail_scratch = pltpu.VMEM((TAIL, PAIR), F32)
    mixed, near, far1, far2, inv_l, inv_d, states = call(
        forward_kernel,
        [spec["qkv"], spec["tail"], spec["start"], spec["blend"], spec["state"]],
        [spec["column"]] * 6 + [spec["states"]],
        [jax.ShapeDtypeStruct((rows, width), BF16)] + [wide] * 5 + [states_shape],
        [key_scratch, key_scratch, state_scratch],
        pairs,
        "forward",
        8000 * big,
        40 * big,
    )(scalars, qkv, tails, start_wide, blend_wide, state_in)

    hidden = residual + jnp.dot(mixed, out_all, preferred_element_type=F32)
    normal_two, scale_two = norm_parts(hidden)
    normed_two = (normal_two * ln2_gain).astype(BF16)
    inner = lax.dot_general(normed_two, in_all, NT, preferred_element_type=F32)
    c0 = math.sqrt(2.0 / math.pi)
    bent = jnp.tanh(c0 * (inner + 0.044715 * (inner * inner * inner)))
    active = (0.5 * inner * (1.0 + bent)).astype(BF16)
    layer_out = (hidden + jnp.dot(active, down_all, preferred_element_type=F32)).astype(BF16)
    d_active = lax.dot_general(cotangent, down_all, NT, preferred_element_type=F32)
    down_grad = lax.dot_general(active, cotangent, TN, preferred_element_type=F32)
    slope = 0.5 * (1.0 + bent) + 0.5 * inner * (1.0 - bent * bent) * c0 * (
        1.0 + 3.0 * 0.044715 * inner * inner
    )
    d_inner = (d_active * slope).astype(BF16)
    in_grad = lax.dot_general(d_inner, normed_two, TN, preferred_element_type=F32)
    d_normed_two = jnp.dot(d_inner, in_all, preferred_element_type=F32)
    d_hidden_part, gain_two_part = norm_back(d_normed_two, ln2_gain, normal_two, scale_two)
    d_hidden = cotangent.astype(F32) + d_hidden_part
    d_branch = d_hidden.astype(BF16)
    d_mixed = lax.dot_general(d_branch, out_all, NT, preferred_element_type=F32).astype(BF16)
    out_grad = lax.dot_general(d_branch, mixed, TN, preferred_element_type=F32)

    in_share = scatter_relative(in_grad, order_a)
    down_share = scatter_relative(down_grad, order_b)
    n_dp = lax.axis_size("dp")
    out_share = scatter_absolute(
        jnp.transpose(
            out_grad.reshape(n_dp, width // n_dp, n_head, width // n_head), (0, 2, 1, 3)
        ),
        order_b,
    ).T

    adjoint, tail_grads, sums = call(
        prologue_kernel,
        [spec["qkv"], spec["tail"], spec["start"], spec["blend"]] + [spec["column"]] * 6,
        [spec["state"], spec["tail"], spec["sums"]],
        [state_shape, tail_shape, jax.ShapeDtypeStruct((24, width), F32)],
        [],
        pairs,
        "prologue",
        500 * big,
        28 * big,
    )(scalars, qkv, tails, start_wide, blend_wide, d_mixed, near, far1, far2, inv_l, inv_d)
    adjoint_in = pass_along(adjoint, keep_all, -1)
    tail_in = lax.ppermute(tail_grads, "head", shift_back)
    blend_part = jnp.sum(sums.reshape(3, 8, blend.shape[1], HEAD_DIM), axis=(1, 3))

    d_qkv = call(
        backward_kernel,
        [spec["qkv"], spec["tail"], spec["start"], spec["blend"]]
        + [spec["column"]] * 5
        + [spec["states"], spec["state"], spec["tail"]],
        spec["qkv"],
        jax.ShapeDtypeStruct((3, rows, width), BF16),
        [key_scratch, key_scratch, state_scratch, tail_scratch, tail_scratch],
        pairs,
        "backward",
        16000 * big,
        40 * big,
    )(
        scalars,
        qkv,
        tails,
        start_wide,
        blend_wide,
        d_mixed,
        near,
        far1,
        inv_l,
        inv_d,
        states,
        adjoint_in,
        tail_in,
    )

    qkv_grad = jnp.einsum("td,cte->cde", normed_one, d_qkv, preferred_element_type=F32)
    d_normed_one = jnp.einsum("cte,cde->td", d_qkv, qkv_all, preferred_element_type=F32)
    d_residual_part, gain_one_part = norm_back(d_normed_one, ln1_gain, normal_one, scale_one)
    input_grad = d_hidden + d_residual_part
    qkv_share = scatter_absolute(
        jnp.transpose(
            qkv_grad.reshape(3, n_dp, width // n_dp, n_head, width // n_head), (1, 3, 0, 2, 4)
        ),
        order_a,
    )
    early = sum_everywhere(
        jnp.concatenate([gain_two_part, blend_part.reshape(-1)])[None], order_b
    )[0]
    gain_two = early[:width]
    blend_sum = early[width:].reshape(blend.shape)
    gain_one = sum_everywhere(gain_one_part[None], order_a)[0]
    return (
        layer_out,
        input_grad,
        gain_one,
        qkv_share,
        out_share,
        blend_sum,
        gain_two,
        in_share,
        down_share,
    )


def solution(mesh):
    return jax.shard_map(
        per_device,
        mesh=mesh,
        in_specs=(
            P(("dp", "head"), None),
            P(),
            P(None, "dp", "head"),
            P("head", "dp"),
            P(),
            P(),
            P(("dp", "head"), None),
            P(("dp", "head"), None),
            P(("dp", "head"), None),
            P("dp", None),
        ),
        out_specs=(
            P(("dp", "head"), None),
            P(("dp", "head"), None),
            P(),
            P(None, "dp", "head"),
            P("head", "dp"),
            P(),
            P(),
            P(("dp", "head"), None),
            P(("dp", "head"), None),
        ),
        check_vma=False,
    )
```

time: 1580 us -> 411 us (0.26)
  matrix products: 620 us -> 72.6 us
  waiting for transfers between devices: 565 us -> 59.4 us
  Pallas kernels: 0 us -> 113 us
  local copies, waits for them, and re-layouts: 149 us -> 46.4 us
  blocking collectives: 85.3 us -> 0 us
  starting transfers between devices: 0.43 us -> 80.4 us
  other arithmetic: 95 us -> 30.7 us
  loops' own time: 40.7 us -> 0 us
    dot_general x258 -> x12, matrix products: 620 us -> 72.6 us  [the longest x1 12.1 us: per_device(): lax.dot_general(cotangent, down_all, NT, preferred_element_type=F32)]
    reduce_scatter x5 -> x0, waiting for transfers between devices: 384 us -> none  [the longest x1 143 us: per_device(): lax.psum_scatter(in_grad, ('dp', 'head'), scatter_dimension=0, tiled=True)]
    all_gather x4 -> x0, waiting for transfers between devices: 128 us -> none  [the longest x1 47 us: per_device(): lax.all_gather(down_weight, ('dp', 'head'), axis=0, tiled=True)]
    pallas_call x0 -> x4, Pallas kernels: none -> 113 us  [the longest x1 60.5 us: per_device(): call(backward_kernel, [spec['qkv'], spec['tail'], spec['start'], spec['bl...]
    ppermute x0 -> x54, starting transfers between devices: none -> 80.4 us  [the longest x50 73.3 us: swap(): return lax.ppermute(array, axis, [(i, i ^ mask) for i in range(size)])]
    ppermute x0 -> x54, waiting for transfers between devices: none -> 59.4 us  [the longest x50 50.5 us: swap(): return lax.ppermute(array, axis, [(i, i ^ mask) for i in range(size)])]
    unnamed x11 -> x0, waiting for transfers between devices: 53.6 us -> none
    another operation x16 -> x0, local copies, waits for them, and re-layouts: 45.5 us -> none  [the longest x7 27.3 us: per_device(): jnp.stack([d_query, d_key, d_value], axis=2)]
  transfers between devices with their start and end apart: 10 -> 54, of which waited for: 9 -> 19; matrix products, arithmetic and copies ran while one was open for 4% -> 26% of each run, Pallas kernels for 0% -> 25%
where the time goes in v1:
time: 411 us; the launch traced here: 405 us
  Pallas kernels  113 us (27%)
  starting transfers between devices  80.4 us (20%)
  matrix products  72.6 us (18%)
  waiting for transfers between devices  59.4 us (14%)
  local copies, waits for them, and re-layouts  46.4 us (11%)
  other arithmetic  30.7 us (7%)
    ppermute x50, starting transfers between devices, swap(): return lax.ppermute(array, axis, [(i, i ^ mask) for i in range(size)])  73.3 us
    pallas_call x1, Pallas kernels, per_device(): call(backward_kernel, [spec['qkv'], spec['tail'], spec['start'], spec['bl...  60.5 us
    ppermute x50, waiting for transfers between devices, swap(): return lax.ppermute(array, axis, [(i, i ^ mask) for i in range(size)])  50.5 us
    pallas_call x1, Pallas kernels, per_device(): call(forward_kernel, [spec['qkv'], spec['tail'], spec['start'], spec['ble...  32.8 us
    unnamed x75, local copies, waits for them, and re-layouts  14.4 us
    dot_general x1, matrix products, per_device(): lax.dot_general(cotangent, down_all, NT, preferred_element_type=F32)  12.1 us
    pallas_call x1, Pallas kernels, per_device(): call(prologue_kernel, [spec['qkv'], spec['tail'], spec['start'], spec['bl...  12 us
    dot_general x1, matrix products, per_device(): inner = lax.dot_general(normed_two, in_all, NT, preferred_element_type=F32)  10.3 us
  transfers between devices with their start and end apart: 54, of which 19 were waited for; matrix products, arithmetic and copies ran while one was open for 26% of the time, Pallas kernels for 25%

profile of v1, /device:TPU:0, one launch (start us, length us, event | category | flops | bytes accessed | tf_op | source)
XLA Modules:
  0.0 405.2 jit_solution(1271212439221236083)
XLA Ops:
  0.6 4.1 %collective-permute-start.7 = (bf16[1,32,256]{2,1,0:T(8,128)(2,1)}, bf16[1,32,256]{2,1,0:T(8,128)(2,1)S(1)}, u32[]{:S(2)}, u32[]{:S(2)}) collective-permute-start(bf16[1,32,256]{2,1,0:T(8,128)(2,1)} %bitcast.358), channel_id=1, source_target_pairs={{0,16},{2,18},{4,20},{6,22},{8,24},{10,26},{12,28},{14,30},{16,0},... | collective-permute-start | bytes 49160 | tf_op jit(solution)/shard_map/ppermute | solution.py:496
  4.9 2.8 collective-permute-start.12
  38.2 5.4 %collective-permute-done.3 = bf16[8,3,32,256]{3,2,1,0:T(8,128)(2,1)S(1)} collective-permute-done((bf16[8,3,32,256]{3,2,1,0:T(8,128)(2,1)S(1)}, bf16[8,3,32,256]{3,2,1,0:T(8,128)(2,1)S(1)}, u32[]{:S(2)}, u32[]{:S(2)}) %collective-permute-start.3) | collective-permute-done | bytes 393248 | tf_op jit(solution)/shard_map/ppermute | solution.py:496
  50.7 2.8 copy.71
  53.4 3.7 reshape.338
  57.2 5.9 %convert_bitcast_fusion.qkv_ref = bf16[3,1536,512]{2,1,0:T(8,128)(2,1)} fusion(bf16[3,512,512]{2,1,0:T(8,128)(2,1)} %reshape.338, bf16[1536,512]{0,1:T(8,128)(2,1)S(1)} %copy.69, f32[512]{0:T(512)S(1)} %copy-done.27, f32[1536]{0:T(1024)S(1)} %add_rsqrt_fusion.1, f32[1536]{0:T(1024)S(1)} %broadcast_multiply_fusion.5), kind=kOutput, calls=%fused_computation.15 | convolution fusion | flops 2422210560 | bytes 7878656 | tf_op jit(solution)/shard_map/td,cde->cte/dot_general | solution.py:650
  63.1 7.9 %ends.1 = f32[4,128,384]{2,1,0:T(8,128)} custom-call(s32[19]{0:T(128)} %pad_add_fusion.scalars, bf16[3,1536,512]{2,1,0:T(8,128)(2,1)} %convert_bitcast_fusion.qkv_ref), custom_call_target="tpu_custom_call" | custom-call | flops 314572800 | bytes 4718592 | tf_op jit(solution)/shard_map/ends/pallas_call | solution.py:659
  72.1 3.0 collective-permute-start.6
  85.9 32.8 %forward.1 = (bf16[1536,512]{1,0:T(8,128)(2,1)}, f32[1536,512]{1,0:T(8,128)}, f32[1536,512]{1,0:T(8,128)}, f32[1536,512]{1,0:T(8,128)}, f32[1536,512]{1,0:T(8,12...) custom-call(s32[19]{0:T(128)} %pad_add_fusion.scalars, bf16[3,1536,512]{2,1,0:T(8,128)(2,1)} %convert_bitcast_fusion.qkv_ref, ...), custom_call_target="tpu_custom_call" | custom-call | flops 6291456000 | bytes 31457280 | tf_op jit(solution)/shard_map/forward/pallas_call | solution.py:668
  123.7 10.3 %multiply_convert_fusion = (bf16[1536,2048]{1,0:T(8,128)(2,1)}, f32[1536,2048]{1,0:T(8,128)}) fusion(bf16[2048,512]{1,0:T(8,128)(2,1)S(1)} %bitcast.327, f32[1536,512]{0,1:T(8,128)S(1)} %get-tuple-element.101, f32[512]{0:T(512)S(1)} %copy-done.26, f32[1536]{0:T(1024)S(1)} %add_rsqrt_fusion, f32[1536]{0:T(1024)S(1)} %broadcast_multiply_fusion.4), kind=kOutput, calls=%fused_computation.11 | convolution fusion | flops 3252682752 | bytes 24131584 | tf_op jit(solution)/shard_map/dot_general | solution.py:683
  134.0 12.1 %fusion.8 = bf16[1536,2048]{1,0:T(8,128)(2,1)S(1)} fusion(f32[1536,2048]{1,0:T(8,128)} %get-tuple-element.103, bf16[2048,512]{1,0:T(8,128)(2,1)S(1)} %bitcast.325, bf16[1536,512]{1,0:T(8,128)(2,1)S(1)} %copy-done.14), kind=kOutput, calls=%fused_computation.10 | convolution fusion | flops 3280994304 | bytes 22544384 | tf_op jit(solution)/shard_map/dot_general | solution.py:688
  146.1 6.2 %fusion.73 = f32[2048,512]{1,0:T(8,128)} fusion(bf16[1536,2048]{1,0:T(8,128)(2,1)S(1)} %fusion.8, f32[1536,512]{0,1:T(8,128)S(1)} %get-tuple-element.101, f32[512]{0:T(512)S(1)} %copy-done.26, f32[1536]{0:T(1024)S(1)} %add_rsqrt_fusion, f32[1536]{0:T(1024)S(1)} %broadcast_multiply_fusion.4), kind=kOutput, calls=%fused_computation.191 | convolution fusion | flops 3224371200 | bytes 13645824 | tf_op jit(solution)/shard_map/dot_general | solution.py:694
  152.3 4.4 %multiply_reduce_fusion = (f32[512]{0:T(512)S(1)}, f32[1536]{0:T(1024)S(1)}, f32[1536]{0:T(1024)S(1)}, f32[1536,512]{0,1:T(8,128)S(1)}) fusion(f32[1536,512]{0,1:T(8,128)S(1)} %get-tuple-element.101, f32[1536]{0:T(1024)S(1)} %add_rsqrt_fusion, f32[1536]{0:T(1024)S(1)} %broadcast_multiply_fusion.4, f32[512]{0:T(512)S(1)} %copy-done.26, ...), kind=kOutput, calls=%fused_computation.31 | convolution fusion | flops 3227513344 | bytes 14708736 | tf_op jit(solution)/shard_map/dot_general | solution.py:695
  161.6 12.0 %prologue.1 = (f32[4,128,384]{2,1,0:T(8,128)}, f32[2,32,512]{2,1,0:T(8,128)}, f32[24,512]{1,0:T(8,128)}) custom-call(s32[19]{0:T(128)} %pad_add_fusion.scalars, bf16[3,1536,512]{2,1,0:T(8,128)(2,1)} %convert_bitcast_fusion.qkv_ref, bf16[2,32,512]{2,1,0:T(8,128)(2,1)} %copy-done.19, s32[1536,128]{1,0:T(8,128)} %broadcast_in_dim.79.start_ref, ...), custom_call_target="tpu_custom_call" | custom-call | flops 393216000 | bytes 22020096 | tf_op jit(solution)/shard_map/prologue/pallas_call | solution.py:712
  177.3 9.1 %fusion.22 = bf16[1536,512]{0,1:T(8,128)(2,1)} fusion(f32[1536,512]{0,1:T(8,128)} %copy-done, bf16[1536,2048]{1,0:T(8,128)(2,1)} %get-tuple-element.102, bf16[2048,512]{1,0:T(8,128)(2,1)} %bitcast.326), kind=kOutput, calls=%fused_computation.37 | convolution fusion | flops 3222798336 | bytes 13107200 | tf_op jit(solution)/shard_map/dot_general | solution.py:687
  186.4 5.9 %fusion.76 = f32[2048,512]{1,0:T(8,128)S(1)} fusion(bf16[1536,2048]{1,0:T(8,128)(2,1)} %get-tuple-element.102, bf16[1536,512]{1,0:T(8,128)(2,1)S(1)} %copy-done.15), kind=kOutput, calls=%fused_computation.194 | convolution fusion | flops 3221225472 | bytes 12058624 | tf_op jit(solution)/shard_map/dot_general | solution.py:689
  196.0 16.4 %collective-permute-start.41 = (f32[1,536]{1,0:T(1,128)S(1)}, f32[1,536]{1,0:T(1,128)S(1)}, u32[]{:S(2)}, u32[]{:S(2)}) collective-permute-start(f32[1,536]{1,0:T(1,128)S(1)} %add.246), channel_id=1, source_target_pairs={{0,1},{1,0},{2,3},{3,2},{4,5},{5,4},{6,7},{7,6},{8,9},{9,8},{10,11... | collective-permute-start | bytes 6440 | tf_op jit(solution)/shard_map/ppermute | solution.py:496
  215.7 3.3 collective-permute-start.42
  220.6 2.8 fusion.26
  234.4 6.3 %collective-permute-done.23.tail_grad_ref = f32[2,32,512]{2,1,0:T(8,128)S(1)} collective-permute-done((f32[2,32,512]{2,1,0:T(8,128)}, f32[2,32,512]{2,1,0:T(8,128)S(1)}, u32[]{:S(2)}, u32[]{:S(2)}) %collective-permute-start.23) | collective-permute-done | bytes 131104 | tf_op jit(solution)/shard_map/ppermute | solution.py:724
  241.6 60.5 %backward.1 = bf16[3,1536,512]{2,1,0:T(8,128)(2,1)} custom-call(s32[19]{0:T(128)} %pad_add_fusion.scalars, bf16[3,1536,512]{2,1,0:T(8,128)(2,1)} %convert_bitcast_fusion.qkv_ref, bf16[2,32,512]{2,1,0:T(8,128)(2,1)} %copy-done.19, s32[1536,128]{1,0:T(8,128)} %broadcast_in_dim.79.start_ref, f32[3,512]{1,0:T(4,128)} %reshape.339.blend_ref, ...), custom_call_target="tpu_custom_call" | custom-call | flops 12582912000 | bytes 31457280 | tf_op jit(solution)/shard_map/backward/pallas_call | solution.py:727
  302.1 7.6 %fusion.20 = (f32[512]{0:T(512)S(1)}, f32[1536]{0:T(1024)}, f32[1536]{0:T(1024)}, f32[1536,512]{0,1:T(8,128)}) fusion(bf16[1536,512]{0,1:T(8,128)(2,1)S(1)} %copy.69, f32[1536]{0:T(1024)S(1)} %add_rsqrt_fusion.1, f32[1536]{0:T(1024)S(1)} %broadcast_multiply_fusion.5, f32[512]{0:T(512)S(1)} %copy-done.27, bf16[3,1536,512]{2,1,0:T(8,128)(2,1)} %backward.1, ...), kind=kOutput, calls=%fused_computation.29 | convolution fusion | flops 2422993408 | bytes 11038720 | tf_op jit(solution)/shard_map/cte,cde->td/dot_general | solution.py:756
  309.7 4.5 %convolution_bitcast_fusion.1 = f32[3,512,512]{1,2,0:T(8,128)} fusion(bf16[3,1536,512]{2,1,0:T(8,128)(2,1)S(1)} %copy-done.34, bf16[1536,512]{0,1:T(8,128)(2,1)S(1)} %copy.69, f32[512]{0:T(512)S(1)} %copy-done.27, f32[1536]{0:T(1024)S(1)} %add_rsqrt_fusion.1, f32[1536]{0:T(1024)S(1)} %broadcast_multiply_fusion.5), kind=kOutput, calls=%fused_computation.49 | convolution fusion | flops 2419851264 | bytes 9451520 | tf_op jit(solution)/shard_map/td,cte->cde/dot_general | solution.py:755
  314.2 2.9 collective-permute-start.24
  317.3 3.6 copy.82
  320.8 5.2 %reshape.364 = f32[3,16,32,2,256]{4,3,2,1,0:T(2,128)} reshape(f32[3,512,512]{2,1,0:T(8,128)} %copy.82) | data formatting | bytes 6291456 | tf_op jit(solution)/shard_map/reshape | solution.py:761
  344.7 3.7 copy.88
  358.4 5.9 %collective-permute-done.50 = bf16[2,4,64,512]{3,2,1,0:T(8,128)(2,1)S(1)} collective-permute-done((bf16[2,4,64,512]{3,2,1,0:T(8,128)(2,1)S(1)}, bf16[2,4,64,512]{3,2,1,0:T(8,128)(2,1)S(1)}, u32[]{:S(2)}, u32[]{:S(2)}) %collective-permute-start.50) | collective-permute-done | bytes 524320 | tf_op jit(solution)/shard_map/ppermute | solution.py:496
  366.7 12.4 %collective-permute-done.30 = bf16[2,2,2,3,32,256]{5,4,3,2,1,0:T(8,128)(2,1)S(1)} collective-permute-done((bf16[2,2,2,3,32,256]{5,4,3,2,1,0:T(8,128)(2,1)S(1)}, bf16[2,2,2,3,32,256]{5,4,3,2,1,0:T(8,128)(2,1)S(1)}, u32[]{:S(2)}, u32[]{:S(2)}) %collective-permute-start.30) | collective-permute-done | bytes 393248 | tf_op jit(solution)/shard_map/ppermute | solution.py:496
  381.6 3.4 collective-permute-done.31
  387.9 2.8 collective-permute-done.32
  393.0 3.8 collective-permute-done.33
  (292 shorter events, 128.9 us)
Async XLA Ops:
  0.6 13.9 %collective-permute-start.7 = (bf16[1,32,256]{2,1,0:T(8,128)(2,1)}, bf16[1,32,256]{2,1,0:T(8,128)(2,1)S(1)}, u32[]{:S(2)}, u32[]{:S(2)}) collective-permute-start(bf16[1,32,256]{2,1,0:T(8,128)(2,1)} %bitcast.358), channel_id=1, source_target_pairs={{0,16},{2,18},{4,20},{6,22},{8,24},{10,26},{12,28},{14,30},{16,0},... | collective-permute-start | bytes 49160 | tf_op jit(solution)/shard_map/ppermute | solution.py:496
  4.8 17.4 %collective-permute-start = (bf16[1,3,32,256]{3,2,1,0:T(8,128)(2,1)}, bf16[1,3,32,256]{3,2,1,0:T(8,128)(2,1)}, u32[]{:S(2)}, u32[]{:S(2)}) collective-permute-start(bf16[1,3,32,256]{3,2,1,0:T(8,128)(2,1)} %bitcast.357), channel_id=1, source_target_pairs={{0,16},{2,18},{4,20},{6,22},{8,24},{10,26},{12,28},{14,30},{16,0},... | collective-permute-start | bytes 147464 | tf_op jit(solution)/shard_map/ppermute | solution.py:496
  4.9 24.5 %collective-permute-start.12 = (bf16[1,64,512]{2,1,0:T(8,128)(2,1)}, bf16[1,64,512]{2,1,0:T(8,128)(2,1)S(1)}, u32[]{:S(2)}, u32[]{:S(2)}) collective-permute-start(bf16[1,64,512]{2,1,0:T(8,128)(2,1)} %bitcast.351), channel_id=1, source_target_pairs={{0,16},{2,18},{4,20},{6,22},{8,24},{10,26},{12,28},{14,30},{16,0},... | collective-permute-start | bytes 196616 | tf_op jit(solution)/shard_map/ppermute | solution.py:496
  7.7 22.2 %collective-permute-start.17 = (bf16[1,64,512]{2,1,0:T(8,128)(2,1)}, bf16[1,64,512]{2,1,0:T(8,128)(2,1)S(1)}, u32[]{:S(2)}, u32[]{:S(2)}) collective-permute-start(bf16[1,64,512]{2,1,0:T(8,128)(2,1)} %bitcast.353), channel_id=1, source_target_pairs={{0,16},{2,18},{4,20},{6,22},{8,24},{10,26},{12,28},{14,30},{16,0},... | collective-permute-start | bytes 196616 | tf_op jit(solution)/shard_map/ppermute | solution.py:496
  23.3 12.6 %collective-permute-start.9 = (bf16[4,32,256]{2,1,0:T(8,128)(2,1)S(1)}, bf16[4,32,256]{2,1,0:T(8,128)(2,1)S(1)}, u32[]{:S(2)}, u32[]{:S(2)}) collective-permute-start(bf16[4,32,256]{2,1,0:T(8,128)(2,1)S(1)} %bitcast.346), channel_id=1, source_target_pairs={{0,1},{1,0},{2,3},{3,2},{4,5},{5,4},{6,7},{7,6},{8,9},{9,8},{10,11... | collective-permute-start | bytes 196616 | tf_op jit(solution)/shard_map/ppermute | solution.py:496
  29.4 8.1 %collective-permute-start.13 = (bf16[2,64,512]{2,1,0:T(8,128)(2,1)S(1)}, bf16[2,64,512]{2,1,0:T(8,128)(2,1)S(1)}, u32[]{:S(2)}, u32[]{:S(2)}) collective-permute-start(bf16[2,64,512]{2,1,0:T(8,128)(2,1)S(1)} %get-tuple-element.91), channel_id=1, source_target_pairs={{0,8},{2,10},{4,12},{6,14},{8,0},{10,2},{12,4},{14,6},{16,24},{18,... | collective-permute-start | bytes 393224 | tf_op jit(solution)/shard_map/ppermute | solution.py:496
  29.9 8.2 %collective-permute-start.18 = (bf16[2,64,512]{2,1,0:T(8,128)(2,1)S(1)}, bf16[2,64,512]{2,1,0:T(8,128)(2,1)S(1)}, u32[]{:S(2)}, u32[]{:S(2)}) collective-permute-start(bf16[2,64,512]{2,1,0:T(8,128)(2,1)S(1)} %get-tuple-element.89), channel_id=1, source_target_pairs={{0,8},{2,10},{4,12},{6,14},{8,0},{10,2},{12,4},{14,6},{16,24},{18,... | collective-permute-start | bytes 393224 | tf_op jit(solution)/shard_map/ppermute | solution.py:496
  33.6 10.1 %collective-permute-start.3 = (bf16[8,3,32,256]{3,2,1,0:T(8,128)(2,1)S(1)}, bf16[8,3,32,256]{3,2,1,0:T(8,128)(2,1)S(1)}, u32[]{:S(2)}, u32[]{:S(2)}) collective-permute-start(bf16[8,3,32,256]{3,2,1,0:T(8,128)(2,1)S(1)} %bitcast.335), channel_id=1, source_target_pairs={{0,1},{1,0},{2,3},{3,2},{4,5},{5,4},{6,7},{7,6},{8,9},{9,8},{10,11... | collective-permute-start | bytes 1179656 | tf_op jit(solution)/shard_map/ppermute | solution.py:496
  38.1 8.7 %collective-permute-start.19 = (bf16[4,64,512]{2,1,0:T(8,128)(2,1)S(1)}, bf16[4,64,512]{2,1,0:T(8,128)(2,1)S(1)}, u32[]{:S(2)}, u32[]{:S(2)}) collective-permute-start(bf16[4,64,512]{2,1,0:T(8,128)(2,1)S(1)} %bitcast.338), channel_id=1, source_target_pairs={{0,1},{1,0},{2,3},{3,2},{4,5},{5,4},{6,7},{7,6},{8,9},{9,8},{10,11... | collective-permute-start | bytes 786440 | tf_op jit(solution)/shard_map/ppermute | solution.py:496
  45.3 30.6 %collective-permute-start.15 = (bf16[8,64,512]{2,1,0:T(8,128)(2,1)}, bf16[8,64,512]{2,1,0:T(8,128)(2,1)}, u32[]{:S(2)}, u32[]{:S(2)}) collective-permute-start(bf16[8,64,512]{2,1,0:T(8,128)(2,1)} %bitcast.54), channel_id=1, source_target_pairs={{0,1},{1,0},{2,3},{3,2},{4,5},{5,4},{6,7},{7,6},{8,9},{9,8},{10,11... | collective-permute-start | bytes 1572872 | tf_op jit(solution)/shard_map/ppermute | solution.py:496
  47.9 31.8 %collective-permute-start.20 = (bf16[8,64,512]{2,1,0:T(8,128)(2,1)}, bf16[8,64,512]{2,1,0:T(8,128)(2,1)}, u32[]{:S(2)}, u32[]{:S(2)}) collective-permute-start(bf16[8,64,512]{2,1,0:T(8,128)(2,1)} %bitcast.70), channel_id=1, source_target_pairs={{0,4},{2,6},{4,0},{6,2},{8,12},{10,14},{12,8},{14,10},{16,20},{18,... | collective-permute-start | bytes 1572872 | tf_op jit(solution)/shard_map/ppermute | solution.py:496
  72.1 11.8 %collective-permute-start.6 = (bf16[4,128,384]{2,1,0:T(8,128)(2,1)S(1)}, bf16[4,128,384]{2,1,0:T(8,128)(2,1)S(1)}, u32[]{:S(2)}, u32[]{:S(2)}) collective-permute-start(bf16[4,128,384]{2,1,0:T(8,128)(2,1)S(1)} %convert_element_type.298), channel_id=1, source_target_pairs={{0,1},{2,3},{4,5},{6,7},{8,9},{10,11},{12,13},{14,15},{16,17},{18,... | collective-permute-start | bytes 1179656 | tf_op jit(solution)/shard_map/ppermute | solution.py:589
  77.2 44.4 %collective-permute-start.16 = (bf16[16,64,512]{2,1,0:T(8,128)(2,1)S(1)}, bf16[16,64,512]{2,1,0:T(8,128)(2,1)S(1)}, u32[]{:S(2)}, u32[]{:S(2)}) collective-permute-start(bf16[16,64,512]{2,1,0:T(8,128)(2,1)S(1)} %bitcast.310), channel_id=1, source_target_pairs={{0,2},{2,0},{4,6},{6,4},{8,10},{10,8},{12,14},{14,12},{16,18},{18,... | collective-permute-start | bytes 3145736 | tf_op jit(solution)/shard_map/ppermute | solution.py:496
  80.9 40.9 %collective-permute-start.21 = (bf16[16,64,512]{2,1,0:T(8,128)(2,1)S(1)}, bf16[16,64,512]{2,1,0:T(8,128)(2,1)}, u32[]{:S(2)}, u32[]{:S(2)}) collective-permute-start(bf16[16,64,512]{2,1,0:T(8,128)(2,1)S(1)} %bitcast.312), channel_id=1, source_target_pairs={{0,2},{2,0},{4,6},{6,4},{8,10},{10,8},{12,14},{14,12},{16,18},{18,... | collective-permute-start | bytes 3145736 | tf_op jit(solution)/shard_map/ppermute | solution.py:496
  174.7 17.7 %collective-permute-start.39 = (f32[1,536]{1,0:T(1,128)S(1)}, f32[1,536]{1,0:T(1,128)S(1)}, u32[]{:S(2)}, u32[]{:S(2)}) collective-permute-start(f32[1,536]{1,0:T(1,128)S(1)} %broadcast_in_dim.85), channel_id=1, source_target_pairs={{0,16},{2,18},{4,20},{6,22},{8,24},{10,26},{12,28},{14,30},{16,0},... | collective-permute-start | bytes 6440 | tf_op jit(solution)/shard_map/ppermute | solution.py:496
  196.0 19.6 %collective-permute-start.41 = (f32[1,536]{1,0:T(1,128)S(1)}, f32[1,536]{1,0:T(1,128)S(1)}, u32[]{:S(2)}, u32[]{:S(2)}) collective-permute-start(f32[1,536]{1,0:T(1,128)S(1)} %add.246), channel_id=1, source_target_pairs={{0,1},{1,0},{2,3},{3,2},{4,5},{5,4},{6,7},{7,6},{8,9},{9,8},{10,11... | collective-permute-start | bytes 6440 | tf_op jit(solution)/shard_map/ppermute | solution.py:496
  213.6 136.1 %collective-permute-start.49 = (bf16[1,16,64,512]{3,2,1,0:T(8,128)(2,1)}, bf16[1,16,64,512]{3,2,1,0:T(8,128)(2,1)}, u32[]{:S(2)}, u32[]{:S(2)}) collective-permute-start(bf16[1,16,64,512]{3,2,1,0:T(8,128)(2,1)} %fusion.27), channel_id=1, source_target_pairs={{0,2},{2,0},{4,6},{6,4},{8,10},{10,8},{12,14},{14,12},{16,18},{18,... | collective-permute-start | bytes 3145736 | tf_op jit(solution)/shard_map/ppermute | solution.py:496
  219.7 11.5 %collective-permute-start.34 = (bf16[2,2,2,2,32,256]{5,4,3,2,1,0:T(8,128)(2,1)}, bf16[2,2,2,2,32,256]{5,4,3,2,1,0:T(8,128)(2,1)}, u32[]{:S(2)}, u32[]{:S(2)}) collective-permute-start(bf16[2,2,2,2,32,256]{5,4,3,2,1,0:T(8,128)(2,1)} %fusion.42), channel_id=1, source_target_pairs={{0,2},{2,0},{4,6},{6,4},{8,10},{10,8},{12,14},{14,12},{16,18},{18,... | collective-permute-start | bytes 786440 | tf_op jit(solution)/shard_map/ppermute | solution.py:496
  220.6 8.1 %collective-permute-start.43 = (f32[1,536]{1,0:T(1,128)S(1)}, f32[1,536]{1,0:T(1,128)S(1)}, u32[]{:S(2)}, u32[]{:S(2)}) collective-permute-start(f32[1,536]{1,0:T(1,128)S(1)} %add.248), channel_id=1, source_target_pairs={{0,2},{2,0},{4,6},{6,4},{8,10},{10,8},{12,14},{14,12},{16,18},{18,... | collective-permute-start | bytes 6440 | tf_op jit(solution)/shard_map/ppermute | solution.py:496
  223.4 130.8 %collective-permute-start.44 = (bf16[1,16,64,512]{3,2,1,0:T(8,128)(2,1)}, bf16[1,16,64,512]{3,2,1,0:T(8,128)(2,1)}, u32[]{:S(2)}, u32[]{:S(2)}) collective-permute-start(bf16[1,16,64,512]{3,2,1,0:T(8,128)(2,1)} %fusion.26), channel_id=1, source_target_pairs={{0,2},{2,0},{4,6},{6,4},{8,10},{10,8},{12,14},{14,12},{16,18},{18,... | collective-permute-start | bytes 3145736 | tf_op jit(solution)/shard_map/ppermute | solution.py:496
  224.8 15.9 %collective-permute-start.22 = (bf16[4,128,384]{2,1,0:T(8,128)(2,1)}, bf16[4,128,384]{2,1,0:T(8,128)(2,1)S(1)}, u32[]{:S(2)}, u32[]{:S(2)}) collective-permute-start(bf16[4,128,384]{2,1,0:T(8,128)(2,1)} %convert_element_type.306), channel_id=1, source_target_pairs={{1,0},{3,2},{5,4},{7,6},{9,8},{11,10},{13,12},{15,14},{17,16},{19,... | collective-permute-start | bytes 1179656 | tf_op jit(solution)/shard_map/ppermute | solution.py:589
  228.6 12.1 %collective-permute-start.23 = (f32[2,32,512]{2,1,0:T(8,128)}, f32[2,32,512]{2,1,0:T(8,128)S(1)}, u32[]{:S(2)}, u32[]{:S(2)}) collective-permute-start(f32[2,32,512]{2,1,0:T(8,128)} %get-tuple-element.27), channel_id=1, source_target_pairs={{1,0},{3,2},{5,4},{7,6},{9,8},{11,10},{13,12},{15,14},{17,16},{19,... | collective-permute-start | bytes 393224 | tf_op jit(solution)/shard_map/ppermute | solution.py:724
  232.3 84.9 %collective-permute-start.35 = (bf16[2,2,2,32,256]{4,3,2,1,0:T(8,128)(2,1)S(1)}, bf16[2,2,2,32,256]{4,3,2,1,0:T(8,128)(2,1)S(1)}, u32[]{:S(2)}, u32[]{:S(2)}) collective-permute-start(bf16[2,2,2,32,256]{4,3,2,1,0:T(8,128)(2,1)S(1)} %fusion.50), channel_id=1, source_target_pairs={{0,4},{2,6},{4,0},{6,2},{8,12},{10,14},{12,8},{14,10},{16,20},{18,... | collective-permute-start | bytes 393224 | tf_op jit(solution)/shard_map/ppermute | solution.py:496
  314.2 14.4 %collective-permute-start.24 = (f32[1,512]{1,0:T(1,128)S(1)}, f32[1,512]{1,0:T(1,128)S(1)}, u32[]{:S(2)}, u32[]{:S(2)}) collective-permute-start(f32[1,512]{1,0:T(1,128)S(1)} %bitcast.360), channel_id=1, source_target_pairs={{0,16},{2,18},{4,20},{6,22},{8,24},{10,26},{12,28},{14,30},{16,0},... | collective-permute-start | bytes 6152 | tf_op jit(solution)/shard_map/ppermute | solution.py:496
  317.2 20.7 %collective-permute-start.36 = (bf16[2,2,32,256]{3,2,1,0:T(8,128)(2,1)S(1)}, bf16[2,2,32,256]{3,2,1,0:T(8,128)(2,1)S(1)}, u32[]{:S(2)}, u32[]{:S(2)}) collective-permute-start(bf16[2,2,32,256]{3,2,1,0:T(8,128)(2,1)S(1)} %fusion.62), channel_id=1, source_target_pairs={{0,1},{1,0},{2,3},{3,2},{4,5},{5,4},{6,7},{7,6},{8,9},{9,8},{10,11... | collective-permute-start | bytes 196616 | tf_op jit(solution)/shard_map/ppermute | solution.py:496
  330.4 25.6 %collective-permute-start.29 = (bf16[2,2,2,2,3,32,256]{6,5,4,3,2,1,0:T(8,128)(2,1)S(1)}, bf16[2,2,2,2,3,32,256]{6,5,4,3,2,1,0:T(8,128)(2,1)S(1)}, u32[]{:S(2)}, u32[]{:S(2)}) collective-permute-start(bf16[2,2,2,2,3,32,256]{6,5,4,3,2,1,0:T(8,128)(2,1)S(1)} %fusion.31), channel_id=1, source_target_pairs={{0,2},{2,0},{4,6},{6,4},{8,10},{10,8},{12,14},{14,12},{16,18},{18,... | collective-permute-start | bytes 2359304 | tf_op jit(solution)/shard_map/ppermute | solution.py:496
  339.5 9.0 %collective-permute-start.28 = (f32[1,512]{1,0:T(1,128)S(1)}, f32[1,512]{1,0:T(1,128)S(1)}, u32[]{:S(2)}, u32[]{:S(2)}) collective-permute-start(f32[1,512]{1,0:T(1,128)S(1)} %add.223), channel_id=1, source_target_pairs={{0,2},{2,0},{4,6},{6,4},{8,10},{10,8},{12,14},{14,12},{16,18},{18,... | collective-permute-start | bytes 6152 | tf_op jit(solution)/shard_map/ppermute | solution.py:496
  352.1 12.2 %collective-permute-start.50 = (bf16[2,4,64,512]{3,2,1,0:T(8,128)(2,1)S(1)}, bf16[2,4,64,512]{3,2,1,0:T(8,128)(2,1)S(1)}, u32[]{:S(2)}, u32[]{:S(2)}) collective-permute-start(bf16[2,4,64,512]{3,2,1,0:T(8,128)(2,1)S(1)} %fusion.38), channel_id=1, source_target_pairs={{0,4},{2,6},{4,0},{6,2},{8,12},{10,14},{12,8},{14,10},{16,20},{18,... | collective-permute-start | bytes 1572872 | tf_op jit(solution)/shard_map/ppermute | solution.py:496
  355.9 24.3 %collective-permute-start.45 = (bf16[1,8,64,512]{3,2,1,0:T(8,128)(2,1)S(1)}, bf16[1,8,64,512]{3,2,1,0:T(8,128)(2,1)S(1)}, u32[]{:S(2)}, u32[]{:S(2)}) collective-permute-start(bf16[1,8,64,512]{3,2,1,0:T(8,128)(2,1)S(1)} %fusion.37), channel_id=1, source_target_pairs={{0,1},{1,0},{2,3},{3,2},{4,5},{5,4},{6,7},{7,6},{8,9},{9,8},{10,11... | collective-permute-start | bytes 1572872 | tf_op jit(solution)/shard_map/ppermute | solution.py:496
  356.4 22.7 %collective-permute-start.30 = (bf16[2,2,2,3,32,256]{5,4,3,2,1,0:T(8,128)(2,1)S(1)}, bf16[2,2,2,3,32,256]{5,4,3,2,1,0:T(8,128)(2,1)S(1)}, u32[]{:S(2)}, u32[]{:S(2)}) collective-permute-start(bf16[2,2,2,3,32,256]{5,4,3,2,1,0:T(8,128)(2,1)S(1)} %fusion.41), channel_id=1, source_target_pairs={{0,1},{1,0},{2,3},{3,2},{4,5},{5,4},{6,7},{7,6},{8,9},{9,8},{10,11... | collective-permute-start | bytes 1179656 | tf_op jit(solution)/shard_map/ppermute | solution.py:496
  364.6 21.0 %collective-permute-start.51 = (bf16[1,4,64,512]{3,2,1,0:T(8,128)(2,1)S(1)}, bf16[1,4,64,512]{3,2,1,0:T(8,128)(2,1)S(1)}, u32[]{:S(2)}, u32[]{:S(2)}) collective-permute-start(bf16[1,4,64,512]{3,2,1,0:T(8,128)(2,1)S(1)} %fusion.44), channel_id=1, source_target_pairs={{0,1},{1,0},{2,3},{3,2},{4,5},{5,4},{6,7},{7,6},{8,9},{9,8},{10,11... | collective-permute-start | bytes 786440 | tf_op jit(solution)/shard_map/ppermute | solution.py:496
  385.7 11.8 %collective-permute-start.52 = (bf16[1,2,64,512]{3,2,1,0:T(8,128)(2,1)S(1)}, bf16[1,2,64,512]{3,2,1,0:T(8,128)(2,1)S(1)}, u32[]{:S(2)}, u32[]{:S(2)}) collective-permute-start(bf16[1,2,64,512]{3,2,1,0:T(8,128)(2,1)S(1)} %fusion.52), channel_id=1, source_target_pairs={{0,8},{2,10},{4,12},{6,14},{8,0},{10,2},{12,4},{14,6},{16,24},{18,... | collective-permute-start | bytes 393224 | tf_op jit(solution)/shard_map/ppermute | solution.py:496
  (57 other events, 494.4 us)

commit v2 on v1

--- a/solution.py
+++ b/solution.py
@@ -97,43 +97,119 @@
     return mm(jnp.concatenate([high, low], axis=1), table.astype(BF16))
 
 
-def load_keys(qkv_ref, tail_ref, keys, values):
+def load_keys(qkv_ref, message_ref, keys, values):
     rows = qkv_ref.shape[1]
-    keys[pl.ds(0, TAIL), :] = tail_ref[0]
+    keys[pl.ds(0, TAIL), :] = message_ref[0, pl.ds(HEAD_DIM, TAIL), :PAIR]
     keys[pl.ds(TAIL, rows), :] = qkv_ref[1]
-    values[pl.ds(0, TAIL), :] = tail_ref[1]
+    values[pl.ds(0, TAIL), :] = message_ref[0, pl.ds(HEAD_DIM, TAIL), PAIR : 2 * PAIR]
     values[pl.ds(TAIL, rows), :] = qkv_ref[2]
 
 
-def ends_kernel(scalars, qkv_ref, out_ref):
-    rows = qkv_ref.shape[1]
-    step_rows = rows // 4
-    last = jnp.maximum(scalars[scalars.shape[0] - 2], 0)
-    out_ref[0] = jnp.zeros(out_ref.shape[1:], F32)
-
-    def body(step, carry):
-        at = pl.multiple_of(step * step_rows, 16)
-        key = qkv_ref[1, pl.ds(at, step_rows), :].astype(F32)
-        value = qkv_ref[2, pl.ds(at, step_rows), :]
-        live = iota((step_rows, PAIR), 0) + at >= last
+def fold_state(wide):
+    kept = block_only(wide)
+    return (kept[:HEAD_DIM] + kept[HEAD_DIM:]).astype(BF16)
+
+
+def unfold_state(message):
+    half = message[:HEAD_DIM].astype(F32)
+    return block_only(jnp.concatenate([half, half], axis=0))
+
+
+def project_kernel(
+    scalars,
+    tokens_ref,
+    gain_ref,
+    shards_ref,
+    qkv_ref,
+    normed_ref,
+    weight_ref,
+    out_weight_ref,
+    message_ref,
+    state,
+    *,
+    spots,
+):
+    step = pl.program_id(0)
+    rows, width = tokens_ref.shape
+    pairs = width // PAIR
+    tall, wide = shards_ref.shape[2:]
+    last = jnp.maximum(scalars[scalars.shape[0] - 3], 0)
+    me = scalars[scalars.shape[0] - 1]
+
+    @pl.when(step == 0)
+    def _():
+        for d, h, spot in spots:
+            piece = shards_ref[me ^ spot]
+            at = (pl.ds(d * tall, tall), pl.ds(h * wide, wide))
+            weight_ref[(slice(None),) + at] = piece[:3]
+            out_weight_ref[at] = piece[3]
+        state[...] = jnp.zeros(state.shape, F32)
+
+    normed = (norm_parts(tokens_ref[...].astype(F32))[0] * gain_ref[...]).astype(BF16)
+    normed_ref[...] = normed
+    for c in range(3):
+        qkv_ref[c] = mm(normed, weight_ref[c]).astype(BF16)
+    live = iota((rows, PAIR), 0) + step * rows >= last
+    ones = jnp.ones((rows, PAIR), BF16)
+    for p in range(pairs):
+        at = pl.ds(p * PAIR, PAIR)
+        key = qkv_ref[1, :, at].astype(F32)
+        value = qkv_ref[2, :, at]
         lifted = jnp.where(live, lift(key), 0.0).astype(BF16)
         bent = jnp.where(live, jnp.tanh(key), 0.0).astype(BF16)
-        ones = jnp.ones((step_rows, PAIR), BF16)
-        out_ref[0, :, : 2 * PAIR] += mm(lifted, jnp.concatenate([value, ones], axis=1), TN)
-        out_ref[0, :, 2 * PAIR :] += mm(bent, value, TN)
-        return carry
-
-    lax.fori_loop(0, 4, body, 0)
-    out_ref[0] = block_only(out_ref[0])
+        state[p, :, : 2 * PAIR] += mm(lifted, jnp.concatenate([value, ones], axis=1), TN)
+        state[p, :, 2 * PAIR :] += mm(bent, value, TN)
+
+    @pl.when(step == pl.num_programs(0) - 1)
+    def _():
+        for p in range(pairs):
+            at = pl.ds(p * PAIR, PAIR)
+            message_ref[p, pl.ds(0, HEAD_DIM), :] = fold_state(state[p])
+            message_ref[p, pl.ds(HEAD_DIM, TAIL), :] = jnp.concatenate(
+                [
+                    qkv_ref[1, pl.ds(rows - TAIL, TAIL), at],
+                    qkv_ref[2, pl.ds(rows - TAIL, TAIL), at],
+                    jnp.zeros((TAIL, PAIR), BF16),
+                ],
+                axis=1,
+            )
+
+
+def weight_grad_kernel(
+    scalars, normed_ref, d_qkv_ref, out_grad_ref, keep_ref, give_ref, whole, *, spots, n_head
+):
+    c = pl.program_id(0)
+    me = scalars[scalars.shape[0] - 1]
+    tall, wide = keep_ref.shape[2:]
+    half = keep_ref.shape[0]
+
+    @pl.when(c < 3)
+    def _():
+        whole[...] = mm(normed_ref[...], d_qkv_ref[0], TN).reshape(whole.shape)
+
+    @pl.when(c == 3)
+    def _():
+        whole[...] = out_grad_ref[...].reshape(whole.shape)
+
+    for d, h, spot in spots:
+        index = me ^ spot
+        value = whole[d, :, pl.ds(h * wide, wide)]
+
+        @pl.when(index < half)
+        def _():
+            keep_ref[index, 0] = value
+
+        @pl.when(index >= half)
+        def _():
+            give_ref[index - half, 0] = value.astype(BF16)
 
 
 def forward_kernel(
     scalars,
     qkv_ref,
-    tail_ref,
+    message_ref,
     start_ref,
     blend_ref,
-    state_in_ref,
     att_ref,
     near_ref,
     far1_ref,
@@ -146,9 +222,9 @@
     state,
 ):
     rows = qkv_ref.shape[1]
-    load_keys(qkv_ref, tail_ref, keys, values)
-    state[...] = state_in_ref[0].astype(F32)
-    count_valid = scalars[scalars.shape[0] - 1]
+    load_keys(qkv_ref, message_ref, keys, values)
+    state[...] = unfold_state(message_ref[0])
+    count_valid = scalars[scalars.shape[0] - 2]
     b0, b1, b2 = (blend_ref[pl.ds(f, 1), :] for f in range(3))
 
     def body(step, carry):
@@ -216,7 +292,7 @@
 def prologue_kernel(
     scalars,
     qkv_ref,
-    tail_ref,
+    message_ref,
     start_ref,
     blend_ref,
     grad_ref,
@@ -225,19 +301,20 @@
     far2_ref,
     invl_ref,
     invd_ref,
-    adjoint_ref,
-    tail_grad_ref,
+    back_ref,
     sums_ref,
+    adjoint,
 ):
     rows = qkv_ref.shape[1]
-    count_valid = scalars[scalars.shape[0] - 1]
+    count_valid = scalars[scalars.shape[0] - 2]
     b0, b1, b2 = (blend_ref[pl.ds(f, 1), :] for f in range(3))
-    adjoint_ref[0] = jnp.zeros(adjoint_ref.shape[1:], F32)
+    adjoint[...] = jnp.zeros(adjoint.shape, F32)
     sums_ref[...] = jnp.zeros(sums_ref.shape, F32)
     lanes = iota((ROWS, PAIR), 1) < HEAD_DIM
 
-    key = jnp.concatenate([tail_ref[0], qkv_ref[1, pl.ds(0, ROWS), :]], axis=0)
-    value = jnp.concatenate([tail_ref[1], qkv_ref[2, pl.ds(0, ROWS), :]], axis=0)
+    tails = message_ref[0, pl.ds(HEAD_DIM, TAIL), :]
+    key = jnp.concatenate([tails[:, :PAIR], qkv_ref[1, pl.ds(0, ROWS), :]], axis=0)
+    value = jnp.concatenate([tails[:, PAIR : 2 * PAIR], qkv_ref[2, pl.ds(0, ROWS), :]], axis=0)
     start = start_ref[pl.ds(0, ROWS), :]
     near_mask, _, _, row, _, _ = masks(0, start)
     query = qkv_ref[0, pl.ds(0, ROWS), :]
@@ -256,8 +333,9 @@
         rows_q,
         rows_g,
     )
-    tail_grad_ref[0] = d_key[:TAIL]
-    tail_grad_ref[1] = fold(mm(weights, rows_g, TN))[:TAIL]
+    back_ref[0, pl.ds(HEAD_DIM, TAIL), :] = jnp.concatenate(
+        [d_key[:TAIL], fold(mm(weights, rows_g, TN))[:TAIL], jnp.zeros((TAIL, PAIR), F32)], axis=1
+    ).astype(BF16)
 
     def body(step, carry):
         at = pl.multiple_of(step * ROWS, 32)
@@ -274,7 +352,7 @@
             (grad_f * far2_ref[pl.ds(at, ROWS), :]).reshape(ROWS // 8, 8, PAIR), axis=0
         )
 
-        @pl.when(scalars[scalars.shape[0] - 3] > at)
+        @pl.when(scalars[scalars.shape[0] - 4] > at)
         def _():
             wide = spread(far1)
             along = jnp.where(lanes, wide[:, :WIN], wide[:, WIN:]).astype(BF16)
@@ -284,15 +362,15 @@
             bent = jnp.where(
                 live, jnp.tanh(query_f) * (b2 / (row - start + 1).astype(F32)), 0.0
             )
-            adjoint_ref[0, :, : 2 * PAIR] += mm(
+            adjoint[:, : 2 * PAIR] += mm(
                 scaled.astype(BF16), jnp.concatenate([grad, along], axis=1), TN
             )
-            adjoint_ref[0, :, 2 * PAIR :] += mm(bent.astype(BF16), grad, TN)
+            adjoint[:, 2 * PAIR :] += mm(bent.astype(BF16), grad, TN)
 
         return carry
 
     lax.fori_loop(0, rows // ROWS, body, 0)
-    adjoint_ref[0] = block_only(adjoint_ref[0])
+    back_ref[0, pl.ds(0, HEAD_DIM), :] = fold_state(adjoint[...])
 
 
 def key_side(adjoint_low, lift_k, bend_k, value):
@@ -307,7 +385,7 @@
 def backward_kernel(
     scalars,
     qkv_ref,
-    tail_ref,
+    message_ref,
     start_ref,
     blend_ref,
     grad_ref,
@@ -316,8 +394,8 @@
     invl_ref,
     invd_ref,
     states_ref,
-    adjoint_in_ref,
-    tail_grad_ref,
+    back_ref,
+    done_ref,
     out_ref,
     keys,
     values,
@@ -327,25 +405,26 @@
 ):
     rows = qkv_ref.shape[1]
     steps = rows // ROWS
-    load_keys(qkv_ref, tail_ref, keys, values)
-    count_valid = scalars[scalars.shape[0] - 1]
-    last = scalars[scalars.shape[0] - 2]
+    load_keys(qkv_ref, message_ref, keys, values)
+    count_valid = scalars[scalars.shape[0] - 2]
+    last = scalars[scalars.shape[0] - 3]
     b0, b1, b2 = (blend_ref[pl.ds(f, 1), :] for f in range(3))
     lanes = iota((ROWS, PAIR), 1) < HEAD_DIM
 
-    arrived = adjoint_in_ref[0].astype(F32)
+    arrived = unfold_state(back_ref[0])
+    tail_grads = back_ref[0, pl.ds(HEAD_DIM, TAIL), :].astype(F32)
     end_key = keys[pl.ds(rows, TAIL), :].astype(F32)
     end_lift, end_bend = lift(end_key), jnp.tanh(end_key)
     end_parts = key_side(
         arrived.astype(BF16), end_lift.astype(BF16), end_bend.astype(BF16), values[pl.ds(rows, TAIL), :]
     )
     live = iota((TAIL, PAIR), 0) + (rows - TAIL) >= last
-    key_carry[...] = tail_grad_ref[0] + jnp.where(
+    key_carry[...] = tail_grads[:, :PAIR] + jnp.where(
         live,
         end_parts[0] * jnp.minimum(end_lift, 1.0) + end_parts[1] * (1.0 - end_bend * end_bend),
         0.0,
     )
-    value_carry[...] = tail_grad_ref[1] + jnp.where(live, end_parts[2], 0.0)
+    value_carry[...] = tail_grads[:, PAIR : 2 * PAIR] + jnp.where(live, end_parts[2], 0.0)
     adjoint[...] = jnp.where(last < rows - TAIL, 1.0, 0.0) * arrived
 
     def body(back, carry):
@@ -440,31 +519,30 @@
     lax.fori_loop(0, steps, body, 0)
 
 
-def pair_specs(rows):
-    column = pl.BlockSpec((rows, PAIR), lambda p, s: (0, p))
+def pair_specs(rows, first=0):
     return {
-        "qkv": pl.BlockSpec((3, rows, PAIR), lambda p, s: (0, 0, p)),
-        "tail": pl.BlockSpec((2, TAIL, PAIR), lambda p, s: (0, 0, p)),
+        "qkv": pl.BlockSpec((3, rows, PAIR), lambda p, s: (0, 0, p + first)),
+        "message": pl.BlockSpec((1, HEAD_DIM + TAIL, 3 * PAIR), lambda p, s: (p + first, 0, 0)),
         "start": pl.BlockSpec((rows, PAIR), lambda p, s: (0, 0)),
-        "blend": pl.BlockSpec((3, PAIR), lambda p, s: (0, p)),
-        "column": column,
-        "state": pl.BlockSpec((1, PAIR, 3 * PAIR), lambda p, s: (p, 0, 0)),
-        "states": pl.BlockSpec((1, rows // ROWS * PAIR, 3 * PAIR), lambda p, s: (p, 0, 0)),
-        "sums": pl.BlockSpec((24, PAIR), lambda p, s: (0, p)),
+        "blend": pl.BlockSpec((3, PAIR), lambda p, s: (0, p + first)),
+        "column": pl.BlockSpec((rows, PAIR), lambda p, s: (0, p + first)),
+        "states": pl.BlockSpec((1, rows // ROWS * PAIR, 3 * PAIR), lambda p, s: (p + first, 0, 0)),
+        "sums": pl.BlockSpec((24, PAIR), lambda p, s: (0, p + first)),
     }
 
 
-def call(kernel, ins, outs, out_shapes, scratch, pairs, name, flops, moved):
+def call(kernel, ins, outs, out_shapes, scratch, grid, name, flops, moved, aliases={}):
     return pl.pallas_call(
         kernel,
         out_shape=out_shapes,
         grid_spec=pltpu.PrefetchScalarGridSpec(
             num_scalar_prefetch=1,
-            grid=(pairs,),
+            grid=(grid,),
             in_specs=ins,
             out_specs=outs,
             scratch_shapes=scratch,
         ),
+        input_output_aliases=aliases,
         compiler_params=pltpu.CompilerParams(
             dimension_semantics=("arbitrary",), vmem_limit_bytes=56 * 1024 * 1024
         ),
@@ -491,101 +569,73 @@
     return [1 << b for b in range(int(math.log2(size)))]
 
 
-def swap(array, axis, mask):
-    size = lax.axis_size(axis)
-    return lax.ppermute(array, axis, [(i, i ^ mask) for i in range(size)])
-
-
-def orders():
+def phases():
     dp = bits(lax.axis_size("dp"))
     core, rest = dp[:1], dp[1:]
     mid = len(rest) // 2
-    y = [("dp", m) for m in rest[:mid]]
-    z = [("dp", m) for m in reversed(rest[mid:])]
-    x = [("head", m) for m in bits(lax.axis_size("head"))]
-    core = [("dp", m) for m in core]
-    return z + y + x + core, z + x + y + core
-
-
-def my_bit(axis, mask):
-    return (lax.axis_index(axis) & mask) > 0
-
-
-def slot(order, axis, mask):
-    main = orders()[0]
-    here = main.index((axis, mask))
-    return sum(1 for pair in order if main.index(pair) < here)
-
-
-def gather_relative(shard, order):
-    block = shard[None]
-    for step, (axis, mask) in enumerate(order):
-        inner = 1 << slot(order[:step], axis, mask)
-        other = swap(block, axis, mask)
-        shape = (block.shape[0] // inner, 1, inner) + shard.shape
-        block = jnp.concatenate([block.reshape(shape), other.reshape(shape)], axis=1)
-        block = block.reshape((-1,) + shard.shape)
-    return block.reshape((-1,) + shard.shape[1:])
-
-
-def scatter_relative(total, order):
-    block = total.reshape((1 << len(order), -1) + total.shape[1:])
-    for step in reversed(range(len(order))):
-        axis, mask = order[step]
-        inner = 1 << slot(order[:step], axis, mask)
-        block = block.reshape((-1, 2, inner) + block.shape[1:])
-        give = block[:, 1].astype(BF16)
-        block = block[:, 0] + swap(give, axis, mask).astype(F32)
-        block = block.reshape((-1,) + block.shape[2:])
-    return block[0]
-
-
-def gather_absolute(shard, order):
-    block = shard[None]
-    for axis, mask in order:
-        other = swap(block, axis, mask)
-        mine = my_bit(axis, mask)
-        block = jnp.stack([jnp.where(mine, other, block), jnp.where(mine, block, other)])
-        block = block.reshape((-1,) + shard.shape)
-    sizes = (2,) * len(order)
-    block = block.reshape(sizes + shard.shape)
-    stacked = list(reversed(order))
-    dp = [stacked.index(("dp", m)) for m in reversed(bits(lax.axis_size("dp")))]
-    head = [stacked.index(("head", m)) for m in reversed(bits(lax.axis_size("head")))]
-    rest = [len(order) + d for d in range(shard.ndim)]
-    block = jnp.transpose(block, dp + head + rest)
-    return block.reshape((lax.axis_size("dp"), lax.axis_size("head")) + shard.shape)
-
-
-def scatter_absolute(total, order):
+    far = [("dp", m) for m in rest[mid:]]
+    near = [("dp", m) for m in rest[:mid]] + [("head", m) for m in bits(lax.axis_size("head"))]
+    groups = []
+    for run in (far, near, [("dp", m) for m in core]):
+        groups += [run[i : i + 2] for i in range(0, len(run), 2)]
+    return groups
+
+
+def relative_bits():
+    return [pair for group in phases() for pair in group]
+
+
+def relative_index(dp_index, head_index):
+    index = 0
+    for place, (axis, mask) in enumerate(relative_bits()):
+        own = dp_index if axis == "dp" else head_index
+        index = index | (((own // mask) & 1) << place)
+    return index
+
+
+def peer(array, group, combo):
     n_dp, n_head = lax.axis_size("dp"), lax.axis_size("head")
-    dp_bits = list(reversed(bits(n_dp)))
-    head_bits = list(reversed(bits(n_head)))
-    shard = total.shape[2:]
-    block = total.reshape((2,) * (len(dp_bits) + len(head_bits)) + shard)
-    left = [("dp", m) for m in dp_bits] + [("head", m) for m in head_bits]
-    for axis, mask in reversed(order):
-        at = left.index((axis, mask))
-        mine = my_bit(axis, mask).astype(jnp.int32)
-        keep = lax.dynamic_index_in_dim(block, mine, at, keepdims=False)
-        give = lax.dynamic_index_in_dim(block, 1 - mine, at, keepdims=False)
-        block = keep + swap(give.astype(BF16), axis, mask).astype(F32)
-        left.pop(at)
-    return block
-
-
-def sum_everywhere(array, order):
-    for axis, mask in order:
-        array = array + swap(array, axis, mask)
+    chosen = [pair for place, pair in enumerate(group) if combo >> place & 1]
+    flip_dp = sum(m for axis, m in chosen if axis == "dp")
+    flip_head = sum(m for axis, m in chosen if axis == "head")
+    pairs = [
+        (d * n_head + h, (d ^ flip_dp) * n_head + (h ^ flip_head))
+        for d in range(n_dp)
+        for h in range(n_head)
+    ]
+    return lax.ppermute(array, ("dp", "head"), pairs)
+
+
+def widen(block, group, axis):
+    others = [peer(block, group, combo) for combo in range(1, 1 << len(group))]
+    return jnp.concatenate([block] + others, axis=axis)
+
+
+def narrow(keep, gives, group):
+    total = keep.astype(F32)
+    for combo, give in enumerate(gives, 1):
+        total = total + peer(give.astype(BF16), group, combo).astype(F32)
+    return total
+
+
+def narrow_axis(total, group, axis):
+    parts = jnp.split(total, 1 << len(group), axis=axis)
+    return narrow(parts[0], parts[1:], group)
+
+
+def sum_everywhere(array):
+    for group in reversed(phases()):
+        array = array + sum(peer(array, group, combo) for combo in range(1, 1 << len(group)))
     return array
 
 
 def pass_along(local, keep, shift):
     size = lax.axis_size("head")
     pairs = [(i, i + shift) for i in range(size) if 0 <= i + shift < size]
-    arrived = None
-    for _ in range(size - 1):
-        total = local if arrived is None else local + keep * arrived.astype(F32)
+    arrived = lax.ppermute(local, "head", pairs)
+    for _ in range(size - 2):
+        rows = iota(local.shape, 1) < HEAD_DIM
+        total = local.astype(F32) + jnp.where(rows, keep * arrived.astype(F32), 0.0)
         arrived = lax.ppermute(total.astype(BF16), "head", pairs)
     return arrived
 
@@ -603,19 +653,21 @@
     lengths,
 ):
     rows, width = tokens.shape
-    n_head = lax.axis_size("head")
+    n_dp, n_head = lax.axis_size("dp"), lax.axis_size("head")
     pairs = width // PAIR
     steps = rows // ROWS
-    order_a, order_b = orders()
-    shift_next = [(i, i + 1) for i in range(n_head - 1)]
-    shift_back = [(i + 1, i) for i in range(n_head - 1)]
-
-    qkv_all = gather_absolute(qkv_weight, order_a)
-    qkv_all = jnp.transpose(qkv_all, (2, 0, 3, 1, 4)).reshape(3, width, width)
-    out_all = gather_absolute(out_weight.T, order_b)
-    out_all = jnp.transpose(out_all, (1, 3, 0, 2)).reshape(width, width)
-    in_all = gather_relative(in_weight, order_a)
-    down_all = gather_relative(down_weight, order_b)
+    groups = phases()
+    spots = [(d, h, relative_index(d, h)) for d in range(n_dp) for h in range(n_head)]
+
+    shards = jnp.concatenate([qkv_weight, out_weight.T[None]], axis=0)[None]
+    feed = jnp.stack([in_weight, down_weight])
+    for group in groups[:-1]:
+        shards = widen(shards, group, 0)
+    shards, feed = lax.optimization_barrier((shards, feed))
+    shards = widen(shards, groups[-1], 0)
+    for group in groups:
+        feed = widen(feed, group, 1)
+    in_all, down_all = feed[0], feed[1]
 
     item_lengths = lengths[0]
     slots = item_lengths.shape[0]
@@ -638,36 +690,58 @@
             carried_rows[None],
             start[rows - 1 :],
             (total - offset)[None],
+            jnp.asarray(relative_index(lax.axis_index("dp"), lax.axis_index("head")), jnp.int32)[None],
         ]
     )
     start_wide = jnp.broadcast_to(start[:, None], (rows, PAIR))
     keep_all = (start[rows - 1] < 0).astype(F32)
     blend_wide = jnp.repeat(blend, HEAD_DIM, axis=1)
 
-    residual = tokens.astype(F32)
-    normal_one, scale_one = norm_parts(residual)
-    normed_one = (normal_one * ln1_gain).astype(BF16)
-    qkv = jnp.einsum("td,cde->cte", normed_one, qkv_all, preferred_element_type=F32).astype(BF16)
-
     spec = pair_specs(rows)
     wide = jax.ShapeDtypeStruct((rows, width), F32)
-    state_shape = jax.ShapeDtypeStruct((pairs, PAIR, 3 * PAIR), F32)
     states_shape = jax.ShapeDtypeStruct((pairs, steps * PAIR, 3 * PAIR), BF16)
-    tail_shape = jax.ShapeDtypeStruct((2, TAIL, width), F32)
+    message_shape = jax.ShapeDtypeStruct((pairs, HEAD_DIM + TAIL, 3 * PAIR), BF16)
     big = rows * width
-
-    ends_state = call(
-        ends_kernel, [spec["qkv"]], spec["state"], state_shape, [], pairs, "ends", 400 * big, 6 * big
-    )(scalars, qkv)
-    tails = lax.ppermute(qkv[1:, rows - TAIL :], "head", shift_next)
-    state_in = pass_along(ends_state, keep_all, 1)
+    part = rows // 3
+
+    def whole_spec(shape):
+        return pl.BlockSpec(shape, lambda p, s: (0,) * len(shape))
+
+    qkv, normed_one, qkv_all, out_all, closing = call(
+        functools.partial(project_kernel, spots=spots),
+        [
+            pl.BlockSpec((part, width), lambda p, s: (p, 0)),
+            whole_spec((1, width)),
+            whole_spec(shards.shape),
+        ],
+        [
+            pl.BlockSpec((3, part, width), lambda p, s: (0, p, 0)),
+            pl.BlockSpec((part, width), lambda p, s: (p, 0)),
+            whole_spec((3, width, width)),
+            whole_spec((width, width)),
+            whole_spec(message_shape.shape),
+        ],
+        [
+            jax.ShapeDtypeStruct((3, rows, width), BF16),
+            jax.ShapeDtypeStruct((rows, width), BF16),
+            jax.ShapeDtypeStruct((3, width, width), BF16),
+            jax.ShapeDtypeStruct((width, width), BF16),
+            message_shape,
+        ],
+        [pltpu.VMEM((pairs, PAIR, 3 * PAIR), F32)],
+        3,
+        "project",
+        6 * big * width,
+        12 * big,
+    )(scalars, tokens, ln1_gain[None], shards)
+    message = pass_along(closing, keep_all, 1)
 
     key_scratch = pltpu.VMEM((rows + TAIL, PAIR), BF16)
     state_scratch = pltpu.VMEM((PAIR, 3 * PAIR), F32)
     tail_scratch = pltpu.VMEM((TAIL, PAIR), F32)
     mixed, near, far1, far2, inv_l, inv_d, states = call(
         forward_kernel,
-        [spec["qkv"], spec["tail"], spec["start"], spec["blend"], spec["state"]],
+        [spec["qkv"], spec["message"], spec["start"], spec["blend"]],
         [spec["column"]] * 6 + [spec["states"]],
         [jax.ShapeDtypeStruct((rows, width), BF16)] + [wide] * 5 + [states_shape],
         [key_scratch, key_scratch, state_scratch],
@@ -675,9 +749,10 @@
         "forward",
         8000 * big,
         40 * big,
-    )(scalars, qkv, tails, start_wide, blend_wide, state_in)
-
-    hidden = residual + jnp.dot(mixed, out_all, preferred_element_type=F32)
+    )(scalars, qkv, message, start_wide, blend_wide)
+
+    residual = tokens.astype(F32)
+    hidden = residual + lax.dot_general(mixed, out_all, NT, preferred_element_type=F32)
     normal_two, scale_two = norm_parts(hidden)
     normed_two = (normal_two * ln2_gain).astype(BF16)
     inner = lax.dot_general(normed_two, in_all, NT, preferred_element_type=F32)
@@ -696,78 +771,99 @@
     d_hidden_part, gain_two_part = norm_back(d_normed_two, ln2_gain, normal_two, scale_two)
     d_hidden = cotangent.astype(F32) + d_hidden_part
     d_branch = d_hidden.astype(BF16)
-    d_mixed = lax.dot_general(d_branch, out_all, NT, preferred_element_type=F32).astype(BF16)
+    d_mixed = jnp.dot(d_branch, out_all, preferred_element_type=F32).astype(BF16)
     out_grad = lax.dot_general(d_branch, mixed, TN, preferred_element_type=F32)
 
-    in_share = scatter_relative(in_grad, order_a)
-    down_share = scatter_relative(down_grad, order_b)
-    n_dp = lax.axis_size("dp")
-    out_share = scatter_absolute(
-        jnp.transpose(
-            out_grad.reshape(n_dp, width // n_dp, n_head, width // n_head), (0, 2, 1, 3)
-        ),
-        order_b,
-    ).T
-
-    adjoint, tail_grads, sums = call(
+    back, sums = call(
         prologue_kernel,
-        [spec["qkv"], spec["tail"], spec["start"], spec["blend"]] + [spec["column"]] * 6,
-        [spec["state"], spec["tail"], spec["sums"]],
-        [state_shape, tail_shape, jax.ShapeDtypeStruct((24, width), F32)],
-        [],
+        [spec["qkv"], spec["message"], spec["start"], spec["blend"]] + [spec["column"]] * 6,
+        [spec["message"], spec["sums"]],
+        [message_shape, jax.ShapeDtypeStruct((24, width), F32)],
+        [state_scratch],
         pairs,
         "prologue",
         500 * big,
         28 * big,
-    )(scalars, qkv, tails, start_wide, blend_wide, d_mixed, near, far1, far2, inv_l, inv_d)
-    adjoint_in = pass_along(adjoint, keep_all, -1)
-    tail_in = lax.ppermute(tail_grads, "head", shift_back)
+    )(scalars, qkv, message, start_wide, blend_wide, d_mixed, near, far1, far2, inv_l, inv_d)
+    back_in = pass_along(back, keep_all, -1)
     blend_part = jnp.sum(sums.reshape(3, 8, blend.shape[1], HEAD_DIM), axis=(1, 3))
 
-    d_qkv = call(
-        backward_kernel,
-        [spec["qkv"], spec["tail"], spec["start"], spec["blend"]]
-        + [spec["column"]] * 5
-        + [spec["states"], spec["state"], spec["tail"]],
-        spec["qkv"],
-        jax.ShapeDtypeStruct((3, rows, width), BF16),
-        [key_scratch, key_scratch, state_scratch, tail_scratch, tail_scratch],
-        pairs,
-        "backward",
-        16000 * big,
-        40 * big,
-    )(
-        scalars,
-        qkv,
-        tails,
-        start_wide,
-        blend_wide,
-        d_mixed,
-        near,
-        far1,
-        inv_l,
-        inv_d,
-        states,
-        adjoint_in,
-        tail_in,
-    )
-
-    qkv_grad = jnp.einsum("td,cte->cde", normed_one, d_qkv, preferred_element_type=F32)
+    half = in_grad.shape[0] // 2
+    keep = jnp.stack([in_grad[:half], down_grad[:half]])
+    give = jnp.stack([in_grad[half:], down_grad[half:]]).astype(BF16)
+    feed_share = narrow(keep, [give], groups[-1])
+    left = list(reversed(groups[:-1]))
+
+    d_qkv = jnp.zeros((3, 8, PAIR), BF16)
+    first = 0
+    for count in (pairs // 4, pairs // 2, pairs // 4):
+        spec = pair_specs(rows, first)
+        more = {12: 0} if first else {}
+        d_qkv = call(
+            backward_kernel,
+            [spec["qkv"], spec["message"], spec["start"], spec["blend"]]
+            + [spec["column"]] * 5
+            + [spec["states"], spec["message"], pl.BlockSpec(memory_space=pl.ANY)],
+            spec["qkv"],
+            jax.ShapeDtypeStruct((3, rows, width), BF16),
+            [key_scratch, key_scratch, state_scratch, tail_scratch, tail_scratch],
+            count,
+            "backward",
+            16000 * big * count // pairs,
+            40 * big * count // pairs,
+            more,
+        )(
+            scalars,
+            qkv,
+            message,
+            start_wide,
+            blend_wide,
+            d_mixed,
+            near,
+            far1,
+            inv_l,
+            inv_d,
+            states,
+            back_in,
+            d_qkv,
+        )
+        first += count
+        if left and first < pairs:
+            feed_share, back_in = lax.optimization_barrier((feed_share, back_in))
+            feed_share = narrow_axis(feed_share, left.pop(0), 1)
+    for group in left:
+        feed_share = narrow_axis(feed_share, group, 1)
+
+    shard_shape = (n_dp * n_head // 2, 4, width // n_dp, width // n_head)
+    shard_spec = pl.BlockSpec((shard_shape[0], 1) + shard_shape[2:], lambda p, s: (0, p, 0, 0))
+    keep, give = call(
+        functools.partial(weight_grad_kernel, spots=spots, n_head=n_head),
+        [
+            whole_spec((rows, width)),
+            pl.BlockSpec((1, rows, width), lambda p, s: (jnp.minimum(p, 2), 0, 0)),
+            whole_spec((width, width)),
+        ],
+        [shard_spec, shard_spec],
+        [jax.ShapeDtypeStruct(shard_shape, F32), jax.ShapeDtypeStruct(shard_shape, BF16)],
+        [pltpu.VMEM((n_dp, width // n_dp, width), F32)],
+        4,
+        "weight_grad",
+        6 * big * width,
+        8 * big,
+    )(scalars, normed_one, d_qkv, out_grad)
+    share = narrow(keep, [give], groups[-1])
+    for group in reversed(groups[:-1]):
+        share = narrow_axis(share, group, 0)
     d_normed_one = jnp.einsum("cte,cde->td", d_qkv, qkv_all, preferred_element_type=F32)
+    normal_one, scale_one = norm_parts(residual)
     d_residual_part, gain_one_part = norm_back(d_normed_one, ln1_gain, normal_one, scale_one)
     input_grad = d_hidden + d_residual_part
-    qkv_share = scatter_absolute(
-        jnp.transpose(
-            qkv_grad.reshape(3, n_dp, width // n_dp, n_head, width // n_head), (1, 3, 0, 2, 4)
-        ),
-        order_a,
-    )
-    early = sum_everywhere(
-        jnp.concatenate([gain_two_part, blend_part.reshape(-1)])[None], order_b
-    )[0]
-    gain_two = early[:width]
-    blend_sum = early[width:].reshape(blend.shape)
-    gain_one = sum_everywhere(gain_one_part[None], order_a)[0]
+    gathered = jnp.concatenate([gain_one_part, gain_two_part, blend_part.reshape(-1)])
+    total_sums = sum_everywhere(gathered[None])[0]
+    gain_one, gain_two = total_sums[:width], total_sums[width : 2 * width]
+    blend_sum = total_sums[2 * width :].reshape(blend.shape)
+    qkv_share, out_share = share[0, :3], share[0, 3].T
+    in_share, down_share = feed_share[0], feed_share[1]
     return (
         layer_out,
         input_grad,

time: 411 us -> 383 us (0.932)
  Pallas kernels: 113 us -> 135 us
  starting transfers between devices: 80.4 us -> 67.1 us
  matrix products: 72.6 us -> 60 us
  waiting for transfers between devices: 59.4 us -> 48.3 us
  local copies, waits for them, and re-layouts: 46.4 us -> 40.6 us
  other arithmetic: 30.7 us -> 26 us
    pallas_call x4 -> x7, Pallas kernels: 113 us -> 135 us  [the longest x3 69.9 us: per_device(): call(backward_kernel, [spec['qkv'], spec['message'], spec['start'], spec[...]
    ppermute x54 -> x37, starting transfers between devices: 80.4 us -> 67.1 us  [the longest x35 61.9 us: peer(): return lax.ppermute(array, ('dp', 'head'), pairs)]
    ppermute x54 -> x37, waiting for transfers between devices: 59.4 us -> 48.3 us  [the longest x35 44.5 us: peer(): return lax.ppermute(array, ('dp', 'head'), pairs)]
    reshape x5 -> x1, local copies, waits for them, and re-layouts: 11.7 us -> 0.66 us  [per_device(): blend_sum = total_sums[2 * width:].reshape(blend.shape)]
    dot_general x4 -> x2, matrix products: 15 us -> 4.75 us  [the longest x1 2.58 us: per_device(): lax.dot_general(mixed, out_all, NT, preferred_element_type=F32)]
    transpose x6 -> x1, local copies, waits for them, and re-layouts: 9.56 us -> 0.62 us  [per_device(): qkv_share, out_share = (share[0, :3], share[0, 3].T)]
    unnamed x75 -> x65, local copies, waits for them, and re-layouts: 14.4 us -> 21.9 us
    concatenate x0 -> x4, local copies, waits for them, and re-layouts: none -> 5.34 us  [the longest x3 3.48 us: widen(): return jnp.concatenate([block] + others, axis=axis)]
  transfers between devices with their start and end apart: 54 -> 37, of which waited for: 19 -> 17; matrix products, arithmetic and copies ran while one was open for 26% -> 19% of each run, Pallas kernels for 25% -> 32%
where the time goes in v2:
time: 383 us; the launch traced here: 379 us
  Pallas kernels  135 us (35%)
  starting transfers between devices  67.1 us (18%)
  matrix products  60 us (16%)
  waiting for transfers between devices  48.3 us (13%)
  local copies, waits for them, and re-layouts  40.6 us (11%)
  other arithmetic  26 us (7%)
    pallas_call x3, Pallas kernels, per_device(): call(backward_kernel, [spec['qkv'], spec['message'], spec['start'], spec[...  69.9 us
    ppermute x35, starting transfers between devices, peer(): return lax.ppermute(array, ('dp', 'head'), pairs)  61.9 us
    ppermute x35, waiting for transfers between devices, peer(): return lax.ppermute(array, ('dp', 'head'), pairs)  44.5 us
    pallas_call x1, Pallas kernels, per_device(): call(forward_kernel, [spec['qkv'], spec['message'], spec['start'], spec['...  33.3 us
    unnamed x65, local copies, waits for them, and re-layouts  21.9 us
    dot_general x1, matrix products, per_device(): lax.dot_general(cotangent, down_all, NT, preferred_element_type=F32)  12.3 us
    pallas_call x1, Pallas kernels, per_device(): call(prologue_kernel, [spec['qkv'], spec['message'], spec['start'], spec[...  11.7 us
    dot_general x1, matrix products, per_device(): inner = lax.dot_general(normed_two, in_all, NT, preferred_element_type=F32)  10.7 us
  transfers between devices with their start and end apart: 37, of which 17 were waited for; matrix products, arithmetic and copies ran while one was open for 19% of the time, Pallas kernels for 32%

profile of v2, /device:TPU:0, one launch (start us, length us, event | category | flops | bytes accessed | tf_op | source)
XLA Modules:
  0.0 378.8 jit_solution(17786767729668233338)
XLA Ops:
  1.6 3.1 collective-permute-start
  17.0 4.8 %collective-permute-done.3 = bf16[4,4,32,256]{3,2,1,0:T(8,128)(2,1)S(1)} collective-permute-done((bf16[4,4,32,256]{3,2,1,0:T(8,128)(2,1)S(1)}, bf16[4,4,32,256]{3,2,1,0:T(8,128)(2,1)S(1)}, u32[]{:S(2)}, u32[]{:S(2)}) %collective-permute-start.3) | collective-permute-done | bytes 262176 | tf_op jit(solution)/shard_map/ppermute | solution.py:606
  34.8 5.7 %collective-permute-done.9 = bf16[2,64,512]{2,1,0:T(8,128)(2,1)S(1)} collective-permute-done((bf16[2,64,512]{2,1,0:T(8,128)(2,1)S(1)}, bf16[2,64,512]{2,1,0:T(8,128)(2,1)S(1)}, u32[]{:S(2)}, u32[]{:S(2)}) %collective-permute-start.9) | collective-permute-done | bytes 131104 | tf_op jit(solution)/shard_map/ppermute | solution.py:606
  49.8 6.8 %collective-permute-done.11 = bf16[2,256,512]{2,1,0:T(8,128)(2,1)} collective-permute-done((bf16[2,256,512]{2,1,0:T(8,128)(2,1)}, bf16[2,256,512]{2,1,0:T(8,128)(2,1)}, u32[]{:S(2)}, u32[]{:S(2)}) %collective-permute-start.11) | collective-permute-done | bytes 524320 | tf_op jit(solution)/shard_map/ppermute | solution.py:606
  60.8 2.9 collective-permute-done.13
  67.5 10.5 %project.1 = (bf16[3,1536,512]{2,1,0:T(8,128)(2,1)}, bf16[1536,512]{1,0:T(8,128)(2,1)}, bf16[3,512,512]{2,1,0:T(8,128)(2,1)}, bf16[512,512]{1,0:T(8,128)(2,1)}, bf16[4,96,384]{2,1,0:T(8,128)(2,1)}) custom-call(s32[20]{0:T(128)} %concatenate.30.scalars, bf16[1536,512]{1,0:T(8,128)(2,1)} %tokens_ref.1, f32[1,512]{1,0:T(1,128)} %bitcast.67, ...), custom_call_target="tpu_custom_call" | custom-call | flops 2415919104 | bytes 9437184 | tf_op jit(solution)/shard_map/project/pallas_call | solution.py:710
  78.0 3.9 %collective-permute-start.7 = (bf16[4,96,384]{2,1,0:T(8,128)(2,1)}, bf16[4,96,384]{2,1,0:T(8,128)(2,1)S(1)}, u32[]{:S(2)}, u32[]{:S(2)}) collective-permute-start(bf16[4,96,384]{2,1,0:T(8,128)(2,1)} %get-tuple-element.33), channel_id=1, source_target_pairs={{0,1},{2,3},{4,5},{6,7},{8,9},{10,11},{12,13},{14,15},{16,17},{18,... | collective-permute-start | bytes 884744 | tf_op jit(solution)/shard_map/ppermute | solution.py:635
  84.9 3.8 collective-permute-done.7.message_ref
  89.8 33.3 %forward.1 = (bf16[1536,512]{1,0:T(8,128)(2,1)}, f32[1536,512]{1,0:T(8,128)}, f32[1536,512]{1,0:T(8,128)}, f32[1536,512]{1,0:T(8,128)}, f32[1536,512]{1,0:T(8,12...) custom-call(s32[20]{0:T(128)} %concatenate.30.scalars, bf16[3,1536,512]{2,1,0:T(8,128)(2,1)} %get-tuple-element.32.qkv_ref, ...), custom_call_target="tpu_custom_call" | custom-call | flops 6291456000 | bytes 31457280 | tf_op jit(solution)/shard_map/forward/pallas_call | solution.py:742
  128.6 10.7 %multiply_convert_fusion = (bf16[1536,2048]{1,0:T(8,128)(2,1)}, f32[1536,2048]{1,0:T(8,128)}) fusion(bf16[2,2048,512]{2,1,0:T(8,128)(2,1)S(1)} %constant_dynamic-update-slice_fusion.18, f32[1536,512]{0,1:T(8,128)S(1)} %get-tuple-element.137, f32[512]{0:T(512)S(1)} %copy-done.20, f32[1536]{0:T(1024)S(1)} %add_rsqrt_fusion.1, ...), kind=kOutput, calls=%fused_computation.11 | convolution fusion | flops 3252682752 | bytes 24135680 | tf_op jit(solution)/shard_map/dot_general | solution.py:758
  139.3 12.3 %fusion.8 = bf16[1536,2048]{1,0:T(8,128)(2,1)S(1)} fusion(f32[1536,2048]{1,0:T(8,128)} %get-tuple-element.139, bf16[1536,512]{1,0:T(8,128)(2,1)S(1)} %copy-done.12, bf16[2,2048,512]{2,1,0:T(8,128)(2,1)S(1)} %constant_dynamic-update-slice_fusion.18), kind=kOutput, calls=%fused_computation.10 | convolution fusion | flops 3280994304 | bytes 22544384 | tf_op jit(solution)/shard_map/dot_general | solution.py:763
  154.2 5.0 %multiply_reduce_fusion = (f32[512]{0:T(512)}, f32[1536]{0:T(1024)S(1)}, f32[1536]{0:T(1024)S(1)}, f32[1536,512]{0,1:T(8,128)S(1)}) fusion(f32[1536,512]{0,1:T(8,128)S(1)} %get-tuple-element.137, f32[1536]{0:T(1024)S(1)} %add_rsqrt_fusion.1, f32[1536]{0:T(1024)S(1)} %broadcast_multiply_fusion.5, f32[512]{0:T(512)S(1)} %copy-done.20, ...), kind=kOutput, calls=%fused_computation.29 | convolution fusion | flops 3227513344 | bytes 14712832 | tf_op jit(solution)/shard_map/dot_general | solution.py:770
  159.3 5.9 %fusion.35 = f32[2048,512]{1,0:T(8,128)S(1)} fusion(bf16[1536,2048]{1,0:T(8,128)(2,1)} %copy-done.24, f32[1536,512]{0,1:T(8,128)S(1)} %get-tuple-element.137, f32[512]{0:T(512)S(1)} %copy-done.20, f32[1536]{0:T(1024)S(1)} %add_rsqrt_fusion.1, f32[1536]{0:T(1024)S(1)} %broadcast_multiply_fusion.5), kind=kOutput, calls=%fused_computation.121 | convolution fusion | flops 3224371200 | bytes 13645824 | tf_op jit(solution)/shard_map/dot_general | solution.py:769
  170.4 11.7 %prologue.1 = (bf16[4,96,384]{2,1,0:T(8,128)(2,1)}, f32[24,512]{1,0:T(8,128)}) custom-call(s32[20]{0:T(128)} %concatenate.30.scalars, bf16[3,1536,512]{2,1,0:T(8,128)(2,1)} %get-tuple-element.32.qkv_ref, bf16[4,96,384]{2,1,0:T(8,128)(2,1)} %copy-done.5, s32[1536,128]{1,0:T(8,128)} %broadcast_in_dim.81.start_ref, f32[3,512]{1,0:T(4,128)} %reshape.96.blend_ref, ...), custom_call_target="tpu_custom_call" | custom-call | flops 393216000 | bytes 22020096 | tf_op jit(solution)/shard_map/prologue/pallas_call | solution.py:777
  183.4 5.8 %fusion.45 = f32[2048,512]{1,0:T(8,128)S(1)} fusion(bf16[1536,2048]{1,0:T(8,128)(2,1)} %get-tuple-element.138, bf16[1536,512]{1,0:T(8,128)(2,1)S(1)} %copy-done.13), kind=kOutput, calls=%fused_computation.130 | convolution fusion | flops 3221225472 | bytes 12058624 | tf_op jit(solution)/shard_map/dot_general | solution.py:764
  192.1 9.0 %fusion.20 = bf16[1536,512]{0,1:T(8,128)(2,1)} fusion(f32[1536,512]{0,1:T(8,128)} %copy-done.1, bf16[1536,2048]{1,0:T(8,128)(2,1)} %get-tuple-element.138, bf16[2,2048,512]{2,1,0:T(8,128)(2,1)} %copy-done.19), kind=kOutput, calls=%fused_computation.35 | convolution fusion | flops 3222798336 | bytes 13107200 | tf_op jit(solution)/shard_map/dot_general | solution.py:762
  203.7 4.1 %slice_bitcast_fusion = (f32[1,1024,512]{2,1,0:T(8,128)S(1)}, f32[1,1024,512]{2,1,0:T(8,128)}) fusion(f32[2048,512]{1,0:T(8,128)} %copy-done.9, f32[2048,512]{1,0:T(8,128)} %copy-done.8), kind=kLoop, calls=%fused_computation.41 | loop fusion | bytes 8388608 | tf_op jit(solution)/shard_map/stack | solution.py:792
  210.6 18.4 %backward.3.done_ref = bf16[3,1536,512]{2,1,0:T(8,128)(2,1)} custom-call(s32[20]{0:T(128)} %concatenate.30.scalars, bf16[3,1536,512]{2,1,0:T(8,128)(2,1)} %get-tuple-element.32.qkv_ref, bf16[4,96,384]{2,1,0:T(8,128)(2,1)} %copy-done.5, s32[1536,128]{1,0:T(8,128)} %broadcast_in_dim.81.start_ref, f32[3,512]{1,0:T(4,128)} %reshape.96.blend_ref, ...), custom_call_target="tpu_custom_call" | custom-call | flops 3145728000 | bytes 7864320 | tf_op jit(solution)/shard_map/backward/pallas_call | solution.py:802
  229.0 3.0 maximum_add_fusion
  234.6 13.5 %collective-permute-start.18 = (bf16[2,256,512]{2,1,0:T(8,128)(2,1)S(1)}, bf16[2,256,512]{2,1,0:T(8,128)(2,1)S(1)}, u32[]{:S(2)}, u32[]{:S(2)}) collective-permute-start(bf16[2,256,512]{2,1,0:T(8,128)(2,1)S(1)} %get-tuple-element.104), channel_id=1, source_target_pairs={{0,1},{1,0},{2,3},{3,2},{4,5},{5,4},{6,7},{7,6},{8,9},{9,8},{10,11... | collective-permute-start | bytes 1572872 | tf_op jit(solution)/shard_map/ppermute | solution.py:606
  248.1 33.0 %backward.4.done_ref = bf16[3,1536,512]{2,1,0:T(8,128)(2,1)} custom-call(s32[20]{0:T(128)} %concatenate.30.scalars, bf16[3,1536,512]{2,1,0:T(8,128)(2,1)} %get-tuple-element.32.qkv_ref, bf16[4,96,384]{2,1,0:T(8,128)(2,1)} %copy-done.5, s32[1536,128]{1,0:T(8,128)} %broadcast_in_dim.81.start_ref, ...), custom_call_target="tpu_custom_call", output_to_operand_aliasing={{}: (12, {})} | custom-call | flops 6291456000 | bytes 15728640 | tf_op jit(solution)/shard_map/backward/pallas_call | solution.py:802
  283.3 11.8 %collective-permute-start.34 = (bf16[2,64,512]{2,1,0:T(8,128)(2,1)}, bf16[2,64,512]{2,1,0:T(8,128)(2,1)S(1)}, u32[]{:S(2)}, u32[]{:S(2)}) collective-permute-start(bf16[2,64,512]{2,1,0:T(8,128)(2,1)} %get-tuple-element.108), channel_id=1, source_target_pairs={{0,8},{1,9},{2,10},{3,11},{4,12},{5,13},{6,14},{7,15},{8,0},{9,1},... | collective-permute-start | bytes 393224 | tf_op jit(solution)/shard_map/ppermute | solution.py:606
  295.1 18.4 %backward.5.d_qkv_ref = bf16[3,1536,512]{2,1,0:T(8,128)(2,1)} custom-call(s32[20]{0:T(128)} %concatenate.30.scalars, bf16[3,1536,512]{2,1,0:T(8,128)(2,1)} %get-tuple-element.32.qkv_ref, bf16[4,96,384]{2,1,0:T(8,128)(2,1)} %copy-done.5, s32[1536,128]{1,0:T(8,128)} %broadcast_in_dim.81.start_ref, ...), custom_call_target="tpu_custom_call", output_to_operand_aliasing={{}: (12, {})} | custom-call | flops 3145728000 | bytes 7864320 | tf_op jit(solution)/shard_map/backward/pallas_call | solution.py:802
  313.6 9.3 %weight_grad.1 = (f32[16,4,32,256]{3,2,1,0:T(8,128)}, bf16[16,4,32,256]{3,2,1,0:T(8,128)(2,1)}) custom-call(s32[20]{0:T(128)} %concatenate.30.scalars, bf16[1536,512]{1,0:T(8,128)(2,1)} %get-tuple-element.49.normed_ref, bf16[3,1536,512]{2,1,0:T(8,128)(2,1)} %backward.5.d_qkv_ref, f32[512,512]{1,0:T(8,128)} %fusion.25.out_grad_ref), custom_call_target="tpu_custom_call" | custom-call | flops 2415919104 | bytes 6291456 | tf_op jit(solution)/shard_map/weight_grad/pallas_call | solution.py:839
  322.9 4.6 %fusion.18 = (f32[512]{0:T(512)S(1)}, f32[1536]{0:T(1024)S(1)}, f32[1536]{0:T(1024)S(1)}, f32[1536,512]{0,1:T(8,128)S(1)}) fusion(bf16[1536,512]{0,1:T(8,128)(2,1)S(1)} %copy.39, f32[1536]{0:T(1024)S(1)} %add_rsqrt_fusion, f32[1536]{0:T(1024)S(1)} %broadcast_multiply_fusion.2, f32[512]{0:T(512)S(1)} %copy-done.21, bf16[3,1536,512]{2,1,0:T(8,128)(2,1)S(1)} %copy-done, ...), kind=kOutput, calls=%fused_computation.27 | convolution fusion | flops 2422993408 | bytes 11038720 | tf_op jit(solution)/shard_map/cte,cde->td/dot_general | solution.py:857
  334.0 2.9 collective-permute-done.23
  337.4 4.0 %collective-permute-start.26 = (f32[1,1048]{1,0:T(1,128)S(1)}, f32[1,1048]{1,0:T(1,128)S(1)}, u32[]{:S(2)}, u32[]{:S(2)}) collective-permute-start(f32[1,1048]{1,0:T(1,128)S(1)} %add_add_fusion.2), channel_id=1, source_target_pairs={{0,24},{1,25},{2,26},{3,27},{4,28},{5,29},{6,30},{7,31},{8,16},{9,... | collective-permute-start | bytes 12584 | tf_op jit(solution)/shard_map/ppermute | solution.py:606
  344.1 3.5 copy.44
  349.8 3.7 fusion.38
  354.2 2.9 collective-permute-start.30
  358.8 4.0 %collective-permute-done.28 = bf16[4,4,32,256]{3,2,1,0:T(8,128)(2,1)S(1)} collective-permute-done((bf16[4,4,32,256]{3,2,1,0:T(8,128)(2,1)S(1)}, bf16[4,4,32,256]{3,2,1,0:T(8,128)(2,1)S(1)}, u32[]{:S(2)}, u32[]{:S(2)}) %collective-permute-start.28) | collective-permute-done | bytes 262176 | tf_op jit(solution)/shard_map/ppermute | solution.py:606
  362.8 3.3 collective-permute-done.30
  (186 shorter events, 101.1 us)
Async XLA Ops:
  1.6 8.9 %collective-permute-start = (bf16[1,4,32,256]{3,2,1,0:T(8,128)(2,1)S(1)}, bf16[1,4,32,256]{3,2,1,0:T(8,128)(2,1)S(1)}, u32[]{:S(2)}, u32[]{:S(2)}) collective-permute-start(bf16[1,4,32,256]{3,2,1,0:T(8,128)(2,1)S(1)} %maximum_bitcast_fusion), channel_id=1, source_target_pairs={{0,8},{1,9},{2,10},{3,11},{4,12},{5,13},{6,14},{7,15},{8,0},{9,1},... | collective-permute-start | bytes 196616 | tf_op jit(solution)/shard_map/ppermute | solution.py:606
  4.7 7.3 %collective-permute-start.1 = (bf16[1,4,32,256]{3,2,1,0:T(8,128)(2,1)S(1)}, bf16[1,4,32,256]{3,2,1,0:T(8,128)(2,1)S(1)}, u32[]{:S(2)}, u32[]{:S(2)}) collective-permute-start(bf16[1,4,32,256]{3,2,1,0:T(8,128)(2,1)S(1)} %maximum_bitcast_fusion), channel_id=1, source_target_pairs={{0,16},{1,17},{2,18},{3,19},{4,20},{5,21},{6,22},{7,23},{8,24},{9,... | collective-permute-start | bytes 196616 | tf_op jit(solution)/shard_map/ppermute | solution.py:606
  7.3 6.1 %collective-permute-start.2 = (bf16[1,4,32,256]{3,2,1,0:T(8,128)(2,1)S(1)}, bf16[1,4,32,256]{3,2,1,0:T(8,128)(2,1)S(1)}, u32[]{:S(2)}, u32[]{:S(2)}) collective-permute-start(bf16[1,4,32,256]{3,2,1,0:T(8,128)(2,1)S(1)} %maximum_bitcast_fusion), channel_id=1, source_target_pairs={{0,24},{1,25},{2,26},{3,27},{4,28},{5,29},{6,30},{7,31},{8,16},{9,... | collective-permute-start | bytes 196616 | tf_op jit(solution)/shard_map/ppermute | solution.py:606
  13.4 8.3 %collective-permute-start.3 = (bf16[4,4,32,256]{3,2,1,0:T(8,128)(2,1)S(1)}, bf16[4,4,32,256]{3,2,1,0:T(8,128)(2,1)S(1)}, u32[]{:S(2)}, u32[]{:S(2)}) collective-permute-start(bf16[4,4,32,256]{3,2,1,0:T(8,128)(2,1)S(1)} %pad_maximum_fusion.2), channel_id=1, source_target_pairs={{0,4},{1,5},{2,6},{3,7},{4,0},{5,1},{6,2},{7,3},{8,12},{9,13},{10,... | collective-permute-start | bytes 786440 | tf_op jit(solution)/shard_map/ppermute | solution.py:606
  15.0 9.0 %collective-permute-start.4 = (bf16[4,4,32,256]{3,2,1,0:T(8,128)(2,1)S(1)}, bf16[4,4,32,256]{3,2,1,0:T(8,128)(2,1)S(1)}, u32[]{:S(2)}, u32[]{:S(2)}) collective-permute-start(bf16[4,4,32,256]{3,2,1,0:T(8,128)(2,1)S(1)} %pad_maximum_fusion.2), channel_id=1, source_target_pairs={{0,1},{1,0},{2,3},{3,2},{4,5},{5,4},{6,7},{7,6},{8,9},{9,8},{10,11... | collective-permute-start | bytes 786440 | tf_op jit(solution)/shard_map/ppermute | solution.py:606
  16.5 10.2 %collective-permute-start.5 = (bf16[4,4,32,256]{3,2,1,0:T(8,128)(2,1)S(1)}, bf16[4,4,32,256]{3,2,1,0:T(8,128)(2,1)S(1)}, u32[]{:S(2)}, u32[]{:S(2)}) collective-permute-start(bf16[4,4,32,256]{3,2,1,0:T(8,128)(2,1)S(1)} %pad_maximum_fusion.2), channel_id=1, source_target_pairs={{0,5},{1,4},{2,7},{3,6},{4,1},{5,0},{6,3},{7,2},{8,13},{9,12},{10,... | collective-permute-start | bytes 786440 | tf_op jit(solution)/shard_map/ppermute | solution.py:606
  26.7 7.3 %collective-permute-start.8 = (bf16[2,64,512]{2,1,0:T(8,128)(2,1)S(1)}, bf16[2,64,512]{2,1,0:T(8,128)(2,1)S(1)}, u32[]{:S(2)}, u32[]{:S(2)}) collective-permute-start(bf16[2,64,512]{2,1,0:T(8,128)(2,1)S(1)} %pad_maximum_fusion.3), channel_id=1, source_target_pairs={{0,8},{1,9},{2,10},{3,11},{4,12},{5,13},{6,14},{7,15},{8,0},{9,1},... | collective-permute-start | bytes 393224 | tf_op jit(solution)/shard_map/ppermute | solution.py:606
  29.7 10.8 %collective-permute-start.9 = (bf16[2,64,512]{2,1,0:T(8,128)(2,1)S(1)}, bf16[2,64,512]{2,1,0:T(8,128)(2,1)S(1)}, u32[]{:S(2)}, u32[]{:S(2)}) collective-permute-start(bf16[2,64,512]{2,1,0:T(8,128)(2,1)S(1)} %pad_maximum_fusion.3), channel_id=1, source_target_pairs={{0,16},{1,17},{2,18},{3,19},{4,20},{5,21},{6,22},{7,23},{8,24},{9,... | collective-permute-start | bytes 393224 | tf_op jit(solution)/shard_map/ppermute | solution.py:606
  32.6 8.7 %collective-permute-start.10 = (bf16[2,64,512]{2,1,0:T(8,128)(2,1)S(1)}, bf16[2,64,512]{2,1,0:T(8,128)(2,1)S(1)}, u32[]{:S(2)}, u32[]{:S(2)}) collective-permute-start(bf16[2,64,512]{2,1,0:T(8,128)(2,1)S(1)} %pad_maximum_fusion.3), channel_id=1, source_target_pairs={{0,24},{1,25},{2,26},{3,27},{4,28},{5,29},{6,30},{7,31},{8,16},{9,... | collective-permute-start | bytes 393224 | tf_op jit(solution)/shard_map/ppermute | solution.py:606
  34.0 30.8 %collective-permute-start.6 = (bf16[16,4,32,256]{3,2,1,0:T(8,128)(2,1)}, bf16[16,4,32,256]{3,2,1,0:T(8,128)(2,1)}, u32[]{:S(2)}, u32[]{:S(2)}) collective-permute-start(bf16[16,4,32,256]{3,2,1,0:T(8,128)(2,1)} %copy-done.14), channel_id=1, source_target_pairs={{0,2},{1,3},{2,0},{3,1},{4,6},{5,7},{6,4},{7,5},{8,10},{9,11},{10,... | collective-permute-start | bytes 3145736 | tf_op jit(solution)/shard_map/ppermute | solution.py:606
  42.1 14.5 %collective-permute-start.11 = (bf16[2,256,512]{2,1,0:T(8,128)(2,1)}, bf16[2,256,512]{2,1,0:T(8,128)(2,1)}, u32[]{:S(2)}, u32[]{:S(2)}) collective-permute-start(bf16[2,256,512]{2,1,0:T(8,128)(2,1)} %get-tuple-element.124), channel_id=1, source_target_pairs={{0,4},{1,5},{2,6},{3,7},{4,0},{5,1},{6,2},{7,3},{8,12},{9,13},{10,... | collective-permute-start | bytes 1572872 | tf_op jit(solution)/shard_map/ppermute | solution.py:606
  43.6 15.1 %collective-permute-start.12 = (bf16[2,256,512]{2,1,0:T(8,128)(2,1)}, bf16[2,256,512]{2,1,0:T(8,128)(2,1)}, u32[]{:S(2)}, u32[]{:S(2)}) collective-permute-start(bf16[2,256,512]{2,1,0:T(8,128)(2,1)} %get-tuple-element.124), channel_id=1, source_target_pairs={{0,1},{1,0},{2,3},{3,2},{4,5},{5,4},{6,7},{7,6},{8,9},{9,8},{10,11... | collective-permute-start | bytes 1572872 | tf_op jit(solution)/shard_map/ppermute | solution.py:606
  45.4 18.3 %collective-permute-start.13 = (bf16[2,256,512]{2,1,0:T(8,128)(2,1)}, bf16[2,256,512]{2,1,0:T(8,128)(2,1)S(1)}, u32[]{:S(2)}, u32[]{:S(2)}) collective-permute-start(bf16[2,256,512]{2,1,0:T(8,128)(2,1)} %get-tuple-element.124), channel_id=1, source_target_pairs={{0,5},{1,4},{2,7},{3,6},{4,1},{5,0},{6,3},{7,2},{8,13},{9,12},{10,... | collective-permute-start | bytes 1572872 | tf_op jit(solution)/shard_map/ppermute | solution.py:606
  64.8 61.4 %collective-permute-start.14 = (bf16[2,1024,512]{2,1,0:T(8,128)(2,1)}, bf16[2,1024,512]{2,1,0:T(8,128)(2,1)}, u32[]{:S(2)}, u32[]{:S(2)}) collective-permute-start(bf16[2,1024,512]{2,1,0:T(8,128)(2,1)} %get-tuple-element.111), channel_id=1, source_target_pairs={{0,2},{1,3},{2,0},{3,1},{4,6},{5,7},{6,4},{7,5},{8,10},{9,11},{10,... | collective-permute-start | bytes 6291464 | tf_op jit(solution)/shard_map/ppermute | solution.py:606
  78.0 10.6 %collective-permute-start.7 = (bf16[4,96,384]{2,1,0:T(8,128)(2,1)}, bf16[4,96,384]{2,1,0:T(8,128)(2,1)S(1)}, u32[]{:S(2)}, u32[]{:S(2)}) collective-permute-start(bf16[4,96,384]{2,1,0:T(8,128)(2,1)} %get-tuple-element.33), channel_id=1, source_target_pairs={{0,1},{2,3},{4,5},{6,7},{8,9},{10,11},{12,13},{14,15},{16,17},{18,... | collective-permute-start | bytes 884744 | tf_op jit(solution)/shard_map/ppermute | solution.py:635
  182.1 27.8 %collective-permute-start.16 = (bf16[4,96,384]{2,1,0:T(8,128)(2,1)}, bf16[4,96,384]{2,1,0:T(8,128)(2,1)S(1)}, u32[]{:S(2)}, u32[]{:S(2)}) collective-permute-start(bf16[4,96,384]{2,1,0:T(8,128)(2,1)} %get-tuple-element.43), channel_id=1, source_target_pairs={{1,0},{3,2},{5,4},{7,6},{9,8},{11,10},{13,12},{15,14},{17,16},{19,... | collective-permute-start | bytes 884744 | tf_op jit(solution)/shard_map/ppermute | solution.py:635
  191.9 37.1 %collective-permute-start.15 = (bf16[2,1024,512]{2,1,0:T(8,128)(2,1)}, bf16[2,1024,512]{2,1,0:T(8,128)(2,1)}, u32[]{:S(2)}, u32[]{:S(2)}) collective-permute-start(bf16[2,1024,512]{2,1,0:T(8,128)(2,1)} %pad_maximum_fusion.1), channel_id=1, source_target_pairs={{0,2},{1,3},{2,0},{3,1},{4,6},{5,7},{6,4},{7,5},{8,10},{9,11},{10,... | collective-permute-start | bytes 6291464 | tf_op jit(solution)/shard_map/ppermute | solution.py:606
  233.1 48.1 %collective-permute-start.17 = (bf16[2,256,512]{2,1,0:T(8,128)(2,1)}, bf16[2,256,512]{2,1,0:T(8,128)(2,1)S(1)}, u32[]{:S(2)}, u32[]{:S(2)}) collective-permute-start(bf16[2,256,512]{2,1,0:T(8,128)(2,1)} %get-tuple-element.102), channel_id=1, source_target_pairs={{0,4},{1,5},{2,6},{3,7},{4,0},{5,1},{6,2},{7,3},{8,12},{9,13},{10,... | collective-permute-start | bytes 1572872 | tf_op jit(solution)/shard_map/ppermute | solution.py:606
  234.6 46.5 %collective-permute-start.18 = (bf16[2,256,512]{2,1,0:T(8,128)(2,1)S(1)}, bf16[2,256,512]{2,1,0:T(8,128)(2,1)S(1)}, u32[]{:S(2)}, u32[]{:S(2)}) collective-permute-start(bf16[2,256,512]{2,1,0:T(8,128)(2,1)S(1)} %get-tuple-element.104), channel_id=1, source_target_pairs={{0,1},{1,0},{2,3},{3,2},{4,5},{5,4},{6,7},{7,6},{8,9},{9,8},{10,11... | collective-permute-start | bytes 1572872 | tf_op jit(solution)/shard_map/ppermute | solution.py:606
  248.1 33.1 %collective-permute-start.19 = (bf16[2,256,512]{2,1,0:T(8,128)(2,1)S(1)}, bf16[2,256,512]{2,1,0:T(8,128)(2,1)}, u32[]{:S(2)}, u32[]{:S(2)}) collective-permute-start(bf16[2,256,512]{2,1,0:T(8,128)(2,1)S(1)} %get-tuple-element.103), channel_id=1, source_target_pairs={{0,5},{1,4},{2,7},{3,6},{4,1},{5,0},{6,3},{7,2},{8,13},{9,12},{10,... | collective-permute-start | bytes 1572872 | tf_op jit(solution)/shard_map/ppermute | solution.py:606
  283.3 70.9 %collective-permute-start.34 = (bf16[2,64,512]{2,1,0:T(8,128)(2,1)}, bf16[2,64,512]{2,1,0:T(8,128)(2,1)S(1)}, u32[]{:S(2)}, u32[]{:S(2)}) collective-permute-start(bf16[2,64,512]{2,1,0:T(8,128)(2,1)} %get-tuple-element.108), channel_id=1, source_target_pairs={{0,8},{1,9},{2,10},{3,11},{4,12},{5,13},{6,14},{7,15},{8,0},{9,1},... | collective-permute-start | bytes 393224 | tf_op jit(solution)/shard_map/ppermute | solution.py:606
  322.9 26.9 %collective-permute-start.27 = (bf16[16,4,32,256]{3,2,1,0:T(8,128)(2,1)}, bf16[16,4,32,256]{3,2,1,0:T(8,128)(2,1)}, u32[]{:S(2)}, u32[]{:S(2)}) collective-permute-start(bf16[16,4,32,256]{3,2,1,0:T(8,128)(2,1)} %get-tuple-element.51), channel_id=1, source_target_pairs={{0,2},{1,3},{2,0},{3,1},{4,6},{5,7},{6,4},{7,5},{8,10},{9,11},{10,... | collective-permute-start | bytes 3145736 | tf_op jit(solution)/shard_map/ppermute | solution.py:606
  336.9 10.7 %collective-permute-start.24 = (f32[1,1048]{1,0:T(1,128)S(1)}, f32[1,1048]{1,0:T(1,128)S(1)}, u32[]{:S(2)}, u32[]{:S(2)}) collective-permute-start(f32[1,1048]{1,0:T(1,128)S(1)} %add_add_fusion.2), channel_id=1, source_target_pairs={{0,8},{1,9},{2,10},{3,11},{4,12},{5,13},{6,14},{7,15},{8,0},{9,1},... | collective-permute-start | bytes 12584 | tf_op jit(solution)/shard_map/ppermute | solution.py:606
  337.0 10.6 %collective-permute-start.25 = (f32[1,1048]{1,0:T(1,128)S(1)}, f32[1,1048]{1,0:T(1,128)S(1)}, u32[]{:S(2)}, u32[]{:S(2)}) collective-permute-start(f32[1,1048]{1,0:T(1,128)S(1)} %add_add_fusion.2), channel_id=1, source_target_pairs={{0,16},{1,17},{2,18},{3,19},{4,20},{5,21},{6,22},{7,23},{8,24},{9,... | collective-permute-start | bytes 12584 | tf_op jit(solution)/shard_map/ppermute | solution.py:606
  337.4 11.8 %collective-permute-start.26 = (f32[1,1048]{1,0:T(1,128)S(1)}, f32[1,1048]{1,0:T(1,128)S(1)}, u32[]{:S(2)}, u32[]{:S(2)}) collective-permute-start(f32[1,1048]{1,0:T(1,128)S(1)} %add_add_fusion.2), channel_id=1, source_target_pairs={{0,24},{1,25},{2,26},{3,27},{4,28},{5,29},{6,30},{7,31},{8,16},{9,... | collective-permute-start | bytes 12584 | tf_op jit(solution)/shard_map/ppermute | solution.py:606
  347.6 10.2 %collective-permute-start.35 = (bf16[2,64,512]{2,1,0:T(8,128)(2,1)}, bf16[2,64,512]{2,1,0:T(8,128)(2,1)}, u32[]{:S(2)}, u32[]{:S(2)}) collective-permute-start(bf16[2,64,512]{2,1,0:T(8,128)(2,1)} %get-tuple-element.110), channel_id=1, source_target_pairs={{0,16},{1,17},{2,18},{3,19},{4,20},{5,21},{6,22},{7,23},{8,24},{9,... | collective-permute-start | bytes 393224 | tf_op jit(solution)/shard_map/ppermute | solution.py:606
  347.6 10.2 %collective-permute-start.36 = (bf16[2,64,512]{2,1,0:T(8,128)(2,1)}, bf16[2,64,512]{2,1,0:T(8,128)(2,1)}, u32[]{:S(2)}, u32[]{:S(2)}) collective-permute-start(bf16[2,64,512]{2,1,0:T(8,128)(2,1)} %get-tuple-element.109), channel_id=1, source_target_pairs={{0,24},{1,25},{2,26},{3,27},{4,28},{5,29},{6,30},{7,31},{8,16},{9,... | collective-permute-start | bytes 393224 | tf_op jit(solution)/shard_map/ppermute | solution.py:606
  353.6 9.2 %collective-permute-start.28 = (bf16[4,4,32,256]{3,2,1,0:T(8,128)(2,1)S(1)}, bf16[4,4,32,256]{3,2,1,0:T(8,128)(2,1)S(1)}, u32[]{:S(2)}, u32[]{:S(2)}) collective-permute-start(bf16[4,4,32,256]{3,2,1,0:T(8,128)(2,1)S(1)} %get-tuple-element.105), channel_id=1, source_target_pairs={{0,4},{1,5},{2,6},{3,7},{4,0},{5,1},{6,2},{7,3},{8,12},{9,13},{10,... | collective-permute-start | bytes 786440 | tf_op jit(solution)/shard_map/ppermute | solution.py:606
  353.7 9.1 %collective-permute-start.29 = (bf16[4,4,32,256]{3,2,1,0:T(8,128)(2,1)S(1)}, bf16[4,4,32,256]{3,2,1,0:T(8,128)(2,1)S(1)}, u32[]{:S(2)}, u32[]{:S(2)}) collective-permute-start(bf16[4,4,32,256]{3,2,1,0:T(8,128)(2,1)S(1)} %get-tuple-element.107), channel_id=1, source_target_pairs={{0,1},{1,0},{2,3},{3,2},{4,5},{5,4},{6,7},{7,6},{8,9},{9,8},{10,11... | collective-permute-start | bytes 786440 | tf_op jit(solution)/shard_map/ppermute | solution.py:606
  354.2 11.9 %collective-permute-start.30 = (bf16[4,4,32,256]{3,2,1,0:T(8,128)(2,1)S(1)}, bf16[4,4,32,256]{3,2,1,0:T(8,128)(2,1)S(1)}, u32[]{:S(2)}, u32[]{:S(2)}) collective-permute-start(bf16[4,4,32,256]{3,2,1,0:T(8,128)(2,1)S(1)} %get-tuple-element.106), channel_id=1, source_target_pairs={{0,5},{1,4},{2,7},{3,6},{4,1},{5,0},{6,3},{7,2},{8,13},{9,12},{10,... | collective-permute-start | bytes 786440 | tf_op jit(solution)/shard_map/ppermute | solution.py:606
  369.9 5.6 %collective-permute-start.32 = (bf16[1,4,32,256]{3,2,1,0:T(8,128)(2,1)S(1)}, bf16[1,4,32,256]{3,2,1,0:T(8,128)(2,1)S(1)}, u32[]{:S(2)}, u32[]{:S(2)}) collective-permute-start(bf16[1,4,32,256]{3,2,1,0:T(8,128)(2,1)S(1)} %get-tuple-element.121), channel_id=1, source_target_pairs={{0,16},{1,17},{2,18},{3,19},{4,20},{5,21},{6,22},{7,23},{8,24},{9,... | collective-permute-start | bytes 196616 | tf_op jit(solution)/shard_map/ppermute | solution.py:606
  371.2 6.1 %collective-permute-start.33 = (bf16[1,4,32,256]{3,2,1,0:T(8,128)(2,1)S(1)}, bf16[1,4,32,256]{3,2,1,0:T(8,128)(2,1)S(1)}, u32[]{:S(2)}, u32[]{:S(2)}) collective-permute-start(bf16[1,4,32,256]{3,2,1,0:T(8,128)(2,1)S(1)} %get-tuple-element.120), channel_id=1, source_target_pairs={{0,24},{1,25},{2,26},{3,27},{4,28},{5,29},{6,30},{7,31},{8,16},{9,... | collective-permute-start | bytes 196616 | tf_op jit(solution)/shard_map/ppermute | solution.py:606
  (30 other events, 296.7 us)

commit v3 on v2

--- a/solution.py
+++ b/solution.py
@@ -16,6 +16,7 @@
 PAIR = 2 * HEAD_DIM
 EPS = 1e-05
 NEG = -1e30
+CARRIED, LAST, VALID, ROW_AT, COLUMN_AT = range(-5, 0)
 F32 = jnp.float32
 BF16 = jnp.bfloat16
 NT = (((1,), (1,)), ((), ()))
@@ -119,30 +120,36 @@
     scalars,
     tokens_ref,
     gain_ref,
-    shards_ref,
+    own_ref,
+    other_ref,
     qkv_ref,
     normed_ref,
     weight_ref,
     out_weight_ref,
     message_ref,
     state,
+    placed,
     *,
-    spots,
+    flips,
 ):
     step = pl.program_id(0)
     rows, width = tokens_ref.shape
     pairs = width // PAIR
-    tall, wide = shards_ref.shape[2:]
-    last = jnp.maximum(scalars[scalars.shape[0] - 3], 0)
-    me = scalars[scalars.shape[0] - 1]
+    half, _, tall, wide = own_ref.shape
+    last = jnp.maximum(scalars[scalars.shape[0] + LAST], 0)
 
     @pl.when(step == 0)
     def _():
-        for d, h, spot in spots:
-            piece = shards_ref[me ^ spot]
-            at = (pl.ds(d * tall, tall), pl.ds(h * wide, wide))
-            weight_ref[(slice(None),) + at] = piece[:3]
-            out_weight_ref[at] = piece[3]
+        for index, (flip_row, flip_column) in enumerate(flips):
+            row = scalars[scalars.shape[0] + ROW_AT] ^ flip_row
+            column = scalars[scalars.shape[0] + COLUMN_AT] ^ flip_column
+            piece = own_ref[index] if index < half else other_ref[index - half]
+            for c in range(4):
+                placed[column, c, row] = piece[c]
+        for h in range(width // wide):
+            at = pl.ds(h * wide, wide)
+            weight_ref[:, :, at] = placed[h, :3].reshape(3, width, wide)
+            out_weight_ref[:, at] = placed[h, 3].reshape(width, wide)
         state[...] = jnp.zeros(state.shape, F32)
 
     normed = (norm_parts(tokens_ref[...].astype(F32))[0] * gain_ref[...]).astype(BF16)
@@ -176,32 +183,31 @@
 
 
 def weight_grad_kernel(
-    scalars, normed_ref, d_qkv_ref, out_grad_ref, keep_ref, give_ref, whole, *, spots, n_head
+    scalars, normed_ref, d_qkv_ref, out_grad_ref, keep_ref, give_ref, whole, *, flips
 ):
     c = pl.program_id(0)
-    me = scalars[scalars.shape[0] - 1]
-    tall, wide = keep_ref.shape[2:]
-    half = keep_ref.shape[0]
+    half, _, tall, wide = keep_ref.shape
+
+    def place(total):
+        for h in range(total.shape[1] // wide):
+            part = total[:, h * wide : (h + 1) * wide]
+            whole[h] = part.reshape(whole.shape[1:])
 
     @pl.when(c < 3)
     def _():
-        whole[...] = mm(normed_ref[...], d_qkv_ref[0], TN).reshape(whole.shape)
+        place(mm(normed_ref[...], d_qkv_ref[0], TN))
 
     @pl.when(c == 3)
     def _():
-        whole[...] = out_grad_ref[...].reshape(whole.shape)
-
-    for d, h, spot in spots:
-        index = me ^ spot
-        value = whole[d, :, pl.ds(h * wide, wide)]
-
-        @pl.when(index < half)
-        def _():
-            keep_ref[index, 0] = value
-
-        @pl.when(index >= half)
-        def _():
-            give_ref[index - half, 0] = value.astype(BF16)
+        place(out_grad_ref[...])
+
+    for index, (flip_row, flip_column) in enumerate(flips):
+        row = scalars[scalars.shape[0] + ROW_AT] ^ flip_row
+        column = scalars[scalars.shape[0] + COLUMN_AT] ^ flip_column
+        if index < half:
+            keep_ref[index, 0] = whole[column, row]
+        else:
+            give_ref[index - half, 0] = whole[column, row].astype(BF16)
 
 
 def forward_kernel(
@@ -224,7 +230,7 @@
     rows = qkv_ref.shape[1]
     load_keys(qkv_ref, message_ref, keys, values)
     state[...] = unfold_state(message_ref[0])
-    count_valid = scalars[scalars.shape[0] - 2]
+    count_valid = scalars[scalars.shape[0] + VALID]
     b0, b1, b2 = (blend_ref[pl.ds(f, 1), :] for f in range(3))
 
     def body(step, carry):
@@ -291,6 +297,91 @@
 
 def prologue_kernel(
     scalars,
+    query_ref,
+    key_ref,
+    message_ref,
+    start_ref,
+    blend_ref,
+    grad_ref,
+    near_ref,
+    far1_ref,
+    invl_ref,
+    invd_ref,
+    back_ref,
+    adjoint,
+):
+    rows = query_ref.shape[1]
+    step_rows = rows // 3
+    count_valid = scalars[scalars.shape[0] + VALID]
+    b0, b1, b2 = (blend_ref[pl.ds(f, 1), :] for f in range(3))
+    adjoint[...] = jnp.zeros(adjoint.shape, F32)
+
+    tails = message_ref[0, pl.ds(HEAD_DIM, TAIL), :]
+    key = jnp.concatenate([tails[:, :PAIR], key_ref[0]], axis=0)
+    value = jnp.concatenate([tails[:, PAIR : 2 * PAIR], key_ref[1]], axis=0)
+    start = start_ref[pl.ds(0, ROWS), :]
+    near_mask, _, _, row, _, _ = masks(0, start)
+    query = query_ref[0, pl.ds(0, ROWS), :]
+    grad_f = jnp.where(row < count_valid, grad_ref[pl.ds(0, ROWS), :].astype(F32), 0.0)
+    grad = grad_f.astype(BF16)
+    scale = b0 * invl_ref[...]
+    rows_q = (query.astype(F32) * (scale * HEAD_DIM**-0.5)).astype(BF16)
+    rows_g = (grad_f * scale).astype(BF16)
+    weights, _, d_key = near_back(
+        query,
+        split_heads(key),
+        mm(grad, split_heads(value), NT),
+        near_mask,
+        spread(grad_f * near_ref[...]),
+        scale * HEAD_DIM**-0.5,
+        rows_q,
+        rows_g,
+    )
+    back_ref[0, pl.ds(HEAD_DIM, TAIL), :] = jnp.concatenate(
+        [d_key[:TAIL], fold(mm(weights, rows_g, TN))[:TAIL], jnp.zeros((TAIL, PAIR), F32)], axis=1
+    ).astype(BF16)
+    heads = same_head().astype(F32).astype(BF16)
+    heads = jnp.concatenate([heads, heads], axis=0)
+
+    for step in range(3):
+        at = step * step_rows
+
+        @pl.when(scalars[scalars.shape[0] + CARRIED] > at)
+        def _():
+            here = pl.ds(at, step_rows)
+            row = iota((step_rows, PAIR), 0) + at
+            start = start_ref[here, :]
+            grad_f = jnp.where(row < count_valid, grad_ref[here, :].astype(F32), 0.0)
+            grad = grad_f.astype(BF16)
+            product = grad_f * far1_ref[here, :]
+            high = product.astype(BF16)
+            low = (product - high.astype(F32)).astype(BF16)
+            along = mm(jnp.concatenate([high, low], axis=1), heads).astype(BF16)
+            query_f = query_ref[0, here, :].astype(F32)
+            live = start < 0
+            scaled = jnp.where(live, lift(query_f) * (b1 * invd_ref[here, :]), 0.0)
+            bent = jnp.where(
+                live, jnp.tanh(query_f) * (b2 / (row - start + 1).astype(F32)), 0.0
+            )
+            adjoint[:, : 2 * PAIR] += mm(
+                scaled.astype(BF16), jnp.concatenate([grad, along], axis=1), TN
+            )
+            adjoint[:, 2 * PAIR :] += mm(bent.astype(BF16), grad, TN)
+
+    back_ref[0, pl.ds(0, HEAD_DIM), :] = fold_state(adjoint[...])
+
+
+def key_side(adjoint_low, lift_k, bend_k, value):
+    ones = jnp.full(value.shape, -1.0 / HEAD_DIM, BF16)
+    d_lift = mm(jnp.concatenate([value, ones], axis=1), adjoint_low[:, : 2 * PAIR], NT)
+    d_bend = mm(value, adjoint_low[:, 2 * PAIR :], NT)
+    both = jnp.concatenate([adjoint_low[:, :PAIR], adjoint_low[:, 2 * PAIR :]], axis=0)
+    d_value = mm(jnp.concatenate([lift_k, bend_k], axis=1), both)
+    return d_lift, d_bend, d_value
+
+
+def backward_kernel(
+    scalars,
     qkv_ref,
     message_ref,
     start_ref,
@@ -301,102 +392,11 @@
     far2_ref,
     invl_ref,
     invd_ref,
-    back_ref,
-    sums_ref,
-    adjoint,
-):
-    rows = qkv_ref.shape[1]
-    count_valid = scalars[scalars.shape[0] - 2]
-    b0, b1, b2 = (blend_ref[pl.ds(f, 1), :] for f in range(3))
-    adjoint[...] = jnp.zeros(adjoint.shape, F32)
-    sums_ref[...] = jnp.zeros(sums_ref.shape, F32)
-    lanes = iota((ROWS, PAIR), 1) < HEAD_DIM
-
-    tails = message_ref[0, pl.ds(HEAD_DIM, TAIL), :]
-    key = jnp.concatenate([tails[:, :PAIR], qkv_ref[1, pl.ds(0, ROWS), :]], axis=0)
-    value = jnp.concatenate([tails[:, PAIR : 2 * PAIR], qkv_ref[2, pl.ds(0, ROWS), :]], axis=0)
-    start = start_ref[pl.ds(0, ROWS), :]
-    near_mask, _, _, row, _, _ = masks(0, start)
-    query = qkv_ref[0, pl.ds(0, ROWS), :]
-    grad_f = jnp.where(row < count_valid, grad_ref[pl.ds(0, ROWS), :].astype(F32), 0.0)
-    grad = grad_f.astype(BF16)
-    scale = b0 * invl_ref[pl.ds(0, ROWS), :]
-    rows_q = (query.astype(F32) * (scale * HEAD_DIM**-0.5)).astype(BF16)
-    rows_g = (grad_f * scale).astype(BF16)
-    weights, _, d_key = near_back(
-        query,
-        split_heads(key),
-        mm(grad, split_heads(value), NT),
-        near_mask,
-        spread(grad_f * near_ref[pl.ds(0, ROWS), :]),
-        scale * HEAD_DIM**-0.5,
-        rows_q,
-        rows_g,
-    )
-    back_ref[0, pl.ds(HEAD_DIM, TAIL), :] = jnp.concatenate(
-        [d_key[:TAIL], fold(mm(weights, rows_g, TN))[:TAIL], jnp.zeros((TAIL, PAIR), F32)], axis=1
-    ).astype(BF16)
-
-    def body(step, carry):
-        at = pl.multiple_of(step * ROWS, 32)
-        row = iota((ROWS, PAIR), 0) + at
-        start = start_ref[pl.ds(at, ROWS), :]
-        grad_f = jnp.where(row < count_valid, grad_ref[pl.ds(at, ROWS), :].astype(F32), 0.0)
-        grad = grad_f.astype(BF16)
-        far1 = grad_f * far1_ref[pl.ds(at, ROWS), :]
-        sums_ref[pl.ds(0, 8), :] += jnp.sum(
-            (grad_f * near_ref[pl.ds(at, ROWS), :]).reshape(ROWS // 8, 8, PAIR), axis=0
-        )
-        sums_ref[pl.ds(8, 8), :] += jnp.sum(far1.reshape(ROWS // 8, 8, PAIR), axis=0)
-        sums_ref[pl.ds(16, 8), :] += jnp.sum(
-            (grad_f * far2_ref[pl.ds(at, ROWS), :]).reshape(ROWS // 8, 8, PAIR), axis=0
-        )
-
-        @pl.when(scalars[scalars.shape[0] - 4] > at)
-        def _():
-            wide = spread(far1)
-            along = jnp.where(lanes, wide[:, :WIN], wide[:, WIN:]).astype(BF16)
-            query_f = qkv_ref[0, pl.ds(at, ROWS), :].astype(F32)
-            live = start < 0
-            scaled = jnp.where(live, lift(query_f) * (b1 * invd_ref[pl.ds(at, ROWS), :]), 0.0)
-            bent = jnp.where(
-                live, jnp.tanh(query_f) * (b2 / (row - start + 1).astype(F32)), 0.0
-            )
-            adjoint[:, : 2 * PAIR] += mm(
-                scaled.astype(BF16), jnp.concatenate([grad, along], axis=1), TN
-            )
-            adjoint[:, 2 * PAIR :] += mm(bent.astype(BF16), grad, TN)
-
-        return carry
-
-    lax.fori_loop(0, rows // ROWS, body, 0)
-    back_ref[0, pl.ds(0, HEAD_DIM), :] = fold_state(adjoint[...])
-
-
-def key_side(adjoint_low, lift_k, bend_k, value):
-    ones = jnp.full(value.shape, -1.0 / HEAD_DIM, BF16)
-    d_lift = mm(jnp.concatenate([value, ones], axis=1), adjoint_low[:, : 2 * PAIR], NT)
-    d_bend = mm(value, adjoint_low[:, 2 * PAIR :], NT)
-    both = jnp.concatenate([adjoint_low[:, :PAIR], adjoint_low[:, 2 * PAIR :]], axis=0)
-    d_value = mm(jnp.concatenate([lift_k, bend_k], axis=1), both)
-    return d_lift, d_bend, d_value
-
-
-def backward_kernel(
-    scalars,
-    qkv_ref,
-    message_ref,
-    start_ref,
-    blend_ref,
-    grad_ref,
-    near_ref,
-    far1_ref,
-    invl_ref,
-    invd_ref,
     states_ref,
     back_ref,
     done_ref,
     out_ref,
+    sums_ref,
     keys,
     values,
     adjoint,
@@ -406,8 +406,8 @@
     rows = qkv_ref.shape[1]
     steps = rows // ROWS
     load_keys(qkv_ref, message_ref, keys, values)
-    count_valid = scalars[scalars.shape[0] - 2]
-    last = scalars[scalars.shape[0] - 3]
+    count_valid = scalars[scalars.shape[0] + VALID]
+    last = scalars[scalars.shape[0] + LAST]
     b0, b1, b2 = (blend_ref[pl.ds(f, 1), :] for f in range(3))
     lanes = iota((ROWS, PAIR), 1) < HEAD_DIM
 
@@ -426,6 +426,10 @@
     )
     value_carry[...] = tail_grads[:, PAIR : 2 * PAIR] + jnp.where(live, end_parts[2], 0.0)
     adjoint[...] = jnp.where(last < rows - TAIL, 1.0, 0.0) * arrived
+    sums_ref[...] = jnp.zeros(sums_ref.shape, F32)
+
+    def add_up(place, product):
+        sums_ref[pl.ds(place, 8), :] += jnp.sum(product.reshape(ROWS // 8, 8, PAIR), axis=0)
 
     def body(back, carry):
         step = steps - 1 - back
@@ -450,17 +454,22 @@
         r2 = b2 / (row - start + 1).astype(F32)
         grad_pair = mm(grad, split_heads(value), NT)
         rows_q = (query_f * (r0 * HEAD_DIM**-0.5)).astype(BF16)
+        near_product = grad_f * near_ref[pl.ds(at, ROWS), :]
         weights, d_query, d_key = near_back(
             query,
             split_heads(key),
             grad_pair,
             near_mask,
-            spread(grad_f * near_ref[pl.ds(at, ROWS), :]),
+            spread(near_product),
             r0 * HEAD_DIM**-0.5,
             rows_q,
             None,
         )
-        spread_far = spread(grad_f * far1_ref[pl.ds(at, ROWS), :])
+        far1_product = grad_f * far1_ref[pl.ds(at, ROWS), :]
+        add_up(0, near_product)
+        add_up(8, far1_product)
+        add_up(16, grad_f * far2_ref[pl.ds(at, ROWS), :])
+        spread_far = spread(far1_product)
         along = jnp.where(lanes, spread_far[:, :WIN], spread_far[:, WIN:])
         shifted = jnp.where(far_two, grad_pair - spread_far, 0.0).astype(BF16)
         plain = jnp.where(far_two, grad_pair, 0.0).astype(BF16)
@@ -519,6 +528,10 @@
     lax.fori_loop(0, steps, body, 0)
 
 
+def resume(kernel, done, scalars, qkv_ref, message_ref, start_ref, blend_ref, *refs):
+    kernel(scalars, qkv_ref, message_ref, start_ref, blend_ref, *refs[done:])
+
+
 def pair_specs(rows, first=0):
     return {
         "qkv": pl.BlockSpec((3, rows, PAIR), lambda p, s: (0, 0, p + first)),
@@ -527,7 +540,9 @@
         "blend": pl.BlockSpec((3, PAIR), lambda p, s: (0, p + first)),
         "column": pl.BlockSpec((rows, PAIR), lambda p, s: (0, p + first)),
         "states": pl.BlockSpec((1, rows // ROWS * PAIR, 3 * PAIR), lambda p, s: (p + first, 0, 0)),
-        "sums": pl.BlockSpec((24, PAIR), lambda p, s: (0, p + first)),
+        "sums": pl.BlockSpec((24, PAIR), lambda p, s: (0, p)),
+        "query": pl.BlockSpec((1, rows, PAIR), lambda p, s: (0, 0, p)),
+        "head_rows": pl.BlockSpec((ROWS, PAIR), lambda p, s: (0, p)),
     }
 
 
@@ -585,12 +600,13 @@
     return [pair for group in phases() for pair in group]
 
 
-def relative_index(dp_index, head_index):
-    index = 0
-    for place, (axis, mask) in enumerate(relative_bits()):
-        own = dp_index if axis == "dp" else head_index
-        index = index | (((own // mask) & 1) << place)
-    return index
+def all_flips():
+    order = relative_bits()
+    flips = []
+    for index in range(1 << len(order)):
+        chosen = [pair for place, pair in enumerate(order) if index >> place & 1]
+        flips.append(tuple(sum(m for a, m in chosen if a == axis) for axis in ("dp", "head")))
+    return flips
 
 
 def peer(array, group, combo):
@@ -606,9 +622,12 @@
     return lax.ppermute(array, ("dp", "head"), pairs)
 
 
-def widen(block, group, axis):
+def widen(block, group, axis, after=None):
     others = [peer(block, group, combo) for combo in range(1, 1 << len(group))]
-    return jnp.concatenate([block] + others, axis=axis)
+    if after is not None:
+        others, after = lax.optimization_barrier((others, after))
+    whole = jnp.concatenate([block] + others, axis=axis)
+    return whole if after is None else (whole, after)
 
 
 def narrow(keep, gives, group):
@@ -657,17 +676,14 @@
     pairs = width // PAIR
     steps = rows // ROWS
     groups = phases()
-    spots = [(d, h, relative_index(d, h)) for d in range(n_dp) for h in range(n_head)]
+    flips = all_flips()
 
     shards = jnp.concatenate([qkv_weight, out_weight.T[None]], axis=0)[None]
     feed = jnp.stack([in_weight, down_weight])
     for group in groups[:-1]:
         shards = widen(shards, group, 0)
-    shards, feed = lax.optimization_barrier((shards, feed))
-    shards = widen(shards, groups[-1], 0)
-    for group in groups:
-        feed = widen(feed, group, 1)
-    in_all, down_all = feed[0], feed[1]
+    others = peer(shards, groups[-1], 1)
+    feed, others = lax.optimization_barrier((feed, others))
 
     item_lengths = lengths[0]
     slots = item_lengths.shape[0]
@@ -690,7 +706,8 @@
             carried_rows[None],
             start[rows - 1 :],
             (total - offset)[None],
-            jnp.asarray(relative_index(lax.axis_index("dp"), lax.axis_index("head")), jnp.int32)[None],
+            lax.axis_index("dp").astype(jnp.int32)[None],
+            lax.axis_index("head").astype(jnp.int32)[None],
         ]
     )
     start_wide = jnp.broadcast_to(start[:, None], (rows, PAIR))
@@ -708,10 +725,11 @@
         return pl.BlockSpec(shape, lambda p, s: (0,) * len(shape))
 
     qkv, normed_one, qkv_all, out_all, closing = call(
-        functools.partial(project_kernel, spots=spots),
+        functools.partial(project_kernel, flips=flips),
         [
             pl.BlockSpec((part, width), lambda p, s: (p, 0)),
             whole_spec((1, width)),
+            whole_spec(shards.shape),
             whole_spec(shards.shape),
         ],
         [
@@ -728,29 +746,48 @@
             jax.ShapeDtypeStruct((width, width), BF16),
             message_shape,
         ],
-        [pltpu.VMEM((pairs, PAIR, 3 * PAIR), F32)],
+        [
+            pltpu.VMEM((pairs, PAIR, 3 * PAIR), F32),
+            pltpu.VMEM((n_head, 4, n_dp, width // n_dp, width // n_head), BF16),
+        ],
         3,
         "project",
         6 * big * width,
         12 * big,
-    )(scalars, tokens, ln1_gain[None], shards)
+    )(scalars, tokens, ln1_gain[None], shards, others)
+    feed = widen(feed, groups[0], 1)
+    feed, closing = lax.optimization_barrier((feed, closing))
     message = pass_along(closing, keep_all, 1)
 
     key_scratch = pltpu.VMEM((rows + TAIL, PAIR), BF16)
     state_scratch = pltpu.VMEM((PAIR, 3 * PAIR), F32)
     tail_scratch = pltpu.VMEM((TAIL, PAIR), F32)
-    mixed, near, far1, far2, inv_l, inv_d, states = call(
-        forward_kernel,
-        [spec["qkv"], spec["message"], spec["start"], spec["blend"]],
-        [spec["column"]] * 6 + [spec["states"]],
-        [jax.ShapeDtypeStruct((rows, width), BF16)] + [wide] * 5 + [states_shape],
-        [key_scratch, key_scratch, state_scratch],
-        pairs,
-        "forward",
-        8000 * big,
-        40 * big,
-    )(scalars, qkv, message, start_wide, blend_wide)
-
+    results = ()
+    count = pairs // 2
+    for first in (0, count):
+        spec = pair_specs(rows, first)
+        results = call(
+            functools.partial(resume, forward_kernel, len(results)),
+            [spec["qkv"], spec["message"], spec["start"], spec["blend"]]
+            + [pl.BlockSpec(memory_space=pl.ANY)] * len(results),
+            [spec["column"]] * 6 + [spec["states"]],
+            [jax.ShapeDtypeStruct((rows, width), BF16)] + [wide] * 5 + [states_shape],
+            [key_scratch, key_scratch, state_scratch],
+            count,
+            "forward",
+            4000 * big,
+            20 * big,
+            {5 + i: i for i in range(len(results))},
+        )(scalars, qkv, message, start_wide, blend_wide, *results)
+        if not first:
+            feed, results = widen(feed, groups[1], 1, results)
+            feed, message = lax.optimization_barrier((feed, message))
+    for group in groups[2:]:
+        feed = widen(feed, group, 1)
+    in_all, down_all = feed[0], feed[1]
+    mixed, near, far1, far2, inv_l, inv_d, states = results
+
+    spec = pair_specs(rows)
     residual = tokens.astype(F32)
     hidden = residual + lax.dot_general(mixed, out_all, NT, preferred_element_type=F32)
     normal_two, scale_two = norm_parts(hidden)
@@ -774,19 +811,30 @@
     d_mixed = jnp.dot(d_branch, out_all, preferred_element_type=F32).astype(BF16)
     out_grad = lax.dot_general(d_branch, mixed, TN, preferred_element_type=F32)
 
-    back, sums = call(
+    front_keys = qkv[1:, :ROWS]
+    back = call(
         prologue_kernel,
-        [spec["qkv"], spec["message"], spec["start"], spec["blend"]] + [spec["column"]] * 6,
-        [spec["message"], spec["sums"]],
-        [message_shape, jax.ShapeDtypeStruct((24, width), F32)],
+        [
+            spec["query"],
+            pl.BlockSpec((2, ROWS, PAIR), lambda p, s: (0, 0, p)),
+            spec["message"],
+            spec["start"],
+            spec["blend"],
+            spec["column"],
+            spec["head_rows"],
+            spec["column"],
+            spec["head_rows"],
+            spec["column"],
+        ],
+        spec["message"],
+        message_shape,
         [state_scratch],
         pairs,
         "prologue",
         500 * big,
-        28 * big,
-    )(scalars, qkv, message, start_wide, blend_wide, d_mixed, near, far1, far2, inv_l, inv_d)
+        20 * big,
+    )(scalars, qkv, front_keys, message, start_wide, blend_wide, d_mixed, near, far1, inv_l, inv_d)
     back_in = pass_along(back, keep_all, -1)
-    blend_part = jnp.sum(sums.reshape(3, 8, blend.shape[1], HEAD_DIM), axis=(1, 3))
 
     half = in_grad.shape[0] // 2
     keep = jnp.stack([in_grad[:half], down_grad[:half]])
@@ -795,17 +843,21 @@
     left = list(reversed(groups[:-1]))
 
     d_qkv = jnp.zeros((3, 8, PAIR), BF16)
+    sums = []
     first = 0
     for count in (pairs // 4, pairs // 2, pairs // 4):
         spec = pair_specs(rows, first)
-        more = {12: 0} if first else {}
-        d_qkv = call(
+        more = {13: 0} if first else {}
+        d_qkv, part_sums = call(
             backward_kernel,
             [spec["qkv"], spec["message"], spec["start"], spec["blend"]]
-            + [spec["column"]] * 5
+            + [spec["column"]] * 6
             + [spec["states"], spec["message"], pl.BlockSpec(memory_space=pl.ANY)],
-            spec["qkv"],
-            jax.ShapeDtypeStruct((3, rows, width), BF16),
+            [spec["qkv"], spec["sums"]],
+            [
+                jax.ShapeDtypeStruct((3, rows, width), BF16),
+                jax.ShapeDtypeStruct((24, count * PAIR), F32),
+            ],
             [key_scratch, key_scratch, state_scratch, tail_scratch, tail_scratch],
             count,
             "backward",
@@ -821,23 +873,28 @@
             d_mixed,
             near,
             far1,
+            far2,
             inv_l,
             inv_d,
             states,
             back_in,
             d_qkv,
         )
+        sums.append(part_sums)
         first += count
         if left and first < pairs:
             feed_share, back_in = lax.optimization_barrier((feed_share, back_in))
             feed_share = narrow_axis(feed_share, left.pop(0), 1)
     for group in left:
         feed_share = narrow_axis(feed_share, group, 1)
+    feed_share, d_qkv = lax.optimization_barrier((feed_share, d_qkv))
+    sums = jnp.concatenate(sums, axis=1)
+    blend_part = jnp.sum(sums.reshape(3, 8, blend.shape[1], HEAD_DIM), axis=(1, 3))
 
     shard_shape = (n_dp * n_head // 2, 4, width // n_dp, width // n_head)
     shard_spec = pl.BlockSpec((shard_shape[0], 1) + shard_shape[2:], lambda p, s: (0, p, 0, 0))
     keep, give = call(
-        functools.partial(weight_grad_kernel, spots=spots, n_head=n_head),
+        functools.partial(weight_grad_kernel, flips=flips),
         [
             whole_spec((rows, width)),
             pl.BlockSpec((1, rows, width), lambda p, s: (jnp.minimum(p, 2), 0, 0)),
@@ -845,13 +902,14 @@
         ],
         [shard_spec, shard_spec],
         [jax.ShapeDtypeStruct(shard_shape, F32), jax.ShapeDtypeStruct(shard_shape, BF16)],
-        [pltpu.VMEM((n_dp, width // n_dp, width), F32)],
+        [pltpu.VMEM((n_head, n_dp, width // n_dp, width // n_head), F32)],
         4,
         "weight_grad",
         6 * big * width,
         8 * big,
     )(scalars, normed_one, d_qkv, out_grad)
     share = narrow(keep, [give], groups[-1])
+    d_qkv, give = lax.optimization_barrier((d_qkv, give))
     for group in reversed(groups[:-1]):
         share = narrow_axis(share, group, 0)
     d_normed_one = jnp.einsum("cte,cde->td", d_qkv, qkv_all, preferred_element_type=F32)

time: 383 us -> 337 us (0.88)
  starting transfers between devices: 67.1 us -> 48.1 us
  waiting for transfers between devices: 48.3 us -> 33.6 us
  local copies, waits for them, and re-layouts: 40.6 us -> 34.3 us
  matrix products: 60 us -> 55.7 us
    ppermute x35, starting transfers between devices: 61.9 us -> 43 us  [peer(): return lax.ppermute(array, ('dp', 'head'), pairs)]
    ppermute x35, waiting for transfers between devices: 44.5 us -> 29.7 us  [peer(): return lax.ppermute(array, ('dp', 'head'), pairs)]
    unnamed x65 -> x54, local copies, waits for them, and re-layouts: 21.9 us -> 12.2 us
    dot_general x1, matrix products: 8.96 us -> 4.89 us  [per_device(): jnp.dot(active, down_all, preferred_element_type=F32)]
    pallas_call x4 -> x5, Pallas kernels: 64.8 us -> 64.5 us  [the longest x2 38.1 us: per_device(): call(functools.partial(resume, forward_kernel, len(results)), [spec['qkv'...]
  transfers between devices with their start and end apart: 37 -> 37, of which waited for: 17 -> 12; matrix products, arithmetic and copies ran while one was open for 19% -> 14% of each run, Pallas kernels for 32% -> 38%
where the time goes in v3:
time: 337 us; the launch traced here: 332 us
  Pallas kernels  136 us (40%)
  matrix products  55.7 us (17%)
  starting transfers between devices  48.1 us (14%)
  local copies, waits for them, and re-layouts  34.3 us (10%)
  waiting for transfers between devices  33.6 us (10%)
  other arithmetic  22.4 us (7%)
    pallas_call x3, Pallas kernels, per_device(): call(backward_kernel, [spec['qkv'], spec['message'], spec['start'], spec[...  71.5 us
    ppermute x35, starting transfers between devices, peer(): return lax.ppermute(array, ('dp', 'head'), pairs)  43 us
    pallas_call x2, Pallas kernels, per_device(): call(functools.partial(resume, forward_kernel, len(results)), [spec['qkv'...  38.1 us
    ppermute x35, waiting for transfers between devices, peer(): return lax.ppermute(array, ('dp', 'head'), pairs)  29.7 us
    dot_general x1, matrix products, per_device(): lax.dot_general(cotangent, down_all, NT, preferred_element_type=F32)  12.5 us
    unnamed x54, local copies, waits for them, and re-layouts  12.2 us
    pallas_call x1, Pallas kernels, per_device(): call(functools.partial(project_kernel, flips=flips), [pl.BlockSpec((part,...  10.4 us
    dot_general x1, matrix products, per_device(): inner = lax.dot_general(normed_two, in_all, NT, preferred_element_type=F32)  9.76 us
  transfers between devices with their start and end apart: 37, of which 12 were waited for; matrix products, arithmetic and copies ran while one was open for 14% of the time, Pallas kernels for 38%

profile of v3, /device:TPU:0, one launch (start us, length us, event | category | flops | bytes accessed | tf_op | source)
XLA Modules:
  0.0 332.0 jit_solution(309106459802689947)
XLA Ops:
  1.5 5.1 %collective-permute-start.2 = (bf16[1,4,32,256]{3,2,1,0:T(8,128)(2,1)S(1)}, bf16[1,4,32,256]{3,2,1,0:T(8,128)(2,1)S(1)}, u32[]{:S(2)}, u32[]{:S(2)}) collective-permute-start(bf16[1,4,32,256]{3,2,1,0:T(8,128)(2,1)S(1)} %maximum_bitcast_fusion), channel_id=1, source_target_pairs={{0,24},{1,25},{2,26},{3,27},{4,28},{5,29},{6,30},{7,31},{8,16},{9,... | collective-permute-start | bytes 196616 | tf_op jit(solution)/shard_map/ppermute | solution.py:622
  9.1 3.1 collective-permute-done.1
  15.8 10.9 %collective-permute-done.3 = bf16[4,4,32,256]{3,2,1,0:T(8,128)(2,1)S(1)} collective-permute-done((bf16[4,4,32,256]{3,2,1,0:T(8,128)(2,1)S(1)}, bf16[4,4,32,256]{3,2,1,0:T(8,128)(2,1)S(1)}, u32[]{:S(2)}, u32[]{:S(2)}) %collective-permute-start.3) | collective-permute-done | bytes 262176 | tf_op jit(solution)/shard_map/ppermute | solution.py:622
  36.4 2.9 collective-permute-start.7
  39.3 10.4 %project.1 = (bf16[3,1536,512]{2,1,0:T(8,128)(2,1)}, bf16[1536,512]{1,0:T(8,128)(2,1)}, bf16[3,512,512]{2,1,0:T(8,128)(2,1)}, bf16[512,512]{1,0:T(8,128)(2,1)}, bf16[4,96,384]{2,1,0:T(8,128)(2,1)}) custom-call(s32[21]{0:T(128)} %concatenate.28.scalars, bf16[1536,512]{1,0:T(8,128)(2,1)} %tokens_ref.1, f32[1,512]{1,0:T(1,128)} %bitcast.70, ...), custom_call_target="tpu_custom_call" | custom-call | flops 2415919104 | bytes 9437184 | tf_op jit(solution)/shard_map/project/pallas_call | solution.py:727
  49.8 3.6 %collective-permute-start.13 = (bf16[4,96,384]{2,1,0:T(8,128)(2,1)}, bf16[4,96,384]{2,1,0:T(8,128)(2,1)S(1)}, u32[]{:S(2)}, u32[]{:S(2)}) collective-permute-start(bf16[4,96,384]{2,1,0:T(8,128)(2,1)} %get-tuple-element.64), channel_id=1, source_target_pairs={{0,1},{2,3},{4,5},{6,7},{8,9},{10,11},{12,13},{14,15},{16,17},{18,... | collective-permute-start | bytes 884744 | tf_op jit(solution)/shard_map/ppermute | solution.py:654
  53.8 2.7 collective-permute-start.11
  62.1 19.2 %forward.2 = (bf16[1536,512]{1,0:T(8,128)(2,1)}, f32[1536,512]{1,0:T(8,128)}, f32[1536,512]{1,0:T(8,128)}, f32[1536,512]{1,0:T(8,128)}, f32[1536,512]{1,0:T(8,12...) custom-call(s32[21]{0:T(128)} %concatenate.28.scalars, ...), custom_call_target="tpu_custom_call" | custom-call | flops 3145728000 | bytes 15728640 | tf_op jit(solution)/shard_map/forward/pallas_call | solution.py:769
  82.0 2.6 pad_maximum_fusion
  90.1 18.9 %forward.3 = (bf16[1536,512]{1,0:T(8,128)(2,1)}, f32[1536,512]{1,0:T(8,128)}, f32[1536,512]{1,0:T(8,128)}, f32[1536,512]{1,0:T(8,128)}, f32[1536,512]{1,0:T(8,12...) custom-call(s32[21]{0:T(128)} %concatenate.28.scalars, ...), custom_call_target="tpu_custom_call", output_to_operand_aliasing={{0}: (5, {}), {1}: (6, {}), {2}: (7, {}), {3}: (8, {}), {4}... | custom-call | flops 3145728000 | bytes 15728640 | tf_op jit(solution)/shard_map/forward/pallas_call | solution.py:769
  114.3 9.8 %multiply_convert_fusion = (bf16[1536,2048]{1,0:T(8,128)(2,1)S(1)}, f32[1536,2048]{1,0:T(8,128)}) fusion(bf16[2,2048,512]{2,1,0:T(8,128)(2,1)S(1)} %constant_dynamic-update-slice_fusion.7, f32[1536,512]{0,1:T(8,128)S(1)} %get-tuple-element.175, f32[512]{0:T(512)S(1)} %copy-done.14, f32[1536]{0:T(1024)S(1)} %add_rsqrt_fusion.1, ...), kind=kOutput, calls=%fused_computation.11 | convolution fusion | flops 3252682752 | bytes 24135680 | tf_op jit(solution)/shard_map/dot_general | solution.py:795
  124.1 4.9 %fusion.20 = bf16[1536,512]{0,1:T(8,128)(2,1)} fusion(f32[1536,512]{0,1:T(8,128)S(1)} %get-tuple-element.175, bf16[1536,2048]{1,0:T(8,128)(2,1)S(1)} %get-tuple-element.176, bf16[2,2048,512]{2,1,0:T(8,128)(2,1)S(1)} %constant_dynamic-update-slice_fusion.7), kind=kOutput, calls=%fused_computation.35 | convolution fusion | flops 3222798336 | bytes 13107200 | tf_op jit(solution)/shard_map/dot_general | solution.py:799
  129.0 5.0 %fusion.45 = f32[2048,512]{1,0:T(8,128)} fusion(bf16[1536,2048]{1,0:T(8,128)(2,1)S(1)} %get-tuple-element.176, bf16[1536,512]{1,0:T(8,128)(2,1)S(1)} %copy-done.10), kind=kOutput, calls=%fused_computation.115 | convolution fusion | flops 3221225472 | bytes 12058624 | tf_op jit(solution)/shard_map/dot_general | solution.py:801
  134.0 12.5 %fusion.8 = bf16[1536,2048]{1,0:T(8,128)(2,1)S(1)} fusion(f32[1536,2048]{1,0:T(8,128)} %get-tuple-element.177, bf16[1536,512]{1,0:T(8,128)(2,1)S(1)} %copy-done.10, bf16[2,2048,512]{2,1,0:T(8,128)(2,1)S(1)} %constant_dynamic-update-slice_fusion.7), kind=kOutput, calls=%fused_computation.10 | convolution fusion | flops 3280994304 | bytes 22544384 | tf_op jit(solution)/shard_map/dot_general | solution.py:800
  146.5 6.6 %multiply_reduce_fusion = (f32[512]{0:T(512)}, f32[1536]{0:T(1024)S(1)}, f32[1536]{0:T(1024)S(1)}, f32[1536,512]{0,1:T(8,128)}) fusion(f32[1536,512]{0,1:T(8,128)S(1)} %get-tuple-element.175, f32[1536]{0:T(1024)S(1)} %add_rsqrt_fusion.1, f32[1536]{0:T(1024)S(1)} %broadcast_multiply_fusion.5, f32[512]{0:T(512)S(1)} %copy-done.14, ...), kind=kOutput, calls=%fused_computation.29 | convolution fusion | flops 3227513344 | bytes 14712832 | tf_op jit(solution)/shard_map/dot_general | solution.py:807
  153.1 5.7 %fusion.35 = f32[2048,512]{1,0:T(8,128)} fusion(bf16[1536,2048]{1,0:T(8,128)(2,1)S(1)} %fusion.8, f32[1536,512]{0,1:T(8,128)S(1)} %get-tuple-element.175, f32[512]{0:T(512)S(1)} %copy-done.14, f32[1536]{0:T(1024)S(1)} %add_rsqrt_fusion.1, f32[1536]{0:T(1024)S(1)} %broadcast_multiply_fusion.5), kind=kOutput, calls=%fused_computation.106 | convolution fusion | flops 3224371200 | bytes 13645824 | tf_op jit(solution)/shard_map/dot_general | solution.py:806
  158.8 2.6 copy.50
  161.4 2.6 fusion.23
  170.1 7.5 %prologue.1 = bf16[4,96,384]{2,1,0:T(8,128)(2,1)} custom-call(s32[21]{0:T(128)} %concatenate.28.scalars, bf16[3,1536,512]{2,1,0:T(8,128)(2,1)} %get-tuple-element.60.qkv_ref.query_ref, bf16[2,96,512]{2,1,0:T(8,128)(2,1)} %slice.69.key_ref, bf16[4,96,384]{2,1,0:T(8,128)(2,1)} %copy-done.5, s32[1536,128]{1,0:T(8,128)} %broadcast_in_dim.85.start_ref, ...), custom_call_target="tpu_custom_call" | custom-call | flops 393216000 | bytes 15728640 | tf_op jit(solution)/shard_map/prologue/pallas_call | solution.py:815
  179.1 4.0 %slice_bitcast_fusion = (f32[1,1024,512]{2,1,0:T(8,128)S(1)}, f32[1,1024,512]{2,1,0:T(8,128)}) fusion(f32[2048,512]{1,0:T(8,128)} %fusion.45, f32[2048,512]{1,0:T(8,128)} %fusion.35), kind=kLoop, calls=%fused_computation.41 | loop fusion | bytes 8388608 | tf_op jit(solution)/shard_map/stack | solution.py:840
  185.1 2.7 collective-permute-done.16.back_ref
  188.5 18.7 %backward.3 = (bf16[3,1536,512]{2,1,0:T(8,128)(2,1)}, f32[24,128]{1,0:T(8,128)}) custom-call(s32[21]{0:T(128)} %concatenate.28.scalars, bf16[3,1536,512]{2,1,0:T(8,128)(2,1)} %get-tuple-element.60.qkv_ref.query_ref, bf16[4,96,384]{2,1,0:T(8,128)(2,1)} %copy-done.5, s32[1536,128]{1,0:T(8,128)} %broadcast_in_dim.85.start_ref, f32[3,512]{1,0:T(4,128)} %reshape.96.blend_ref, ...), custom_call_target="tpu_custom_call" | custom-call | flops 3145728000 | bytes 7864320 | tf_op jit(solution)/shard_map/backward/pallas_call | solution.py:851
  207.2 3.0 maximum_add_fusion
  211.4 4.5 %collective-permute-start.17 = (bf16[2,256,512]{2,1,0:T(8,128)(2,1)}, bf16[2,256,512]{2,1,0:T(8,128)(2,1)S(1)}, u32[]{:S(2)}, u32[]{:S(2)}) collective-permute-start(bf16[2,256,512]{2,1,0:T(8,128)(2,1)} %get-tuple-element.158), channel_id=1, source_target_pairs={{0,4},{1,5},{2,6},{3,7},{4,0},{5,1},{6,2},{7,3},{8,12},{9,13},{10,... | collective-permute-start | bytes 1572872 | tf_op jit(solution)/shard_map/ppermute | solution.py:622
  217.3 33.9 %backward.4 = (bf16[3,1536,512]{2,1,0:T(8,128)(2,1)}, f32[24,256]{1,0:T(8,128)}) custom-call(s32[21]{0:T(128)} %concatenate.28.scalars, bf16[3,1536,512]{2,1,0:T(8,128)(2,1)} %get-tuple-element.60.qkv_ref.query_ref, bf16[4,96,384]{2,1,0:T(8,128)(2,1)} %copy-done.5, s32[1536,128]{1,0:T(8,128)} %broadcast_in_dim.85.start_ref, ...), custom_call_target="tpu_custom_call", output_to_operand_aliasing={{0}: (13, {})} | custom-call | flops 6291456000 | bytes 15728640 | tf_op jit(solution)/shard_map/backward/pallas_call | solution.py:851
  256.8 18.9 %backward.5 = (bf16[3,1536,512]{2,1,0:T(8,128)(2,1)}, f32[24,128]{1,0:T(8,128)}) custom-call(s32[21]{0:T(128)} %concatenate.28.scalars, bf16[3,1536,512]{2,1,0:T(8,128)(2,1)} %get-tuple-element.60.qkv_ref.query_ref, bf16[4,96,384]{2,1,0:T(8,128)(2,1)} %copy-done.5, s32[1536,128]{1,0:T(8,128)} %broadcast_in_dim.85.start_ref, ...), custom_call_target="tpu_custom_call", output_to_operand_aliasing={{0}: (13, {})} | custom-call | flops 3145728000 | bytes 7864320 | tf_op jit(solution)/shard_map/backward/pallas_call | solution.py:851
  277.3 8.5 %weight_grad.1 = (f32[16,4,32,256]{3,2,1,0:T(8,128)}, bf16[16,4,32,256]{3,2,1,0:T(8,128)(2,1)}) custom-call(s32[21]{0:T(128)} %concatenate.28.scalars, bf16[1536,512]{1,0:T(8,128)(2,1)} %get-tuple-element.100.normed_ref, bf16[3,1536,512]{2,1,0:T(8,128)(2,1)} %get-tuple-element.102.d_qkv_ref, f32[512,512]{1,0:T(8,128)} %fusion.25.out_grad_ref), custom_call_target="tpu_custom_call" | custom-call | flops 2415919104 | bytes 6291456 | tf_op jit(solution)/shard_map/weight_grad/pallas_call | solution.py:896
  285.9 4.6 %fusion.18 = (f32[512]{0:T(512)S(1)}, f32[1536]{0:T(1024)S(1)}, f32[1536]{0:T(1024)S(1)}, f32[1536,512]{0,1:T(8,128)S(1)}) fusion(bf16[1536,512]{0,1:T(8,128)(2,1)S(1)} %copy.46, f32[1536]{0:T(1024)S(1)} %add_rsqrt_fusion, f32[1536]{0:T(1024)S(1)} %broadcast_multiply_fusion.2, f32[512]{0:T(512)S(1)} %copy-done.15, bf16[3,1536,512]{2,1,0:T(8,128)(2,1)S(1)} %bitcast.65, ...), kind=kOutput, calls=%fused_computation.27 | convolution fusion | flops 2422993408 | bytes 11038720 | tf_op jit(solution)/shard_map/cte,cde->td/dot_general | solution.py:915
  291.0 2.7 fusion.17
  298.0 3.5 %copy.51 = f32[1536,512]{1,0:T(8,128)} copy(f32[1536,512]{0,1:T(8,128)} %fusion.17) | data formatting | bytes 6291456
  301.6 2.5 collective-permute-start.29
  312.4 8.3 %collective-permute-done.31 = bf16[4,4,32,256]{3,2,1,0:T(8,128)(2,1)S(1)} collective-permute-done((bf16[4,4,32,256]{3,2,1,0:T(8,128)(2,1)S(1)}, bf16[4,4,32,256]{3,2,1,0:T(8,128)(2,1)S(1)}, u32[]{:S(2)}, u32[]{:S(2)}) %collective-permute-start.31) | collective-permute-done | bytes 262176 | tf_op jit(solution)/shard_map/ppermute | solution.py:622
  (179 shorter events, 77.7 us)
Async XLA Ops:
  1.5 7.6 %collective-permute-start.2 = (bf16[1,4,32,256]{3,2,1,0:T(8,128)(2,1)S(1)}, bf16[1,4,32,256]{3,2,1,0:T(8,128)(2,1)S(1)}, u32[]{:S(2)}, u32[]{:S(2)}) collective-permute-start(bf16[1,4,32,256]{3,2,1,0:T(8,128)(2,1)S(1)} %maximum_bitcast_fusion), channel_id=1, source_target_pairs={{0,24},{1,25},{2,26},{3,27},{4,28},{5,29},{6,30},{7,31},{8,16},{9,... | collective-permute-start | bytes 196616 | tf_op jit(solution)/shard_map/ppermute | solution.py:622
  12.2 14.7 %collective-permute-start.5 = (bf16[4,4,32,256]{3,2,1,0:T(8,128)(2,1)S(1)}, bf16[4,4,32,256]{3,2,1,0:T(8,128)(2,1)S(1)}, u32[]{:S(2)}, u32[]{:S(2)}) collective-permute-start(bf16[4,4,32,256]{3,2,1,0:T(8,128)(2,1)S(1)} %pad_maximum_fusion.3), channel_id=1, source_target_pairs={{0,5},{1,4},{2,7},{3,6},{4,1},{5,0},{6,3},{7,2},{8,13},{9,12},{10,... | collective-permute-start | bytes 786440 | tf_op jit(solution)/shard_map/ppermute | solution.py:622
  14.7 12.2 %collective-permute-start.4 = (bf16[4,4,32,256]{3,2,1,0:T(8,128)(2,1)S(1)}, bf16[4,4,32,256]{3,2,1,0:T(8,128)(2,1)S(1)}, u32[]{:S(2)}, u32[]{:S(2)}) collective-permute-start(bf16[4,4,32,256]{3,2,1,0:T(8,128)(2,1)S(1)} %pad_maximum_fusion.3), channel_id=1, source_target_pairs={{0,1},{1,0},{2,3},{3,2},{4,5},{5,4},{6,7},{7,6},{8,9},{9,8},{10,11... | collective-permute-start | bytes 786440 | tf_op jit(solution)/shard_map/ppermute | solution.py:622
  15.3 11.4 %collective-permute-start.3 = (bf16[4,4,32,256]{3,2,1,0:T(8,128)(2,1)S(1)}, bf16[4,4,32,256]{3,2,1,0:T(8,128)(2,1)S(1)}, u32[]{:S(2)}, u32[]{:S(2)}) collective-permute-start(bf16[4,4,32,256]{3,2,1,0:T(8,128)(2,1)S(1)} %pad_maximum_fusion.3), channel_id=1, source_target_pairs={{0,4},{1,5},{2,6},{3,7},{4,0},{5,1},{6,2},{7,3},{8,12},{9,13},{10,... | collective-permute-start | bytes 786440 | tf_op jit(solution)/shard_map/ppermute | solution.py:622
  27.0 7.9 %collective-permute-start.6 = (bf16[16,4,32,256]{3,2,1,0:T(8,128)(2,1)S(1)}, bf16[16,4,32,256]{3,2,1,0:T(8,128)(2,1)S(1)}, u32[]{:S(2)}, u32[]{:S(2)}) collective-permute-start(bf16[16,4,32,256]{3,2,1,0:T(8,128)(2,1)S(1)} %constant_dynamic-update-slice_fusion.own_ref), channel_id=1, source_target_pairs={{0,2},{1,3},{2,0},{3,1},{4,6},{5,7},{6,4},{7,5},{8,10},{9,11},{10,... | collective-permute-start | bytes 3145736 | tf_op jit(solution)/shard_map/ppermute | solution.py:622
  34.9 14.9 %collective-permute-start.9 = (bf16[2,64,512]{2,1,0:T(8,128)(2,1)S(1)}, bf16[2,64,512]{2,1,0:T(8,128)(2,1)S(1)}, u32[]{:S(2)}, u32[]{:S(2)}) collective-permute-start(bf16[2,64,512]{2,1,0:T(8,128)(2,1)S(1)} %pad_maximum_fusion.4), channel_id=1, source_target_pairs={{0,24},{1,25},{2,26},{3,27},{4,28},{5,29},{6,30},{7,31},{8,16},{9,... | collective-permute-start | bytes 393224 | tf_op jit(solution)/shard_map/ppermute | solution.py:622
  36.4 13.4 %collective-permute-start.8 = (bf16[2,64,512]{2,1,0:T(8,128)(2,1)S(1)}, bf16[2,64,512]{2,1,0:T(8,128)(2,1)S(1)}, u32[]{:S(2)}, u32[]{:S(2)}) collective-permute-start(bf16[2,64,512]{2,1,0:T(8,128)(2,1)S(1)} %pad_maximum_fusion.4), channel_id=1, source_target_pairs={{0,16},{1,17},{2,18},{3,19},{4,20},{5,21},{6,22},{7,23},{8,24},{9,... | collective-permute-start | bytes 393224 | tf_op jit(solution)/shard_map/ppermute | solution.py:622
  36.4 13.4 %collective-permute-start.7 = (bf16[2,64,512]{2,1,0:T(8,128)(2,1)S(1)}, bf16[2,64,512]{2,1,0:T(8,128)(2,1)S(1)}, u32[]{:S(2)}, u32[]{:S(2)}) collective-permute-start(bf16[2,64,512]{2,1,0:T(8,128)(2,1)S(1)} %pad_maximum_fusion.4), channel_id=1, source_target_pairs={{0,8},{1,9},{2,10},{3,11},{4,12},{5,13},{6,14},{7,15},{8,0},{9,1},... | collective-permute-start | bytes 393224 | tf_op jit(solution)/shard_map/ppermute | solution.py:622
  49.8 11.1 %collective-permute-start.13 = (bf16[4,96,384]{2,1,0:T(8,128)(2,1)}, bf16[4,96,384]{2,1,0:T(8,128)(2,1)S(1)}, u32[]{:S(2)}, u32[]{:S(2)}) collective-permute-start(bf16[4,96,384]{2,1,0:T(8,128)(2,1)} %get-tuple-element.64), channel_id=1, source_target_pairs={{0,1},{2,3},{4,5},{6,7},{8,9},{10,11},{12,13},{14,15},{16,17},{18,... | collective-permute-start | bytes 884744 | tf_op jit(solution)/shard_map/ppermute | solution.py:654
  53.4 27.8 %collective-permute-start.12 = (bf16[2,256,512]{2,1,0:T(8,128)(2,1)S(1)}, bf16[2,256,512]{2,1,0:T(8,128)(2,1)S(1)}, u32[]{:S(2)}, u32[]{:S(2)}) collective-permute-start(bf16[2,256,512]{2,1,0:T(8,128)(2,1)S(1)} %pad_maximum_fusion.2), channel_id=1, source_target_pairs={{0,5},{1,4},{2,7},{3,6},{4,1},{5,0},{6,3},{7,2},{8,13},{9,12},{10,... | collective-permute-start | bytes 1572872 | tf_op jit(solution)/shard_map/ppermute | solution.py:622
  53.8 28.2 %collective-permute-start.11 = (bf16[2,256,512]{2,1,0:T(8,128)(2,1)S(1)}, bf16[2,256,512]{2,1,0:T(8,128)(2,1)S(1)}, u32[]{:S(2)}, u32[]{:S(2)}) collective-permute-start(bf16[2,256,512]{2,1,0:T(8,128)(2,1)S(1)} %pad_maximum_fusion.2), channel_id=1, source_target_pairs={{0,1},{1,0},{2,3},{3,2},{4,5},{5,4},{6,7},{7,6},{8,9},{9,8},{10,11... | collective-permute-start | bytes 1572872 | tf_op jit(solution)/shard_map/ppermute | solution.py:622
  56.4 25.6 %collective-permute-start.10 = (bf16[2,256,512]{2,1,0:T(8,128)(2,1)S(1)}, bf16[2,256,512]{2,1,0:T(8,128)(2,1)}, u32[]{:S(2)}, u32[]{:S(2)}) collective-permute-start(bf16[2,256,512]{2,1,0:T(8,128)(2,1)S(1)} %pad_maximum_fusion.2), channel_id=1, source_target_pairs={{0,4},{1,5},{2,6},{3,7},{4,0},{5,1},{6,2},{7,3},{8,12},{9,13},{10,... | collective-permute-start | bytes 1572872 | tf_op jit(solution)/shard_map/ppermute | solution.py:622
  84.6 27.4 %collective-permute-start.14 = (bf16[2,1024,512]{2,1,0:T(8,128)(2,1)}, bf16[2,1024,512]{2,1,0:T(8,128)(2,1)}, u32[]{:S(2)}, u32[]{:S(2)}) collective-permute-start(bf16[2,1024,512]{2,1,0:T(8,128)(2,1)} %pad_maximum_fusion), channel_id=1, source_target_pairs={{0,2},{1,3},{2,0},{3,1},{4,6},{5,7},{6,4},{7,5},{8,10},{9,11},{10,... | collective-permute-start | bytes 6291464 | tf_op jit(solution)/shard_map/ppermute | solution.py:622
  165.6 41.6 %collective-permute-start.15 = (bf16[2,1024,512]{2,1,0:T(8,128)(2,1)}, bf16[2,1024,512]{2,1,0:T(8,128)(2,1)}, u32[]{:S(2)}, u32[]{:S(2)}) collective-permute-start(bf16[2,1024,512]{2,1,0:T(8,128)(2,1)} %pad_maximum_fusion.1), channel_id=1, source_target_pairs={{0,2},{1,3},{2,0},{3,1},{4,6},{5,7},{6,4},{7,5},{8,10},{9,11},{10,... | collective-permute-start | bytes 6291464 | tf_op jit(solution)/shard_map/ppermute | solution.py:622
  177.6 10.1 %collective-permute-start.16 = (bf16[4,96,384]{2,1,0:T(8,128)(2,1)}, bf16[4,96,384]{2,1,0:T(8,128)(2,1)S(1)}, u32[]{:S(2)}, u32[]{:S(2)}) collective-permute-start(bf16[4,96,384]{2,1,0:T(8,128)(2,1)} %prologue.1), channel_id=1, source_target_pairs={{1,0},{3,2},{5,4},{7,6},{9,8},{11,10},{13,12},{15,14},{17,16},{19,... | collective-permute-start | bytes 884744 | tf_op jit(solution)/shard_map/ppermute | solution.py:654
  211.4 39.8 %collective-permute-start.17 = (bf16[2,256,512]{2,1,0:T(8,128)(2,1)}, bf16[2,256,512]{2,1,0:T(8,128)(2,1)S(1)}, u32[]{:S(2)}, u32[]{:S(2)}) collective-permute-start(bf16[2,256,512]{2,1,0:T(8,128)(2,1)} %get-tuple-element.158), channel_id=1, source_target_pairs={{0,4},{1,5},{2,6},{3,7},{4,0},{5,1},{6,2},{7,3},{8,12},{9,13},{10,... | collective-permute-start | bytes 1572872 | tf_op jit(solution)/shard_map/ppermute | solution.py:622
  215.9 35.4 %collective-permute-start.19 = (bf16[2,256,512]{2,1,0:T(8,128)(2,1)S(1)}, bf16[2,256,512]{2,1,0:T(8,128)(2,1)S(1)}, u32[]{:S(2)}, u32[]{:S(2)}) collective-permute-start(bf16[2,256,512]{2,1,0:T(8,128)(2,1)S(1)} %get-tuple-element.159), channel_id=1, source_target_pairs={{0,5},{1,4},{2,7},{3,6},{4,1},{5,0},{6,3},{7,2},{8,13},{9,12},{10,... | collective-permute-start | bytes 1572872 | tf_op jit(solution)/shard_map/ppermute | solution.py:622
  215.9 35.4 %collective-permute-start.18 = (bf16[2,256,512]{2,1,0:T(8,128)(2,1)S(1)}, bf16[2,256,512]{2,1,0:T(8,128)(2,1)}, u32[]{:S(2)}, u32[]{:S(2)}) collective-permute-start(bf16[2,256,512]{2,1,0:T(8,128)(2,1)S(1)} %get-tuple-element.160), channel_id=1, source_target_pairs={{0,1},{1,0},{2,3},{3,2},{4,5},{5,4},{6,7},{7,6},{8,9},{9,8},{10,11... | collective-permute-start | bytes 1572872 | tf_op jit(solution)/shard_map/ppermute | solution.py:622
  253.3 23.9 %collective-permute-start.20 = (bf16[2,64,512]{2,1,0:T(8,128)(2,1)}, bf16[2,64,512]{2,1,0:T(8,128)(2,1)S(1)}, u32[]{:S(2)}, u32[]{:S(2)}) collective-permute-start(bf16[2,64,512]{2,1,0:T(8,128)(2,1)} %get-tuple-element.164), channel_id=1, source_target_pairs={{0,8},{1,9},{2,10},{3,11},{4,12},{5,13},{6,14},{7,15},{8,0},{9,1},... | collective-permute-start | bytes 393224 | tf_op jit(solution)/shard_map/ppermute | solution.py:622
  253.6 23.6 %collective-permute-start.22 = (bf16[2,64,512]{2,1,0:T(8,128)(2,1)S(1)}, bf16[2,64,512]{2,1,0:T(8,128)(2,1)S(1)}, u32[]{:S(2)}, u32[]{:S(2)}) collective-permute-start(bf16[2,64,512]{2,1,0:T(8,128)(2,1)S(1)} %get-tuple-element.165), channel_id=1, source_target_pairs={{0,24},{1,25},{2,26},{3,27},{4,28},{5,29},{6,30},{7,31},{8,16},{9,... | collective-permute-start | bytes 393224 | tf_op jit(solution)/shard_map/ppermute | solution.py:622
  255.8 21.4 %collective-permute-start.21 = (bf16[2,64,512]{2,1,0:T(8,128)(2,1)S(1)}, bf16[2,64,512]{2,1,0:T(8,128)(2,1)S(1)}, u32[]{:S(2)}, u32[]{:S(2)}) collective-permute-start(bf16[2,64,512]{2,1,0:T(8,128)(2,1)S(1)} %get-tuple-element.166), channel_id=1, source_target_pairs={{0,16},{1,17},{2,18},{3,19},{4,20},{5,21},{6,22},{7,23},{8,24},{9,... | collective-permute-start | bytes 393224 | tf_op jit(solution)/shard_map/ppermute | solution.py:622
  285.8 20.2 %collective-permute-start.30 = (bf16[16,4,32,256]{3,2,1,0:T(8,128)(2,1)}, bf16[16,4,32,256]{3,2,1,0:T(8,128)(2,1)S(1)}, u32[]{:S(2)}, u32[]{:S(2)}) collective-permute-start(bf16[16,4,32,256]{3,2,1,0:T(8,128)(2,1)} %get-tuple-element.101), channel_id=1, source_target_pairs={{0,2},{1,3},{2,0},{3,1},{4,6},{5,7},{6,4},{7,5},{8,10},{9,11},{10,... | collective-permute-start | bytes 3145736 | tf_op jit(solution)/shard_map/ppermute | solution.py:622
  293.7 7.8 %collective-permute-start.26 = (f32[1,1048]{1,0:T(1,128)S(1)}, f32[1,1048]{1,0:T(1,128)S(1)}, u32[]{:S(2)}, u32[]{:S(2)}) collective-permute-start(f32[1,1048]{1,0:T(1,128)S(1)} %reshape_add_fusion), channel_id=1, source_target_pairs={{0,5},{1,4},{2,7},{3,6},{4,1},{5,0},{6,3},{7,2},{8,13},{9,12},{10,... | collective-permute-start | bytes 12584 | tf_op jit(solution)/shard_map/ppermute | solution.py:622
  295.3 6.3 %collective-permute-start.25 = (f32[1,1048]{1,0:T(1,128)S(1)}, f32[1,1048]{1,0:T(1,128)S(1)}, u32[]{:S(2)}, u32[]{:S(2)}) collective-permute-start(f32[1,1048]{1,0:T(1,128)S(1)} %reshape_add_fusion), channel_id=1, source_target_pairs={{0,1},{1,0},{2,3},{3,2},{4,5},{5,4},{6,7},{7,6},{8,9},{9,8},{10,11... | collective-permute-start | bytes 12584 | tf_op jit(solution)/shard_map/ppermute | solution.py:622
  301.6 8.8 %collective-permute-start.29 = (f32[1,1048]{1,0:T(1,128)S(1)}, f32[1,1048]{1,0:T(1,128)S(1)}, u32[]{:S(2)}, u32[]{:S(2)}) collective-permute-start(f32[1,1048]{1,0:T(1,128)S(1)} %add_add_fusion.2), channel_id=1, source_target_pairs={{0,24},{1,25},{2,26},{3,27},{4,28},{5,29},{6,30},{7,31},{8,16},{9,... | collective-permute-start | bytes 12584 | tf_op jit(solution)/shard_map/ppermute | solution.py:622
  304.1 7.7 %collective-permute-start.28 = (f32[1,1048]{1,0:T(1,128)S(1)}, f32[1,1048]{1,0:T(1,128)S(1)}, u32[]{:S(2)}, u32[]{:S(2)}) collective-permute-start(f32[1,1048]{1,0:T(1,128)S(1)} %add_add_fusion.2), channel_id=1, source_target_pairs={{0,16},{1,17},{2,18},{3,19},{4,20},{5,21},{6,22},{7,23},{8,24},{9,... | collective-permute-start | bytes 12584 | tf_op jit(solution)/shard_map/ppermute | solution.py:622
  304.3 7.5 %collective-permute-start.27 = (f32[1,1048]{1,0:T(1,128)S(1)}, f32[1,1048]{1,0:T(1,128)S(1)}, u32[]{:S(2)}, u32[]{:S(2)}) collective-permute-start(f32[1,1048]{1,0:T(1,128)S(1)} %add_add_fusion.2), channel_id=1, source_target_pairs={{0,8},{1,9},{2,10},{3,11},{4,12},{5,13},{6,14},{7,15},{8,0},{9,1},... | collective-permute-start | bytes 12584 | tf_op jit(solution)/shard_map/ppermute | solution.py:622
  308.1 12.5 %collective-permute-start.31 = (bf16[4,4,32,256]{3,2,1,0:T(8,128)(2,1)S(1)}, bf16[4,4,32,256]{3,2,1,0:T(8,128)(2,1)S(1)}, u32[]{:S(2)}, u32[]{:S(2)}) collective-permute-start(bf16[4,4,32,256]{3,2,1,0:T(8,128)(2,1)S(1)} %get-tuple-element.161), channel_id=1, source_target_pairs={{0,4},{1,5},{2,6},{3,7},{4,0},{5,1},{6,2},{7,3},{8,12},{9,13},{10,... | collective-permute-start | bytes 786440 | tf_op jit(solution)/shard_map/ppermute | solution.py:622
  310.2 10.4 %collective-permute-start.33 = (bf16[4,4,32,256]{3,2,1,0:T(8,128)(2,1)S(1)}, bf16[4,4,32,256]{3,2,1,0:T(8,128)(2,1)S(1)}, u32[]{:S(2)}, u32[]{:S(2)}) collective-permute-start(bf16[4,4,32,256]{3,2,1,0:T(8,128)(2,1)S(1)} %get-tuple-element.162), channel_id=1, source_target_pairs={{0,5},{1,4},{2,7},{3,6},{4,1},{5,0},{6,3},{7,2},{8,13},{9,12},{10,... | collective-permute-start | bytes 786440 | tf_op jit(solution)/shard_map/ppermute | solution.py:622
  310.4 11.6 %collective-permute-start.32 = (bf16[4,4,32,256]{3,2,1,0:T(8,128)(2,1)S(1)}, bf16[4,4,32,256]{3,2,1,0:T(8,128)(2,1)S(1)}, u32[]{:S(2)}, u32[]{:S(2)}) collective-permute-start(bf16[4,4,32,256]{3,2,1,0:T(8,128)(2,1)S(1)} %get-tuple-element.163), channel_id=1, source_target_pairs={{0,1},{1,0},{2,3},{3,2},{4,5},{5,4},{6,7},{7,6},{8,9},{9,8},{10,11... | collective-permute-start | bytes 786440 | tf_op jit(solution)/shard_map/ppermute | solution.py:622
  322.5 6.1 %collective-permute-start.36 = (bf16[1,4,32,256]{3,2,1,0:T(8,128)(2,1)S(1)}, bf16[1,4,32,256]{3,2,1,0:T(8,128)(2,1)S(1)}, u32[]{:S(2)}, u32[]{:S(2)}) collective-permute-start(bf16[1,4,32,256]{3,2,1,0:T(8,128)(2,1)S(1)} %get-tuple-element.170), channel_id=1, source_target_pairs={{0,24},{1,25},{2,26},{3,27},{4,28},{5,29},{6,30},{7,31},{8,16},{9,... | collective-permute-start | bytes 196616 | tf_op jit(solution)/shard_map/ppermute | solution.py:622
  324.6 5.9 %collective-permute-start.35 = (bf16[1,4,32,256]{3,2,1,0:T(8,128)(2,1)S(1)}, bf16[1,4,32,256]{3,2,1,0:T(8,128)(2,1)S(1)}, u32[]{:S(2)}, u32[]{:S(2)}) collective-permute-start(bf16[1,4,32,256]{3,2,1,0:T(8,128)(2,1)S(1)} %get-tuple-element.171), channel_id=1, source_target_pairs={{0,16},{1,17},{2,18},{3,19},{4,20},{5,21},{6,22},{7,23},{8,24},{9,... | collective-permute-start | bytes 196616 | tf_op jit(solution)/shard_map/ppermute | solution.py:622
  (27 other events, 226.6 us)

commit v4 on v3

--- a/solution.py
+++ b/solution.py
@@ -183,7 +183,17 @@
 
 
 def weight_grad_kernel(
-    scalars, normed_ref, d_qkv_ref, out_grad_ref, keep_ref, give_ref, whole, *, flips
+    scalars,
+    normed_ref,
+    d_qkv_ref,
+    out_grad_ref,
+    weight_ref,
+    keep_ref,
+    give_ref,
+    gain_ref,
+    whole,
+    *,
+    flips,
 ):
     c = pl.program_id(0)
     half, _, tall, wide = keep_ref.shape
@@ -193,9 +203,19 @@
             part = total[:, h * wide : (h + 1) * wide]
             whole[h] = part.reshape(whole.shape[1:])
 
+    @pl.when(c == 0)
+    def _():
+        gain_ref[...] = jnp.zeros(gain_ref.shape, F32)
+
     @pl.when(c < 3)
     def _():
-        place(mm(normed_ref[...], d_qkv_ref[0], TN))
+        total = mm(normed_ref[...], d_qkv_ref[0], TN)
+        place(total)
+        product = total * weight_ref[0].astype(F32)
+        high = product.astype(BF16)
+        low = (product - high.astype(F32)).astype(BF16)
+        ones = jnp.ones((8, product.shape[1]), BF16)
+        gain_ref[...] += mm(ones, high, NT) + mm(ones, low, NT)
 
     @pl.when(c == 3)
     def _():
@@ -528,6 +548,109 @@
     lax.fori_loop(0, steps, body, 0)
 
 
+def feed_kernel(
+    scalars,
+    mixed_ref,
+    tokens_ref,
+    cotangent_ref,
+    out_weight_ref,
+    gain_ref,
+    own_ref,
+    other_ref,
+    layer_ref,
+    d_hidden_ref,
+    d_branch_ref,
+    d_mixed_ref,
+    normed_ref,
+    active_ref,
+    d_inner_ref,
+    sums_ref,
+):
+    c0 = math.sqrt(2.0 / math.pi)
+    hidden = tokens_ref[...].astype(F32) + mm(mixed_ref[...], out_weight_ref[...], NT)
+    normal, scale = norm_parts(hidden)
+    normed = (normal * gain_ref[...]).astype(BF16)
+    normed_ref[...] = normed
+    cotangent = cotangent_ref[...]
+    half, width = own_ref.shape[1:]
+    chunk = min(512, half)
+    layer = hidden
+    d_normed = jnp.zeros(hidden.shape, F32)
+    for place, ref in enumerate((own_ref, other_ref)):
+        for first in range(0, half, chunk):
+            into = ref[0, pl.ds(first, chunk), :]
+            down = ref[1, pl.ds(first, chunk), :]
+            inner = mm(normed, into, NT)
+            d_active = mm(cotangent, down, NT)
+            square = inner * inner
+            bent = jnp.tanh(inner * (c0 + (c0 * 0.044715) * square))
+            gate = 0.5 + 0.5 * bent
+            active = (inner * gate).astype(BF16)
+            slope = gate + inner * (0.5 - 0.5 * bent * bent) * (
+                c0 + (3.0 * 0.044715 * c0) * square
+            )
+            d_inner = (d_active * slope).astype(BF16)
+            at = pl.ds(place * half + first, chunk)
+            active_ref[:, at] = active
+            d_inner_ref[:, at] = d_inner
+            layer = layer + mm(active, down)
+            d_normed = d_normed + mm(d_inner, into)
+    layer_ref[...] = layer.astype(BF16)
+    d_part, gain_rows = norm_back(d_normed, gain_ref[...], normal, scale)
+    d_hidden = cotangent.astype(F32) + d_part
+    d_hidden_ref[...] = d_hidden
+    d_branch = d_hidden.astype(BF16)
+    d_branch_ref[...] = d_branch
+    d_mixed_ref[...] = mm(d_branch, out_weight_ref[...]).astype(BF16)
+
+    @pl.when(pl.program_id(0) == 0)
+    def _():
+        sums_ref[...] = jnp.zeros(sums_ref.shape, F32)
+
+    sums_ref[...] += gain_rows
+
+
+def feed_grad_kernel(
+    scalars,
+    normed_ref,
+    cotangent_ref,
+    active_ref,
+    d_inner_ref,
+    mixed_ref,
+    d_branch_ref,
+    keep_ref,
+    give_ref,
+    out_grad_ref,
+):
+    step = pl.program_id(0)
+    steps = pl.num_programs(0)
+
+    @pl.when(step == 0)
+    def _():
+        out_grad_ref[...] = mm(d_branch_ref[...], mixed_ref[...], TN)
+
+    @pl.when(step < steps // 2)
+    def _():
+        keep_ref[0] = mm(d_inner_ref[...], normed_ref[...], TN)
+        keep_ref[1] = mm(active_ref[...], cotangent_ref[...], TN)
+
+    @pl.when(step >= steps // 2)
+    def _():
+        give_ref[0] = mm(d_inner_ref[...], normed_ref[...], TN).astype(BF16)
+        give_ref[1] = mm(active_ref[...], cotangent_ref[...], TN).astype(BF16)
+
+
+def input_kernel(
+    scalars, d_qkv_ref, weight_ref, tokens_ref, d_hidden_ref, gain_ref, input_grad_ref
+):
+    d_normed = mm(d_qkv_ref[0], weight_ref[0], NT)
+    for c in range(1, 3):
+        d_normed = d_normed + mm(d_qkv_ref[c], weight_ref[c], NT)
+    normal, scale = norm_parts(tokens_ref[...].astype(F32))
+    d_part, _ = norm_back(d_normed, gain_ref[...], normal, scale)
+    input_grad_ref[...] = d_hidden_ref[...] + d_part
+
+
 def resume(kernel, done, scalars, qkv_ref, message_ref, start_ref, blend_ref, *refs):
     kernel(scalars, qkv_ref, message_ref, start_ref, blend_ref, *refs[done:])
 
@@ -577,7 +700,8 @@
     e = d_out * gain
     inner = jnp.mean(e, axis=-1, keepdims=True)
     along = jnp.mean(e * normal, axis=-1, keepdims=True)
-    return scale * (e - inner - normal * along), jnp.sum(d_out * normal, axis=0)
+    rows = jnp.sum((d_out * normal).reshape(-1, 8, d_out.shape[1]), axis=0)
+    return scale * (e - inner - normal * along), rows
 
 
 def bits(size):
@@ -642,10 +766,8 @@
     return narrow(parts[0], parts[1:], group)
 
 
-def sum_everywhere(array):
-    for group in reversed(phases()):
-        array = array + sum(peer(array, group, combo) for combo in range(1, 1 << len(group)))
-    return array
+def add_peers(array, group):
+    return array + sum(peer(array, group, combo) for combo in range(1, 1 << len(group)))
 
 
 def pass_along(local, keep, shift):
@@ -782,34 +904,35 @@
         if not first:
             feed, results = widen(feed, groups[1], 1, results)
             feed, message = lax.optimization_barrier((feed, message))
-    for group in groups[2:]:
+    for group in groups[2:-1]:
         feed = widen(feed, group, 1)
-    in_all, down_all = feed[0], feed[1]
+    feed_other = peer(feed, groups[-1], 1)
     mixed, near, far1, far2, inv_l, inv_d, states = results
 
     spec = pair_specs(rows)
-    residual = tokens.astype(F32)
-    hidden = residual + lax.dot_general(mixed, out_all, NT, preferred_element_type=F32)
-    normal_two, scale_two = norm_parts(hidden)
-    normed_two = (normal_two * ln2_gain).astype(BF16)
-    inner = lax.dot_general(normed_two, in_all, NT, preferred_element_type=F32)
-    c0 = math.sqrt(2.0 / math.pi)
-    bent = jnp.tanh(c0 * (inner + 0.044715 * (inner * inner * inner)))
-    active = (0.5 * inner * (1.0 + bent)).astype(BF16)
-    layer_out = (hidden + jnp.dot(active, down_all, preferred_element_type=F32)).astype(BF16)
-    d_active = lax.dot_general(cotangent, down_all, NT, preferred_element_type=F32)
-    down_grad = lax.dot_general(active, cotangent, TN, preferred_element_type=F32)
-    slope = 0.5 * (1.0 + bent) + 0.5 * inner * (1.0 - bent * bent) * c0 * (
-        1.0 + 3.0 * 0.044715 * inner * inner
-    )
-    d_inner = (d_active * slope).astype(BF16)
-    in_grad = lax.dot_general(d_inner, normed_two, TN, preferred_element_type=F32)
-    d_normed_two = jnp.dot(d_inner, in_all, preferred_element_type=F32)
-    d_hidden_part, gain_two_part = norm_back(d_normed_two, ln2_gain, normal_two, scale_two)
-    d_hidden = cotangent.astype(F32) + d_hidden_part
-    d_branch = d_hidden.astype(BF16)
-    d_mixed = jnp.dot(d_branch, out_all, preferred_element_type=F32).astype(BF16)
-    out_grad = lax.dot_general(d_branch, mixed, TN, preferred_element_type=F32)
+    low = jax.ShapeDtypeStruct((rows, width), BF16)
+    row_spec = pl.BlockSpec((part, width), lambda p, s: (p, 0))
+    hidden_units = 2 * feed.shape[1]
+    unit_spec = pl.BlockSpec((part, hidden_units), lambda p, s: (p, 0))
+    unit_shape = jax.ShapeDtypeStruct((rows, hidden_units), BF16)
+    sums_shape = jax.ShapeDtypeStruct((8, width), F32)
+    layer_out, d_hidden, d_branch, d_mixed, normed_two, active, d_inner, gain_two_rows = call(
+        feed_kernel,
+        [row_spec] * 3
+        + [
+            whole_spec((width, width)),
+            whole_spec((1, width)),
+            whole_spec(feed.shape),
+            whole_spec(feed.shape),
+        ],
+        [row_spec] * 5 + [unit_spec] * 2 + [whole_spec((8, width))],
+        [low, wide, low, low, low, unit_shape, unit_shape, sums_shape],
+        [],
+        3,
+        "feed",
+        8 * big * hidden_units,
+        32 * big,
+    )(scalars, mixed, tokens, cotangent, out_all, ln2_gain[None], feed, feed_other)
 
     front_keys = qkv[1:, :ROWS]
     back = call(
@@ -834,11 +957,31 @@
         500 * big,
         20 * big,
     )(scalars, qkv, front_keys, message, start_wide, blend_wide, d_mixed, near, far1, inv_l, inv_d)
+    d_inner, _ = lax.optimization_barrier((d_inner, back))
     back_in = pass_along(back, keep_all, -1)
 
-    half = in_grad.shape[0] // 2
-    keep = jnp.stack([in_grad[:half], down_grad[:half]])
-    give = jnp.stack([in_grad[half:], down_grad[half:]]).astype(BF16)
+    unit = hidden_units // 4
+    columns = pl.BlockSpec((rows, unit), lambda p, s: (0, p))
+    half_shape = (2, 2 * unit, width)
+    keep, give, out_grad = call(
+        feed_grad_kernel,
+        [whole_spec((rows, width))] * 2 + [columns] * 2 + [whole_spec((rows, width))] * 2,
+        [
+            pl.BlockSpec((2, unit, width), lambda p, s: (0, jnp.minimum(p, 1), 0)),
+            pl.BlockSpec((2, unit, width), lambda p, s: (0, jnp.maximum(p - 2, 0), 0)),
+            whole_spec((width, width)),
+        ],
+        [
+            jax.ShapeDtypeStruct(half_shape, F32),
+            jax.ShapeDtypeStruct(half_shape, BF16),
+            jax.ShapeDtypeStruct((width, width), F32),
+        ],
+        [],
+        4,
+        "feed_grad",
+        4 * big * hidden_units,
+        24 * big,
+    )(scalars, normed_two, cotangent, active, d_inner, mixed, d_branch)
     feed_share = narrow(keep, [give], groups[-1])
     left = list(reversed(groups[:-1]))
 
@@ -883,7 +1026,7 @@
         sums.append(part_sums)
         first += count
         if left and first < pairs:
-            feed_share, back_in = lax.optimization_barrier((feed_share, back_in))
+            _, back_in = lax.optimization_barrier((feed_share, back_in))
             feed_share = narrow_axis(feed_share, left.pop(0), 1)
     for group in left:
         feed_share = narrow_axis(feed_share, group, 1)
@@ -893,31 +1036,53 @@
 
     shard_shape = (n_dp * n_head // 2, 4, width // n_dp, width // n_head)
     shard_spec = pl.BlockSpec((shard_shape[0], 1) + shard_shape[2:], lambda p, s: (0, p, 0, 0))
-    keep, give = call(
+    keep, give, gain_one_rows = call(
         functools.partial(weight_grad_kernel, flips=flips),
         [
             whole_spec((rows, width)),
             pl.BlockSpec((1, rows, width), lambda p, s: (jnp.minimum(p, 2), 0, 0)),
             whole_spec((width, width)),
+            pl.BlockSpec((1, width, width), lambda p, s: (jnp.minimum(p, 2), 0, 0)),
         ],
-        [shard_spec, shard_spec],
-        [jax.ShapeDtypeStruct(shard_shape, F32), jax.ShapeDtypeStruct(shard_shape, BF16)],
+        [shard_spec, shard_spec, whole_spec((8, width))],
+        [
+            jax.ShapeDtypeStruct(shard_shape, F32),
+            jax.ShapeDtypeStruct(shard_shape, BF16),
+            sums_shape,
+        ],
         [pltpu.VMEM((n_head, n_dp, width // n_dp, width // n_head), F32)],
         4,
         "weight_grad",
         6 * big * width,
         8 * big,
-    )(scalars, normed_one, d_qkv, out_grad)
+    )(scalars, normed_one, d_qkv, out_grad, qkv_all)
+    parts = [gain_one_rows[0] / ln1_gain, jnp.sum(gain_two_rows, axis=0), blend_part.reshape(-1)]
+    total_sums = jnp.concatenate(parts)[None]
     share = narrow(keep, [give], groups[-1])
+    total_sums = add_peers(total_sums, groups[-1])
+    for group in reversed(groups[:-1]):
+        _, total_sums = lax.optimization_barrier((share, total_sums))
+        share = narrow_axis(share, group, 0)
+        total_sums = add_peers(total_sums, group)
     d_qkv, give = lax.optimization_barrier((d_qkv, give))
-    for group in reversed(groups[:-1]):
-        share = narrow_axis(share, group, 0)
-    d_normed_one = jnp.einsum("cte,cde->td", d_qkv, qkv_all, preferred_element_type=F32)
-    normal_one, scale_one = norm_parts(residual)
-    d_residual_part, gain_one_part = norm_back(d_normed_one, ln1_gain, normal_one, scale_one)
-    input_grad = d_hidden + d_residual_part
-    gathered = jnp.concatenate([gain_one_part, gain_two_part, blend_part.reshape(-1)])
-    total_sums = sum_everywhere(gathered[None])[0]
+    input_grad = call(
+        input_kernel,
+        [
+            pl.BlockSpec((3, part, width), lambda p, s: (0, p, 0)),
+            whole_spec((3, width, width)),
+            row_spec,
+            row_spec,
+            whole_spec((1, width)),
+        ],
+        row_spec,
+        wide,
+        [],
+        3,
+        "input",
+        6 * big * width,
+        24 * big,
+    )(scalars, d_qkv, qkv_all, tokens, d_hidden, ln1_gain[None])
+    total_sums = total_sums[0]
     gain_one, gain_two = total_sums[:width], total_sums[width : 2 * width]
     blend_sum = total_sums[2 * width :].reshape(blend.shape)
     qkv_share, out_share = share[0, :3], share[0, 3].T

time: 337 us -> 308 us (0.914); the launches traced: 332 us -> 307 us
  matrix products: 55.7 us -> 0 us
  Pallas kernels: 136 us -> 189 us
  local copies, waits for them, and re-layouts: 34.3 us -> 13.5 us
  waiting for transfers between devices: 33.6 us -> 47.5 us
  other arithmetic: 22.4 us -> 9.95 us
    dot_general x10 -> x0, matrix products: 55.7 us -> none  [the longest x1 12.5 us: per_device(): lax.dot_general(cotangent, down_all, NT, preferred_element_type=F32)]
    pallas_call x0 -> x3, Pallas kernels: none -> 53.2 us  [the longest x1 28.1 us: per_device(): call(feed_kernel, [row_spec] * 3 + [whole_spec((width, width)), whole_spe...]
    ppermute x2, waiting for transfers between devices: 3.91 us -> 17.8 us  [pass_along(): arrived = lax.ppermute(local, 'head', pairs)]
    unnamed x54 -> x33, local copies, waits for them, and re-layouts: 12.2 us -> 1.51 us
    another operation x2 -> x0, local copies, waits for them, and re-layouts: 6.66 us -> none  [the longest x1 4.01 us: per_device(): keep = jnp.stack([in_grad[:half], down_grad[:half]])]
    add x4 -> x2, other arithmetic: 4.37 us -> 0.09 us  [narrow(): total = total + peer(give.astype(BF16), group, combo).astype(F32)]
    add x5 -> x3, other arithmetic: 3.75 us -> 0.03 us  [add_peers(): array + sum((peer(array, group, combo) for combo in range(1, 1 << len(gro...]
  transfers between devices with their start and end apart: 37 -> 37, of which waited for: 12 -> 11; matrix products, arithmetic and copies ran while one was open for 14% -> 5% of each run, Pallas kernels for 38% -> 42%
where the time goes in v4:
time: 308 us; the launch traced here: 307 us
  Pallas kernels  189 us (61%)
  waiting for transfers between devices  47.5 us (15%)
  starting transfers between devices  45.4 us (15%)
  local copies, waits for them, and re-layouts  13.5 us (4%)
  other arithmetic  9.95 us (3%)
    pallas_call x3, Pallas kernels, per_device(): call(backward_kernel, [spec['qkv'], spec['message'], spec['start'], spec[...  71.4 us
    ppermute x35, starting transfers between devices, peer(): return lax.ppermute(array, ('dp', 'head'), pairs)  40.5 us
    pallas_call x2, Pallas kernels, per_device(): call(functools.partial(resume, forward_kernel, len(results)), [spec['qkv'...  38 us
    ppermute x35, waiting for transfers between devices, peer(): return lax.ppermute(array, ('dp', 'head'), pairs)  29.8 us
    pallas_call x1, Pallas kernels, per_device(): call(feed_kernel, [row_spec] * 3 + [whole_spec((width, width)), whole_spe...  28.1 us
    ppermute x2, waiting for transfers between devices, pass_along(): arrived = lax.ppermute(local, 'head', pairs)  17.8 us
    pallas_call x1, Pallas kernels, per_device(): call(feed_grad_kernel, [whole_spec((rows, width))] * 2 + [columns] * 2 +...  16.1 us
    pallas_call x1, Pallas kernels, per_device(): call(functools.partial(project_kernel, flips=flips), [pl.BlockSpec((part,...  10.6 us
  transfers between devices with their start and end apart: 37, of which 11 were waited for; matrix products, arithmetic and copies ran while one was open for 5% of the time, Pallas kernels for 42%

profile of v4, /device:TPU:0, one launch (start us, length us, event | category | flops | bytes accessed | tf_op | source)
XLA Modules:
  0.0 307.5 jit_solution(11825654970467066070)
XLA Ops:
  1.5 5.1 %collective-permute-start.2 = (bf16[1,4,32,256]{3,2,1,0:T(8,128)(2,1)S(1)}, bf16[1,4,32,256]{3,2,1,0:T(8,128)(2,1)S(1)}, u32[]{:S(2)}, u32[]{:S(2)}) collective-permute-start(bf16[1,4,32,256]{3,2,1,0:T(8,128)(2,1)S(1)} %maximum_bitcast_fusion), channel_id=1, source_target_pairs={{0,24},{1,25},{2,26},{3,27},{4,28},{5,29},{6,30},{7,31},{8,16},{9,... | collective-permute-start | bytes 196616 | tf_op jit(solution)/shard_map/ppermute | solution.py:746
  9.1 3.1 %collective-permute-done.1 = bf16[1,4,32,256]{3,2,1,0:T(8,128)(2,1)S(1)} collective-permute-done((bf16[1,4,32,256]{3,2,1,0:T(8,128)(2,1)S(1)}, bf16[1,4,32,256]{3,2,1,0:T(8,128)(2,1)S(1)}, u32[]{:S(2)}, u32[]{:S(2)}) %collective-permute-start.1) | collective-permute-done | bytes 65568 | tf_op jit(solution)/shard_map/ppermute | solution.py:746
  12.2 2.5 collective-permute-start.5
  15.8 10.9 %collective-permute-done.3 = bf16[4,4,32,256]{3,2,1,0:T(8,128)(2,1)S(1)} collective-permute-done((bf16[4,4,32,256]{3,2,1,0:T(8,128)(2,1)S(1)}, bf16[4,4,32,256]{3,2,1,0:T(8,128)(2,1)S(1)}, u32[]{:S(2)}, u32[]{:S(2)}) %collective-permute-start.3) | collective-permute-done | bytes 262176 | tf_op jit(solution)/shard_map/ppermute | solution.py:746
  32.0 1.9 concatenate.25.scalars
  34.8 1.6 collective-permute-start.9
  36.4 2.9 collective-permute-start.7
  39.3 10.6 %project.1 = (bf16[3,1536,512]{2,1,0:T(8,128)(2,1)}, bf16[1536,512]{1,0:T(8,128)(2,1)}, bf16[3,512,512]{2,1,0:T(8,128)(2,1)}, bf16[512,512]{1,0:T(8,128)(2,1)}, bf16[4,96,384]{2,1,0:T(8,128)(2,1)}) custom-call(s32[21]{0:T(128)} %concatenate.25.scalars, bf16[1536,512]{1,0:T(8,128)(2,1)} %tokens_ref.5, f32[1,512]{1,0:T(1,128)} %bitcast.34, ...), custom_call_target="tpu_custom_call" | custom-call | flops 2415919104 | bytes 9437184 | tf_op jit(solution)/shard_map/project/pallas_call | solution.py:849
  49.9 3.6 %collective-permute-start.13 = (bf16[4,96,384]{2,1,0:T(8,128)(2,1)}, bf16[4,96,384]{2,1,0:T(8,128)(2,1)S(1)}, u32[]{:S(2)}, u32[]{:S(2)}) collective-permute-start(bf16[4,96,384]{2,1,0:T(8,128)(2,1)} %get-tuple-element.77), channel_id=1, source_target_pairs={{0,1},{2,3},{4,5},{6,7},{8,9},{10,11},{12,13},{14,15},{16,17},{18,... | collective-permute-start | bytes 884744 | tf_op jit(solution)/shard_map/ppermute | solution.py:776
  53.8 2.7 collective-permute-start.11
  57.8 3.2 %collective-permute-done.13.message_ref = bf16[4,96,384]{2,1,0:T(8,128)(2,1)S(1)} collective-permute-done((bf16[4,96,384]{2,1,0:T(8,128)(2,1)}, bf16[4,96,384]{2,1,0:T(8,128)(2,1)S(1)}, u32[]{:S(2)}, u32[]{:S(2)}) %collective-permute-start.13) | collective-permute-done | bytes 294944 | tf_op jit(solution)/shard_map/ppermute | solution.py:776
  62.2 19.2 %forward.2 = (bf16[1536,512]{1,0:T(8,128)(2,1)}, f32[1536,512]{1,0:T(8,128)}, f32[1536,512]{1,0:T(8,128)}, f32[1536,512]{1,0:T(8,128)}, f32[1536,512]{1,0:T(8,12...) custom-call(s32[21]{0:T(128)} %concatenate.25.scalars, ...), custom_call_target="tpu_custom_call" | custom-call | flops 3145728000 | bytes 15728640 | tf_op jit(solution)/shard_map/forward/pallas_call | solution.py:891
  82.3 1.8 slice.46.key_ref
  84.1 18.8 %forward.3 = (bf16[1536,512]{1,0:T(8,128)(2,1)}, f32[1536,512]{1,0:T(8,128)}, f32[1536,512]{1,0:T(8,128)}, f32[1536,512]{1,0:T(8,128)}, f32[1536,512]{1,0:T(8,12...) custom-call(s32[21]{0:T(128)} %concatenate.25.scalars, ...), custom_call_target="tpu_custom_call", output_to_operand_aliasing={{0}: (5, {}), {1}: (6, {}), {2}: (7, {}), {3}: (8, {}), {4}... | custom-call | flops 3145728000 | bytes 15728640 | tf_op jit(solution)/shard_map/forward/pallas_call | solution.py:891
  104.2 28.1 %feed.1 = (bf16[1536,512]{1,0:T(8,128)(2,1)}, f32[1536,512]{1,0:T(8,128)}, bf16[1536,512]{1,0:T(8,128)(2,1)}, bf16[1536,512]{1,0:T(8,128)(2,1)}, bf16[1536,512]{...) custom-call(s32[21]{0:T(128)} %concatenate.25.scalars, ...), custom_call_target="tpu_custom_call" | custom-call | flops 12884901888 | bytes 25165824 | tf_op jit(solution)/shard_map/feed/pallas_call | solution.py:919
  132.4 7.4 %prologue.1 = bf16[4,96,384]{2,1,0:T(8,128)(2,1)} custom-call(s32[21]{0:T(128)} %concatenate.25.scalars, bf16[3,1536,512]{2,1,0:T(8,128)(2,1)} %get-tuple-element.73.qkv_ref.query_ref, bf16[2,96,512]{2,1,0:T(8,128)(2,1)} %slice.46.key_ref, bf16[4,96,384]{2,1,0:T(8,128)(2,1)} %copy-done, s32[1536,128]{1,0:T(8,128)} %broadcast_in_dim.78.start_ref, ...), custom_call_target="tpu_custom_call" | custom-call | flops 393216000 | bytes 15728640 | tf_op jit(solution)/shard_map/prologue/pallas_call | solution.py:938
  139.7 16.1 %feed_grad.1 = (f32[2,1024,512]{2,1,0:T(8,128)}, bf16[2,1024,512]{2,1,0:T(8,128)(2,1)}, f32[512,512]{1,0:T(8,128)}) custom-call(s32[21]{0:T(128)} %concatenate.25.scalars, bf16[1536,512]{1,0:T(8,128)(2,1)} %get-tuple-element.100.normed_ref, bf16[1536,512]{1,0:T(8,128)(2,1)} %cotangent_ref.3, bf16[1536,2048]{1,0:T(8,128)(2,1)} %get-tuple-element.101.active_ref, ...), custom_call_target="tpu_custom_call" | custom-call | flops 6442450944 | bytes 18874368 | tf_op jit(solution)/shard_map/feed_grad/pallas_call | solution.py:966
  157.5 14.6 %collective-permute-done.22.back_ref = bf16[4,96,384]{2,1,0:T(8,128)(2,1)S(1)} collective-permute-done((bf16[4,96,384]{2,1,0:T(8,128)(2,1)S(1)}, bf16[4,96,384]{2,1,0:T(8,128)(2,1)S(1)}, u32[]{:S(2)}, u32[]{:S(2)}) %collective-permute-start.22) | collective-permute-done | bytes 294944 | tf_op jit(solution)/shard_map/ppermute | solution.py:776
  172.8 18.7 %backward.3 = (bf16[3,1536,512]{2,1,0:T(8,128)(2,1)}, f32[24,128]{1,0:T(8,128)}) custom-call(s32[21]{0:T(128)} %concatenate.25.scalars, bf16[3,1536,512]{2,1,0:T(8,128)(2,1)} %get-tuple-element.73.qkv_ref.query_ref, bf16[4,96,384]{2,1,0:T(8,128)(2,1)} %copy-done, s32[1536,128]{1,0:T(8,128)} %broadcast_in_dim.78.start_ref, f32[3,512]{1,0:T(4,128)} %reshape.54.blend_ref, ...), custom_call_target="tpu_custom_call" | custom-call | flops 3145728000 | bytes 7864320 | tf_op jit(solution)/shard_map/backward/pallas_call | solution.py:994
  191.5 3.0 fusion.16
  195.8 2.5 collective-permute-start.17
  198.3 33.9 %backward.4 = (bf16[3,1536,512]{2,1,0:T(8,128)(2,1)}, f32[24,256]{1,0:T(8,128)}) custom-call(s32[21]{0:T(128)} %concatenate.25.scalars, bf16[3,1536,512]{2,1,0:T(8,128)(2,1)} %get-tuple-element.73.qkv_ref.query_ref, bf16[4,96,384]{2,1,0:T(8,128)(2,1)} %copy-done, s32[1536,128]{1,0:T(8,128)} %broadcast_in_dim.78.start_ref, ...), custom_call_target="tpu_custom_call", output_to_operand_aliasing={{0}: (13, {})} | custom-call | flops 6291456000 | bytes 15728640 | tf_op jit(solution)/shard_map/backward/pallas_call | solution.py:994
  232.8 3.3 %collective-permute-start.20 = (bf16[2,64,512]{2,1,0:T(8,128)(2,1)S(1)}, bf16[2,64,512]{2,1,0:T(8,128)(2,1)S(1)}, u32[]{:S(2)}, u32[]{:S(2)}) collective-permute-start(bf16[2,64,512]{2,1,0:T(8,128)(2,1)S(1)} %get-tuple-element.154), channel_id=1, source_target_pairs={{0,16},{1,17},{2,18},{3,19},{4,20},{5,21},{6,22},{7,23},{8,24},{9,... | collective-permute-start | bytes 393224 | tf_op jit(solution)/shard_map/ppermute | solution.py:746
  236.1 18.7 %backward.5 = (bf16[3,1536,512]{2,1,0:T(8,128)(2,1)}, f32[24,128]{1,0:T(8,128)}) custom-call(s32[21]{0:T(128)} %concatenate.25.scalars, bf16[3,1536,512]{2,1,0:T(8,128)(2,1)} %get-tuple-element.73.qkv_ref.query_ref, bf16[4,96,384]{2,1,0:T(8,128)(2,1)} %copy-done, s32[1536,128]{1,0:T(8,128)} %broadcast_in_dim.78.start_ref, ...), custom_call_target="tpu_custom_call", output_to_operand_aliasing={{0}: (13, {})} | custom-call | flops 3145728000 | bytes 7864320 | tf_op jit(solution)/shard_map/backward/pallas_call | solution.py:994
  255.0 8.9 %weight_grad.1 = (f32[16,4,32,256]{3,2,1,0:T(8,128)}, bf16[16,4,32,256]{3,2,1,0:T(8,128)(2,1)}, f32[8,512]{1,0:T(8,128)}) custom-call(s32[21]{0:T(128)} %concatenate.25.scalars, bf16[1536,512]{1,0:T(8,128)(2,1)} %get-tuple-element.120.normed_ref, bf16[3,1536,512]{2,1,0:T(8,128)(2,1)} %get-tuple-element.124.d_qkv_ref, ...), custom_call_target="tpu_custom_call" | custom-call | flops 2415919104 | bytes 6291456 | tf_op jit(solution)/shard_map/weight_grad/pallas_call | solution.py:1039
  266.2 9.0 %input.1 = f32[1536,512]{1,0:T(8,128)} custom-call(s32[21]{0:T(128)} %concatenate.25.scalars, bf16[3,1536,512]{2,1,0:T(8,128)(2,1)} %get-tuple-element.124.d_qkv_ref, bf16[3,512,512]{2,1,0:T(8,128)(2,1)} %get-tuple-element.122.weight_ref, bf16[1536,512]{1,0:T(8,128)(2,1)} %tokens_ref.5, f32[1536,512]{1,0:T(8,128)} %get-tuple-element.125.d_hidden_ref, ...), custom_call_target="tpu_custom_call" | custom-call | flops 2415919104 | bytes 18874368 | tf_op jit(solution)/shard_map/input/pallas_call | solution.py:1068
  277.3 1.9 collective-permute-start.28
  280.8 2.0 collective-permute-start.25
  282.9 9.5 %collective-permute-done.24 = bf16[4,4,32,256]{3,2,1,0:T(8,128)(2,1)S(1)} collective-permute-done((bf16[4,4,32,256]{3,2,1,0:T(8,128)(2,1)S(1)}, bf16[4,4,32,256]{3,2,1,0:T(8,128)(2,1)S(1)}, u32[]{:S(2)}, u32[]{:S(2)}) %collective-permute-start.24) | collective-permute-done | bytes 262176 | tf_op jit(solution)/shard_map/ppermute | solution.py:746
  294.8 1.6 collective-permute-start.32
  296.4 1.9 collective-permute-start.31
  299.8 2.0 collective-permute-start.35
  (135 shorter events, 34.7 us)
Async XLA Ops:
  1.5 7.6 %collective-permute-start.2 = (bf16[1,4,32,256]{3,2,1,0:T(8,128)(2,1)S(1)}, bf16[1,4,32,256]{3,2,1,0:T(8,128)(2,1)S(1)}, u32[]{:S(2)}, u32[]{:S(2)}) collective-permute-start(bf16[1,4,32,256]{3,2,1,0:T(8,128)(2,1)S(1)} %maximum_bitcast_fusion), channel_id=1, source_target_pairs={{0,24},{1,25},{2,26},{3,27},{4,28},{5,29},{6,30},{7,31},{8,16},{9,... | collective-permute-start | bytes 196616 | tf_op jit(solution)/shard_map/ppermute | solution.py:746
  6.6 5.6 %collective-permute-start.1 = (bf16[1,4,32,256]{3,2,1,0:T(8,128)(2,1)S(1)}, bf16[1,4,32,256]{3,2,1,0:T(8,128)(2,1)S(1)}, u32[]{:S(2)}, u32[]{:S(2)}) collective-permute-start(bf16[1,4,32,256]{3,2,1,0:T(8,128)(2,1)S(1)} %maximum_bitcast_fusion), channel_id=1, source_target_pairs={{0,16},{1,17},{2,18},{3,19},{4,20},{5,21},{6,22},{7,23},{8,24},{9,... | collective-permute-start | bytes 196616 | tf_op jit(solution)/shard_map/ppermute | solution.py:746
  12.2 14.7 %collective-permute-start.5 = (bf16[4,4,32,256]{3,2,1,0:T(8,128)(2,1)S(1)}, bf16[4,4,32,256]{3,2,1,0:T(8,128)(2,1)S(1)}, u32[]{:S(2)}, u32[]{:S(2)}) collective-permute-start(bf16[4,4,32,256]{3,2,1,0:T(8,128)(2,1)S(1)} %pad_maximum_fusion.2), channel_id=1, source_target_pairs={{0,5},{1,4},{2,7},{3,6},{4,1},{5,0},{6,3},{7,2},{8,13},{9,12},{10,... | collective-permute-start | bytes 786440 | tf_op jit(solution)/shard_map/ppermute | solution.py:746
  14.7 12.2 %collective-permute-start.4 = (bf16[4,4,32,256]{3,2,1,0:T(8,128)(2,1)S(1)}, bf16[4,4,32,256]{3,2,1,0:T(8,128)(2,1)S(1)}, u32[]{:S(2)}, u32[]{:S(2)}) collective-permute-start(bf16[4,4,32,256]{3,2,1,0:T(8,128)(2,1)S(1)} %pad_maximum_fusion.2), channel_id=1, source_target_pairs={{0,1},{1,0},{2,3},{3,2},{4,5},{5,4},{6,7},{7,6},{8,9},{9,8},{10,11... | collective-permute-start | bytes 786440 | tf_op jit(solution)/shard_map/ppermute | solution.py:746
  15.3 11.4 %collective-permute-start.3 = (bf16[4,4,32,256]{3,2,1,0:T(8,128)(2,1)S(1)}, bf16[4,4,32,256]{3,2,1,0:T(8,128)(2,1)S(1)}, u32[]{:S(2)}, u32[]{:S(2)}) collective-permute-start(bf16[4,4,32,256]{3,2,1,0:T(8,128)(2,1)S(1)} %pad_maximum_fusion.2), channel_id=1, source_target_pairs={{0,4},{1,5},{2,6},{3,7},{4,0},{5,1},{6,2},{7,3},{8,12},{9,13},{10,... | collective-permute-start | bytes 786440 | tf_op jit(solution)/shard_map/ppermute | solution.py:746
  27.0 7.8 %collective-permute-start.6 = (bf16[16,4,32,256]{3,2,1,0:T(8,128)(2,1)S(1)}, bf16[16,4,32,256]{3,2,1,0:T(8,128)(2,1)S(1)}, u32[]{:S(2)}, u32[]{:S(2)}) collective-permute-start(bf16[16,4,32,256]{3,2,1,0:T(8,128)(2,1)S(1)} %constant_dynamic-update-slice_fusion.own_ref), channel_id=1, source_target_pairs={{0,2},{1,3},{2,0},{3,1},{4,6},{5,7},{6,4},{7,5},{8,10},{9,11},{10,... | collective-permute-start | bytes 3145736 | tf_op jit(solution)/shard_map/ppermute | solution.py:746
  34.8 15.0 %collective-permute-start.9 = (bf16[2,64,512]{2,1,0:T(8,128)(2,1)S(1)}, bf16[2,64,512]{2,1,0:T(8,128)(2,1)S(1)}, u32[]{:S(2)}, u32[]{:S(2)}) collective-permute-start(bf16[2,64,512]{2,1,0:T(8,128)(2,1)S(1)} %pad_maximum_fusion.3), channel_id=1, source_target_pairs={{0,24},{1,25},{2,26},{3,27},{4,28},{5,29},{6,30},{7,31},{8,16},{9,... | collective-permute-start | bytes 393224 | tf_op jit(solution)/shard_map/ppermute | solution.py:746
  36.4 13.5 %collective-permute-start.8 = (bf16[2,64,512]{2,1,0:T(8,128)(2,1)S(1)}, bf16[2,64,512]{2,1,0:T(8,128)(2,1)S(1)}, u32[]{:S(2)}, u32[]{:S(2)}) collective-permute-start(bf16[2,64,512]{2,1,0:T(8,128)(2,1)S(1)} %pad_maximum_fusion.3), channel_id=1, source_target_pairs={{0,16},{1,17},{2,18},{3,19},{4,20},{5,21},{6,22},{7,23},{8,24},{9,... | collective-permute-start | bytes 393224 | tf_op jit(solution)/shard_map/ppermute | solution.py:746
  36.4 13.5 %collective-permute-start.7 = (bf16[2,64,512]{2,1,0:T(8,128)(2,1)S(1)}, bf16[2,64,512]{2,1,0:T(8,128)(2,1)S(1)}, u32[]{:S(2)}, u32[]{:S(2)}) collective-permute-start(bf16[2,64,512]{2,1,0:T(8,128)(2,1)S(1)} %pad_maximum_fusion.3), channel_id=1, source_target_pairs={{0,8},{1,9},{2,10},{3,11},{4,12},{5,13},{6,14},{7,15},{8,0},{9,1},... | collective-permute-start | bytes 393224 | tf_op jit(solution)/shard_map/ppermute | solution.py:746
  49.9 11.1 %collective-permute-start.13 = (bf16[4,96,384]{2,1,0:T(8,128)(2,1)}, bf16[4,96,384]{2,1,0:T(8,128)(2,1)S(1)}, u32[]{:S(2)}, u32[]{:S(2)}) collective-permute-start(bf16[4,96,384]{2,1,0:T(8,128)(2,1)} %get-tuple-element.77), channel_id=1, source_target_pairs={{0,1},{2,3},{4,5},{6,7},{8,9},{10,11},{12,13},{14,15},{16,17},{18,... | collective-permute-start | bytes 884744 | tf_op jit(solution)/shard_map/ppermute | solution.py:776
  53.5 27.8 %collective-permute-start.12 = (bf16[2,256,512]{2,1,0:T(8,128)(2,1)S(1)}, bf16[2,256,512]{2,1,0:T(8,128)(2,1)S(1)}, u32[]{:S(2)}, u32[]{:S(2)}) collective-permute-start(bf16[2,256,512]{2,1,0:T(8,128)(2,1)S(1)} %pad_maximum_fusion.1), channel_id=1, source_target_pairs={{0,5},{1,4},{2,7},{3,6},{4,1},{5,0},{6,3},{7,2},{8,13},{9,12},{10,... | collective-permute-start | bytes 1572872 | tf_op jit(solution)/shard_map/ppermute | solution.py:746
  53.8 28.2 %collective-permute-start.11 = (bf16[2,256,512]{2,1,0:T(8,128)(2,1)S(1)}, bf16[2,256,512]{2,1,0:T(8,128)(2,1)S(1)}, u32[]{:S(2)}, u32[]{:S(2)}) collective-permute-start(bf16[2,256,512]{2,1,0:T(8,128)(2,1)S(1)} %pad_maximum_fusion.1), channel_id=1, source_target_pairs={{0,1},{1,0},{2,3},{3,2},{4,5},{5,4},{6,7},{7,6},{8,9},{9,8},{10,11... | collective-permute-start | bytes 1572872 | tf_op jit(solution)/shard_map/ppermute | solution.py:746
  56.5 25.6 %collective-permute-start.10 = (bf16[2,256,512]{2,1,0:T(8,128)(2,1)S(1)}, bf16[2,256,512]{2,1,0:T(8,128)(2,1)S(1)}, u32[]{:S(2)}, u32[]{:S(2)}) collective-permute-start(bf16[2,256,512]{2,1,0:T(8,128)(2,1)S(1)} %pad_maximum_fusion.1), channel_id=1, source_target_pairs={{0,4},{1,5},{2,6},{3,7},{4,0},{5,1},{6,2},{7,3},{8,12},{9,13},{10,... | collective-permute-start | bytes 1572872 | tf_op jit(solution)/shard_map/ppermute | solution.py:746
  82.2 20.7 %collective-permute-start.14 = (bf16[2,1024,512]{2,1,0:T(8,128)(2,1)S(1)}, bf16[2,1024,512]{2,1,0:T(8,128)(2,1)S(1)}, u32[]{:S(2)}, u32[]{:S(2)}) collective-permute-start(bf16[2,1024,512]{2,1,0:T(8,128)(2,1)S(1)} %pad_maximum_fusion.own_ref), channel_id=1, source_target_pairs={{0,2},{1,3},{2,0},{3,1},{4,6},{5,7},{6,4},{7,5},{8,10},{9,11},{10,... | collective-permute-start | bytes 6291464 | tf_op jit(solution)/shard_map/ppermute | solution.py:746
  155.8 35.7 %collective-permute-start.15 = (bf16[2,1024,512]{2,1,0:T(8,128)(2,1)}, bf16[2,1024,512]{2,1,0:T(8,128)(2,1)S(1)}, u32[]{:S(2)}, u32[]{:S(2)}) collective-permute-start(bf16[2,1024,512]{2,1,0:T(8,128)(2,1)} %get-tuple-element.111), channel_id=1, source_target_pairs={{0,2},{1,3},{2,0},{3,1},{4,6},{5,7},{6,4},{7,5},{8,10},{9,11},{10,... | collective-permute-start | bytes 6291464 | tf_op jit(solution)/shard_map/ppermute | solution.py:746
  156.2 15.9 %collective-permute-start.22 = (bf16[4,96,384]{2,1,0:T(8,128)(2,1)S(1)}, bf16[4,96,384]{2,1,0:T(8,128)(2,1)S(1)}, u32[]{:S(2)}, u32[]{:S(2)}) collective-permute-start(bf16[4,96,384]{2,1,0:T(8,128)(2,1)S(1)} %copy-done.4), channel_id=1, source_target_pairs={{1,0},{3,2},{5,4},{7,6},{9,8},{11,10},{13,12},{15,14},{17,16},{19,... | collective-permute-start | bytes 884744 | tf_op jit(solution)/shard_map/ppermute | solution.py:776
  194.7 37.4 %collective-permute-start.16 = (bf16[2,256,512]{2,1,0:T(8,128)(2,1)S(1)}, bf16[2,256,512]{2,1,0:T(8,128)(2,1)S(1)}, u32[]{:S(2)}, u32[]{:S(2)}) collective-permute-start(bf16[2,256,512]{2,1,0:T(8,128)(2,1)S(1)} %get-tuple-element.146), channel_id=1, source_target_pairs={{0,4},{1,5},{2,6},{3,7},{4,0},{5,1},{6,2},{7,3},{8,12},{9,13},{10,... | collective-permute-start | bytes 1572872 | tf_op jit(solution)/shard_map/ppermute | solution.py:746
  194.8 37.4 %collective-permute-start.18 = (bf16[2,256,512]{2,1,0:T(8,128)(2,1)S(1)}, bf16[2,256,512]{2,1,0:T(8,128)(2,1)S(1)}, u32[]{:S(2)}, u32[]{:S(2)}) collective-permute-start(bf16[2,256,512]{2,1,0:T(8,128)(2,1)S(1)} %get-tuple-element.147), channel_id=1, source_target_pairs={{0,5},{1,4},{2,7},{3,6},{4,1},{5,0},{6,3},{7,2},{8,13},{9,12},{10,... | collective-permute-start | bytes 1572872 | tf_op jit(solution)/shard_map/ppermute | solution.py:746
  195.8 36.4 %collective-permute-start.17 = (bf16[2,256,512]{2,1,0:T(8,128)(2,1)S(1)}, bf16[2,256,512]{2,1,0:T(8,128)(2,1)S(1)}, u32[]{:S(2)}, u32[]{:S(2)}) collective-permute-start(bf16[2,256,512]{2,1,0:T(8,128)(2,1)S(1)} %get-tuple-element.148), channel_id=1, source_target_pairs={{0,1},{1,0},{2,3},{3,2},{4,5},{5,4},{6,7},{7,6},{8,9},{9,8},{10,11... | collective-permute-start | bytes 1572872 | tf_op jit(solution)/shard_map/ppermute | solution.py:746
  232.5 22.3 %collective-permute-start.19 = (bf16[2,64,512]{2,1,0:T(8,128)(2,1)S(1)}, bf16[2,64,512]{2,1,0:T(8,128)(2,1)S(1)}, u32[]{:S(2)}, u32[]{:S(2)}) collective-permute-start(bf16[2,64,512]{2,1,0:T(8,128)(2,1)S(1)} %get-tuple-element.152), channel_id=1, source_target_pairs={{0,8},{1,9},{2,10},{3,11},{4,12},{5,13},{6,14},{7,15},{8,0},{9,1},... | collective-permute-start | bytes 393224 | tf_op jit(solution)/shard_map/ppermute | solution.py:746
  232.8 22.1 %collective-permute-start.21 = (bf16[2,64,512]{2,1,0:T(8,128)(2,1)S(1)}, bf16[2,64,512]{2,1,0:T(8,128)(2,1)S(1)}, u32[]{:S(2)}, u32[]{:S(2)}) collective-permute-start(bf16[2,64,512]{2,1,0:T(8,128)(2,1)S(1)} %get-tuple-element.153), channel_id=1, source_target_pairs={{0,24},{1,25},{2,26},{3,27},{4,28},{5,29},{6,30},{7,31},{8,16},{9,... | collective-permute-start | bytes 393224 | tf_op jit(solution)/shard_map/ppermute | solution.py:746
  232.8 22.1 %collective-permute-start.20 = (bf16[2,64,512]{2,1,0:T(8,128)(2,1)S(1)}, bf16[2,64,512]{2,1,0:T(8,128)(2,1)S(1)}, u32[]{:S(2)}, u32[]{:S(2)}) collective-permute-start(bf16[2,64,512]{2,1,0:T(8,128)(2,1)S(1)} %get-tuple-element.154), channel_id=1, source_target_pairs={{0,16},{1,17},{2,18},{3,19},{4,20},{5,21},{6,22},{7,23},{8,24},{9,... | collective-permute-start | bytes 393224 | tf_op jit(solution)/shard_map/ppermute | solution.py:746
  263.9 11.3 %collective-permute-start.23 = (bf16[16,4,32,256]{3,2,1,0:T(8,128)(2,1)}, bf16[16,4,32,256]{3,2,1,0:T(8,128)(2,1)S(1)}, u32[]{:S(2)}, u32[]{:S(2)}) collective-permute-start(bf16[16,4,32,256]{3,2,1,0:T(8,128)(2,1)} %get-tuple-element.123), channel_id=1, source_target_pairs={{0,2},{1,3},{2,0},{3,1},{4,6},{5,7},{6,4},{7,5},{8,10},{9,11},{10,... | collective-permute-start | bytes 3145736 | tf_op jit(solution)/shard_map/ppermute | solution.py:746
  265.0 10.3 %collective-permute-start.27 = (f32[1,1048]{1,0:T(1,128)S(1)}, f32[1,1048]{1,0:T(1,128)S(1)}, u32[]{:S(2)}, u32[]{:S(2)}) collective-permute-start(f32[1,1048]{1,0:T(1,128)S(1)} %broadcast_in_dim.82), channel_id=1, source_target_pairs={{0,2},{1,3},{2,0},{3,1},{4,6},{5,7},{6,4},{7,5},{8,10},{9,11},{10,... | collective-permute-start | bytes 12584 | tf_op jit(solution)/shard_map/ppermute | solution.py:746
  275.8 7.1 %collective-permute-start.29 = (f32[1,1048]{1,0:T(1,128)S(1)}, f32[1,1048]{1,0:T(1,128)S(1)}, u32[]{:S(2)}, u32[]{:S(2)}) collective-permute-start(f32[1,1048]{1,0:T(1,128)S(1)} %reshape_add_fusion), channel_id=1, source_target_pairs={{0,1},{1,0},{2,3},{3,2},{4,5},{5,4},{6,7},{7,6},{8,9},{9,8},{10,11... | collective-permute-start | bytes 12584 | tf_op jit(solution)/shard_map/ppermute | solution.py:746
  279.3 13.1 %collective-permute-start.24 = (bf16[4,4,32,256]{3,2,1,0:T(8,128)(2,1)S(1)}, bf16[4,4,32,256]{3,2,1,0:T(8,128)(2,1)S(1)}, u32[]{:S(2)}, u32[]{:S(2)}) collective-permute-start(bf16[4,4,32,256]{3,2,1,0:T(8,128)(2,1)S(1)} %get-tuple-element.149), channel_id=1, source_target_pairs={{0,4},{1,5},{2,6},{3,7},{4,0},{5,1},{6,2},{7,3},{8,12},{9,13},{10,... | collective-permute-start | bytes 786440 | tf_op jit(solution)/shard_map/ppermute | solution.py:746
  279.4 12.9 %collective-permute-start.26 = (bf16[4,4,32,256]{3,2,1,0:T(8,128)(2,1)S(1)}, bf16[4,4,32,256]{3,2,1,0:T(8,128)(2,1)S(1)}, u32[]{:S(2)}, u32[]{:S(2)}) collective-permute-start(bf16[4,4,32,256]{3,2,1,0:T(8,128)(2,1)S(1)} %get-tuple-element.150), channel_id=1, source_target_pairs={{0,5},{1,4},{2,7},{3,6},{4,1},{5,0},{6,3},{7,2},{8,13},{9,12},{10,... | collective-permute-start | bytes 786440 | tf_op jit(solution)/shard_map/ppermute | solution.py:746
  280.8 12.8 %collective-permute-start.25 = (bf16[4,4,32,256]{3,2,1,0:T(8,128)(2,1)S(1)}, bf16[4,4,32,256]{3,2,1,0:T(8,128)(2,1)S(1)}, u32[]{:S(2)}, u32[]{:S(2)}) collective-permute-start(bf16[4,4,32,256]{3,2,1,0:T(8,128)(2,1)S(1)} %get-tuple-element.151), channel_id=1, source_target_pairs={{0,1},{1,0},{2,3},{3,2},{4,5},{5,4},{6,7},{7,6},{8,9},{9,8},{10,11... | collective-permute-start | bytes 786440 | tf_op jit(solution)/shard_map/ppermute | solution.py:746
  293.8 6.0 %collective-permute-start.33 = (f32[1,1048]{1,0:T(1,128)S(1)}, f32[1,1048]{1,0:T(1,128)S(1)}, u32[]{:S(2)}, u32[]{:S(2)}) collective-permute-start(f32[1,1048]{1,0:T(1,128)S(1)} %add_add_fusion.2), channel_id=1, source_target_pairs={{0,24},{1,25},{2,26},{3,27},{4,28},{5,29},{6,30},{7,31},{8,16},{9,... | collective-permute-start | bytes 12584 | tf_op jit(solution)/shard_map/ppermute | solution.py:746
  294.8 7.1 %collective-permute-start.32 = (f32[1,1048]{1,0:T(1,128)S(1)}, f32[1,1048]{1,0:T(1,128)S(1)}, u32[]{:S(2)}, u32[]{:S(2)}) collective-permute-start(f32[1,1048]{1,0:T(1,128)S(1)} %add_add_fusion.2), channel_id=1, source_target_pairs={{0,16},{1,17},{2,18},{3,19},{4,20},{5,21},{6,22},{7,23},{8,24},{9,... | collective-permute-start | bytes 12584 | tf_op jit(solution)/shard_map/ppermute | solution.py:746
  298.5 6.2 %collective-permute-start.36 = (bf16[1,4,32,256]{3,2,1,0:T(8,128)(2,1)S(1)}, bf16[1,4,32,256]{3,2,1,0:T(8,128)(2,1)S(1)}, u32[]{:S(2)}, u32[]{:S(2)}) collective-permute-start(bf16[1,4,32,256]{3,2,1,0:T(8,128)(2,1)S(1)} %get-tuple-element.158), channel_id=1, source_target_pairs={{0,24},{1,25},{2,26},{3,27},{4,28},{5,29},{6,30},{7,31},{8,16},{9,... | collective-permute-start | bytes 196616 | tf_op jit(solution)/shard_map/ppermute | solution.py:746
  299.8 6.4 %collective-permute-start.35 = (bf16[1,4,32,256]{3,2,1,0:T(8,128)(2,1)S(1)}, bf16[1,4,32,256]{3,2,1,0:T(8,128)(2,1)S(1)}, u32[]{:S(2)}, u32[]{:S(2)}) collective-permute-start(bf16[1,4,32,256]{3,2,1,0:T(8,128)(2,1)S(1)} %get-tuple-element.159), channel_id=1, source_target_pairs={{0,16},{1,17},{2,18},{3,19},{4,20},{5,21},{6,22},{7,23},{8,24},{9,... | collective-permute-start | bytes 196616 | tf_op jit(solution)/shard_map/ppermute | solution.py:746
  (19 other events, 165.2 us)

commit v5 on v4

--- a/solution.py
+++ b/solution.py
@@ -304,7 +304,7 @@
         state[...] = keep * before + block_only(added)
         return carry
 
-    lax.fori_loop(0, rows // ROWS, body, 0, unroll=2)
+    lax.fori_loop(0, rows // ROWS, body, 0, unroll=4)
 
 
 def near_back(query, key_heads, grad_pair, near_mask, spread_near, scale_q, rows_q, rows_g):
@@ -319,6 +319,7 @@
     scalars,
     query_ref,
     key_ref,
+    value_ref,
     message_ref,
     start_ref,
     blend_ref,
@@ -338,7 +339,7 @@
 
     tails = message_ref[0, pl.ds(HEAD_DIM, TAIL), :]
     key = jnp.concatenate([tails[:, :PAIR], key_ref[0]], axis=0)
-    value = jnp.concatenate([tails[:, PAIR : 2 * PAIR], key_ref[1]], axis=0)
+    value = jnp.concatenate([tails[:, PAIR : 2 * PAIR], value_ref[0]], axis=0)
     start = start_ref[pl.ds(0, ROWS), :]
     near_mask, _, _, row, _, _ = masks(0, start)
     query = query_ref[0, pl.ds(0, ROWS), :]
@@ -545,7 +546,7 @@
         adjoint[...] = keep * after + block_only(jnp.concatenate([from_lift, from_bend], axis=1))
         return carry
 
-    lax.fori_loop(0, steps, body, 0)
+    lax.fori_loop(0, steps, body, 0, unroll=4)
 
 
 def feed_kernel(
@@ -611,33 +612,16 @@
 
 
 def feed_grad_kernel(
-    scalars,
-    normed_ref,
-    cotangent_ref,
-    active_ref,
-    d_inner_ref,
-    mixed_ref,
-    d_branch_ref,
-    keep_ref,
-    give_ref,
-    out_grad_ref,
+    scalars, normed_ref, cotangent_ref, active_ref, d_inner_ref, *refs
 ):
-    step = pl.program_id(0)
-    steps = pl.num_programs(0)
-
-    @pl.when(step == 0)
-    def _():
-        out_grad_ref[...] = mm(d_branch_ref[...], mixed_ref[...], TN)
-
-    @pl.when(step < steps // 2)
-    def _():
-        keep_ref[0] = mm(d_inner_ref[...], normed_ref[...], TN)
-        keep_ref[1] = mm(active_ref[...], cotangent_ref[...], TN)
-
-    @pl.when(step >= steps // 2)
-    def _():
-        give_ref[0] = mm(d_inner_ref[...], normed_ref[...], TN).astype(BF16)
-        give_ref[1] = mm(active_ref[...], cotangent_ref[...], TN).astype(BF16)
+    refs[-1][0] = mm(d_inner_ref[...], normed_ref[...], TN).astype(refs[-1].dtype)
+    refs[-1][1] = mm(active_ref[...], cotangent_ref[...], TN).astype(refs[-1].dtype)
+    if len(refs) > 1:
+        mixed_ref, d_branch_ref, out_grad_ref, _ = refs
+
+        @pl.when(pl.program_id(0) == 0)
+        def _():
+            out_grad_ref[...] = mm(d_branch_ref[...], mixed_ref[...], TN)
 
 
 def input_kernel(
@@ -754,20 +738,16 @@
     return whole if after is None else (whole, after)
 
 
-def narrow(keep, gives, group):
-    total = keep.astype(F32)
-    for combo, give in enumerate(gives, 1):
-        total = total + peer(give.astype(BF16), group, combo).astype(F32)
-    return total
-
-
-def narrow_axis(total, group, axis):
+def narrow(keep, gives, group, after=None):
+    arrived = [peer(give.astype(BF16), group, combo) for combo, give in enumerate(gives, 1)]
+    if after is not None:
+        arrived, _ = lax.optimization_barrier((arrived, after))
+    return keep.astype(F32) + sum(part.astype(F32) for part in arrived)
+
+
+def narrow_axis(total, group, axis, after=None):
     parts = jnp.split(total, 1 << len(group), axis=axis)
-    return narrow(parts[0], parts[1:], group)
-
-
-def add_peers(array, group):
-    return array + sum(peer(array, group, combo) for combo in range(1, 1 << len(group)))
+    return narrow(parts[0], parts[1:], group, after)
 
 
 def pass_along(local, keep, shift):
@@ -802,10 +782,13 @@
 
     shards = jnp.concatenate([qkv_weight, out_weight.T[None]], axis=0)[None]
     feed = jnp.stack([in_weight, down_weight])
-    for group in groups[:-1]:
+    shards = widen(shards, groups[0], 0)
+    feed, _ = lax.optimization_barrier((feed, shards))
+    feed = widen(feed, groups[0][:1], 1)
+    for group in groups[1:-1]:
         shards = widen(shards, group, 0)
+    shards, feed = lax.optimization_barrier((shards, feed))
     others = peer(shards, groups[-1], 1)
-    feed, others = lax.optimization_barrier((feed, others))
 
     item_lengths = lengths[0]
     slots = item_lengths.shape[0]
@@ -877,8 +860,8 @@
         6 * big * width,
         12 * big,
     )(scalars, tokens, ln1_gain[None], shards, others)
-    feed = widen(feed, groups[0], 1)
-    feed, closing = lax.optimization_barrier((feed, closing))
+    for pair in groups[0][1:]:
+        feed, _ = widen(feed, [pair], 1, closing)
     message = pass_along(closing, keep_all, 1)
 
     key_scratch = pltpu.VMEM((rows + TAIL, PAIR), BF16)
@@ -934,12 +917,12 @@
         32 * big,
     )(scalars, mixed, tokens, cotangent, out_all, ln2_gain[None], feed, feed_other)
 
-    front_keys = qkv[1:, :ROWS]
     back = call(
         prologue_kernel,
         [
             spec["query"],
-            pl.BlockSpec((2, ROWS, PAIR), lambda p, s: (0, 0, p)),
+            pl.BlockSpec((1, ROWS, PAIR), lambda p, s: (1, 0, p)),
+            pl.BlockSpec((1, ROWS, PAIR), lambda p, s: (2, 0, p)),
             spec["message"],
             spec["start"],
             spec["blend"],
@@ -956,32 +939,39 @@
         "prologue",
         500 * big,
         20 * big,
-    )(scalars, qkv, front_keys, message, start_wide, blend_wide, d_mixed, near, far1, inv_l, inv_d)
+    )(scalars, qkv, qkv, qkv, message, start_wide, blend_wide, d_mixed, near, far1, inv_l, inv_d)
     d_inner, _ = lax.optimization_barrier((d_inner, back))
     back_in = pass_along(back, keep_all, -1)
 
     unit = hidden_units // 4
-    columns = pl.BlockSpec((rows, unit), lambda p, s: (0, p))
     half_shape = (2, 2 * unit, width)
-    keep, give, out_grad = call(
-        feed_grad_kernel,
-        [whole_spec((rows, width))] * 2 + [columns] * 2 + [whole_spec((rows, width))] * 2,
-        [
-            pl.BlockSpec((2, unit, width), lambda p, s: (0, jnp.minimum(p, 1), 0)),
-            pl.BlockSpec((2, unit, width), lambda p, s: (0, jnp.maximum(p - 2, 0), 0)),
-            whole_spec((width, width)),
-        ],
-        [
-            jax.ShapeDtypeStruct(half_shape, F32),
-            jax.ShapeDtypeStruct(half_shape, BF16),
-            jax.ShapeDtypeStruct((width, width), F32),
-        ],
-        [],
-        4,
-        "feed_grad",
-        4 * big * hidden_units,
-        24 * big,
-    )(scalars, normed_two, cotangent, active, d_inner, mixed, d_branch)
+    whole_rows = whole_spec((rows, width))
+
+    def feed_grad(place, kind, d_inner, more_ins, more_in_specs, more_outs, more_out_specs):
+        columns = pl.BlockSpec((rows, unit), lambda p, s: (0, p + 2 * place))
+        return call(
+            feed_grad_kernel,
+            [whole_rows] * 2 + [columns] * 2 + more_in_specs,
+            more_out_specs + [pl.BlockSpec((2, unit, width), lambda p, s: (0, p, 0))],
+            more_outs + [jax.ShapeDtypeStruct(half_shape, kind)],
+            [],
+            2,
+            "feed_grad",
+            2 * big * hidden_units,
+            12 * big,
+        )(scalars, normed_two, cotangent, active, d_inner, *more_ins)
+
+    out_grad, keep = feed_grad(
+        0,
+        F32,
+        d_inner,
+        [mixed, d_branch],
+        [whole_rows] * 2,
+        [jax.ShapeDtypeStruct((width, width), F32)],
+        [whole_spec((width, width))],
+    )
+    d_inner, back_in, out_grad = lax.optimization_barrier((d_inner, back_in, out_grad))
+    (give,) = feed_grad(1, BF16, d_inner, [], [], [], [])
     feed_share = narrow(keep, [give], groups[-1])
     left = list(reversed(groups[:-1]))
 
@@ -1059,12 +1049,10 @@
     parts = [gain_one_rows[0] / ln1_gain, jnp.sum(gain_two_rows, axis=0), blend_part.reshape(-1)]
     total_sums = jnp.concatenate(parts)[None]
     share = narrow(keep, [give], groups[-1])
-    total_sums = add_peers(total_sums, groups[-1])
-    for group in reversed(groups[:-1]):
-        _, total_sums = lax.optimization_barrier((share, total_sums))
-        share = narrow_axis(share, group, 0)
-        total_sums = add_peers(total_sums, group)
-    d_qkv, give = lax.optimization_barrier((d_qkv, give))
+    hops = list(reversed(relative_bits()))
+    total_sums = total_sums + peer(total_sums, [hops[0]], 1)
+    total_sums, d_qkv, _ = lax.optimization_barrier((total_sums, d_qkv, share))
+    total_sums = total_sums + peer(total_sums, [hops[1]], 1)
     input_grad = call(
         input_kernel,
         [
@@ -1082,6 +1070,16 @@
         6 * big * width,
         24 * big,
     )(scalars, d_qkv, qkv_all, tokens, d_hidden, ln1_gain[None])
+    share = narrow_axis(share, groups[-2], 0, input_grad)
+    total_sums, _ = lax.optimization_barrier((total_sums, input_grad))
+    total_sums = total_sums + peer(total_sums, [hops[2]], 1)
+    for group in reversed(groups[:-2]):
+        parts = jnp.split(share, 1 << len(group), axis=0)
+        gives = [part.astype(BF16) for part in parts[1:]]
+        total_sums, _ = lax.optimization_barrier((total_sums, gives))
+        share = narrow(parts[0], gives, group)
+    for pair in hops[3:]:
+        total_sums = total_sums + peer(total_sums, [pair], 1)
     total_sums = total_sums[0]
     gain_one, gain_two = total_sums[:width], total_sums[width : 2 * width]
     blend_sum = total_sums[2 * width :].reshape(blend.shape)

time: 308 us -> 285 us (0.925)
  waiting for transfers between devices: 47.5 us -> 27.7 us
  Pallas kernels: 189 us -> 183 us
    ppermute x2, waiting for transfers between devices: 17.8 us -> 3.09 us  [pass_along(): arrived = lax.ppermute(local, 'head', pairs)]
    pallas_call x3, Pallas kernels: 71.4 us -> 64.1 us  [per_device(): call(backward_kernel, [spec['qkv'], spec['message'], spec['start'], spec[...]
    ppermute x35 -> x32, waiting for transfers between devices: 29.8 us -> 24.6 us  [peer(): return lax.ppermute(array, ('dp', 'head'), pairs)]
    pallas_call x2 -> x3, Pallas kernels: 23.4 us -> 26.8 us  [the longest x2 19 us: feed_grad(): call(feed_grad_kernel, [whole_rows] * 2 + [columns] * 2 + more_in_specs,...]
    ppermute x35 -> x32, starting transfers between devices: 40.5 us -> 41.8 us  [peer(): return lax.ppermute(array, ('dp', 'head'), pairs)]
  transfers between devices with their start and end apart: 37 -> 34, of which waited for: 11 -> 14; matrix products, arithmetic and copies ran while one was open for 5% -> 6% of each run, Pallas kernels for 42% -> 46%
where the time goes in v5:
time: 285 us; the launch traced here: 284 us
  Pallas kernels  183 us (64%)
  starting transfers between devices  46.9 us (16%)
  waiting for transfers between devices  27.7 us (10%)
  local copies, waits for them, and re-layouts  14.2 us (5%)
  other arithmetic  10.8 us (4%)
    pallas_call x3, Pallas kernels, per_device(): call(backward_kernel, [spec['qkv'], spec['message'], spec['start'], spec[...  64.1 us
    ppermute x32, starting transfers between devices, peer(): return lax.ppermute(array, ('dp', 'head'), pairs)  41.8 us
    pallas_call x2, Pallas kernels, per_device(): call(functools.partial(resume, forward_kernel, len(results)), [spec['qkv'...  35.6 us
    pallas_call x1, Pallas kernels, per_device(): call(feed_kernel, [row_spec] * 3 + [whole_spec((width, width)), whole_spe...  28.1 us
    ppermute x32, waiting for transfers between devices, peer(): return lax.ppermute(array, ('dp', 'head'), pairs)  24.6 us
    pallas_call x2, Pallas kernels, feed_grad(): call(feed_grad_kernel, [whole_rows] * 2 + [columns] * 2 + more_in_specs,...  19 us
    pallas_call x1, Pallas kernels, per_device(): call(functools.partial(project_kernel, flips=flips), [pl.BlockSpec((part,...  10.6 us
    pallas_call x1, Pallas kernels, per_device(): call(functools.partial(weight_grad_kernel, flips=flips), [whole_spec((row...  8.86 us
  transfers between devices with their start and end apart: 34, of which 14 were waited for; matrix products, arithmetic and copies ran while one was open for 6% of the time, Pallas kernels for 46%

profile of v5, /device:TPU:0, one launch (start us, length us, event | category | flops | bytes accessed | tf_op | source)
XLA Modules:
  0.0 284.3 jit_solution(18261781563322513057)
XLA Ops:
  1.5 5.1 %collective-permute-start.2 = (bf16[1,4,32,256]{3,2,1,0:T(8,128)(2,1)S(1)}, bf16[1,4,32,256]{3,2,1,0:T(8,128)(2,1)S(1)}, u32[]{:S(2)}, u32[]{:S(2)}) collective-permute-start(bf16[1,4,32,256]{3,2,1,0:T(8,128)(2,1)S(1)} %maximum_bitcast_fusion), channel_id=1, source_target_pairs={{0,24},{1,25},{2,26},{3,27},{4,28},{5,29},{6,30},{7,31},{8,16},{9,... | collective-permute-start | bytes 196616 | tf_op jit(solution)/shard_map/ppermute | solution.py:730
  9.1 3.1 %collective-permute-done.1 = bf16[1,4,32,256]{3,2,1,0:T(8,128)(2,1)S(1)} collective-permute-done((bf16[1,4,32,256]{3,2,1,0:T(8,128)(2,1)S(1)}, bf16[1,4,32,256]{3,2,1,0:T(8,128)(2,1)S(1)}, u32[]{:S(2)}, u32[]{:S(2)}) %collective-permute-start.1) | collective-permute-done | bytes 65568 | tf_op jit(solution)/shard_map/ppermute | solution.py:730
  12.2 2.5 collective-permute-start.5
  16.9 3.9 %collective-permute-done.6 = bf16[2,64,512]{2,1,0:T(8,128)(2,1)S(1)} collective-permute-done((bf16[2,64,512]{2,1,0:T(8,128)(2,1)S(1)}, bf16[2,64,512]{2,1,0:T(8,128)(2,1)S(1)}, u32[]{:S(2)}, u32[]{:S(2)}) %collective-permute-start.6) | collective-permute-done | bytes 131104 | tf_op jit(solution)/shard_map/ppermute | solution.py:730
  20.8 5.9 %collective-permute-done.3 = bf16[4,4,32,256]{3,2,1,0:T(8,128)(2,1)S(1)} collective-permute-done((bf16[4,4,32,256]{3,2,1,0:T(8,128)(2,1)S(1)}, bf16[4,4,32,256]{3,2,1,0:T(8,128)(2,1)S(1)}, u32[]{:S(2)}, u32[]{:S(2)}) %collective-permute-start.3) | collective-permute-done | bytes 262176 | tf_op jit(solution)/shard_map/ppermute | solution.py:730
  31.4 1.9 concatenate.29.scalars
  35.2 10.6 %project.1 = (bf16[3,1536,512]{2,1,0:T(8,128)(2,1)}, bf16[1536,512]{1,0:T(8,128)(2,1)}, bf16[3,512,512]{2,1,0:T(8,128)(2,1)}, bf16[512,512]{1,0:T(8,128)(2,1)}, bf16[4,96,384]{2,1,0:T(8,128)(2,1)}) custom-call(s32[21]{0:T(128)} %concatenate.29.scalars, bf16[1536,512]{1,0:T(8,128)(2,1)} %tokens_ref.5, f32[1,512]{1,0:T(1,128)} %bitcast.34, ...), custom_call_target="tpu_custom_call" | custom-call | flops 2415919104 | bytes 9437184 | tf_op jit(solution)/shard_map/project/pallas_call | solution.py:832
  45.8 3.6 %collective-permute-start.12 = (bf16[4,96,384]{2,1,0:T(8,128)(2,1)}, bf16[4,96,384]{2,1,0:T(8,128)(2,1)S(1)}, u32[]{:S(2)}, u32[]{:S(2)}) collective-permute-start(bf16[4,96,384]{2,1,0:T(8,128)(2,1)} %get-tuple-element.82), channel_id=1, source_target_pairs={{0,1},{2,3},{4,5},{6,7},{8,9},{10,11},{12,13},{14,15},{16,17},{18,... | collective-permute-start | bytes 884744 | tf_op jit(solution)/shard_map/ppermute | solution.py:756
  51.0 2.1 collective-permute-start.10
  54.4 2.5 collective-permute-done.12.message_ref
  58.1 18.1 %forward.2 = (bf16[1536,512]{1,0:T(8,128)(2,1)}, f32[1536,512]{1,0:T(8,128)}, f32[1536,512]{1,0:T(8,128)}, f32[1536,512]{1,0:T(8,128)}, f32[1536,512]{1,0:T(8,12...) custom-call(s32[21]{0:T(128)} %concatenate.29.scalars, ...), custom_call_target="tpu_custom_call" | custom-call | flops 3145728000 | bytes 15728640 | tf_op jit(solution)/shard_map/forward/pallas_call | solution.py:874
  76.1 2.4 collective-permute-done.10
  78.8 17.6 %forward.3 = (bf16[1536,512]{1,0:T(8,128)(2,1)}, f32[1536,512]{1,0:T(8,128)}, f32[1536,512]{1,0:T(8,128)}, f32[1536,512]{1,0:T(8,128)}, f32[1536,512]{1,0:T(8,12...) custom-call(s32[21]{0:T(128)} %concatenate.29.scalars, ...), custom_call_target="tpu_custom_call", output_to_operand_aliasing={{0}: (5, {}), {1}: (6, {}), {2}: (7, {}), {3}: (8, {}), {4}... | custom-call | flops 3145728000 | bytes 15728640 | tf_op jit(solution)/shard_map/forward/pallas_call | solution.py:874
  97.7 28.1 %feed.1 = (bf16[1536,512]{1,0:T(8,128)(2,1)}, f32[1536,512]{1,0:T(8,128)}, bf16[1536,512]{1,0:T(8,128)(2,1)}, bf16[1536,512]{1,0:T(8,128)(2,1)}, bf16[1536,512]{...) custom-call(s32[21]{0:T(128)} %concatenate.29.scalars, ...), custom_call_target="tpu_custom_call" | custom-call | flops 12884901888 | bytes 25165824 | tf_op jit(solution)/shard_map/feed/pallas_call | solution.py:902
  125.8 7.8 %prologue.1 = bf16[4,96,384]{2,1,0:T(8,128)(2,1)} custom-call(s32[21]{0:T(128)} %concatenate.29.scalars, bf16[3,1536,512]{2,1,0:T(8,128)(2,1)} %get-tuple-element.80.qkv_ref.query_ref.key_ref.value_ref, bf16[3,1536,512]{2,1,0:T(8,128)(2,1)} %get-tuple-element.80.qkv_ref.query_ref.key_ref.value_ref, ...), custom_call_target="tpu_custom_call" | custom-call | flops 393216000 | bytes 15728640 | tf_op jit(solution)/shard_map/prologue/pallas_call | solution.py:920
  135.1 10.8 %feed_grad.2 = (f32[512,512]{1,0:T(8,128)}, f32[2,1024,512]{2,1,0:T(8,128)}) custom-call(s32[21]{0:T(128)} %concatenate.29.scalars, bf16[1536,512]{1,0:T(8,128)(2,1)} %get-tuple-element.107.normed_ref, bf16[1536,512]{1,0:T(8,128)(2,1)} %cotangent_ref.5, bf16[1536,2048]{1,0:T(8,128)(2,1)} %get-tuple-element.108.active_ref, ...), custom_call_target="tpu_custom_call" | custom-call | flops 3221225472 | bytes 9437184 | tf_op jit(solution)/shard_map/feed_grad/pallas_call | solution.py:952
  146.5 8.2 %feed_grad.3 = bf16[2,1024,512]{2,1,0:T(8,128)(2,1)} custom-call(s32[21]{0:T(128)} %concatenate.29.scalars, bf16[1536,512]{1,0:T(8,128)(2,1)} %get-tuple-element.107.normed_ref, bf16[1536,512]{1,0:T(8,128)(2,1)} %cotangent_ref.5, bf16[1536,2048]{1,0:T(8,128)(2,1)} %get-tuple-element.108.active_ref, bf16[1536,2048]{1,0:T(8,128)(2,1)} %get-tuple-element.119.d_inner_ref), custom_call_target="tpu_custom_call" | custom-call | flops 3221225472 | bytes 9437184 | tf_op jit(solution)/shard_map/feed_grad/pallas_call | solution.py:952
  155.3 16.9 %backward.3 = (bf16[3,1536,512]{2,1,0:T(8,128)(2,1)}, f32[24,128]{1,0:T(8,128)}) custom-call(s32[21]{0:T(128)} %concatenate.29.scalars, bf16[3,1536,512]{2,1,0:T(8,128)(2,1)} %get-tuple-element.80.qkv_ref.query_ref.key_ref.value_ref, bf16[4,96,384]{2,1,0:T(8,128)(2,1)} %copy-done, s32[1536,128]{1,0:T(8,128)} %broadcast_in_dim.78.start_ref, ...), custom_call_target="tpu_custom_call" | custom-call | flops 3145728000 | bytes 7864320 | tf_op jit(solution)/shard_map/backward/pallas_call | solution.py:984
  172.2 3.1 %fusion.6 = (bf16[2,1024,512]{2,1,0:T(8,128)(2,1)S(1)}, f32[2,1024,512]{2,1,0:T(8,128)S(1)}) fusion(f32[2,1024,512]{2,1,0:T(8,128)} %get-tuple-element.117, bf16[2,1024,512]{2,1,0:T(8,128)(2,1)S(1)} %collective-permute-done.15), kind=kLoop, calls=%fused_computation.47 | loop fusion | flops 3145728 | bytes 12582912 | tf_op jit(solution)/shard_map/convert.11
  175.5 4.9 %collective-permute-start.16 = (bf16[2,256,512]{2,1,0:T(8,128)(2,1)S(1)}, bf16[2,256,512]{2,1,0:T(8,128)(2,1)S(1)}, u32[]{:S(2)}, u32[]{:S(2)}) collective-permute-start(bf16[2,256,512]{2,1,0:T(8,128)(2,1)S(1)} %get-tuple-element.158), channel_id=1, source_target_pairs={{0,4},{1,5},{2,6},{3,7},{4,0},{5,1},{6,2},{7,3},{8,12},{9,13},{10,... | collective-permute-start | bytes 1572872 | tf_op jit(solution)/shard_map/ppermute | solution.py:730
  180.4 3.2 %collective-permute-start.18 = (bf16[2,256,512]{2,1,0:T(8,128)(2,1)S(1)}, bf16[2,256,512]{2,1,0:T(8,128)(2,1)S(1)}, u32[]{:S(2)}, u32[]{:S(2)}) collective-permute-start(bf16[2,256,512]{2,1,0:T(8,128)(2,1)S(1)} %get-tuple-element.159), channel_id=1, source_target_pairs={{0,5},{1,4},{2,7},{3,6},{4,1},{5,0},{6,3},{7,2},{8,13},{9,12},{10,... | collective-permute-start | bytes 1572872 | tf_op jit(solution)/shard_map/ppermute | solution.py:730
  184.1 30.1 %backward.4 = (bf16[3,1536,512]{2,1,0:T(8,128)(2,1)}, f32[24,256]{1,0:T(8,128)}) custom-call(s32[21]{0:T(128)} %concatenate.29.scalars, bf16[3,1536,512]{2,1,0:T(8,128)(2,1)} %get-tuple-element.80.qkv_ref.query_ref.key_ref.value_ref, bf16[4,96,384]{2,1,0:T(8,128)(2,1)} %copy-done, ...), custom_call_target="tpu_custom_call", output_to_operand_aliasing={{0}: (13, {})} | custom-call | flops 6291456000 | bytes 15728640 | tf_op jit(solution)/shard_map/backward/pallas_call | solution.py:984
  218.1 17.2 %backward.5 = (bf16[3,1536,512]{2,1,0:T(8,128)(2,1)}, f32[24,128]{1,0:T(8,128)}) custom-call(s32[21]{0:T(128)} %concatenate.29.scalars, bf16[3,1536,512]{2,1,0:T(8,128)(2,1)} %get-tuple-element.80.qkv_ref.query_ref.key_ref.value_ref, bf16[4,96,384]{2,1,0:T(8,128)(2,1)} %copy-done, ...), custom_call_target="tpu_custom_call", output_to_operand_aliasing={{0}: (13, {})} | custom-call | flops 3145728000 | bytes 7864320 | tf_op jit(solution)/shard_map/backward/pallas_call | solution.py:984
  235.4 8.9 %weight_grad.1 = (f32[16,4,32,256]{3,2,1,0:T(8,128)}, bf16[16,4,32,256]{3,2,1,0:T(8,128)(2,1)}, f32[8,512]{1,0:T(8,128)}) custom-call(s32[21]{0:T(128)} %concatenate.29.scalars, bf16[1536,512]{1,0:T(8,128)(2,1)} %get-tuple-element.106.normed_ref, bf16[3,1536,512]{2,1,0:T(8,128)(2,1)} %get-tuple-element.138.d_qkv_ref, ...), custom_call_target="tpu_custom_call" | custom-call | flops 2415919104 | bytes 6291456 | tf_op jit(solution)/shard_map/weight_grad/pallas_call | solution.py:1029
  247.2 2.1 fusion.4
  249.3 3.0 %collective-permute-start.28 = (bf16[4,4,32,256]{3,2,1,0:T(8,128)(2,1)S(1)}, bf16[4,4,32,256]{3,2,1,0:T(8,128)(2,1)S(1)}, u32[]{:S(2)}, u32[]{:S(2)}) collective-permute-start(bf16[4,4,32,256]{3,2,1,0:T(8,128)(2,1)S(1)} %get-tuple-element.161), channel_id=1, source_target_pairs={{0,5},{1,4},{2,7},{3,6},{4,1},{5,0},{6,3},{7,2},{8,13},{9,12},{10,... | collective-permute-start | bytes 786440 | tf_op jit(solution)/shard_map/ppermute | solution.py:730
  253.0 1.8 collective-permute-start.24
  254.8 8.9 %input.1 = f32[1536,512]{1,0:T(8,128)} custom-call(s32[21]{0:T(128)} %concatenate.29.scalars, bf16[3,1536,512]{2,1,0:T(8,128)(2,1)} %get-tuple-element.138.d_qkv_ref, bf16[3,512,512]{2,1,0:T(8,128)(2,1)} %get-tuple-element.130.weight_ref, bf16[1536,512]{1,0:T(8,128)(2,1)} %tokens_ref.5, f32[1536,512]{1,0:T(8,128)} %get-tuple-element.139.d_hidden_ref, ...), custom_call_target="tpu_custom_call" | custom-call | flops 2415919104 | bytes 18874368 | tf_op jit(solution)/shard_map/input/pallas_call | solution.py:1056
  265.4 2.6 collective-permute-done.25
  269.5 3.3 %collective-permute-done.29 = f32[1,1048]{1,0:T(1,128)S(1)} collective-permute-done((f32[1,1048]{1,0:T(1,128)S(1)}, f32[1,1048]{1,0:T(1,128)S(1)}, u32[]{:S(2)}, u32[]{:S(2)}) %collective-permute-start.29) | collective-permute-done | bytes 4224 | tf_op jit(solution)/shard_map/ppermute | solution.py:730
  272.8 2.7 collective-permute-start.30
  277.7 2.9 %collective-permute-start.31 = (bf16[1,4,32,256]{3,2,1,0:T(8,128)(2,1)S(1)}, bf16[1,4,32,256]{3,2,1,0:T(8,128)(2,1)S(1)}, u32[]{:S(2)}, u32[]{:S(2)}) collective-permute-start(bf16[1,4,32,256]{3,2,1,0:T(8,128)(2,1)S(1)} %get-tuple-element.171), channel_id=1, source_target_pairs={{0,8},{1,9},{2,10},{3,11},{4,12},{5,13},{6,14},{7,15},{8,0},{9,1},... | collective-permute-start | bytes 196616 | tf_op jit(solution)/shard_map/ppermute | solution.py:730
  (135 shorter events, 37.0 us)
Async XLA Ops:
  1.5 7.6 %collective-permute-start.2 = (bf16[1,4,32,256]{3,2,1,0:T(8,128)(2,1)S(1)}, bf16[1,4,32,256]{3,2,1,0:T(8,128)(2,1)S(1)}, u32[]{:S(2)}, u32[]{:S(2)}) collective-permute-start(bf16[1,4,32,256]{3,2,1,0:T(8,128)(2,1)S(1)} %maximum_bitcast_fusion), channel_id=1, source_target_pairs={{0,24},{1,25},{2,26},{3,27},{4,28},{5,29},{6,30},{7,31},{8,16},{9,... | collective-permute-start | bytes 196616 | tf_op jit(solution)/shard_map/ppermute | solution.py:730
  6.6 5.6 %collective-permute-start.1 = (bf16[1,4,32,256]{3,2,1,0:T(8,128)(2,1)S(1)}, bf16[1,4,32,256]{3,2,1,0:T(8,128)(2,1)S(1)}, u32[]{:S(2)}, u32[]{:S(2)}) collective-permute-start(bf16[1,4,32,256]{3,2,1,0:T(8,128)(2,1)S(1)} %maximum_bitcast_fusion), channel_id=1, source_target_pairs={{0,16},{1,17},{2,18},{3,19},{4,20},{5,21},{6,22},{7,23},{8,24},{9,... | collective-permute-start | bytes 196616 | tf_op jit(solution)/shard_map/ppermute | solution.py:730
  6.6 5.6 %collective-permute-start = (bf16[1,4,32,256]{3,2,1,0:T(8,128)(2,1)S(1)}, bf16[1,4,32,256]{3,2,1,0:T(8,128)(2,1)S(1)}, u32[]{:S(2)}, u32[]{:S(2)}) collective-permute-start(bf16[1,4,32,256]{3,2,1,0:T(8,128)(2,1)S(1)} %maximum_bitcast_fusion), channel_id=1, source_target_pairs={{0,8},{1,9},{2,10},{3,11},{4,12},{5,13},{6,14},{7,15},{8,0},{9,1},... | collective-permute-start | bytes 196616 | tf_op jit(solution)/shard_map/ppermute | solution.py:730
  12.2 14.7 %collective-permute-start.5 = (bf16[4,4,32,256]{3,2,1,0:T(8,128)(2,1)S(1)}, bf16[4,4,32,256]{3,2,1,0:T(8,128)(2,1)S(1)}, u32[]{:S(2)}, u32[]{:S(2)}) collective-permute-start(bf16[4,4,32,256]{3,2,1,0:T(8,128)(2,1)S(1)} %pad_maximum_fusion), channel_id=1, source_target_pairs={{0,5},{1,4},{2,7},{3,6},{4,1},{5,0},{6,3},{7,2},{8,13},{9,12},{10,... | collective-permute-start | bytes 786440 | tf_op jit(solution)/shard_map/ppermute | solution.py:730
  14.8 12.2 %collective-permute-start.4 = (bf16[4,4,32,256]{3,2,1,0:T(8,128)(2,1)S(1)}, bf16[4,4,32,256]{3,2,1,0:T(8,128)(2,1)S(1)}, u32[]{:S(2)}, u32[]{:S(2)}) collective-permute-start(bf16[4,4,32,256]{3,2,1,0:T(8,128)(2,1)S(1)} %pad_maximum_fusion), channel_id=1, source_target_pairs={{0,1},{1,0},{2,3},{3,2},{4,5},{5,4},{6,7},{7,6},{8,9},{9,8},{10,11... | collective-permute-start | bytes 786440 | tf_op jit(solution)/shard_map/ppermute | solution.py:730
  15.3 11.4 %collective-permute-start.3 = (bf16[4,4,32,256]{3,2,1,0:T(8,128)(2,1)S(1)}, bf16[4,4,32,256]{3,2,1,0:T(8,128)(2,1)S(1)}, u32[]{:S(2)}, u32[]{:S(2)}) collective-permute-start(bf16[4,4,32,256]{3,2,1,0:T(8,128)(2,1)S(1)} %pad_maximum_fusion), channel_id=1, source_target_pairs={{0,4},{1,5},{2,6},{3,7},{4,0},{5,1},{6,2},{7,3},{8,12},{9,13},{10,... | collective-permute-start | bytes 786440 | tf_op jit(solution)/shard_map/ppermute | solution.py:730
  15.8 5.0 %collective-permute-start.6 = (bf16[2,64,512]{2,1,0:T(8,128)(2,1)S(1)}, bf16[2,64,512]{2,1,0:T(8,128)(2,1)S(1)}, u32[]{:S(2)}, u32[]{:S(2)}) collective-permute-start(bf16[2,64,512]{2,1,0:T(8,128)(2,1)S(1)} %pad_maximum_fusion.2), channel_id=1, source_target_pairs={{0,8},{1,9},{2,10},{3,11},{4,12},{5,13},{6,14},{7,15},{8,0},{9,1},... | collective-permute-start | bytes 393224 | tf_op jit(solution)/shard_map/ppermute | solution.py:730
  27.0 7.3 %collective-permute-start.7 = (bf16[16,4,32,256]{3,2,1,0:T(8,128)(2,1)S(1)}, bf16[16,4,32,256]{3,2,1,0:T(8,128)(2,1)S(1)}, u32[]{:S(2)}, u32[]{:S(2)}) collective-permute-start(bf16[16,4,32,256]{3,2,1,0:T(8,128)(2,1)S(1)} %constant_dynamic-update-slice_fusion.own_ref), channel_id=1, source_target_pairs={{0,2},{1,3},{2,0},{3,1},{4,6},{5,7},{6,4},{7,5},{8,10},{9,11},{10,... | collective-permute-start | bytes 3145736 | tf_op jit(solution)/shard_map/ppermute | solution.py:730
  33.3 16.1 %collective-permute-start.8 = (bf16[2,128,512]{2,1,0:T(8,128)(2,1)S(1)}, bf16[2,128,512]{2,1,0:T(8,128)(2,1)S(1)}, u32[]{:S(2)}, u32[]{:S(2)}) collective-permute-start(bf16[2,128,512]{2,1,0:T(8,128)(2,1)S(1)} %pad_maximum_fusion.1), channel_id=1, source_target_pairs={{0,16},{1,17},{2,18},{3,19},{4,20},{5,21},{6,22},{7,23},{8,24},{9,... | collective-permute-start | bytes 786440 | tf_op jit(solution)/shard_map/ppermute | solution.py:730
  45.8 11.1 %collective-permute-start.12 = (bf16[4,96,384]{2,1,0:T(8,128)(2,1)}, bf16[4,96,384]{2,1,0:T(8,128)(2,1)S(1)}, u32[]{:S(2)}, u32[]{:S(2)}) collective-permute-start(bf16[4,96,384]{2,1,0:T(8,128)(2,1)} %get-tuple-element.82), channel_id=1, source_target_pairs={{0,1},{2,3},{4,5},{6,7},{8,9},{10,11},{12,13},{14,15},{16,17},{18,... | collective-permute-start | bytes 884744 | tf_op jit(solution)/shard_map/ppermute | solution.py:756
  50.2 26.0 %collective-permute-start.11 = (bf16[2,256,512]{2,1,0:T(8,128)(2,1)S(1)}, bf16[2,256,512]{2,1,0:T(8,128)(2,1)S(1)}, u32[]{:S(2)}, u32[]{:S(2)}) collective-permute-start(bf16[2,256,512]{2,1,0:T(8,128)(2,1)S(1)} %get-tuple-element.172), channel_id=1, source_target_pairs={{0,5},{1,4},{2,7},{3,6},{4,1},{5,0},{6,3},{7,2},{8,13},{9,12},{10,... | collective-permute-start | bytes 1572872 | tf_op jit(solution)/shard_map/ppermute | solution.py:730
  51.0 27.5 %collective-permute-start.10 = (bf16[2,256,512]{2,1,0:T(8,128)(2,1)S(1)}, bf16[2,256,512]{2,1,0:T(8,128)(2,1)S(1)}, u32[]{:S(2)}, u32[]{:S(2)}) collective-permute-start(bf16[2,256,512]{2,1,0:T(8,128)(2,1)S(1)} %get-tuple-element.172), channel_id=1, source_target_pairs={{0,1},{1,0},{2,3},{3,2},{4,5},{5,4},{6,7},{7,6},{8,9},{9,8},{10,11... | collective-permute-start | bytes 1572872 | tf_op jit(solution)/shard_map/ppermute | solution.py:730
  53.1 25.5 %collective-permute-start.9 = (bf16[2,256,512]{2,1,0:T(8,128)(2,1)S(1)}, bf16[2,256,512]{2,1,0:T(8,128)(2,1)S(1)}, u32[]{:S(2)}, u32[]{:S(2)}) collective-permute-start(bf16[2,256,512]{2,1,0:T(8,128)(2,1)S(1)} %get-tuple-element.172), channel_id=1, source_target_pairs={{0,4},{1,5},{2,6},{3,7},{4,0},{5,1},{6,2},{7,3},{8,12},{9,13},{10,... | collective-permute-start | bytes 1572872 | tf_op jit(solution)/shard_map/ppermute | solution.py:730
  78.7 17.6 %collective-permute-start.13 = (bf16[2,1024,512]{2,1,0:T(8,128)(2,1)S(1)}, bf16[2,1024,512]{2,1,0:T(8,128)(2,1)S(1)}, u32[]{:S(2)}, u32[]{:S(2)}) collective-permute-start(bf16[2,1024,512]{2,1,0:T(8,128)(2,1)S(1)} %constant_dynamic-update-slice_fusion.9.own_ref), channel_id=1, source_target_pairs={{0,2},{1,3},{2,0},{3,1},{4,6},{5,7},{6,4},{7,5},{8,10},{9,11},{10,... | collective-permute-start | bytes 6291464 | tf_op jit(solution)/shard_map/ppermute | solution.py:730
  133.6 12.9 %collective-permute-start.14 = (bf16[4,96,384]{2,1,0:T(8,128)(2,1)}, bf16[4,96,384]{2,1,0:T(8,128)(2,1)S(1)}, u32[]{:S(2)}, u32[]{:S(2)}) collective-permute-start(bf16[4,96,384]{2,1,0:T(8,128)(2,1)} %prologue.1), channel_id=1, source_target_pairs={{1,0},{3,2},{5,4},{7,6},{9,8},{11,10},{13,12},{15,14},{17,16},{19,... | collective-permute-start | bytes 884744 | tf_op jit(solution)/shard_map/ppermute | solution.py:756
  154.7 17.5 %collective-permute-start.15 = (bf16[2,1024,512]{2,1,0:T(8,128)(2,1)}, bf16[2,1024,512]{2,1,0:T(8,128)(2,1)S(1)}, u32[]{:S(2)}, u32[]{:S(2)}) collective-permute-start(bf16[2,1024,512]{2,1,0:T(8,128)(2,1)} %feed_grad.3), channel_id=1, source_target_pairs={{0,2},{1,3},{2,0},{3,1},{4,6},{5,7},{6,4},{7,5},{8,10},{9,11},{10,... | collective-permute-start | bytes 6291464 | tf_op jit(solution)/shard_map/ppermute | solution.py:730
  175.5 38.7 %collective-permute-start.16 = (bf16[2,256,512]{2,1,0:T(8,128)(2,1)S(1)}, bf16[2,256,512]{2,1,0:T(8,128)(2,1)S(1)}, u32[]{:S(2)}, u32[]{:S(2)}) collective-permute-start(bf16[2,256,512]{2,1,0:T(8,128)(2,1)S(1)} %get-tuple-element.158), channel_id=1, source_target_pairs={{0,4},{1,5},{2,6},{3,7},{4,0},{5,1},{6,2},{7,3},{8,12},{9,13},{10,... | collective-permute-start | bytes 1572872 | tf_op jit(solution)/shard_map/ppermute | solution.py:730
  180.4 33.8 %collective-permute-start.18 = (bf16[2,256,512]{2,1,0:T(8,128)(2,1)S(1)}, bf16[2,256,512]{2,1,0:T(8,128)(2,1)S(1)}, u32[]{:S(2)}, u32[]{:S(2)}) collective-permute-start(bf16[2,256,512]{2,1,0:T(8,128)(2,1)S(1)} %get-tuple-element.159), channel_id=1, source_target_pairs={{0,5},{1,4},{2,7},{3,6},{4,1},{5,0},{6,3},{7,2},{8,13},{9,12},{10,... | collective-permute-start | bytes 1572872 | tf_op jit(solution)/shard_map/ppermute | solution.py:730
  183.6 30.6 %collective-permute-start.17 = (bf16[2,256,512]{2,1,0:T(8,128)(2,1)S(1)}, bf16[2,256,512]{2,1,0:T(8,128)(2,1)S(1)}, u32[]{:S(2)}, u32[]{:S(2)}) collective-permute-start(bf16[2,256,512]{2,1,0:T(8,128)(2,1)S(1)} %get-tuple-element.160), channel_id=1, source_target_pairs={{0,1},{1,0},{2,3},{3,2},{4,5},{5,4},{6,7},{7,6},{8,9},{9,8},{10,11... | collective-permute-start | bytes 1572872 | tf_op jit(solution)/shard_map/ppermute | solution.py:730
  214.5 20.7 %collective-permute-start.19 = (bf16[2,64,512]{2,1,0:T(8,128)(2,1)S(1)}, bf16[2,64,512]{2,1,0:T(8,128)(2,1)S(1)}, u32[]{:S(2)}, u32[]{:S(2)}) collective-permute-start(bf16[2,64,512]{2,1,0:T(8,128)(2,1)S(1)} %get-tuple-element.164), channel_id=1, source_target_pairs={{0,8},{1,9},{2,10},{3,11},{4,12},{5,13},{6,14},{7,15},{8,0},{9,1},... | collective-permute-start | bytes 393224 | tf_op jit(solution)/shard_map/ppermute | solution.py:730
  216.4 18.9 %collective-permute-start.21 = (bf16[2,64,512]{2,1,0:T(8,128)(2,1)S(1)}, bf16[2,64,512]{2,1,0:T(8,128)(2,1)S(1)}, u32[]{:S(2)}, u32[]{:S(2)}) collective-permute-start(bf16[2,64,512]{2,1,0:T(8,128)(2,1)S(1)} %get-tuple-element.165), channel_id=1, source_target_pairs={{0,24},{1,25},{2,26},{3,27},{4,28},{5,29},{6,30},{7,31},{8,16},{9,... | collective-permute-start | bytes 393224 | tf_op jit(solution)/shard_map/ppermute | solution.py:730
  216.4 18.9 %collective-permute-start.20 = (bf16[2,64,512]{2,1,0:T(8,128)(2,1)S(1)}, bf16[2,64,512]{2,1,0:T(8,128)(2,1)S(1)}, u32[]{:S(2)}, u32[]{:S(2)}) collective-permute-start(bf16[2,64,512]{2,1,0:T(8,128)(2,1)S(1)} %get-tuple-element.166), channel_id=1, source_target_pairs={{0,16},{1,17},{2,18},{3,19},{4,20},{5,21},{6,22},{7,23},{8,24},{9,... | collective-permute-start | bytes 393224 | tf_op jit(solution)/shard_map/ppermute | solution.py:730
  245.4 7.6 %collective-permute-start.22 = (f32[1,1048]{1,0:T(1,128)S(1)}, f32[1,1048]{1,0:T(1,128)S(1)}, u32[]{:S(2)}, u32[]{:S(2)}) collective-permute-start(f32[1,1048]{1,0:T(1,128)S(1)} %broadcast_in_dim.82), channel_id=1, source_target_pairs={{0,2},{1,3},{2,0},{3,1},{4,6},{5,7},{6,4},{7,5},{8,10},{9,11},{10,... | collective-permute-start | bytes 12584 | tf_op jit(solution)/shard_map/ppermute | solution.py:730
  249.3 18.7 %collective-permute-start.28 = (bf16[4,4,32,256]{3,2,1,0:T(8,128)(2,1)S(1)}, bf16[4,4,32,256]{3,2,1,0:T(8,128)(2,1)S(1)}, u32[]{:S(2)}, u32[]{:S(2)}) collective-permute-start(bf16[4,4,32,256]{3,2,1,0:T(8,128)(2,1)S(1)} %get-tuple-element.161), channel_id=1, source_target_pairs={{0,5},{1,4},{2,7},{3,6},{4,1},{5,0},{6,3},{7,2},{8,13},{9,12},{10,... | collective-permute-start | bytes 786440 | tf_op jit(solution)/shard_map/ppermute | solution.py:730
  252.3 15.7 %collective-permute-start.27 = (bf16[4,4,32,256]{3,2,1,0:T(8,128)(2,1)S(1)}, bf16[4,4,32,256]{3,2,1,0:T(8,128)(2,1)S(1)}, u32[]{:S(2)}, u32[]{:S(2)}) collective-permute-start(bf16[4,4,32,256]{3,2,1,0:T(8,128)(2,1)S(1)} %get-tuple-element.162), channel_id=1, source_target_pairs={{0,1},{1,0},{2,3},{3,2},{4,5},{5,4},{6,7},{7,6},{8,9},{9,8},{10,11... | collective-permute-start | bytes 786440 | tf_op jit(solution)/shard_map/ppermute | solution.py:730
  252.3 15.7 %collective-permute-start.26 = (bf16[4,4,32,256]{3,2,1,0:T(8,128)(2,1)S(1)}, bf16[4,4,32,256]{3,2,1,0:T(8,128)(2,1)S(1)}, u32[]{:S(2)}, u32[]{:S(2)}) collective-permute-start(bf16[4,4,32,256]{3,2,1,0:T(8,128)(2,1)S(1)} %get-tuple-element.163), channel_id=1, source_target_pairs={{0,4},{1,5},{2,6},{3,7},{4,0},{5,1},{6,2},{7,3},{8,12},{9,13},{10,... | collective-permute-start | bytes 786440 | tf_op jit(solution)/shard_map/ppermute | solution.py:730
  253.0 11.4 %collective-permute-start.24 = (f32[1,1048]{1,0:T(1,128)S(1)}, f32[1,1048]{1,0:T(1,128)S(1)}, u32[]{:S(2)}, u32[]{:S(2)}) collective-permute-start(f32[1,1048]{1,0:T(1,128)S(1)} %reshape_add_fusion), channel_id=1, source_target_pairs={{0,1},{1,0},{2,3},{3,2},{4,5},{5,4},{6,7},{7,6},{8,9},{9,8},{10,11... | collective-permute-start | bytes 12584 | tf_op jit(solution)/shard_map/ppermute | solution.py:730
  268.2 4.6 %collective-permute-start.29 = (f32[1,1048]{1,0:T(1,128)S(1)}, f32[1,1048]{1,0:T(1,128)S(1)}, u32[]{:S(2)}, u32[]{:S(2)}) collective-permute-start(f32[1,1048]{1,0:T(1,128)S(1)} %add.91), channel_id=1, source_target_pairs={{0,16},{1,17},{2,18},{3,19},{4,20},{5,21},{6,22},{7,23},{8,24},{9,... | collective-permute-start | bytes 12584 | tf_op jit(solution)/shard_map/ppermute | solution.py:730
  272.8 7.8 %collective-permute-start.30 = (f32[1,1048]{1,0:T(1,128)S(1)}, f32[1,1048]{1,0:T(1,128)S(1)}, u32[]{:S(2)}, u32[]{:S(2)}) collective-permute-start(f32[1,1048]{1,0:T(1,128)S(1)} %add.95), channel_id=1, source_target_pairs={{0,8},{1,9},{2,10},{3,11},{4,12},{5,13},{6,14},{7,15},{8,0},{9,1},... | collective-permute-start | bytes 12584 | tf_op jit(solution)/shard_map/ppermute | solution.py:730
  276.2 6.1 %collective-permute-start.33 = (bf16[1,4,32,256]{3,2,1,0:T(8,128)(2,1)S(1)}, bf16[1,4,32,256]{3,2,1,0:T(8,128)(2,1)S(1)}, u32[]{:S(2)}, u32[]{:S(2)}) collective-permute-start(bf16[1,4,32,256]{3,2,1,0:T(8,128)(2,1)S(1)} %get-tuple-element.169), channel_id=1, source_target_pairs={{0,24},{1,25},{2,26},{3,27},{4,28},{5,29},{6,30},{7,31},{8,16},{9,... | collective-permute-start | bytes 196616 | tf_op jit(solution)/shard_map/ppermute | solution.py:730
  276.2 6.1 %collective-permute-start.32 = (bf16[1,4,32,256]{3,2,1,0:T(8,128)(2,1)S(1)}, bf16[1,4,32,256]{3,2,1,0:T(8,128)(2,1)S(1)}, u32[]{:S(2)}, u32[]{:S(2)}) collective-permute-start(bf16[1,4,32,256]{3,2,1,0:T(8,128)(2,1)S(1)} %get-tuple-element.170), channel_id=1, source_target_pairs={{0,16},{1,17},{2,18},{3,19},{4,20},{5,21},{6,22},{7,23},{8,24},{9,... | collective-permute-start | bytes 196616 | tf_op jit(solution)/shard_map/ppermute | solution.py:730
  277.7 5.3 %collective-permute-start.31 = (bf16[1,4,32,256]{3,2,1,0:T(8,128)(2,1)S(1)}, bf16[1,4,32,256]{3,2,1,0:T(8,128)(2,1)S(1)}, u32[]{:S(2)}, u32[]{:S(2)}) collective-permute-start(bf16[1,4,32,256]{3,2,1,0:T(8,128)(2,1)S(1)} %get-tuple-element.171), channel_id=1, source_target_pairs={{0,8},{1,9},{2,10},{3,11},{4,12},{5,13},{6,14},{7,15},{8,0},{9,1},... | collective-permute-start | bytes 196616 | tf_op jit(solution)/shard_map/ppermute | solution.py:730
  (16 other events, 154.4 us)

commit v6 on v5

--- a/solution.py
+++ b/solution.py
@@ -80,8 +80,11 @@
     return near, far, start < floor, row, floor, first
 
 
-def near_weights(query, key_heads, near):
-    scores = mm(query, key_heads, NT) * (HEAD_DIM**-0.5)
+def near_scores(query, key_heads):
+    return mm(query * jnp.asarray(HEAD_DIM**-0.5, BF16), key_heads, NT)
+
+
+def near_weights(scores, near):
     parts = []
     for h in range(2):
         part = jnp.where(near, scores[:, h * WIN : (h + 1) * WIN], NEG)
@@ -90,12 +93,11 @@
 
 
 def spread(product):
-    high = product.astype(BF16)
-    low = (product - high.astype(F32)).astype(BF16)
-    table = (
-        ((iota((2 * PAIR, 2 * WIN), 0) % PAIR) < HEAD_DIM) == (iota((2 * PAIR, 2 * WIN), 1) < WIN)
-    ).astype(F32)
-    return mm(jnp.concatenate([high, low], axis=1), table.astype(BF16))
+    first = iota(product.shape, 1) < HEAD_DIM
+    sums = [
+        jnp.sum(jnp.where(keep, product, 0.0), axis=1, keepdims=True) for keep in (first, ~first)
+    ]
+    return jnp.concatenate([jnp.broadcast_to(part, (ROWS, WIN)) for part in sums], axis=1)
 
 
 def load_keys(qkv_ref, message_ref, keys, values):
@@ -268,24 +270,34 @@
         bend_k = jnp.tanh(key_f)
         ones = jnp.ones((WIN, PAIR), BF16)
         value_heads = jnp.concatenate([split_heads(value), split_heads(ones)], axis=1)
-        weights = near_weights(query, split_heads(key), near_mask).astype(BF16)
-        near_out = mm(weights, value_heads)
-        inv_l = 1.0 / near_out[:, PAIR:]
-        near = near_out[:, :PAIR] * inv_l
         before = state[...]
         before_low = before.astype(BF16)
+        scores = near_scores(query, split_heads(key))
+        pair_weight = mm(lift_q, split_heads(lift_k.astype(BF16)), NT)
+        pair_bend = mm(bend_q, split_heads(bend_k.astype(BF16)), NT)
+        elu_state = mm(lift_q, before_low[:, : 2 * PAIR])
+        tanh_state = mm(bend_q, before_low[:, 2 * PAIR :])
         states_ref[0, pl.ds(pl.multiple_of(step * PAIR, PAIR), PAIR), :] = before_low
+        closing = scalars[step]
+        live = iota((ROWS, PAIR), 0) + first >= jnp.maximum(closing, floor)
+        lifted = jnp.where(live, lift_k[:ROWS], 0.0).astype(BF16)
+        bent = jnp.where(live, bend_k[:ROWS], 0.0).astype(BF16)
+        with_ones = jnp.concatenate([value[:ROWS], ones[:ROWS]], axis=1)
+        added = jnp.concatenate([mm(lifted, with_ones, TN), mm(bent, value[:ROWS], TN)], axis=1)
+        keep = (closing < floor).astype(F32)
+        state[...] = keep * before + block_only(added)
         far_two = two(far_mask)
-        pair_weight = jnp.where(far_two, mm(lift_q, split_heads(lift_k.astype(BF16)), NT), 0.0)
-        elu_out = mm(pair_weight.astype(BF16), value_heads)
-        elu_state = mm(lift_q, before_low[:, : 2 * PAIR])
+        pair_weight = jnp.where(far_two, pair_weight, 0.0).astype(BF16)
+        pair_bend = jnp.where(far_two, pair_bend, 0.0).astype(BF16)
+        elu_out = mm(pair_weight, value_heads)
+        tanh_out = mm(pair_bend, value_heads[:, :PAIR]) + jnp.where(carried, tanh_state, 0.0)
+        weights = near_weights(scores, near_mask).astype(BF16)
+        near_out = mm(weights, value_heads)
         numerator = elu_out[:, :PAIR] + jnp.where(carried, elu_state[:, :PAIR], 0.0)
         inv_d = 1.0 / (elu_out[:, PAIR:] + jnp.where(carried, elu_state[:, PAIR:], 0.0))
         far1 = numerator * inv_d
-        pair_bend = jnp.where(far_two, mm(bend_q, split_heads(bend_k.astype(BF16)), NT), 0.0)
-        tanh_out = mm(pair_bend.astype(BF16), value_heads[:, :PAIR]) + jnp.where(
-            carried, mm(bend_q, before_low[:, 2 * PAIR :]), 0.0
-        )
+        inv_l = 1.0 / near_out[:, PAIR:]
+        near = near_out[:, :PAIR] * inv_l
         far2 = tanh_out / (row - start + 1).astype(F32)
         mixed = jnp.where(row < count_valid, b0 * near + b1 * far1 + b2 * far2, 0.0)
         att_ref[pl.ds(at, ROWS), :] = mixed.astype(BF16)
@@ -294,25 +306,14 @@
         far2_ref[pl.ds(at, ROWS), :] = far2
         invl_ref[pl.ds(at, ROWS), :] = inv_l
         invd_ref[pl.ds(at, ROWS), :] = inv_d
-        closing = scalars[step]
-        live = iota((ROWS, PAIR), 0) + first >= jnp.maximum(closing, floor)
-        lifted = jnp.where(live, lift_k[:ROWS], 0.0).astype(BF16)
-        bent = jnp.where(live, bend_k[:ROWS], 0.0).astype(BF16)
-        with_ones = jnp.concatenate([value[:ROWS], ones[:ROWS]], axis=1)
-        added = jnp.concatenate([mm(lifted, with_ones, TN), mm(bent, value[:ROWS], TN)], axis=1)
-        keep = (closing < floor).astype(F32)
-        state[...] = keep * before + block_only(added)
         return carry
 
     lax.fori_loop(0, rows // ROWS, body, 0, unroll=4)
 
 
-def near_back(query, key_heads, grad_pair, near_mask, spread_near, scale_q, rows_q, rows_g):
-    weights = near_weights(query, key_heads, near_mask)
-    shifted = (weights * (grad_pair - spread_near)).astype(BF16)
-    d_query = mm(shifted, key_heads) * scale_q
-    d_key = fold(mm(shifted, rows_q, TN))
-    return weights.astype(BF16), d_query, d_key
+def near_back(scores, grad_pair, near_mask, spread_near):
+    weights = near_weights(scores, near_mask)
+    return weights.astype(BF16), (weights * (grad_pair - spread_near)).astype(BF16)
 
 
 def prologue_kernel(
@@ -348,16 +349,13 @@
     scale = b0 * invl_ref[...]
     rows_q = (query.astype(F32) * (scale * HEAD_DIM**-0.5)).astype(BF16)
     rows_g = (grad_f * scale).astype(BF16)
-    weights, _, d_key = near_back(
-        query,
-        split_heads(key),
+    weights, shifted = near_back(
+        near_scores(query, split_heads(key)),
         mm(grad, split_heads(value), NT),
         near_mask,
         spread(grad_f * near_ref[...]),
-        scale * HEAD_DIM**-0.5,
-        rows_q,
-        rows_g,
     )
+    d_key = fold(mm(shifted, rows_q, TN))
     back_ref[0, pl.ds(HEAD_DIM, TAIL), :] = jnp.concatenate(
         [d_key[:TAIL], fold(mm(weights, rows_g, TN))[:TAIL], jnp.zeros((TAIL, PAIR), F32)], axis=1
     ).astype(BF16)
@@ -473,33 +471,43 @@
         r0 = b0 * invl_ref[pl.ds(at, ROWS), :]
         r1 = b1 * invd_ref[pl.ds(at, ROWS), :]
         r2 = b2 / (row - start + 1).astype(F32)
+        key_heads = split_heads(key)
+        before = states_ref[0, pl.ds(pl.multiple_of(step * PAIR, PAIR), PAIR), :]
+        near_product = grad_f * near_ref[pl.ds(at, ROWS), :]
+        far1_product = grad_f * far1_ref[pl.ds(at, ROWS), :]
         grad_pair = mm(grad, split_heads(value), NT)
+        scores = near_scores(query, key_heads)
+        pair_weight = mm(lift_q, lift_heads, NT)
+        pair_bend = mm(bend_q, bend_heads, NT)
+        state_bend = mm(grad, before[:, 2 * PAIR :], NT)
+        spread_far = spread(far1_product)
+        spread_near = spread(near_product)
+        along = jnp.where(lanes, spread_far[:, :WIN], spread_far[:, WIN:])
+        scaled_along = (along * (-1.0 / HEAD_DIM)).astype(BF16)
+        state_lift = mm(jnp.concatenate([grad, scaled_along], axis=1), before[:, : 2 * PAIR], NT)
+        after = adjoint[...]
+        parts = key_side(after.astype(BF16), lift_k[:ROWS], bend_k[:ROWS], value[:ROWS])
         rows_q = (query_f * (r0 * HEAD_DIM**-0.5)).astype(BF16)
-        near_product = grad_f * near_ref[pl.ds(at, ROWS), :]
-        weights, d_query, d_key = near_back(
-            query,
-            split_heads(key),
-            grad_pair,
-            near_mask,
-            spread(near_product),
-            r0 * HEAD_DIM**-0.5,
-            rows_q,
-            None,
+        rows_a = lift_qf * r1
+        rows_t = bend_qf * r2
+        from_lift = mm(
+            jnp.where(carried, rows_a, 0.0).astype(BF16),
+            jnp.concatenate([grad, along.astype(BF16)], axis=1),
+            TN,
         )
-        far1_product = grad_f * far1_ref[pl.ds(at, ROWS), :]
+        from_bend = mm(jnp.where(carried, rows_t, 0.0).astype(BF16), grad, TN)
+        closing = scalars[step]
+        keep = (closing < floor).astype(F32)
+        adjoint[...] = keep * after + block_only(jnp.concatenate([from_lift, from_bend], axis=1))
         add_up(0, near_product)
         add_up(8, far1_product)
         add_up(16, grad_f * far2_ref[pl.ds(at, ROWS), :])
-        spread_far = spread(far1_product)
-        along = jnp.where(lanes, spread_far[:, :WIN], spread_far[:, WIN:])
         shifted = jnp.where(far_two, grad_pair - spread_far, 0.0).astype(BF16)
         plain = jnp.where(far_two, grad_pair, 0.0).astype(BF16)
-        pair_weight = jnp.where(far_two, mm(lift_q, lift_heads, NT), 0.0).astype(BF16)
-        pair_bend = jnp.where(far_two, mm(bend_q, bend_heads, NT), 0.0).astype(BF16)
-        before = states_ref[0, pl.ds(pl.multiple_of(step * PAIR, PAIR), PAIR), :]
-        scaled_along = (along * (-1.0 / HEAD_DIM)).astype(BF16)
-        state_lift = mm(jnp.concatenate([grad, scaled_along], axis=1), before[:, : 2 * PAIR], NT)
-        state_bend = mm(grad, before[:, 2 * PAIR :], NT)
+        pair_weight = jnp.where(far_two, pair_weight, 0.0).astype(BF16)
+        pair_bend = jnp.where(far_two, pair_bend, 0.0).astype(BF16)
+        weights, shifted_near = near_back(scores, grad_pair, near_mask, spread_near)
+        d_query = mm(shifted_near, key_heads) * (r0 * HEAD_DIM**-0.5)
         d_query = (
             d_query
             + (mm(shifted, lift_heads) + jnp.where(carried, state_lift, 0.0))
@@ -508,8 +516,7 @@
             * (r2 * (1.0 - bend_qf * bend_qf))
         )
         out_ref[0, pl.ds(at, ROWS), :] = d_query.astype(BF16)
-        rows_a = lift_qf * r1
-        rows_t = bend_qf * r2
+        d_key = fold(mm(shifted_near, rows_q, TN))
         d_lift = fold(mm(shifted, rows_a.astype(BF16), TN))
         d_bend = fold(mm(plain, rows_t.astype(BF16), TN))
         d_value = fold(
@@ -519,9 +526,6 @@
                 TN,
             )
         )
-        after = adjoint[...]
-        parts = key_side(after.astype(BF16), lift_k[:ROWS], bend_k[:ROWS], value[:ROWS])
-        closing = scalars[step]
         live = iota((ROWS, PAIR), 0) + first >= jnp.maximum(closing, floor)
         pad = jnp.zeros((TAIL, PAIR), F32)
         d_lift = d_lift + jnp.concatenate([jnp.where(live, parts[0], 0.0), pad], axis=0)
@@ -536,14 +540,6 @@
         ).astype(BF16)
         key_carry[...] = d_key[:TAIL]
         value_carry[...] = d_value[:TAIL]
-        from_lift = mm(
-            jnp.where(carried, rows_a, 0.0).astype(BF16),
-            jnp.concatenate([grad, along.astype(BF16)], axis=1),
-            TN,
-        )
-        from_bend = mm(jnp.where(carried, rows_t, 0.0).astype(BF16), grad, TN)
-        keep = (closing < floor).astype(F32)
-        adjoint[...] = keep * after + block_only(jnp.concatenate([from_lift, from_bend], axis=1))
         return carry
 
     lax.fori_loop(0, steps, body, 0, unroll=4)

time: 285 us -> 266 us (0.933)
  Pallas kernels: 183 us -> 160 us
    pallas_call x3, Pallas kernels: 64.1 us -> 49 us  [per_device(): call(backward_kernel, [spec['qkv'], spec['message'], spec['start'], spec[...]
    pallas_call x2, Pallas kernels: 35.6 us -> 27.3 us  [per_device(): call(functools.partial(resume, forward_kernel, len(results)), [spec['qkv'...]
  transfers between devices with their start and end apart: 34 -> 34, of which waited for: 14 -> 14; matrix products, arithmetic and copies ran while one was open for 6% -> 6% of each run, Pallas kernels for 46% -> 40%
where the time goes in v6:
time: 266 us
  Pallas kernels  160 us (60%)
  starting transfers between devices  49.2 us (18%)
  waiting for transfers between devices  29.9 us (11%)
  local copies, waits for them, and re-layouts  14.2 us (5%)
  other arithmetic  10.8 us (4%)
    pallas_call x3, Pallas kernels, per_device(): call(backward_kernel, [spec['qkv'], spec['message'], spec['start'], spec[...  49 us
    ppermute x32, starting transfers between devices, peer(): return lax.ppermute(array, ('dp', 'head'), pairs)  44.1 us
    pallas_call x1, Pallas kernels, per_device(): call(feed_kernel, [row_spec] * 3 + [whole_spec((width, width)), whole_spe...  28.1 us
    pallas_call x2, Pallas kernels, per_device(): call(functools.partial(resume, forward_kernel, len(results)), [spec['qkv'...  27.3 us
    ppermute x32, waiting for transfers between devices, peer(): return lax.ppermute(array, ('dp', 'head'), pairs)  26.9 us
    pallas_call x2, Pallas kernels, feed_grad(): call(feed_grad_kernel, [whole_rows] * 2 + [columns] * 2 + more_in_specs,...  19 us
    pallas_call x1, Pallas kernels, per_device(): call(functools.partial(project_kernel, flips=flips), [pl.BlockSpec((part,...  10.6 us
    pallas_call x1, Pallas kernels, per_device(): call(functools.partial(weight_grad_kernel, flips=flips), [whole_spec((row...  9.12 us
  transfers between devices with their start and end apart: 34, of which 14 were waited for; matrix products, arithmetic and copies ran while one was open for 6% of the time, Pallas kernels for 40%

profile of v6, /device:TPU:0, one launch (start us, length us, event | category | flops | bytes accessed | tf_op | source)
XLA Modules:
  0.0 265.5 jit_solution(2929353280129069311)
XLA Ops:
  1.5 5.1 %collective-permute-start.2 = (bf16[1,4,32,256]{3,2,1,0:T(8,128)(2,1)S(1)}, bf16[1,4,32,256]{3,2,1,0:T(8,128)(2,1)S(1)}, u32[]{:S(2)}, u32[]{:S(2)}) collective-permute-start(bf16[1,4,32,256]{3,2,1,0:T(8,128)(2,1)S(1)} %maximum_bitcast_fusion), channel_id=1, source_target_pairs={{0,24},{1,25},{2,26},{3,27},{4,28},{5,29},{6,30},{7,31},{8,16},{9,... | collective-permute-start | bytes 196616 | tf_op jit(solution)/shard_map/ppermute | solution.py:726
  9.1 3.1 %collective-permute-done.1 = bf16[1,4,32,256]{3,2,1,0:T(8,128)(2,1)S(1)} collective-permute-done((bf16[1,4,32,256]{3,2,1,0:T(8,128)(2,1)S(1)}, bf16[1,4,32,256]{3,2,1,0:T(8,128)(2,1)S(1)}, u32[]{:S(2)}, u32[]{:S(2)}) %collective-permute-start.1) | collective-permute-done | bytes 65568 | tf_op jit(solution)/shard_map/ppermute | solution.py:726
  12.2 2.5 collective-permute-start.5
  16.9 3.9 %collective-permute-done.6 = bf16[2,64,512]{2,1,0:T(8,128)(2,1)S(1)} collective-permute-done((bf16[2,64,512]{2,1,0:T(8,128)(2,1)S(1)}, bf16[2,64,512]{2,1,0:T(8,128)(2,1)S(1)}, u32[]{:S(2)}, u32[]{:S(2)}) %collective-permute-start.6) | collective-permute-done | bytes 131104 | tf_op jit(solution)/shard_map/ppermute | solution.py:726
  20.8 5.9 %collective-permute-done.3 = bf16[4,4,32,256]{3,2,1,0:T(8,128)(2,1)S(1)} collective-permute-done((bf16[4,4,32,256]{3,2,1,0:T(8,128)(2,1)S(1)}, bf16[4,4,32,256]{3,2,1,0:T(8,128)(2,1)S(1)}, u32[]{:S(2)}, u32[]{:S(2)}) %collective-permute-start.3) | collective-permute-done | bytes 262176 | tf_op jit(solution)/shard_map/ppermute | solution.py:726
  35.2 10.6 %project.1 = (bf16[3,1536,512]{2,1,0:T(8,128)(2,1)}, bf16[1536,512]{1,0:T(8,128)(2,1)}, bf16[3,512,512]{2,1,0:T(8,128)(2,1)}, bf16[512,512]{1,0:T(8,128)(2,1)}, bf16[4,96,384]{2,1,0:T(8,128)(2,1)}) custom-call(s32[21]{0:T(128)} %concatenate.29.scalars, bf16[1536,512]{1,0:T(8,128)(2,1)} %tokens_ref.5, f32[1,512]{1,0:T(1,128)} %bitcast.34, ...), custom_call_target="tpu_custom_call" | custom-call | flops 2415919104 | bytes 9437184 | tf_op jit(solution)/shard_map/project/pallas_call | solution.py:828
  45.8 3.6 %collective-permute-start.12 = (bf16[4,96,384]{2,1,0:T(8,128)(2,1)}, bf16[4,96,384]{2,1,0:T(8,128)(2,1)S(1)}, u32[]{:S(2)}, u32[]{:S(2)}) collective-permute-start(bf16[4,96,384]{2,1,0:T(8,128)(2,1)} %get-tuple-element.82), channel_id=1, source_target_pairs={{0,1},{2,3},{4,5},{6,7},{8,9},{10,11},{12,13},{14,15},{16,17},{18,... | collective-permute-start | bytes 884744 | tf_op jit(solution)/shard_map/ppermute | solution.py:752
  51.0 2.1 collective-permute-start.10
  54.4 2.5 collective-permute-done.12.message_ref
  58.1 13.9 %forward.2 = (bf16[1536,512]{1,0:T(8,128)(2,1)}, f32[1536,512]{1,0:T(8,128)}, f32[1536,512]{1,0:T(8,128)}, f32[1536,512]{1,0:T(8,128)}, f32[1536,512]{1,0:T(8,12...) custom-call(s32[21]{0:T(128)} %concatenate.29.scalars, ...), custom_call_target="tpu_custom_call" | custom-call | flops 3145728000 | bytes 15728640 | tf_op jit(solution)/shard_map/forward/pallas_call | solution.py:870
  72.0 6.6 %collective-permute-done.10 = bf16[2,256,512]{2,1,0:T(8,128)(2,1)S(1)} collective-permute-done((bf16[2,256,512]{2,1,0:T(8,128)(2,1)S(1)}, bf16[2,256,512]{2,1,0:T(8,128)(2,1)S(1)}, u32[]{:S(2)}, u32[]{:S(2)}) %collective-permute-start.10) | collective-permute-done | bytes 524320 | tf_op jit(solution)/shard_map/ppermute | solution.py:726
  78.8 13.4 %forward.3 = (bf16[1536,512]{1,0:T(8,128)(2,1)}, f32[1536,512]{1,0:T(8,128)}, f32[1536,512]{1,0:T(8,128)}, f32[1536,512]{1,0:T(8,128)}, f32[1536,512]{1,0:T(8,12...) custom-call(s32[21]{0:T(128)} %concatenate.29.scalars, ...), custom_call_target="tpu_custom_call", output_to_operand_aliasing={{0}: (5, {}), {1}: (6, {}), {2}: (7, {}), {3}: (8, {}), {4}... | custom-call | flops 3145728000 | bytes 15728640 | tf_op jit(solution)/shard_map/forward/pallas_call | solution.py:870
  93.5 28.1 %feed.1 = (bf16[1536,512]{1,0:T(8,128)(2,1)}, f32[1536,512]{1,0:T(8,128)}, bf16[1536,512]{1,0:T(8,128)(2,1)}, bf16[1536,512]{1,0:T(8,128)(2,1)}, bf16[1536,512]{...) custom-call(s32[21]{0:T(128)} %concatenate.29.scalars, ...), custom_call_target="tpu_custom_call" | custom-call | flops 12884901888 | bytes 25165824 | tf_op jit(solution)/shard_map/feed/pallas_call | solution.py:898
  121.6 7.7 %prologue.1 = bf16[4,96,384]{2,1,0:T(8,128)(2,1)} custom-call(s32[21]{0:T(128)} %concatenate.29.scalars, bf16[3,1536,512]{2,1,0:T(8,128)(2,1)} %get-tuple-element.80.qkv_ref.query_ref.key_ref.value_ref, bf16[3,1536,512]{2,1,0:T(8,128)(2,1)} %get-tuple-element.80.qkv_ref.query_ref.key_ref.value_ref, ...), custom_call_target="tpu_custom_call" | custom-call | flops 393216000 | bytes 15728640 | tf_op jit(solution)/shard_map/prologue/pallas_call | solution.py:916
  130.8 10.8 %feed_grad.2 = (f32[512,512]{1,0:T(8,128)}, f32[2,1024,512]{2,1,0:T(8,128)}) custom-call(s32[21]{0:T(128)} %concatenate.29.scalars, bf16[1536,512]{1,0:T(8,128)(2,1)} %get-tuple-element.107.normed_ref, bf16[1536,512]{1,0:T(8,128)(2,1)} %cotangent_ref.5, bf16[1536,2048]{1,0:T(8,128)(2,1)} %get-tuple-element.108.active_ref, ...), custom_call_target="tpu_custom_call" | custom-call | flops 3221225472 | bytes 9437184 | tf_op jit(solution)/shard_map/feed_grad/pallas_call | solution.py:948
  142.1 8.2 %feed_grad.3 = bf16[2,1024,512]{2,1,0:T(8,128)(2,1)} custom-call(s32[21]{0:T(128)} %concatenate.29.scalars, bf16[1536,512]{1,0:T(8,128)(2,1)} %get-tuple-element.107.normed_ref, bf16[1536,512]{1,0:T(8,128)(2,1)} %cotangent_ref.5, bf16[1536,2048]{1,0:T(8,128)(2,1)} %get-tuple-element.108.active_ref, bf16[1536,2048]{1,0:T(8,128)(2,1)} %get-tuple-element.119.d_inner_ref), custom_call_target="tpu_custom_call" | custom-call | flops 3221225472 | bytes 9437184 | tf_op jit(solution)/shard_map/feed_grad/pallas_call | solution.py:948
  152.5 13.2 %backward.3 = (bf16[3,1536,512]{2,1,0:T(8,128)(2,1)}, f32[24,128]{1,0:T(8,128)}) custom-call(s32[21]{0:T(128)} %concatenate.29.scalars, bf16[3,1536,512]{2,1,0:T(8,128)(2,1)} %get-tuple-element.80.qkv_ref.query_ref.key_ref.value_ref, bf16[4,96,384]{2,1,0:T(8,128)(2,1)} %copy-done, s32[1536,128]{1,0:T(8,128)} %broadcast_in_dim.78.start_ref, ...), custom_call_target="tpu_custom_call" | custom-call | flops 3145728000 | bytes 7864320 | tf_op jit(solution)/shard_map/backward/pallas_call | solution.py:980
  165.7 3.1 %fusion.6 = (bf16[2,1024,512]{2,1,0:T(8,128)(2,1)S(1)}, f32[2,1024,512]{2,1,0:T(8,128)S(1)}) fusion(f32[2,1024,512]{2,1,0:T(8,128)} %get-tuple-element.117, bf16[2,1024,512]{2,1,0:T(8,128)(2,1)S(1)} %collective-permute-done.15), kind=kLoop, calls=%fused_computation.47 | loop fusion | flops 3145728 | bytes 12582912 | tf_op jit(solution)/shard_map/convert.11
  169.0 7.0 %collective-permute-start.18 = (bf16[2,256,512]{2,1,0:T(8,128)(2,1)S(1)}, bf16[2,256,512]{2,1,0:T(8,128)(2,1)S(1)}, u32[]{:S(2)}, u32[]{:S(2)}) collective-permute-start(bf16[2,256,512]{2,1,0:T(8,128)(2,1)S(1)} %get-tuple-element.159), channel_id=1, source_target_pairs={{0,5},{1,4},{2,7},{3,6},{4,1},{5,0},{6,3},{7,2},{8,13},{9,12},{10,... | collective-permute-start | bytes 1572872 | tf_op jit(solution)/shard_map/ppermute | solution.py:726
  176.0 22.6 %backward.4 = (bf16[3,1536,512]{2,1,0:T(8,128)(2,1)}, f32[24,256]{1,0:T(8,128)}) custom-call(s32[21]{0:T(128)} %concatenate.29.scalars, bf16[3,1536,512]{2,1,0:T(8,128)(2,1)} %get-tuple-element.80.qkv_ref.query_ref.key_ref.value_ref, bf16[4,96,384]{2,1,0:T(8,128)(2,1)} %copy-done, ...), custom_call_target="tpu_custom_call", output_to_operand_aliasing={{0}: (13, {})} | custom-call | flops 6291456000 | bytes 15728640 | tf_op jit(solution)/shard_map/backward/pallas_call | solution.py:980
  199.0 2.3 collective-permute-start.19
  201.3 2.3 collective-permute-start.21
  203.6 13.2 %backward.5 = (bf16[3,1536,512]{2,1,0:T(8,128)(2,1)}, f32[24,128]{1,0:T(8,128)}) custom-call(s32[21]{0:T(128)} %concatenate.29.scalars, bf16[3,1536,512]{2,1,0:T(8,128)(2,1)} %get-tuple-element.80.qkv_ref.query_ref.key_ref.value_ref, bf16[4,96,384]{2,1,0:T(8,128)(2,1)} %copy-done, ...), custom_call_target="tpu_custom_call", output_to_operand_aliasing={{0}: (13, {})} | custom-call | flops 3145728000 | bytes 7864320 | tf_op jit(solution)/shard_map/backward/pallas_call | solution.py:980
  217.0 9.1 %weight_grad.1 = (f32[16,4,32,256]{3,2,1,0:T(8,128)}, bf16[16,4,32,256]{3,2,1,0:T(8,128)(2,1)}, f32[8,512]{1,0:T(8,128)}) custom-call(s32[21]{0:T(128)} %concatenate.29.scalars, bf16[1536,512]{1,0:T(8,128)(2,1)} %get-tuple-element.106.normed_ref, bf16[3,1536,512]{2,1,0:T(8,128)(2,1)} %get-tuple-element.138.d_qkv_ref, ...), custom_call_target="tpu_custom_call" | custom-call | flops 2415919104 | bytes 6291456 | tf_op jit(solution)/shard_map/weight_grad/pallas_call | solution.py:1025
  229.0 2.1 fusion.4
  231.2 2.7 %collective-permute-start.28 = (bf16[4,4,32,256]{3,2,1,0:T(8,128)(2,1)S(1)}, bf16[4,4,32,256]{3,2,1,0:T(8,128)(2,1)S(1)}, u32[]{:S(2)}, u32[]{:S(2)}) collective-permute-start(bf16[4,4,32,256]{3,2,1,0:T(8,128)(2,1)S(1)} %get-tuple-element.161), channel_id=1, source_target_pairs={{0,5},{1,4},{2,7},{3,6},{4,1},{5,0},{6,3},{7,2},{8,13},{9,12},{10,... | collective-permute-start | bytes 786440 | tf_op jit(solution)/shard_map/ppermute | solution.py:726
  236.4 8.9 %input.1 = f32[1536,512]{1,0:T(8,128)} custom-call(s32[21]{0:T(128)} %concatenate.29.scalars, bf16[3,1536,512]{2,1,0:T(8,128)(2,1)} %get-tuple-element.138.d_qkv_ref, bf16[3,512,512]{2,1,0:T(8,128)(2,1)} %get-tuple-element.130.weight_ref, bf16[1536,512]{1,0:T(8,128)(2,1)} %tokens_ref.5, f32[1536,512]{1,0:T(8,128)} %get-tuple-element.139.d_hidden_ref, ...), custom_call_target="tpu_custom_call" | custom-call | flops 2415919104 | bytes 18874368 | tf_op jit(solution)/shard_map/input/pallas_call | solution.py:1052
  247.0 2.2 collective-permute-done.25
  249.4 3.0 %collective-permute-start.29 = (f32[1,1048]{1,0:T(1,128)S(1)}, f32[1,1048]{1,0:T(1,128)S(1)}, u32[]{:S(2)}, u32[]{:S(2)}) collective-permute-start(f32[1,1048]{1,0:T(1,128)S(1)} %add.91), channel_id=1, source_target_pairs={{0,16},{1,17},{2,18},{3,19},{4,20},{5,21},{6,22},{7,23},{8,24},{9,... | collective-permute-start | bytes 12584 | tf_op jit(solution)/shard_map/ppermute | solution.py:726
  254.0 2.1 collective-permute-start.30
  256.7 2.3 collective-permute-start.33
  259.1 2.1 collective-permute-start.31
  (135 shorter events, 37.7 us)
Async XLA Ops:
  1.5 7.6 %collective-permute-start.2 = (bf16[1,4,32,256]{3,2,1,0:T(8,128)(2,1)S(1)}, bf16[1,4,32,256]{3,2,1,0:T(8,128)(2,1)S(1)}, u32[]{:S(2)}, u32[]{:S(2)}) collective-permute-start(bf16[1,4,32,256]{3,2,1,0:T(8,128)(2,1)S(1)} %maximum_bitcast_fusion), channel_id=1, source_target_pairs={{0,24},{1,25},{2,26},{3,27},{4,28},{5,29},{6,30},{7,31},{8,16},{9,... | collective-permute-start | bytes 196616 | tf_op jit(solution)/shard_map/ppermute | solution.py:726
  6.6 5.6 %collective-permute-start.1 = (bf16[1,4,32,256]{3,2,1,0:T(8,128)(2,1)S(1)}, bf16[1,4,32,256]{3,2,1,0:T(8,128)(2,1)S(1)}, u32[]{:S(2)}, u32[]{:S(2)}) collective-permute-start(bf16[1,4,32,256]{3,2,1,0:T(8,128)(2,1)S(1)} %maximum_bitcast_fusion), channel_id=1, source_target_pairs={{0,16},{1,17},{2,18},{3,19},{4,20},{5,21},{6,22},{7,23},{8,24},{9,... | collective-permute-start | bytes 196616 | tf_op jit(solution)/shard_map/ppermute | solution.py:726
  6.6 5.6 %collective-permute-start = (bf16[1,4,32,256]{3,2,1,0:T(8,128)(2,1)S(1)}, bf16[1,4,32,256]{3,2,1,0:T(8,128)(2,1)S(1)}, u32[]{:S(2)}, u32[]{:S(2)}) collective-permute-start(bf16[1,4,32,256]{3,2,1,0:T(8,128)(2,1)S(1)} %maximum_bitcast_fusion), channel_id=1, source_target_pairs={{0,8},{1,9},{2,10},{3,11},{4,12},{5,13},{6,14},{7,15},{8,0},{9,1},... | collective-permute-start | bytes 196616 | tf_op jit(solution)/shard_map/ppermute | solution.py:726
  12.2 14.7 %collective-permute-start.5 = (bf16[4,4,32,256]{3,2,1,0:T(8,128)(2,1)S(1)}, bf16[4,4,32,256]{3,2,1,0:T(8,128)(2,1)S(1)}, u32[]{:S(2)}, u32[]{:S(2)}) collective-permute-start(bf16[4,4,32,256]{3,2,1,0:T(8,128)(2,1)S(1)} %pad_maximum_fusion), channel_id=1, source_target_pairs={{0,5},{1,4},{2,7},{3,6},{4,1},{5,0},{6,3},{7,2},{8,13},{9,12},{10,... | collective-permute-start | bytes 786440 | tf_op jit(solution)/shard_map/ppermute | solution.py:726
  14.8 12.2 %collective-permute-start.4 = (bf16[4,4,32,256]{3,2,1,0:T(8,128)(2,1)S(1)}, bf16[4,4,32,256]{3,2,1,0:T(8,128)(2,1)S(1)}, u32[]{:S(2)}, u32[]{:S(2)}) collective-permute-start(bf16[4,4,32,256]{3,2,1,0:T(8,128)(2,1)S(1)} %pad_maximum_fusion), channel_id=1, source_target_pairs={{0,1},{1,0},{2,3},{3,2},{4,5},{5,4},{6,7},{7,6},{8,9},{9,8},{10,11... | collective-permute-start | bytes 786440 | tf_op jit(solution)/shard_map/ppermute | solution.py:726
  15.3 11.4 %collective-permute-start.3 = (bf16[4,4,32,256]{3,2,1,0:T(8,128)(2,1)S(1)}, bf16[4,4,32,256]{3,2,1,0:T(8,128)(2,1)S(1)}, u32[]{:S(2)}, u32[]{:S(2)}) collective-permute-start(bf16[4,4,32,256]{3,2,1,0:T(8,128)(2,1)S(1)} %pad_maximum_fusion), channel_id=1, source_target_pairs={{0,4},{1,5},{2,6},{3,7},{4,0},{5,1},{6,2},{7,3},{8,12},{9,13},{10,... | collective-permute-start | bytes 786440 | tf_op jit(solution)/shard_map/ppermute | solution.py:726
  15.8 5.0 %collective-permute-start.6 = (bf16[2,64,512]{2,1,0:T(8,128)(2,1)S(1)}, bf16[2,64,512]{2,1,0:T(8,128)(2,1)S(1)}, u32[]{:S(2)}, u32[]{:S(2)}) collective-permute-start(bf16[2,64,512]{2,1,0:T(8,128)(2,1)S(1)} %pad_maximum_fusion.2), channel_id=1, source_target_pairs={{0,8},{1,9},{2,10},{3,11},{4,12},{5,13},{6,14},{7,15},{8,0},{9,1},... | collective-permute-start | bytes 393224 | tf_op jit(solution)/shard_map/ppermute | solution.py:726
  27.0 7.3 %collective-permute-start.7 = (bf16[16,4,32,256]{3,2,1,0:T(8,128)(2,1)S(1)}, bf16[16,4,32,256]{3,2,1,0:T(8,128)(2,1)S(1)}, u32[]{:S(2)}, u32[]{:S(2)}) collective-permute-start(bf16[16,4,32,256]{3,2,1,0:T(8,128)(2,1)S(1)} %constant_dynamic-update-slice_fusion.own_ref), channel_id=1, source_target_pairs={{0,2},{1,3},{2,0},{3,1},{4,6},{5,7},{6,4},{7,5},{8,10},{9,11},{10,... | collective-permute-start | bytes 3145736 | tf_op jit(solution)/shard_map/ppermute | solution.py:726
  33.3 16.1 %collective-permute-start.8 = (bf16[2,128,512]{2,1,0:T(8,128)(2,1)S(1)}, bf16[2,128,512]{2,1,0:T(8,128)(2,1)S(1)}, u32[]{:S(2)}, u32[]{:S(2)}) collective-permute-start(bf16[2,128,512]{2,1,0:T(8,128)(2,1)S(1)} %pad_maximum_fusion.1), channel_id=1, source_target_pairs={{0,16},{1,17},{2,18},{3,19},{4,20},{5,21},{6,22},{7,23},{8,24},{9,... | collective-permute-start | bytes 786440 | tf_op jit(solution)/shard_map/ppermute | solution.py:726
  45.8 11.1 %collective-permute-start.12 = (bf16[4,96,384]{2,1,0:T(8,128)(2,1)}, bf16[4,96,384]{2,1,0:T(8,128)(2,1)S(1)}, u32[]{:S(2)}, u32[]{:S(2)}) collective-permute-start(bf16[4,96,384]{2,1,0:T(8,128)(2,1)} %get-tuple-element.82), channel_id=1, source_target_pairs={{0,1},{2,3},{4,5},{6,7},{8,9},{10,11},{12,13},{14,15},{16,17},{18,... | collective-permute-start | bytes 884744 | tf_op jit(solution)/shard_map/ppermute | solution.py:752
  50.2 21.8 %collective-permute-start.11 = (bf16[2,256,512]{2,1,0:T(8,128)(2,1)S(1)}, bf16[2,256,512]{2,1,0:T(8,128)(2,1)S(1)}, u32[]{:S(2)}, u32[]{:S(2)}) collective-permute-start(bf16[2,256,512]{2,1,0:T(8,128)(2,1)S(1)} %get-tuple-element.172), channel_id=1, source_target_pairs={{0,5},{1,4},{2,7},{3,6},{4,1},{5,0},{6,3},{7,2},{8,13},{9,12},{10,... | collective-permute-start | bytes 1572872 | tf_op jit(solution)/shard_map/ppermute | solution.py:726
  51.0 27.5 %collective-permute-start.10 = (bf16[2,256,512]{2,1,0:T(8,128)(2,1)S(1)}, bf16[2,256,512]{2,1,0:T(8,128)(2,1)S(1)}, u32[]{:S(2)}, u32[]{:S(2)}) collective-permute-start(bf16[2,256,512]{2,1,0:T(8,128)(2,1)S(1)} %get-tuple-element.172), channel_id=1, source_target_pairs={{0,1},{1,0},{2,3},{3,2},{4,5},{5,4},{6,7},{7,6},{8,9},{9,8},{10,11... | collective-permute-start | bytes 1572872 | tf_op jit(solution)/shard_map/ppermute | solution.py:726
  53.1 25.5 %collective-permute-start.9 = (bf16[2,256,512]{2,1,0:T(8,128)(2,1)S(1)}, bf16[2,256,512]{2,1,0:T(8,128)(2,1)S(1)}, u32[]{:S(2)}, u32[]{:S(2)}) collective-permute-start(bf16[2,256,512]{2,1,0:T(8,128)(2,1)S(1)} %get-tuple-element.172), channel_id=1, source_target_pairs={{0,4},{1,5},{2,6},{3,7},{4,0},{5,1},{6,2},{7,3},{8,12},{9,13},{10,... | collective-permute-start | bytes 1572872 | tf_op jit(solution)/shard_map/ppermute | solution.py:726
  78.7 13.5 %collective-permute-start.13 = (bf16[2,1024,512]{2,1,0:T(8,128)(2,1)S(1)}, bf16[2,1024,512]{2,1,0:T(8,128)(2,1)S(1)}, u32[]{:S(2)}, u32[]{:S(2)}) collective-permute-start(bf16[2,1024,512]{2,1,0:T(8,128)(2,1)S(1)} %constant_dynamic-update-slice_fusion.9.own_ref), channel_id=1, source_target_pairs={{0,2},{1,3},{2,0},{3,1},{4,6},{5,7},{6,4},{7,5},{8,10},{9,11},{10,... | collective-permute-start | bytes 6291464 | tf_op jit(solution)/shard_map/ppermute | solution.py:726
  129.3 12.8 %collective-permute-start.14 = (bf16[4,96,384]{2,1,0:T(8,128)(2,1)}, bf16[4,96,384]{2,1,0:T(8,128)(2,1)S(1)}, u32[]{:S(2)}, u32[]{:S(2)}) collective-permute-start(bf16[4,96,384]{2,1,0:T(8,128)(2,1)} %prologue.1), channel_id=1, source_target_pairs={{1,0},{3,2},{5,4},{7,6},{9,8},{11,10},{13,12},{15,14},{17,16},{19,... | collective-permute-start | bytes 884744 | tf_op jit(solution)/shard_map/ppermute | solution.py:752
  150.3 15.3 %collective-permute-start.15 = (bf16[2,1024,512]{2,1,0:T(8,128)(2,1)}, bf16[2,1024,512]{2,1,0:T(8,128)(2,1)S(1)}, u32[]{:S(2)}, u32[]{:S(2)}) collective-permute-start(bf16[2,1024,512]{2,1,0:T(8,128)(2,1)} %feed_grad.3), channel_id=1, source_target_pairs={{0,2},{1,3},{2,0},{3,1},{4,6},{5,7},{6,4},{7,5},{8,10},{9,11},{10,... | collective-permute-start | bytes 6291464 | tf_op jit(solution)/shard_map/ppermute | solution.py:726
  168.9 29.7 %collective-permute-start.16 = (bf16[2,256,512]{2,1,0:T(8,128)(2,1)S(1)}, bf16[2,256,512]{2,1,0:T(8,128)(2,1)S(1)}, u32[]{:S(2)}, u32[]{:S(2)}) collective-permute-start(bf16[2,256,512]{2,1,0:T(8,128)(2,1)S(1)} %get-tuple-element.158), channel_id=1, source_target_pairs={{0,4},{1,5},{2,6},{3,7},{4,0},{5,1},{6,2},{7,3},{8,12},{9,13},{10,... | collective-permute-start | bytes 1572872 | tf_op jit(solution)/shard_map/ppermute | solution.py:726
  169.0 29.7 %collective-permute-start.18 = (bf16[2,256,512]{2,1,0:T(8,128)(2,1)S(1)}, bf16[2,256,512]{2,1,0:T(8,128)(2,1)S(1)}, u32[]{:S(2)}, u32[]{:S(2)}) collective-permute-start(bf16[2,256,512]{2,1,0:T(8,128)(2,1)S(1)} %get-tuple-element.159), channel_id=1, source_target_pairs={{0,5},{1,4},{2,7},{3,6},{4,1},{5,0},{6,3},{7,2},{8,13},{9,12},{10,... | collective-permute-start | bytes 1572872 | tf_op jit(solution)/shard_map/ppermute | solution.py:726
  176.0 22.6 %collective-permute-start.17 = (bf16[2,256,512]{2,1,0:T(8,128)(2,1)S(1)}, bf16[2,256,512]{2,1,0:T(8,128)(2,1)S(1)}, u32[]{:S(2)}, u32[]{:S(2)}) collective-permute-start(bf16[2,256,512]{2,1,0:T(8,128)(2,1)S(1)} %get-tuple-element.160), channel_id=1, source_target_pairs={{0,1},{1,0},{2,3},{3,2},{4,5},{5,4},{6,7},{7,6},{8,9},{9,8},{10,11... | collective-permute-start | bytes 1572872 | tf_op jit(solution)/shard_map/ppermute | solution.py:726
  199.0 17.8 %collective-permute-start.19 = (bf16[2,64,512]{2,1,0:T(8,128)(2,1)S(1)}, bf16[2,64,512]{2,1,0:T(8,128)(2,1)S(1)}, u32[]{:S(2)}, u32[]{:S(2)}) collective-permute-start(bf16[2,64,512]{2,1,0:T(8,128)(2,1)S(1)} %get-tuple-element.164), channel_id=1, source_target_pairs={{0,8},{1,9},{2,10},{3,11},{4,12},{5,13},{6,14},{7,15},{8,0},{9,1},... | collective-permute-start | bytes 393224 | tf_op jit(solution)/shard_map/ppermute | solution.py:726
  201.3 15.5 %collective-permute-start.21 = (bf16[2,64,512]{2,1,0:T(8,128)(2,1)S(1)}, bf16[2,64,512]{2,1,0:T(8,128)(2,1)S(1)}, u32[]{:S(2)}, u32[]{:S(2)}) collective-permute-start(bf16[2,64,512]{2,1,0:T(8,128)(2,1)S(1)} %get-tuple-element.165), channel_id=1, source_target_pairs={{0,24},{1,25},{2,26},{3,27},{4,28},{5,29},{6,30},{7,31},{8,16},{9,... | collective-permute-start | bytes 393224 | tf_op jit(solution)/shard_map/ppermute | solution.py:726
  203.6 13.2 %collective-permute-start.20 = (bf16[2,64,512]{2,1,0:T(8,128)(2,1)S(1)}, bf16[2,64,512]{2,1,0:T(8,128)(2,1)S(1)}, u32[]{:S(2)}, u32[]{:S(2)}) collective-permute-start(bf16[2,64,512]{2,1,0:T(8,128)(2,1)S(1)} %get-tuple-element.166), channel_id=1, source_target_pairs={{0,16},{1,17},{2,18},{3,19},{4,20},{5,21},{6,22},{7,23},{8,24},{9,... | collective-permute-start | bytes 393224 | tf_op jit(solution)/shard_map/ppermute | solution.py:726
  227.2 7.5 %collective-permute-start.22 = (f32[1,1048]{1,0:T(1,128)S(1)}, f32[1,1048]{1,0:T(1,128)S(1)}, u32[]{:S(2)}, u32[]{:S(2)}) collective-permute-start(f32[1,1048]{1,0:T(1,128)S(1)} %broadcast_in_dim.82), channel_id=1, source_target_pairs={{0,2},{1,3},{2,0},{3,1},{4,6},{5,7},{6,4},{7,5},{8,10},{9,11},{10,... | collective-permute-start | bytes 12584 | tf_op jit(solution)/shard_map/ppermute | solution.py:726
  231.2 18.0 %collective-permute-start.28 = (bf16[4,4,32,256]{3,2,1,0:T(8,128)(2,1)S(1)}, bf16[4,4,32,256]{3,2,1,0:T(8,128)(2,1)S(1)}, u32[]{:S(2)}, u32[]{:S(2)}) collective-permute-start(bf16[4,4,32,256]{3,2,1,0:T(8,128)(2,1)S(1)} %get-tuple-element.161), channel_id=1, source_target_pairs={{0,5},{1,4},{2,7},{3,6},{4,1},{5,0},{6,3},{7,2},{8,13},{9,12},{10,... | collective-permute-start | bytes 786440 | tf_op jit(solution)/shard_map/ppermute | solution.py:726
  233.9 15.3 %collective-permute-start.27 = (bf16[4,4,32,256]{3,2,1,0:T(8,128)(2,1)S(1)}, bf16[4,4,32,256]{3,2,1,0:T(8,128)(2,1)S(1)}, u32[]{:S(2)}, u32[]{:S(2)}) collective-permute-start(bf16[4,4,32,256]{3,2,1,0:T(8,128)(2,1)S(1)} %get-tuple-element.162), channel_id=1, source_target_pairs={{0,1},{1,0},{2,3},{3,2},{4,5},{5,4},{6,7},{7,6},{8,9},{9,8},{10,11... | collective-permute-start | bytes 786440 | tf_op jit(solution)/shard_map/ppermute | solution.py:726
  233.9 15.3 %collective-permute-start.26 = (bf16[4,4,32,256]{3,2,1,0:T(8,128)(2,1)S(1)}, bf16[4,4,32,256]{3,2,1,0:T(8,128)(2,1)S(1)}, u32[]{:S(2)}, u32[]{:S(2)}) collective-permute-start(bf16[4,4,32,256]{3,2,1,0:T(8,128)(2,1)S(1)} %get-tuple-element.163), channel_id=1, source_target_pairs={{0,4},{1,5},{2,6},{3,7},{4,0},{5,1},{6,2},{7,3},{8,12},{9,13},{10,... | collective-permute-start | bytes 786440 | tf_op jit(solution)/shard_map/ppermute | solution.py:726
  234.8 10.8 %collective-permute-start.24 = (f32[1,1048]{1,0:T(1,128)S(1)}, f32[1,1048]{1,0:T(1,128)S(1)}, u32[]{:S(2)}, u32[]{:S(2)}) collective-permute-start(f32[1,1048]{1,0:T(1,128)S(1)} %reshape_add_fusion), channel_id=1, source_target_pairs={{0,1},{1,0},{2,3},{3,2},{4,5},{5,4},{6,7},{7,6},{8,9},{9,8},{10,11... | collective-permute-start | bytes 12584 | tf_op jit(solution)/shard_map/ppermute | solution.py:726
  249.4 4.6 %collective-permute-start.29 = (f32[1,1048]{1,0:T(1,128)S(1)}, f32[1,1048]{1,0:T(1,128)S(1)}, u32[]{:S(2)}, u32[]{:S(2)}) collective-permute-start(f32[1,1048]{1,0:T(1,128)S(1)} %add.91), channel_id=1, source_target_pairs={{0,16},{1,17},{2,18},{3,19},{4,20},{5,21},{6,22},{7,23},{8,24},{9,... | collective-permute-start | bytes 12584 | tf_op jit(solution)/shard_map/ppermute | solution.py:726
  254.0 7.2 %collective-permute-start.30 = (f32[1,1048]{1,0:T(1,128)S(1)}, f32[1,1048]{1,0:T(1,128)S(1)}, u32[]{:S(2)}, u32[]{:S(2)}) collective-permute-start(f32[1,1048]{1,0:T(1,128)S(1)} %add.95), channel_id=1, source_target_pairs={{0,8},{1,9},{2,10},{3,11},{4,12},{5,13},{6,14},{7,15},{8,0},{9,1},... | collective-permute-start | bytes 12584 | tf_op jit(solution)/shard_map/ppermute | solution.py:726
  256.7 6.1 %collective-permute-start.33 = (bf16[1,4,32,256]{3,2,1,0:T(8,128)(2,1)S(1)}, bf16[1,4,32,256]{3,2,1,0:T(8,128)(2,1)S(1)}, u32[]{:S(2)}, u32[]{:S(2)}) collective-permute-start(bf16[1,4,32,256]{3,2,1,0:T(8,128)(2,1)S(1)} %get-tuple-element.169), channel_id=1, source_target_pairs={{0,24},{1,25},{2,26},{3,27},{4,28},{5,29},{6,30},{7,31},{8,16},{9,... | collective-permute-start | bytes 196616 | tf_op jit(solution)/shard_map/ppermute | solution.py:726
  259.0 5.2 %collective-permute-start.32 = (bf16[1,4,32,256]{3,2,1,0:T(8,128)(2,1)S(1)}, bf16[1,4,32,256]{3,2,1,0:T(8,128)(2,1)S(1)}, u32[]{:S(2)}, u32[]{:S(2)}) collective-permute-start(bf16[1,4,32,256]{3,2,1,0:T(8,128)(2,1)S(1)} %get-tuple-element.170), channel_id=1, source_target_pairs={{0,16},{1,17},{2,18},{3,19},{4,20},{5,21},{6,22},{7,23},{8,24},{9,... | collective-permute-start | bytes 196616 | tf_op jit(solution)/shard_map/ppermute | solution.py:726
  259.1 5.2 %collective-permute-start.31 = (bf16[1,4,32,256]{3,2,1,0:T(8,128)(2,1)S(1)}, bf16[1,4,32,256]{3,2,1,0:T(8,128)(2,1)S(1)}, u32[]{:S(2)}, u32[]{:S(2)}) collective-permute-start(bf16[1,4,32,256]{3,2,1,0:T(8,128)(2,1)S(1)} %get-tuple-element.171), channel_id=1, source_target_pairs={{0,8},{1,9},{2,10},{3,11},{4,12},{5,13},{6,14},{7,15},{8,0},{9,1},... | collective-permute-start | bytes 196616 | tf_op jit(solution)/shard_map/ppermute | solution.py:726
  (16 other events, 151.5 us)

commit v7 on v6

--- a/solution.py
+++ b/solution.py
@@ -156,7 +156,7 @@
 
     normed = (norm_parts(tokens_ref[...].astype(F32))[0] * gain_ref[...]).astype(BF16)
     normed_ref[...] = normed
-    for c in range(3):
+    for c in (1, 2, 0):
         qkv_ref[c] = mm(normed, weight_ref[c]).astype(BF16)
     live = iota((rows, PAIR), 0) + step * rows >= last
     ones = jnp.ones((rows, PAIR), BF16)
@@ -255,7 +255,7 @@
     count_valid = scalars[scalars.shape[0] + VALID]
     b0, b1, b2 = (blend_ref[pl.ds(f, 1), :] for f in range(3))
 
-    def body(step, carry):
+    def begin(step):
         at = pl.multiple_of(step * ROWS, 32)
         query = qkv_ref[0, pl.ds(at, ROWS), :]
         key = keys[pl.ds(at, WIN), :]
@@ -286,29 +286,37 @@
         added = jnp.concatenate([mm(lifted, with_ones, TN), mm(bent, value[:ROWS], TN)], axis=1)
         keep = (closing < floor).astype(F32)
         state[...] = keep * before + block_only(added)
-        far_two = two(far_mask)
-        pair_weight = jnp.where(far_two, pair_weight, 0.0).astype(BF16)
-        pair_bend = jnp.where(far_two, pair_bend, 0.0).astype(BF16)
-        elu_out = mm(pair_weight, value_heads)
-        tanh_out = mm(pair_bend, value_heads[:, :PAIR]) + jnp.where(carried, tanh_state, 0.0)
-        weights = near_weights(scores, near_mask).astype(BF16)
-        near_out = mm(weights, value_heads)
-        numerator = elu_out[:, :PAIR] + jnp.where(carried, elu_state[:, :PAIR], 0.0)
-        inv_d = 1.0 / (elu_out[:, PAIR:] + jnp.where(carried, elu_state[:, PAIR:], 0.0))
-        far1 = numerator * inv_d
-        inv_l = 1.0 / near_out[:, PAIR:]
-        near = near_out[:, :PAIR] * inv_l
-        far2 = tanh_out / (row - start + 1).astype(F32)
-        mixed = jnp.where(row < count_valid, b0 * near + b1 * far1 + b2 * far2, 0.0)
-        att_ref[pl.ds(at, ROWS), :] = mixed.astype(BF16)
-        near_ref[pl.ds(at, ROWS), :] = near
-        far1_ref[pl.ds(at, ROWS), :] = far1
-        far2_ref[pl.ds(at, ROWS), :] = far2
-        invl_ref[pl.ds(at, ROWS), :] = inv_l
-        invd_ref[pl.ds(at, ROWS), :] = inv_d
+        def finish():
+            far_two = two(far_mask)
+            low_weight = jnp.where(far_two, pair_weight, 0.0).astype(BF16)
+            low_bend = jnp.where(far_two, pair_bend, 0.0).astype(BF16)
+            elu_out = mm(low_weight, value_heads)
+            tanh_out = mm(low_bend, value_heads[:, :PAIR]) + jnp.where(carried, tanh_state, 0.0)
+            weights = near_weights(scores, near_mask).astype(BF16)
+            near_out = mm(weights, value_heads)
+            numerator = elu_out[:, :PAIR] + jnp.where(carried, elu_state[:, :PAIR], 0.0)
+            inv_d = 1.0 / (elu_out[:, PAIR:] + jnp.where(carried, elu_state[:, PAIR:], 0.0))
+            far1 = numerator * inv_d
+            inv_l = 1.0 / near_out[:, PAIR:]
+            near = near_out[:, :PAIR] * inv_l
+            far2 = tanh_out / (row - start + 1).astype(F32)
+            mixed = jnp.where(row < count_valid, b0 * near + b1 * far1 + b2 * far2, 0.0)
+            att_ref[pl.ds(at, ROWS), :] = mixed.astype(BF16)
+            near_ref[pl.ds(at, ROWS), :] = near
+            far1_ref[pl.ds(at, ROWS), :] = far1
+            far2_ref[pl.ds(at, ROWS), :] = far2
+            invl_ref[pl.ds(at, ROWS), :] = inv_l
+            invd_ref[pl.ds(at, ROWS), :] = inv_d
+
+        return finish
+
+    def body(both, carry):
+        finishes = [begin(both * 2 + half) for half in range(2)]
+        for finish in finishes:
+            finish()
         return carry
 
-    lax.fori_loop(0, rows // ROWS, body, 0, unroll=4)
+    lax.fori_loop(0, rows // ROWS // 2, body, 0, unroll=2)
 
 
 def near_back(scores, grad_pair, near_mask, spread_near):
@@ -450,7 +458,7 @@
     def add_up(place, product):
         sums_ref[pl.ds(place, 8), :] += jnp.sum(product.reshape(ROWS // 8, 8, PAIR), axis=0)
 
-    def body(back, carry):
+    def begin(back):
         step = steps - 1 - back
         at = pl.multiple_of(step * ROWS, 32)
         query = qkv_ref[0, pl.ds(at, ROWS), :]
@@ -502,47 +510,55 @@
         add_up(0, near_product)
         add_up(8, far1_product)
         add_up(16, grad_f * far2_ref[pl.ds(at, ROWS), :])
-        shifted = jnp.where(far_two, grad_pair - spread_far, 0.0).astype(BF16)
-        plain = jnp.where(far_two, grad_pair, 0.0).astype(BF16)
-        pair_weight = jnp.where(far_two, pair_weight, 0.0).astype(BF16)
-        pair_bend = jnp.where(far_two, pair_bend, 0.0).astype(BF16)
-        weights, shifted_near = near_back(scores, grad_pair, near_mask, spread_near)
-        d_query = mm(shifted_near, key_heads) * (r0 * HEAD_DIM**-0.5)
-        d_query = (
-            d_query
-            + (mm(shifted, lift_heads) + jnp.where(carried, state_lift, 0.0))
-            * (r1 * jnp.minimum(lift_qf, 1.0))
-            + (mm(plain, bend_heads) + jnp.where(carried, state_bend, 0.0))
-            * (r2 * (1.0 - bend_qf * bend_qf))
-        )
-        out_ref[0, pl.ds(at, ROWS), :] = d_query.astype(BF16)
-        d_key = fold(mm(shifted_near, rows_q, TN))
-        d_lift = fold(mm(shifted, rows_a.astype(BF16), TN))
-        d_bend = fold(mm(plain, rows_t.astype(BF16), TN))
-        d_value = fold(
-            mm(
-                jnp.concatenate([weights, pair_weight, pair_bend], axis=0),
-                jnp.concatenate([grad_f * r0, grad_f * r1, grad_f * r2], axis=0).astype(BF16),
-                TN,
+        def finish():
+            shifted = jnp.where(far_two, grad_pair - spread_far, 0.0).astype(BF16)
+            plain = jnp.where(far_two, grad_pair, 0.0).astype(BF16)
+            low_weight = jnp.where(far_two, pair_weight, 0.0).astype(BF16)
+            low_bend = jnp.where(far_two, pair_bend, 0.0).astype(BF16)
+            weights, shifted_near = near_back(scores, grad_pair, near_mask, spread_near)
+            d_query = mm(shifted_near, key_heads) * (r0 * HEAD_DIM**-0.5)
+            d_query = (
+                d_query
+                + (mm(shifted, lift_heads) + jnp.where(carried, state_lift, 0.0))
+                * (r1 * jnp.minimum(lift_qf, 1.0))
+                + (mm(plain, bend_heads) + jnp.where(carried, state_bend, 0.0))
+                * (r2 * (1.0 - bend_qf * bend_qf))
             )
-        )
-        live = iota((ROWS, PAIR), 0) + first >= jnp.maximum(closing, floor)
-        pad = jnp.zeros((TAIL, PAIR), F32)
-        d_lift = d_lift + jnp.concatenate([jnp.where(live, parts[0], 0.0), pad], axis=0)
-        d_bend = d_bend + jnp.concatenate([jnp.where(live, parts[1], 0.0), pad], axis=0)
-        d_value = d_value + jnp.concatenate([jnp.where(live, parts[2], 0.0), pad], axis=0)
-        d_key = d_key + d_lift * jnp.minimum(lift_kf, 1.0) + d_bend * (1.0 - bend_kf * bend_kf)
-        out_ref[1, pl.ds(at, ROWS), :] = jnp.concatenate(
-            [d_key[TAIL:ROWS], d_key[ROWS:] + key_carry[...]], axis=0
-        ).astype(BF16)
-        out_ref[2, pl.ds(at, ROWS), :] = jnp.concatenate(
-            [d_value[TAIL:ROWS], d_value[ROWS:] + value_carry[...]], axis=0
-        ).astype(BF16)
-        key_carry[...] = d_key[:TAIL]
-        value_carry[...] = d_value[:TAIL]
+            out_ref[0, pl.ds(at, ROWS), :] = d_query.astype(BF16)
+            d_key = fold(mm(shifted_near, rows_q, TN))
+            d_lift = fold(mm(shifted, rows_a.astype(BF16), TN))
+            d_bend = fold(mm(plain, rows_t.astype(BF16), TN))
+            d_value = fold(
+                mm(
+                    jnp.concatenate([weights, low_weight, low_bend], axis=0),
+                    jnp.concatenate([grad_f * r0, grad_f * r1, grad_f * r2], axis=0).astype(BF16),
+                    TN,
+                )
+            )
+            live = iota((ROWS, PAIR), 0) + first >= jnp.maximum(closing, floor)
+            pad = jnp.zeros((TAIL, PAIR), F32)
+            d_lift = d_lift + jnp.concatenate([jnp.where(live, parts[0], 0.0), pad], axis=0)
+            d_bend = d_bend + jnp.concatenate([jnp.where(live, parts[1], 0.0), pad], axis=0)
+            d_value = d_value + jnp.concatenate([jnp.where(live, parts[2], 0.0), pad], axis=0)
+            d_key = d_key + d_lift * jnp.minimum(lift_kf, 1.0) + d_bend * (1.0 - bend_kf * bend_kf)
+            out_ref[1, pl.ds(at, ROWS), :] = jnp.concatenate(
+                [d_key[TAIL:ROWS], d_key[ROWS:] + key_carry[...]], axis=0
+            ).astype(BF16)
+            out_ref[2, pl.ds(at, ROWS), :] = jnp.concatenate(
+                [d_value[TAIL:ROWS], d_value[ROWS:] + value_carry[...]], axis=0
+            ).astype(BF16)
+            key_carry[...] = d_key[:TAIL]
+            value_carry[...] = d_value[:TAIL]
+
+        return finish
+
+    def body(both, carry):
+        finishes = [begin(both * 2 + half) for half in range(2)]
+        for finish in finishes:
+            finish()
         return carry
 
-    lax.fori_loop(0, steps, body, 0, unroll=4)
+    lax.fori_loop(0, steps // 2, body, 0, unroll=2)
 
 
 def feed_kernel(
@@ -573,25 +589,30 @@
     chunk = min(512, half)
     layer = hidden
     d_normed = jnp.zeros(hidden.shape, F32)
-    for place, ref in enumerate((own_ref, other_ref)):
-        for first in range(0, half, chunk):
-            into = ref[0, pl.ds(first, chunk), :]
-            down = ref[1, pl.ds(first, chunk), :]
-            inner = mm(normed, into, NT)
-            d_active = mm(cotangent, down, NT)
-            square = inner * inner
-            bent = jnp.tanh(inner * (c0 + (c0 * 0.044715) * square))
-            gate = 0.5 + 0.5 * bent
-            active = (inner * gate).astype(BF16)
-            slope = gate + inner * (0.5 - 0.5 * bent * bent) * (
-                c0 + (3.0 * 0.044715 * c0) * square
-            )
-            d_inner = (d_active * slope).astype(BF16)
-            at = pl.ds(place * half + first, chunk)
-            active_ref[:, at] = active
-            d_inner_ref[:, at] = d_inner
-            layer = layer + mm(active, down)
-            d_normed = d_normed + mm(d_inner, into)
+    slots = [(ref, first) for ref in (own_ref, other_ref) for first in range(0, half, chunk)]
+
+    def opening(slot):
+        ref, first = slot
+        into = ref[0, pl.ds(first, chunk), :]
+        down = ref[1, pl.ds(first, chunk), :]
+        return into, down, mm(normed, into, NT), mm(cotangent, down, NT)
+
+    ready = opening(slots[0])
+    for place in range(len(slots)):
+        into, down, inner, d_active = ready
+        if place + 1 < len(slots):
+            ready = opening(slots[place + 1])
+        square = inner * inner
+        bent = jnp.tanh(inner * (c0 + (c0 * 0.044715) * square))
+        gate = 0.5 + 0.5 * bent
+        active = (inner * gate).astype(BF16)
+        slope = gate + inner * (0.5 - 0.5 * bent * bent) * (c0 + (3.0 * 0.044715 * c0) * square)
+        d_inner = (d_active * slope).astype(BF16)
+        at = pl.ds(place * chunk, chunk)
+        active_ref[:, at] = active
+        d_inner_ref[:, at] = d_inner
+        layer = layer + mm(active, down)
+        d_normed = d_normed + mm(d_inner, into)
     layer_ref[...] = layer.astype(BF16)
     d_part, gain_rows = norm_back(d_normed, gain_ref[...], normal, scale)
     d_hidden = cotangent.astype(F32) + d_part
@@ -864,8 +885,8 @@
     state_scratch = pltpu.VMEM((PAIR, 3 * PAIR), F32)
     tail_scratch = pltpu.VMEM((TAIL, PAIR), F32)
     results = ()
-    count = pairs // 2
-    for first in (0, count):
+    most = pairs - pairs // 4
+    for first, count in ((0, most), (most, pairs - most)):
         spec = pair_specs(rows, first)
         results = call(
             functools.partial(resume, forward_kernel, len(results)),
@@ -876,8 +897,8 @@
             [key_scratch, key_scratch, state_scratch],
             count,
             "forward",
-            4000 * big,
-            20 * big,
+            8000 * big * count // pairs,
+            40 * big * count // pairs,
             {5 + i: i for i in range(len(results))},
         )(scalars, qkv, message, start_wide, blend_wide, *results)
         if not first:
@@ -1049,19 +1070,21 @@
     total_sums = total_sums + peer(total_sums, [hops[0]], 1)
     total_sums, d_qkv, _ = lax.optimization_barrier((total_sums, d_qkv, share))
     total_sums = total_sums + peer(total_sums, [hops[1]], 1)
+    fine = rows // 6
+    fine_spec = pl.BlockSpec((fine, width), lambda p, s: (p, 0))
     input_grad = call(
         input_kernel,
         [
-            pl.BlockSpec((3, part, width), lambda p, s: (0, p, 0)),
+            pl.BlockSpec((3, fine, width), lambda p, s: (0, p, 0)),
             whole_spec((3, width, width)),
-            row_spec,
-            row_spec,
+            fine_spec,
+            fine_spec,
             whole_spec((1, width)),
         ],
-        row_spec,
+        fine_spec,
         wide,
         [],
-        3,
+        6,
         "input",
         6 * big * width,
         24 * big,

time: 266 us -> 258 us (0.970)
  Pallas kernels: 160 us -> 155 us
where the time goes in v7:
time: 258 us; the launch traced here: 257 us
  Pallas kernels  155 us (60%)
  starting transfers between devices  47.7 us (18%)
  waiting for transfers between devices  28.1 us (11%)
  local copies, waits for them, and re-layouts  14.2 us (6%)
  other arithmetic  10.8 us (4%)
    pallas_call x3, Pallas kernels, per_device(): call(backward_kernel, [spec['qkv'], spec['message'], spec['start'], spec[...  47 us
    ppermute x32, starting transfers between devices, peer(): return lax.ppermute(array, ('dp', 'head'), pairs)  42.6 us
    pallas_call x2, Pallas kernels, per_device(): call(functools.partial(resume, forward_kernel, len(results)), [spec['qkv'...  26.2 us
    pallas_call x1, Pallas kernels, per_device(): call(feed_kernel, [row_spec] * 3 + [whole_spec((width, width)), whole_spe...  26.1 us
    ppermute x32, waiting for transfers between devices, peer(): return lax.ppermute(array, ('dp', 'head'), pairs)  25.8 us
    pallas_call x2, Pallas kernels, feed_grad(): call(feed_grad_kernel, [whole_rows] * 2 + [columns] * 2 + more_in_specs,...  19 us
    pallas_call x1, Pallas kernels, per_device(): call(functools.partial(project_kernel, flips=flips), [pl.BlockSpec((part,...  10.1 us
    pallas_call x1, Pallas kernels, per_device(): call(input_kernel, [pl.BlockSpec((3, fine, width), lambda p, s: (0, p, 0)...  9.67 us
  transfers between devices with their start and end apart: 34, of which 14 were waited for; matrix products, arithmetic and copies ran while one was open for 6% of the time, Pallas kernels for 40%

profile of v7, /device:TPU:0, one launch (start us, length us, event | category | flops | bytes accessed | tf_op | source)
XLA Modules:
  0.0 257.1 jit_solution(4964911664609072695)
XLA Ops:
  1.5 5.1 %collective-permute-start.2 = (bf16[1,4,32,256]{3,2,1,0:T(8,128)(2,1)S(1)}, bf16[1,4,32,256]{3,2,1,0:T(8,128)(2,1)S(1)}, u32[]{:S(2)}, u32[]{:S(2)}) collective-permute-start(bf16[1,4,32,256]{3,2,1,0:T(8,128)(2,1)S(1)} %maximum_bitcast_fusion), channel_id=1, source_target_pairs={{0,24},{1,25},{2,26},{3,27},{4,28},{5,29},{6,30},{7,31},{8,16},{9,... | collective-permute-start | bytes 196616 | tf_op jit(solution)/shard_map/ppermute | solution.py:747
  9.1 3.1 %collective-permute-done.1 = bf16[1,4,32,256]{3,2,1,0:T(8,128)(2,1)S(1)} collective-permute-done((bf16[1,4,32,256]{3,2,1,0:T(8,128)(2,1)S(1)}, bf16[1,4,32,256]{3,2,1,0:T(8,128)(2,1)S(1)}, u32[]{:S(2)}, u32[]{:S(2)}) %collective-permute-start.1) | collective-permute-done | bytes 65568 | tf_op jit(solution)/shard_map/ppermute | solution.py:747
  12.2 2.5 collective-permute-start.5
  16.9 3.9 %collective-permute-done.6 = bf16[2,64,512]{2,1,0:T(8,128)(2,1)S(1)} collective-permute-done((bf16[2,64,512]{2,1,0:T(8,128)(2,1)S(1)}, bf16[2,64,512]{2,1,0:T(8,128)(2,1)S(1)}, u32[]{:S(2)}, u32[]{:S(2)}) %collective-permute-start.6) | collective-permute-done | bytes 131104 | tf_op jit(solution)/shard_map/ppermute | solution.py:747
  20.8 5.9 %collective-permute-done.3 = bf16[4,4,32,256]{3,2,1,0:T(8,128)(2,1)S(1)} collective-permute-done((bf16[4,4,32,256]{3,2,1,0:T(8,128)(2,1)S(1)}, bf16[4,4,32,256]{3,2,1,0:T(8,128)(2,1)S(1)}, u32[]{:S(2)}, u32[]{:S(2)}) %collective-permute-start.3) | collective-permute-done | bytes 262176 | tf_op jit(solution)/shard_map/ppermute | solution.py:747
  31.4 1.9 concatenate.29.scalars
  34.5 10.1 %project.1 = (bf16[3,1536,512]{2,1,0:T(8,128)(2,1)}, bf16[1536,512]{1,0:T(8,128)(2,1)}, bf16[3,512,512]{2,1,0:T(8,128)(2,1)}, bf16[512,512]{1,0:T(8,128)(2,1)}, bf16[4,96,384]{2,1,0:T(8,128)(2,1)}) custom-call(s32[21]{0:T(128)} %concatenate.29.scalars, bf16[1536,512]{1,0:T(8,128)(2,1)} %tokens_ref.5, f32[1,512]{1,0:T(1,128)} %bitcast.34, ...), custom_call_target="tpu_custom_call" | custom-call | flops 2415919104 | bytes 9437184 | tf_op jit(solution)/shard_map/project/pallas_call | solution.py:849
  44.6 3.6 %collective-permute-start.12 = (bf16[4,96,384]{2,1,0:T(8,128)(2,1)}, bf16[4,96,384]{2,1,0:T(8,128)(2,1)S(1)}, u32[]{:S(2)}, u32[]{:S(2)}) collective-permute-start(bf16[4,96,384]{2,1,0:T(8,128)(2,1)} %get-tuple-element.82), channel_id=1, source_target_pairs={{0,1},{2,3},{4,5},{6,7},{8,9},{10,11},{12,13},{14,15},{16,17},{18,... | collective-permute-start | bytes 884744 | tf_op jit(solution)/shard_map/ppermute | solution.py:773
  53.9 1.7 collective-permute-done.12.message_ref
  56.8 17.3 %forward.2 = (bf16[1536,512]{1,0:T(8,128)(2,1)}, f32[1536,512]{1,0:T(8,128)}, f32[1536,512]{1,0:T(8,128)}, f32[1536,512]{1,0:T(8,128)}, f32[1536,512]{1,0:T(8,12...) custom-call(s32[21]{0:T(128)} %concatenate.29.scalars, ...), custom_call_target="tpu_custom_call" | custom-call | flops 4718592000 | bytes 23592960 | tf_op jit(solution)/shard_map/forward/pallas_call | solution.py:891
  74.2 3.1 %collective-permute-done.10 = bf16[2,256,512]{2,1,0:T(8,128)(2,1)S(1)} collective-permute-done((bf16[2,256,512]{2,1,0:T(8,128)(2,1)S(1)}, bf16[2,256,512]{2,1,0:T(8,128)(2,1)S(1)}, u32[]{:S(2)}, u32[]{:S(2)}) %collective-permute-start.10) | collective-permute-done | bytes 524320 | tf_op jit(solution)/shard_map/ppermute | solution.py:747
  77.5 8.9 %forward.3 = (bf16[1536,512]{1,0:T(8,128)(2,1)}, f32[1536,512]{1,0:T(8,128)}, f32[1536,512]{1,0:T(8,128)}, f32[1536,512]{1,0:T(8,128)}, f32[1536,512]{1,0:T(8,12...) custom-call(s32[21]{0:T(128)} %concatenate.29.scalars, ...), custom_call_target="tpu_custom_call", output_to_operand_aliasing={{0}: (5, {}), {1}: (6, {}), {2}: (7, {}), {3}: (8, {}), {4}... | custom-call | flops 1572864000 | bytes 7864320 | tf_op jit(solution)/shard_map/forward/pallas_call | solution.py:891
  87.7 26.1 %feed.1 = (bf16[1536,512]{1,0:T(8,128)(2,1)}, f32[1536,512]{1,0:T(8,128)}, bf16[1536,512]{1,0:T(8,128)(2,1)}, bf16[1536,512]{1,0:T(8,128)(2,1)}, bf16[1536,512]{...) custom-call(s32[21]{0:T(128)} %concatenate.29.scalars, ...), custom_call_target="tpu_custom_call" | custom-call | flops 12884901888 | bytes 25165824 | tf_op jit(solution)/shard_map/feed/pallas_call | solution.py:919
  113.8 7.7 %prologue.1 = bf16[4,96,384]{2,1,0:T(8,128)(2,1)} custom-call(s32[21]{0:T(128)} %concatenate.29.scalars, bf16[3,1536,512]{2,1,0:T(8,128)(2,1)} %get-tuple-element.80.qkv_ref.query_ref.key_ref.value_ref, bf16[3,1536,512]{2,1,0:T(8,128)(2,1)} %get-tuple-element.80.qkv_ref.query_ref.key_ref.value_ref, ...), custom_call_target="tpu_custom_call" | custom-call | flops 393216000 | bytes 15728640 | tf_op jit(solution)/shard_map/prologue/pallas_call | solution.py:937
  123.0 10.8 %feed_grad.2 = (f32[512,512]{1,0:T(8,128)}, f32[2,1024,512]{2,1,0:T(8,128)}) custom-call(s32[21]{0:T(128)} %concatenate.29.scalars, bf16[1536,512]{1,0:T(8,128)(2,1)} %get-tuple-element.107.normed_ref, bf16[1536,512]{1,0:T(8,128)(2,1)} %cotangent_ref.5, bf16[1536,2048]{1,0:T(8,128)(2,1)} %get-tuple-element.108.active_ref, ...), custom_call_target="tpu_custom_call" | custom-call | flops 3221225472 | bytes 9437184 | tf_op jit(solution)/shard_map/feed_grad/pallas_call | solution.py:969
  134.4 8.2 %feed_grad.3 = bf16[2,1024,512]{2,1,0:T(8,128)(2,1)} custom-call(s32[21]{0:T(128)} %concatenate.29.scalars, bf16[1536,512]{1,0:T(8,128)(2,1)} %get-tuple-element.107.normed_ref, bf16[1536,512]{1,0:T(8,128)(2,1)} %cotangent_ref.5, bf16[1536,2048]{1,0:T(8,128)(2,1)} %get-tuple-element.108.active_ref, bf16[1536,2048]{1,0:T(8,128)(2,1)} %get-tuple-element.119.d_inner_ref), custom_call_target="tpu_custom_call" | custom-call | flops 3221225472 | bytes 9437184 | tf_op jit(solution)/shard_map/feed_grad/pallas_call | solution.py:969
  143.2 12.7 %backward.3 = (bf16[3,1536,512]{2,1,0:T(8,128)(2,1)}, f32[24,128]{1,0:T(8,128)}) custom-call(s32[21]{0:T(128)} %concatenate.29.scalars, bf16[3,1536,512]{2,1,0:T(8,128)(2,1)} %get-tuple-element.80.qkv_ref.query_ref.key_ref.value_ref, bf16[4,96,384]{2,1,0:T(8,128)(2,1)} %copy-done, s32[1536,128]{1,0:T(8,128)} %broadcast_in_dim.78.start_ref, ...), custom_call_target="tpu_custom_call" | custom-call | flops 3145728000 | bytes 7864320 | tf_op jit(solution)/shard_map/backward/pallas_call | solution.py:1001
  155.9 3.1 %fusion.6 = (bf16[2,1024,512]{2,1,0:T(8,128)(2,1)S(1)}, f32[2,1024,512]{2,1,0:T(8,128)S(1)}) fusion(f32[2,1024,512]{2,1,0:T(8,128)} %get-tuple-element.117, bf16[2,1024,512]{2,1,0:T(8,128)(2,1)S(1)} %collective-permute-done.15), kind=kLoop, calls=%fused_computation.47 | loop fusion | flops 3145728 | bytes 12582912 | tf_op jit(solution)/shard_map/convert.11
  160.7 4.7 %collective-permute-start.18 = (bf16[2,256,512]{2,1,0:T(8,128)(2,1)S(1)}, bf16[2,256,512]{2,1,0:T(8,128)(2,1)S(1)}, u32[]{:S(2)}, u32[]{:S(2)}) collective-permute-start(bf16[2,256,512]{2,1,0:T(8,128)(2,1)S(1)} %get-tuple-element.159), channel_id=1, source_target_pairs={{0,5},{1,4},{2,7},{3,6},{4,1},{5,0},{6,3},{7,2},{8,13},{9,12},{10,... | collective-permute-start | bytes 1572872 | tf_op jit(solution)/shard_map/ppermute | solution.py:747
  165.4 21.6 %backward.4 = (bf16[3,1536,512]{2,1,0:T(8,128)(2,1)}, f32[24,256]{1,0:T(8,128)}) custom-call(s32[21]{0:T(128)} %concatenate.29.scalars, bf16[3,1536,512]{2,1,0:T(8,128)(2,1)} %get-tuple-element.80.qkv_ref.query_ref.key_ref.value_ref, bf16[4,96,384]{2,1,0:T(8,128)(2,1)} %copy-done, ...), custom_call_target="tpu_custom_call", output_to_operand_aliasing={{0}: (13, {})} | custom-call | flops 6291456000 | bytes 15728640 | tf_op jit(solution)/shard_map/backward/pallas_call | solution.py:1001
  188.6 1.8 collective-permute-start.19
  190.4 5.0 %collective-permute-start.21 = (bf16[2,64,512]{2,1,0:T(8,128)(2,1)S(1)}, bf16[2,64,512]{2,1,0:T(8,128)(2,1)S(1)}, u32[]{:S(2)}, u32[]{:S(2)}) collective-permute-start(bf16[2,64,512]{2,1,0:T(8,128)(2,1)S(1)} %get-tuple-element.165), channel_id=1, source_target_pairs={{0,24},{1,25},{2,26},{3,27},{4,28},{5,29},{6,30},{7,31},{8,16},{9,... | collective-permute-start | bytes 393224 | tf_op jit(solution)/shard_map/ppermute | solution.py:747
  195.3 12.7 %backward.5 = (bf16[3,1536,512]{2,1,0:T(8,128)(2,1)}, f32[24,128]{1,0:T(8,128)}) custom-call(s32[21]{0:T(128)} %concatenate.29.scalars, bf16[3,1536,512]{2,1,0:T(8,128)(2,1)} %get-tuple-element.80.qkv_ref.query_ref.key_ref.value_ref, bf16[4,96,384]{2,1,0:T(8,128)(2,1)} %copy-done, ...), custom_call_target="tpu_custom_call", output_to_operand_aliasing={{0}: (13, {})} | custom-call | flops 3145728000 | bytes 7864320 | tf_op jit(solution)/shard_map/backward/pallas_call | solution.py:1001
  208.2 8.9 %weight_grad.1 = (f32[16,4,32,256]{3,2,1,0:T(8,128)}, bf16[16,4,32,256]{3,2,1,0:T(8,128)(2,1)}, f32[8,512]{1,0:T(8,128)}) custom-call(s32[21]{0:T(128)} %concatenate.29.scalars, bf16[1536,512]{1,0:T(8,128)(2,1)} %get-tuple-element.106.normed_ref, bf16[3,1536,512]{2,1,0:T(8,128)(2,1)} %get-tuple-element.138.d_qkv_ref, ...), custom_call_target="tpu_custom_call" | custom-call | flops 2415919104 | bytes 6291456 | tf_op jit(solution)/shard_map/weight_grad/pallas_call | solution.py:1046
  220.0 2.1 fusion.4
  222.2 2.7 %collective-permute-start.28 = (bf16[4,4,32,256]{3,2,1,0:T(8,128)(2,1)S(1)}, bf16[4,4,32,256]{3,2,1,0:T(8,128)(2,1)S(1)}, u32[]{:S(2)}, u32[]{:S(2)}) collective-permute-start(bf16[4,4,32,256]{3,2,1,0:T(8,128)(2,1)S(1)} %get-tuple-element.161), channel_id=1, source_target_pairs={{0,5},{1,4},{2,7},{3,6},{4,1},{5,0},{6,3},{7,2},{8,13},{9,12},{10,... | collective-permute-start | bytes 786440 | tf_op jit(solution)/shard_map/ppermute | solution.py:747
  227.3 9.7 %input.1 = f32[1536,512]{1,0:T(8,128)} custom-call(s32[21]{0:T(128)} %concatenate.29.scalars, bf16[3,1536,512]{2,1,0:T(8,128)(2,1)} %get-tuple-element.138.d_qkv_ref, bf16[3,512,512]{2,1,0:T(8,128)(2,1)} %get-tuple-element.130.weight_ref, bf16[1536,512]{1,0:T(8,128)(2,1)} %tokens_ref.5, f32[1536,512]{1,0:T(8,128)} %get-tuple-element.139.d_hidden_ref, ...), custom_call_target="tpu_custom_call" | custom-call | flops 2415919104 | bytes 18874368 | tf_op jit(solution)/shard_map/input/pallas_call | solution.py:1075
  237.0 1.7 collective-permute-start.25
  238.7 2.0 collective-permute-done.25
  240.9 3.0 %collective-permute-start.29 = (f32[1,1048]{1,0:T(1,128)S(1)}, f32[1,1048]{1,0:T(1,128)S(1)}, u32[]{:S(2)}, u32[]{:S(2)}) collective-permute-start(f32[1,1048]{1,0:T(1,128)S(1)} %add.91), channel_id=1, source_target_pairs={{0,16},{1,17},{2,18},{3,19},{4,20},{5,21},{6,22},{7,23},{8,24},{9,... | collective-permute-start | bytes 12584 | tf_op jit(solution)/shard_map/ppermute | solution.py:747
  246.8 3.8 %collective-permute-start.33 = (bf16[1,4,32,256]{3,2,1,0:T(8,128)(2,1)S(1)}, bf16[1,4,32,256]{3,2,1,0:T(8,128)(2,1)S(1)}, u32[]{:S(2)}, u32[]{:S(2)}) collective-permute-start(bf16[1,4,32,256]{3,2,1,0:T(8,128)(2,1)S(1)} %get-tuple-element.169), channel_id=1, source_target_pairs={{0,24},{1,25},{2,26},{3,27},{4,28},{5,29},{6,30},{7,31},{8,16},{9,... | collective-permute-start | bytes 196616 | tf_op jit(solution)/shard_map/ppermute | solution.py:747
  252.9 2.9 %collective-permute-done.32 = bf16[1,4,32,256]{3,2,1,0:T(8,128)(2,1)S(1)} collective-permute-done((bf16[1,4,32,256]{3,2,1,0:T(8,128)(2,1)S(1)}, bf16[1,4,32,256]{3,2,1,0:T(8,128)(2,1)S(1)}, u32[]{:S(2)}, u32[]{:S(2)}) %collective-permute-start.32) | collective-permute-done | bytes 65568 | tf_op jit(solution)/shard_map/ppermute | solution.py:747
  (135 shorter events, 37.1 us)
Async XLA Ops:
  1.5 7.6 %collective-permute-start.2 = (bf16[1,4,32,256]{3,2,1,0:T(8,128)(2,1)S(1)}, bf16[1,4,32,256]{3,2,1,0:T(8,128)(2,1)S(1)}, u32[]{:S(2)}, u32[]{:S(2)}) collective-permute-start(bf16[1,4,32,256]{3,2,1,0:T(8,128)(2,1)S(1)} %maximum_bitcast_fusion), channel_id=1, source_target_pairs={{0,24},{1,25},{2,26},{3,27},{4,28},{5,29},{6,30},{7,31},{8,16},{9,... | collective-permute-start | bytes 196616 | tf_op jit(solution)/shard_map/ppermute | solution.py:747
  6.6 5.6 %collective-permute-start.1 = (bf16[1,4,32,256]{3,2,1,0:T(8,128)(2,1)S(1)}, bf16[1,4,32,256]{3,2,1,0:T(8,128)(2,1)S(1)}, u32[]{:S(2)}, u32[]{:S(2)}) collective-permute-start(bf16[1,4,32,256]{3,2,1,0:T(8,128)(2,1)S(1)} %maximum_bitcast_fusion), channel_id=1, source_target_pairs={{0,16},{1,17},{2,18},{3,19},{4,20},{5,21},{6,22},{7,23},{8,24},{9,... | collective-permute-start | bytes 196616 | tf_op jit(solution)/shard_map/ppermute | solution.py:747
  6.6 5.6 %collective-permute-start = (bf16[1,4,32,256]{3,2,1,0:T(8,128)(2,1)S(1)}, bf16[1,4,32,256]{3,2,1,0:T(8,128)(2,1)S(1)}, u32[]{:S(2)}, u32[]{:S(2)}) collective-permute-start(bf16[1,4,32,256]{3,2,1,0:T(8,128)(2,1)S(1)} %maximum_bitcast_fusion), channel_id=1, source_target_pairs={{0,8},{1,9},{2,10},{3,11},{4,12},{5,13},{6,14},{7,15},{8,0},{9,1},... | collective-permute-start | bytes 196616 | tf_op jit(solution)/shard_map/ppermute | solution.py:747
  12.2 14.7 %collective-permute-start.5 = (bf16[4,4,32,256]{3,2,1,0:T(8,128)(2,1)S(1)}, bf16[4,4,32,256]{3,2,1,0:T(8,128)(2,1)S(1)}, u32[]{:S(2)}, u32[]{:S(2)}) collective-permute-start(bf16[4,4,32,256]{3,2,1,0:T(8,128)(2,1)S(1)} %pad_maximum_fusion), channel_id=1, source_target_pairs={{0,5},{1,4},{2,7},{3,6},{4,1},{5,0},{6,3},{7,2},{8,13},{9,12},{10,... | collective-permute-start | bytes 786440 | tf_op jit(solution)/shard_map/ppermute | solution.py:747
  14.8 12.2 %collective-permute-start.4 = (bf16[4,4,32,256]{3,2,1,0:T(8,128)(2,1)S(1)}, bf16[4,4,32,256]{3,2,1,0:T(8,128)(2,1)S(1)}, u32[]{:S(2)}, u32[]{:S(2)}) collective-permute-start(bf16[4,4,32,256]{3,2,1,0:T(8,128)(2,1)S(1)} %pad_maximum_fusion), channel_id=1, source_target_pairs={{0,1},{1,0},{2,3},{3,2},{4,5},{5,4},{6,7},{7,6},{8,9},{9,8},{10,11... | collective-permute-start | bytes 786440 | tf_op jit(solution)/shard_map/ppermute | solution.py:747
  15.3 11.4 %collective-permute-start.3 = (bf16[4,4,32,256]{3,2,1,0:T(8,128)(2,1)S(1)}, bf16[4,4,32,256]{3,2,1,0:T(8,128)(2,1)S(1)}, u32[]{:S(2)}, u32[]{:S(2)}) collective-permute-start(bf16[4,4,32,256]{3,2,1,0:T(8,128)(2,1)S(1)} %pad_maximum_fusion), channel_id=1, source_target_pairs={{0,4},{1,5},{2,6},{3,7},{4,0},{5,1},{6,2},{7,3},{8,12},{9,13},{10,... | collective-permute-start | bytes 786440 | tf_op jit(solution)/shard_map/ppermute | solution.py:747
  15.8 5.0 %collective-permute-start.6 = (bf16[2,64,512]{2,1,0:T(8,128)(2,1)S(1)}, bf16[2,64,512]{2,1,0:T(8,128)(2,1)S(1)}, u32[]{:S(2)}, u32[]{:S(2)}) collective-permute-start(bf16[2,64,512]{2,1,0:T(8,128)(2,1)S(1)} %pad_maximum_fusion.2), channel_id=1, source_target_pairs={{0,8},{1,9},{2,10},{3,11},{4,12},{5,13},{6,14},{7,15},{8,0},{9,1},... | collective-permute-start | bytes 393224 | tf_op jit(solution)/shard_map/ppermute | solution.py:747
  27.0 6.5 %collective-permute-start.7 = (bf16[16,4,32,256]{3,2,1,0:T(8,128)(2,1)S(1)}, bf16[16,4,32,256]{3,2,1,0:T(8,128)(2,1)S(1)}, u32[]{:S(2)}, u32[]{:S(2)}) collective-permute-start(bf16[16,4,32,256]{3,2,1,0:T(8,128)(2,1)S(1)} %constant_dynamic-update-slice_fusion.own_ref), channel_id=1, source_target_pairs={{0,2},{1,3},{2,0},{3,1},{4,6},{5,7},{6,4},{7,5},{8,10},{9,11},{10,... | collective-permute-start | bytes 3145736 | tf_op jit(solution)/shard_map/ppermute | solution.py:747
  33.3 15.7 %collective-permute-start.8 = (bf16[2,128,512]{2,1,0:T(8,128)(2,1)S(1)}, bf16[2,128,512]{2,1,0:T(8,128)(2,1)S(1)}, u32[]{:S(2)}, u32[]{:S(2)}) collective-permute-start(bf16[2,128,512]{2,1,0:T(8,128)(2,1)S(1)} %pad_maximum_fusion.1), channel_id=1, source_target_pairs={{0,16},{1,17},{2,18},{3,19},{4,20},{5,21},{6,22},{7,23},{8,24},{9,... | collective-permute-start | bytes 786440 | tf_op jit(solution)/shard_map/ppermute | solution.py:747
  44.6 11.1 %collective-permute-start.12 = (bf16[4,96,384]{2,1,0:T(8,128)(2,1)}, bf16[4,96,384]{2,1,0:T(8,128)(2,1)S(1)}, u32[]{:S(2)}, u32[]{:S(2)}) collective-permute-start(bf16[4,96,384]{2,1,0:T(8,128)(2,1)} %get-tuple-element.82), channel_id=1, source_target_pairs={{0,1},{2,3},{4,5},{6,7},{8,9},{10,11},{12,13},{14,15},{16,17},{18,... | collective-permute-start | bytes 884744 | tf_op jit(solution)/shard_map/ppermute | solution.py:773
  49.7 24.5 %collective-permute-start.11 = (bf16[2,256,512]{2,1,0:T(8,128)(2,1)S(1)}, bf16[2,256,512]{2,1,0:T(8,128)(2,1)S(1)}, u32[]{:S(2)}, u32[]{:S(2)}) collective-permute-start(bf16[2,256,512]{2,1,0:T(8,128)(2,1)S(1)} %get-tuple-element.172), channel_id=1, source_target_pairs={{0,5},{1,4},{2,7},{3,6},{4,1},{5,0},{6,3},{7,2},{8,13},{9,12},{10,... | collective-permute-start | bytes 1572872 | tf_op jit(solution)/shard_map/ppermute | solution.py:747
  51.0 26.3 %collective-permute-start.10 = (bf16[2,256,512]{2,1,0:T(8,128)(2,1)S(1)}, bf16[2,256,512]{2,1,0:T(8,128)(2,1)S(1)}, u32[]{:S(2)}, u32[]{:S(2)}) collective-permute-start(bf16[2,256,512]{2,1,0:T(8,128)(2,1)S(1)} %get-tuple-element.172), channel_id=1, source_target_pairs={{0,1},{1,0},{2,3},{3,2},{4,5},{5,4},{6,7},{7,6},{8,9},{9,8},{10,11... | collective-permute-start | bytes 1572872 | tf_op jit(solution)/shard_map/ppermute | solution.py:747
  52.6 24.7 %collective-permute-start.9 = (bf16[2,256,512]{2,1,0:T(8,128)(2,1)S(1)}, bf16[2,256,512]{2,1,0:T(8,128)(2,1)S(1)}, u32[]{:S(2)}, u32[]{:S(2)}) collective-permute-start(bf16[2,256,512]{2,1,0:T(8,128)(2,1)S(1)} %get-tuple-element.172), channel_id=1, source_target_pairs={{0,4},{1,5},{2,6},{3,7},{4,0},{5,1},{6,2},{7,3},{8,12},{9,13},{10,... | collective-permute-start | bytes 1572872 | tf_op jit(solution)/shard_map/ppermute | solution.py:747
  77.5 8.9 %collective-permute-start.13 = (bf16[2,1024,512]{2,1,0:T(8,128)(2,1)S(1)}, bf16[2,1024,512]{2,1,0:T(8,128)(2,1)S(1)}, u32[]{:S(2)}, u32[]{:S(2)}) collective-permute-start(bf16[2,1024,512]{2,1,0:T(8,128)(2,1)S(1)} %constant_dynamic-update-slice_fusion.9.own_ref), channel_id=1, source_target_pairs={{0,2},{1,3},{2,0},{3,1},{4,6},{5,7},{6,4},{7,5},{8,10},{9,11},{10,... | collective-permute-start | bytes 6291464 | tf_op jit(solution)/shard_map/ppermute | solution.py:747
  121.5 12.9 %collective-permute-start.14 = (bf16[4,96,384]{2,1,0:T(8,128)(2,1)}, bf16[4,96,384]{2,1,0:T(8,128)(2,1)S(1)}, u32[]{:S(2)}, u32[]{:S(2)}) collective-permute-start(bf16[4,96,384]{2,1,0:T(8,128)(2,1)} %prologue.1), channel_id=1, source_target_pairs={{1,0},{3,2},{5,4},{7,6},{9,8},{11,10},{13,12},{15,14},{17,16},{19,... | collective-permute-start | bytes 884744 | tf_op jit(solution)/shard_map/ppermute | solution.py:773
  142.6 13.3 %collective-permute-start.15 = (bf16[2,1024,512]{2,1,0:T(8,128)(2,1)}, bf16[2,1024,512]{2,1,0:T(8,128)(2,1)S(1)}, u32[]{:S(2)}, u32[]{:S(2)}) collective-permute-start(bf16[2,1024,512]{2,1,0:T(8,128)(2,1)} %feed_grad.3), channel_id=1, source_target_pairs={{0,2},{1,3},{2,0},{3,1},{4,6},{5,7},{6,4},{7,5},{8,10},{9,11},{10,... | collective-permute-start | bytes 6291464 | tf_op jit(solution)/shard_map/ppermute | solution.py:747
  159.2 27.7 %collective-permute-start.16 = (bf16[2,256,512]{2,1,0:T(8,128)(2,1)S(1)}, bf16[2,256,512]{2,1,0:T(8,128)(2,1)S(1)}, u32[]{:S(2)}, u32[]{:S(2)}) collective-permute-start(bf16[2,256,512]{2,1,0:T(8,128)(2,1)S(1)} %get-tuple-element.158), channel_id=1, source_target_pairs={{0,4},{1,5},{2,6},{3,7},{4,0},{5,1},{6,2},{7,3},{8,12},{9,13},{10,... | collective-permute-start | bytes 1572872 | tf_op jit(solution)/shard_map/ppermute | solution.py:747
  160.7 26.2 %collective-permute-start.18 = (bf16[2,256,512]{2,1,0:T(8,128)(2,1)S(1)}, bf16[2,256,512]{2,1,0:T(8,128)(2,1)S(1)}, u32[]{:S(2)}, u32[]{:S(2)}) collective-permute-start(bf16[2,256,512]{2,1,0:T(8,128)(2,1)S(1)} %get-tuple-element.159), channel_id=1, source_target_pairs={{0,5},{1,4},{2,7},{3,6},{4,1},{5,0},{6,3},{7,2},{8,13},{9,12},{10,... | collective-permute-start | bytes 1572872 | tf_op jit(solution)/shard_map/ppermute | solution.py:747
  165.4 22.9 %collective-permute-start.17 = (bf16[2,256,512]{2,1,0:T(8,128)(2,1)S(1)}, bf16[2,256,512]{2,1,0:T(8,128)(2,1)S(1)}, u32[]{:S(2)}, u32[]{:S(2)}) collective-permute-start(bf16[2,256,512]{2,1,0:T(8,128)(2,1)S(1)} %get-tuple-element.160), channel_id=1, source_target_pairs={{0,1},{1,0},{2,3},{3,2},{4,5},{5,4},{6,7},{7,6},{8,9},{9,8},{10,11... | collective-permute-start | bytes 1572872 | tf_op jit(solution)/shard_map/ppermute | solution.py:747
  188.6 19.5 %collective-permute-start.19 = (bf16[2,64,512]{2,1,0:T(8,128)(2,1)S(1)}, bf16[2,64,512]{2,1,0:T(8,128)(2,1)S(1)}, u32[]{:S(2)}, u32[]{:S(2)}) collective-permute-start(bf16[2,64,512]{2,1,0:T(8,128)(2,1)S(1)} %get-tuple-element.164), channel_id=1, source_target_pairs={{0,8},{1,9},{2,10},{3,11},{4,12},{5,13},{6,14},{7,15},{8,0},{9,1},... | collective-permute-start | bytes 393224 | tf_op jit(solution)/shard_map/ppermute | solution.py:747
  190.4 17.7 %collective-permute-start.21 = (bf16[2,64,512]{2,1,0:T(8,128)(2,1)S(1)}, bf16[2,64,512]{2,1,0:T(8,128)(2,1)S(1)}, u32[]{:S(2)}, u32[]{:S(2)}) collective-permute-start(bf16[2,64,512]{2,1,0:T(8,128)(2,1)S(1)} %get-tuple-element.165), channel_id=1, source_target_pairs={{0,24},{1,25},{2,26},{3,27},{4,28},{5,29},{6,30},{7,31},{8,16},{9,... | collective-permute-start | bytes 393224 | tf_op jit(solution)/shard_map/ppermute | solution.py:747
  195.3 12.7 %collective-permute-start.20 = (bf16[2,64,512]{2,1,0:T(8,128)(2,1)S(1)}, bf16[2,64,512]{2,1,0:T(8,128)(2,1)S(1)}, u32[]{:S(2)}, u32[]{:S(2)}) collective-permute-start(bf16[2,64,512]{2,1,0:T(8,128)(2,1)S(1)} %get-tuple-element.166), channel_id=1, source_target_pairs={{0,16},{1,17},{2,18},{3,19},{4,20},{5,21},{6,22},{7,23},{8,24},{9,... | collective-permute-start | bytes 393224 | tf_op jit(solution)/shard_map/ppermute | solution.py:747
  218.2 7.5 %collective-permute-start.22 = (f32[1,1048]{1,0:T(1,128)S(1)}, f32[1,1048]{1,0:T(1,128)S(1)}, u32[]{:S(2)}, u32[]{:S(2)}) collective-permute-start(f32[1,1048]{1,0:T(1,128)S(1)} %broadcast_in_dim.82), channel_id=1, source_target_pairs={{0,2},{1,3},{2,0},{3,1},{4,6},{5,7},{6,4},{7,5},{8,10},{9,11},{10,... | collective-permute-start | bytes 12584 | tf_op jit(solution)/shard_map/ppermute | solution.py:747
  222.2 18.5 %collective-permute-start.28 = (bf16[4,4,32,256]{3,2,1,0:T(8,128)(2,1)S(1)}, bf16[4,4,32,256]{3,2,1,0:T(8,128)(2,1)S(1)}, u32[]{:S(2)}, u32[]{:S(2)}) collective-permute-start(bf16[4,4,32,256]{3,2,1,0:T(8,128)(2,1)S(1)} %get-tuple-element.161), channel_id=1, source_target_pairs={{0,5},{1,4},{2,7},{3,6},{4,1},{5,0},{6,3},{7,2},{8,13},{9,12},{10,... | collective-permute-start | bytes 786440 | tf_op jit(solution)/shard_map/ppermute | solution.py:747
  224.9 15.8 %collective-permute-start.27 = (bf16[4,4,32,256]{3,2,1,0:T(8,128)(2,1)S(1)}, bf16[4,4,32,256]{3,2,1,0:T(8,128)(2,1)S(1)}, u32[]{:S(2)}, u32[]{:S(2)}) collective-permute-start(bf16[4,4,32,256]{3,2,1,0:T(8,128)(2,1)S(1)} %get-tuple-element.162), channel_id=1, source_target_pairs={{0,1},{1,0},{2,3},{3,2},{4,5},{5,4},{6,7},{7,6},{8,9},{9,8},{10,11... | collective-permute-start | bytes 786440 | tf_op jit(solution)/shard_map/ppermute | solution.py:747
  224.9 15.8 %collective-permute-start.26 = (bf16[4,4,32,256]{3,2,1,0:T(8,128)(2,1)S(1)}, bf16[4,4,32,256]{3,2,1,0:T(8,128)(2,1)S(1)}, u32[]{:S(2)}, u32[]{:S(2)}) collective-permute-start(bf16[4,4,32,256]{3,2,1,0:T(8,128)(2,1)S(1)} %get-tuple-element.163), channel_id=1, source_target_pairs={{0,4},{1,5},{2,6},{3,7},{4,0},{5,1},{6,2},{7,3},{8,12},{9,13},{10,... | collective-permute-start | bytes 786440 | tf_op jit(solution)/shard_map/ppermute | solution.py:747
  225.7 11.3 %collective-permute-start.24 = (f32[1,1048]{1,0:T(1,128)S(1)}, f32[1,1048]{1,0:T(1,128)S(1)}, u32[]{:S(2)}, u32[]{:S(2)}) collective-permute-start(f32[1,1048]{1,0:T(1,128)S(1)} %reshape_add_fusion), channel_id=1, source_target_pairs={{0,1},{1,0},{2,3},{3,2},{4,5},{5,4},{6,7},{7,6},{8,9},{9,8},{10,11... | collective-permute-start | bytes 12584 | tf_op jit(solution)/shard_map/ppermute | solution.py:747
  240.9 4.6 %collective-permute-start.29 = (f32[1,1048]{1,0:T(1,128)S(1)}, f32[1,1048]{1,0:T(1,128)S(1)}, u32[]{:S(2)}, u32[]{:S(2)}) collective-permute-start(f32[1,1048]{1,0:T(1,128)S(1)} %add.91), channel_id=1, source_target_pairs={{0,16},{1,17},{2,18},{3,19},{4,20},{5,21},{6,22},{7,23},{8,24},{9,... | collective-permute-start | bytes 12584 | tf_op jit(solution)/shard_map/ppermute | solution.py:747
  245.5 5.6 %collective-permute-start.30 = (f32[1,1048]{1,0:T(1,128)S(1)}, f32[1,1048]{1,0:T(1,128)S(1)}, u32[]{:S(2)}, u32[]{:S(2)}) collective-permute-start(f32[1,1048]{1,0:T(1,128)S(1)} %add.95), channel_id=1, source_target_pairs={{0,8},{1,9},{2,10},{3,11},{4,12},{5,13},{6,14},{7,15},{8,0},{9,1},... | collective-permute-start | bytes 12584 | tf_op jit(solution)/shard_map/ppermute | solution.py:747
  246.8 6.1 %collective-permute-start.33 = (bf16[1,4,32,256]{3,2,1,0:T(8,128)(2,1)S(1)}, bf16[1,4,32,256]{3,2,1,0:T(8,128)(2,1)S(1)}, u32[]{:S(2)}, u32[]{:S(2)}) collective-permute-start(bf16[1,4,32,256]{3,2,1,0:T(8,128)(2,1)S(1)} %get-tuple-element.169), channel_id=1, source_target_pairs={{0,24},{1,25},{2,26},{3,27},{4,28},{5,29},{6,30},{7,31},{8,16},{9,... | collective-permute-start | bytes 196616 | tf_op jit(solution)/shard_map/ppermute | solution.py:747
  250.6 5.2 %collective-permute-start.32 = (bf16[1,4,32,256]{3,2,1,0:T(8,128)(2,1)S(1)}, bf16[1,4,32,256]{3,2,1,0:T(8,128)(2,1)S(1)}, u32[]{:S(2)}, u32[]{:S(2)}) collective-permute-start(bf16[1,4,32,256]{3,2,1,0:T(8,128)(2,1)S(1)} %get-tuple-element.170), channel_id=1, source_target_pairs={{0,16},{1,17},{2,18},{3,19},{4,20},{5,21},{6,22},{7,23},{8,24},{9,... | collective-permute-start | bytes 196616 | tf_op jit(solution)/shard_map/ppermute | solution.py:747
  250.6 5.2 %collective-permute-start.31 = (bf16[1,4,32,256]{3,2,1,0:T(8,128)(2,1)S(1)}, bf16[1,4,32,256]{3,2,1,0:T(8,128)(2,1)S(1)}, u32[]{:S(2)}, u32[]{:S(2)}) collective-permute-start(bf16[1,4,32,256]{3,2,1,0:T(8,128)(2,1)S(1)} %get-tuple-element.171), channel_id=1, source_target_pairs={{0,8},{1,9},{2,10},{3,11},{4,12},{5,13},{6,14},{7,15},{8,0},{9,1},... | collective-permute-start | bytes 196616 | tf_op jit(solution)/shard_map/ppermute | solution.py:747
  (16 other events, 145.3 us)

commit v8 on v7

--- a/solution.py
+++ b/solution.py
@@ -69,25 +69,24 @@
     return jnp.concatenate([half, half], axis=1)
 
 
-def masks(step, start):
-    row = iota((ROWS, WIN), 0) + step * ROWS
-    first = step * ROWS - TAIL
-    key = iota((ROWS, WIN), 1) + first
+def masks(row, start, first):
+    key = iota(row.shape, 1) + first
     floor = jnp.maximum(first, 0)
     causal = key <= row
     near = causal & (key >= jnp.maximum(start, row - (BAND - 1)))
     far = causal & (key >= jnp.maximum(start, floor))
-    return near, far, start < floor, row, floor, first
+    count = 1.0 / (row - start + 1).astype(F32)
+    return jnp.where(near, 0.0, NEG), far.astype(F32), jnp.where(start < floor, -count, count)
 
 
 def near_scores(query, key_heads):
     return mm(query * jnp.asarray(HEAD_DIM**-0.5, BF16), key_heads, NT)
 
 
-def near_weights(scores, near):
+def near_weights(scores, bias):
     parts = []
     for h in range(2):
-        part = jnp.where(near, scores[:, h * WIN : (h + 1) * WIN], NEG)
+        part = scores[:, h * WIN : (h + 1) * WIN] + bias
         parts.append(jnp.exp(part - jnp.max(part, axis=1, keepdims=True)))
     return jnp.concatenate(parts, axis=1)
 
@@ -236,7 +235,9 @@
     scalars,
     qkv_ref,
     message_ref,
-    start_ref,
+    bias_ref,
+    far_ref,
+    tally_ref,
     blend_ref,
     att_ref,
     near_ref,
@@ -260,12 +261,15 @@
         query = qkv_ref[0, pl.ds(at, ROWS), :]
         key = keys[pl.ds(at, WIN), :]
         value = values[pl.ds(at, WIN), :]
-        start = start_ref[pl.ds(at, ROWS), :]
-        near_mask, far_mask, carried, row, floor, first = masks(step, start)
+        first = step * ROWS - TAIL
+        floor = jnp.maximum(first, 0)
+        tally = tally_ref[pl.ds(at, ROWS), :]
+        carried = tally < 0.0
+        far_two = two(far_ref[pl.ds(at, ROWS), :].astype(F32))
         query_f = query.astype(F32)
         key_f = key.astype(F32)
-        lift_q = lift(query_f).astype(BF16)
-        bend_q = jnp.tanh(query_f).astype(BF16)
+        lift_qf, bend_qf = lift(query_f), jnp.tanh(query_f)
+        lift_q, bend_q = lift_qf.astype(BF16), bend_qf.astype(BF16)
         lift_k = lift(key_f)
         bend_k = jnp.tanh(key_f)
         ones = jnp.ones((WIN, PAIR), BF16)
@@ -275,8 +279,10 @@
         scores = near_scores(query, split_heads(key))
         pair_weight = mm(lift_q, split_heads(lift_k.astype(BF16)), NT)
         pair_bend = mm(bend_q, split_heads(bend_k.astype(BF16)), NT)
-        elu_state = mm(lift_q, before_low[:, : 2 * PAIR])
-        tanh_state = mm(bend_q, before_low[:, 2 * PAIR :])
+        elu_state = mm(
+            jnp.where(carried, lift_qf, 0.0).astype(BF16), before_low[:, : 2 * PAIR]
+        )
+        tanh_state = mm(jnp.where(carried, bend_qf, 0.0).astype(BF16), before_low[:, 2 * PAIR :])
         states_ref[0, pl.ds(pl.multiple_of(step * PAIR, PAIR), PAIR), :] = before_low
         closing = scalars[step]
         live = iota((ROWS, PAIR), 0) + first >= jnp.maximum(closing, floor)
@@ -287,19 +293,19 @@
         keep = (closing < floor).astype(F32)
         state[...] = keep * before + block_only(added)
         def finish():
-            far_two = two(far_mask)
-            low_weight = jnp.where(far_two, pair_weight, 0.0).astype(BF16)
-            low_bend = jnp.where(far_two, pair_bend, 0.0).astype(BF16)
+            low_weight = (pair_weight * far_two).astype(BF16)
+            low_bend = (pair_bend * far_two).astype(BF16)
             elu_out = mm(low_weight, value_heads)
-            tanh_out = mm(low_bend, value_heads[:, :PAIR]) + jnp.where(carried, tanh_state, 0.0)
-            weights = near_weights(scores, near_mask).astype(BF16)
+            tanh_out = mm(low_bend, value_heads[:, :PAIR]) + tanh_state
+            weights = near_weights(scores, bias_ref[pl.ds(at, ROWS), :].astype(F32)).astype(BF16)
             near_out = mm(weights, value_heads)
-            numerator = elu_out[:, :PAIR] + jnp.where(carried, elu_state[:, :PAIR], 0.0)
-            inv_d = 1.0 / (elu_out[:, PAIR:] + jnp.where(carried, elu_state[:, PAIR:], 0.0))
+            numerator = elu_out[:, :PAIR] + elu_state[:, :PAIR]
+            inv_d = 1.0 / (elu_out[:, PAIR:] + elu_state[:, PAIR:])
             far1 = numerator * inv_d
             inv_l = 1.0 / near_out[:, PAIR:]
             near = near_out[:, :PAIR] * inv_l
-            far2 = tanh_out / (row - start + 1).astype(F32)
+            far2 = tanh_out * jnp.abs(tally)
+            row = iota((ROWS, PAIR), 0) + at
             mixed = jnp.where(row < count_valid, b0 * near + b1 * far1 + b2 * far2, 0.0)
             att_ref[pl.ds(at, ROWS), :] = mixed.astype(BF16)
             near_ref[pl.ds(at, ROWS), :] = near
@@ -319,8 +325,8 @@
     lax.fori_loop(0, rows // ROWS // 2, body, 0, unroll=2)
 
 
-def near_back(scores, grad_pair, near_mask, spread_near):
-    weights = near_weights(scores, near_mask)
+def near_back(scores, grad_pair, bias, spread_near):
+    weights = near_weights(scores, bias)
     return weights.astype(BF16), (weights * (grad_pair - spread_near)).astype(BF16)
 
 
@@ -342,7 +348,6 @@
 ):
     rows = query_ref.shape[1]
     step_rows = rows // 3
-    count_valid = scalars[scalars.shape[0] + VALID]
     b0, b1, b2 = (blend_ref[pl.ds(f, 1), :] for f in range(3))
     adjoint[...] = jnp.zeros(adjoint.shape, F32)
 
@@ -350,17 +355,18 @@
     key = jnp.concatenate([tails[:, :PAIR], key_ref[0]], axis=0)
     value = jnp.concatenate([tails[:, PAIR : 2 * PAIR], value_ref[0]], axis=0)
     start = start_ref[pl.ds(0, ROWS), :]
-    near_mask, _, _, row, _, _ = masks(0, start)
+    row = iota((ROWS, WIN), 0)
+    bias, _, _ = masks(row, start, -TAIL)
     query = query_ref[0, pl.ds(0, ROWS), :]
-    grad_f = jnp.where(row < count_valid, grad_ref[pl.ds(0, ROWS), :].astype(F32), 0.0)
-    grad = grad_f.astype(BF16)
+    grad = grad_ref[pl.ds(0, ROWS), :]
+    grad_f = grad.astype(F32)
     scale = b0 * invl_ref[...]
     rows_q = (query.astype(F32) * (scale * HEAD_DIM**-0.5)).astype(BF16)
     rows_g = (grad_f * scale).astype(BF16)
     weights, shifted = near_back(
         near_scores(query, split_heads(key)),
         mm(grad, split_heads(value), NT),
-        near_mask,
+        bias,
         spread(grad_f * near_ref[...]),
     )
     d_key = fold(mm(shifted, rows_q, TN))
@@ -378,8 +384,8 @@
             here = pl.ds(at, step_rows)
             row = iota((step_rows, PAIR), 0) + at
             start = start_ref[here, :]
-            grad_f = jnp.where(row < count_valid, grad_ref[here, :].astype(F32), 0.0)
-            grad = grad_f.astype(BF16)
+            grad = grad_ref[here, :]
+            grad_f = grad.astype(F32)
             product = grad_f * far1_ref[here, :]
             high = product.astype(BF16)
             low = (product - high.astype(F32)).astype(BF16)
@@ -411,7 +417,9 @@
     scalars,
     qkv_ref,
     message_ref,
-    start_ref,
+    bias_ref,
+    far_ref,
+    tally_ref,
     blend_ref,
     grad_ref,
     near_ref,
@@ -433,7 +441,6 @@
     rows = qkv_ref.shape[1]
     steps = rows // ROWS
     load_keys(qkv_ref, message_ref, keys, values)
-    count_valid = scalars[scalars.shape[0] + VALID]
     last = scalars[scalars.shape[0] + LAST]
     b0, b1, b2 = (blend_ref[pl.ds(f, 1), :] for f in range(3))
     lanes = iota((ROWS, PAIR), 1) < HEAD_DIM
@@ -464,11 +471,13 @@
         query = qkv_ref[0, pl.ds(at, ROWS), :]
         key = keys[pl.ds(at, WIN), :]
         value = values[pl.ds(at, WIN), :]
-        start = start_ref[pl.ds(at, ROWS), :]
-        near_mask, far_mask, carried, row, floor, first = masks(step, start)
-        far_two = two(far_mask)
-        grad_f = jnp.where(row < count_valid, grad_ref[pl.ds(at, ROWS), :].astype(F32), 0.0)
-        grad = grad_f.astype(BF16)
+        first = step * ROWS - TAIL
+        floor = jnp.maximum(first, 0)
+        tally = tally_ref[pl.ds(at, ROWS), :]
+        carried = tally < 0.0
+        far_two = two(far_ref[pl.ds(at, ROWS), :].astype(F32))
+        grad = grad_ref[pl.ds(at, ROWS), :]
+        grad_f = grad.astype(F32)
         query_f = query.astype(F32)
         key_f = key.astype(F32)
         lift_qf, bend_qf = lift(query_f), jnp.tanh(query_f)
@@ -478,7 +487,7 @@
         lift_heads, bend_heads = split_heads(lift_k), split_heads(bend_k)
         r0 = b0 * invl_ref[pl.ds(at, ROWS), :]
         r1 = b1 * invd_ref[pl.ds(at, ROWS), :]
-        r2 = b2 / (row - start + 1).astype(F32)
+        r2 = b2 * jnp.abs(tally)
         key_heads = split_heads(key)
         before = states_ref[0, pl.ds(pl.multiple_of(step * PAIR, PAIR), PAIR), :]
         near_product = grad_f * near_ref[pl.ds(at, ROWS), :]
@@ -511,11 +520,13 @@
         add_up(8, far1_product)
         add_up(16, grad_f * far2_ref[pl.ds(at, ROWS), :])
         def finish():
-            shifted = jnp.where(far_two, grad_pair - spread_far, 0.0).astype(BF16)
-            plain = jnp.where(far_two, grad_pair, 0.0).astype(BF16)
-            low_weight = jnp.where(far_two, pair_weight, 0.0).astype(BF16)
-            low_bend = jnp.where(far_two, pair_bend, 0.0).astype(BF16)
-            weights, shifted_near = near_back(scores, grad_pair, near_mask, spread_near)
+            shifted = ((grad_pair - spread_far) * far_two).astype(BF16)
+            plain = (grad_pair * far_two).astype(BF16)
+            low_weight = (pair_weight * far_two).astype(BF16)
+            low_bend = (pair_bend * far_two).astype(BF16)
+            weights, shifted_near = near_back(
+                scores, grad_pair, bias_ref[pl.ds(at, ROWS), :].astype(F32), spread_near
+            )
             d_query = mm(shifted_near, key_heads) * (r0 * HEAD_DIM**-0.5)
             d_query = (
                 d_query
@@ -619,7 +630,9 @@
     d_hidden_ref[...] = d_hidden
     d_branch = d_hidden.astype(BF16)
     d_branch_ref[...] = d_branch
-    d_mixed_ref[...] = mm(d_branch, out_weight_ref[...]).astype(BF16)
+    row = iota(hidden.shape, 0) + pl.program_id(0) * hidden.shape[0]
+    d_mixed = mm(d_branch, out_weight_ref[...])
+    d_mixed_ref[...] = jnp.where(row < scalars[scalars.shape[0] + VALID], d_mixed, 0.0).astype(BF16)
 
     @pl.when(pl.program_id(0) == 0)
     def _():
@@ -652,8 +665,8 @@
     input_grad_ref[...] = d_hidden_ref[...] + d_part
 
 
-def resume(kernel, done, scalars, qkv_ref, message_ref, start_ref, blend_ref, *refs):
-    kernel(scalars, qkv_ref, message_ref, start_ref, blend_ref, *refs[done:])
+def resume(kernel, ins, done, *refs):
+    kernel(*refs[:ins], *refs[ins + done :])
 
 
 def pair_specs(rows, first=0):
@@ -833,6 +846,9 @@
         ]
     )
     start_wide = jnp.broadcast_to(start[:, None], (rows, PAIR))
+    row_wide = jnp.broadcast_to(local[:, None], (rows, PAIR))
+    bias, far, tally = masks(row_wide, start_wide, row_wide // ROWS * ROWS - TAIL)
+    tables = (bias.astype(BF16), far.astype(BF16), tally)
     keep_all = (start[rows - 1] < 0).astype(F32)
     blend_wide = jnp.repeat(blend, HEAD_DIM, axis=1)
 
@@ -846,6 +862,7 @@
     def whole_spec(shape):
         return pl.BlockSpec(shape, lambda p, s: (0,) * len(shape))
 
+    others, start_wide, tables = lax.optimization_barrier((others, start_wide, tables))
     qkv, normed_one, qkv_all, out_all, closing = call(
         functools.partial(project_kernel, flips=flips),
         [
@@ -889,8 +906,10 @@
     for first, count in ((0, most), (most, pairs - most)):
         spec = pair_specs(rows, first)
         results = call(
-            functools.partial(resume, forward_kernel, len(results)),
-            [spec["qkv"], spec["message"], spec["start"], spec["blend"]]
+            functools.partial(resume, forward_kernel, 7, len(results)),
+            [spec["qkv"], spec["message"]]
+            + [spec["start"]] * 3
+            + [spec["blend"]]
             + [pl.BlockSpec(memory_space=pl.ANY)] * len(results),
             [spec["column"]] * 6 + [spec["states"]],
             [jax.ShapeDtypeStruct((rows, width), BF16)] + [wide] * 5 + [states_shape],
@@ -899,8 +918,8 @@
             "forward",
             8000 * big * count // pairs,
             40 * big * count // pairs,
-            {5 + i: i for i in range(len(results))},
-        )(scalars, qkv, message, start_wide, blend_wide, *results)
+            {7 + i: i for i in range(len(results))},
+        )(scalars, qkv, message, *tables, blend_wide, *results)
         if not first:
             feed, results = widen(feed, groups[1], 1, results)
             feed, message = lax.optimization_barrier((feed, message))
@@ -978,6 +997,8 @@
             12 * big,
         )(scalars, normed_two, cotangent, active, d_inner, *more_ins)
 
+    (give,) = feed_grad(1, BF16, d_inner, [], [], [], [])
+    d_inner, _ = lax.optimization_barrier((d_inner, give))
     out_grad, keep = feed_grad(
         0,
         F32,
@@ -987,20 +1008,22 @@
         [jax.ShapeDtypeStruct((width, width), F32)],
         [whole_spec((width, width))],
     )
-    d_inner, back_in, out_grad = lax.optimization_barrier((d_inner, back_in, out_grad))
-    (give,) = feed_grad(1, BF16, d_inner, [], [], [], [])
     feed_share = narrow(keep, [give], groups[-1])
     left = list(reversed(groups[:-1]))
+    _, back_in = lax.optimization_barrier((feed_share, back_in))
+    feed_share = narrow_axis(feed_share, left.pop(0), 1)
 
     d_qkv = jnp.zeros((3, 8, PAIR), BF16)
     sums = []
     first = 0
-    for count in (pairs // 4, pairs // 2, pairs // 4):
+    for count in (most, pairs - most):
         spec = pair_specs(rows, first)
-        more = {13: 0} if first else {}
+        more = {15: 0} if first else {}
         d_qkv, part_sums = call(
             backward_kernel,
-            [spec["qkv"], spec["message"], spec["start"], spec["blend"]]
+            [spec["qkv"], spec["message"]]
+            + [spec["start"]] * 3
+            + [spec["blend"]]
             + [spec["column"]] * 6
             + [spec["states"], spec["message"], pl.BlockSpec(memory_space=pl.ANY)],
             [spec["qkv"], spec["sums"]],
@@ -1018,7 +1041,7 @@
             scalars,
             qkv,
             message,
-            start_wide,
+            *tables,
             blend_wide,
             d_mixed,
             near,
@@ -1070,21 +1093,19 @@
     total_sums = total_sums + peer(total_sums, [hops[0]], 1)
     total_sums, d_qkv, _ = lax.optimization_barrier((total_sums, d_qkv, share))
     total_sums = total_sums + peer(total_sums, [hops[1]], 1)
-    fine = rows // 6
-    fine_spec = pl.BlockSpec((fine, width), lambda p, s: (p, 0))
     input_grad = call(
         input_kernel,
         [
-            pl.BlockSpec((3, fine, width), lambda p, s: (0, p, 0)),
+            pl.BlockSpec((3, part, width), lambda p, s: (0, p, 0)),
             whole_spec((3, width, width)),
-            fine_spec,
-            fine_spec,
+            row_spec,
+            row_spec,
             whole_spec((1, width)),
         ],
-        fine_spec,
+        row_spec,
         wide,
         [],
-        6,
+        3,
         "input",
         6 * big * width,
         24 * big,

time: 258 us -> 254 us (0.984)
  Pallas kernels: 155 us -> 148 us
  other arithmetic: 10.8 us -> 17.2 us
  waiting for transfers between devices: 28.1 us -> 23.4 us
    pallas_call x6 -> x5, Pallas kernels: 82.8 us -> 76.3 us  [the longest x2 40.8 us: per_device(): call(backward_kernel, [spec['qkv'], spec['message']] + [spec['start']] *...]
    ppermute x32, waiting for transfers between devices: 25.8 us -> 21.6 us  [peer(): return lax.ppermute(array, ('dp', 'head'), pairs)]
    select_n x0 -> x1, other arithmetic: none -> 3.29 us  [masks(): jnp.where(start < floor, -count, count)]
  transfers between devices with their start and end apart: 34 -> 34, of which waited for: 14 -> 10; matrix products, arithmetic and copies ran while one was open for 6% -> 10% of each run, Pallas kernels for 40% -> 39%
where the time goes in v8:
time: 254 us; the launch traced here: 252 us
  Pallas kernels  148 us (58%)
  starting transfers between devices  47.9 us (19%)
  waiting for transfers between devices  23.4 us (9%)
  other arithmetic  17.2 us (7%)
  local copies, waits for them, and re-layouts  13.9 us (5%)
    ppermute x32, starting transfers between devices, peer(): return lax.ppermute(array, ('dp', 'head'), pairs)  42.8 us
    pallas_call x2, Pallas kernels, per_device(): call(backward_kernel, [spec['qkv'], spec['message']] + [spec['start']] *...  40.8 us
    pallas_call x2, Pallas kernels, per_device(): call(functools.partial(resume, forward_kernel, 7, len(results)), [spec['q...  26.6 us
    pallas_call x1, Pallas kernels, per_device(): call(feed_kernel, [row_spec] * 3 + [whole_spec((width, width)), whole_spe...  26.1 us
    ppermute x32, waiting for transfers between devices, peer(): return lax.ppermute(array, ('dp', 'head'), pairs)  21.6 us
    pallas_call x2, Pallas kernels, feed_grad(): call(feed_grad_kernel, [whole_rows] * 2 + [columns] * 2 + more_in_specs,...  19.2 us
    pallas_call x1, Pallas kernels, per_device(): call(functools.partial(project_kernel, flips=flips), [pl.BlockSpec((part,...  10.2 us
    pallas_call x1, Pallas kernels, per_device(): call(functools.partial(weight_grad_kernel, flips=flips), [whole_spec((row...  8.87 us
  transfers between devices with their start and end apart: 34, of which 10 were waited for; matrix products, arithmetic and copies ran while one was open for 10% of the time, Pallas kernels for 39%

profile of v8, /device:TPU:0, one launch (start us, length us, event | category | flops | bytes accessed | tf_op | source)
XLA Modules:
  0.0 252.4 jit_solution(15245362860012500503)
XLA Ops:
  1.5 5.1 %collective-permute-start.2 = (bf16[1,4,32,256]{3,2,1,0:T(8,128)(2,1)S(1)}, bf16[1,4,32,256]{3,2,1,0:T(8,128)(2,1)S(1)}, u32[]{:S(2)}, u32[]{:S(2)}) collective-permute-start(bf16[1,4,32,256]{3,2,1,0:T(8,128)(2,1)S(1)} %maximum_bitcast_fusion), channel_id=1, source_target_pairs={{0,24},{1,25},{2,26},{3,27},{4,28},{5,29},{6,30},{7,31},{8,16},{9,... | collective-permute-start | bytes 196616 | tf_op jit(solution)/shard_map/ppermute | solution.py:760
  13.8 1.9 concatenate.29.scalars.refs_0_
  15.8 2.7 %collective-permute-start.5 = (bf16[4,4,32,256]{3,2,1,0:T(8,128)(2,1)S(1)}, bf16[4,4,32,256]{3,2,1,0:T(8,128)(2,1)S(1)}, u32[]{:S(2)}, u32[]{:S(2)}) collective-permute-start(bf16[4,4,32,256]{3,2,1,0:T(8,128)(2,1)S(1)} %pad_maximum_fusion), channel_id=1, source_target_pairs={{0,5},{1,4},{2,7},{3,6},{4,1},{5,0},{6,3},{7,2},{8,13},{9,12},{10,... | collective-permute-start | bytes 786440 | tf_op jit(solution)/shard_map/ppermute | solution.py:760
  20.8 3.6 %collective-permute-done.6 = bf16[2,64,512]{2,1,0:T(8,128)(2,1)S(1)} collective-permute-done((bf16[2,64,512]{2,1,0:T(8,128)(2,1)S(1)}, bf16[2,64,512]{2,1,0:T(8,128)(2,1)S(1)}, u32[]{:S(2)}, u32[]{:S(2)}) %collective-permute-start.6) | collective-permute-done | bytes 131104 | tf_op jit(solution)/shard_map/ppermute | solution.py:760
  24.4 5.5 %collective-permute-done.3 = bf16[4,4,32,256]{3,2,1,0:T(8,128)(2,1)S(1)} collective-permute-done((bf16[4,4,32,256]{3,2,1,0:T(8,128)(2,1)S(1)}, bf16[4,4,32,256]{3,2,1,0:T(8,128)(2,1)S(1)}, u32[]{:S(2)}, u32[]{:S(2)}) %collective-permute-start.3) | collective-permute-done | bytes 262176 | tf_op jit(solution)/shard_map/ppermute | solution.py:760
  30.1 2.4 convert_convert_fusion.refs_4_.far_ref
  32.5 3.3 %fusion.6 = (f32[1536,128]{1,0:T(8,128)}, bf16[1536,128]{1,0:T(8,128)(2,1)}) fusion(f32[1536]{0:T(1024)S(1)} %convert_divide_fusion, f32[1536]{0:T(1024)S(1)} %get-tuple-element.157, s32[1536]{0:T(1024)S(1)} %get-tuple-element.184, s32[1536]{0:T(1024)S(1)} %get-tuple-element.185, s32[1536]{0:T(1024)S(1)} %get-tuple-element.158, ...), kind=kLoop, calls=%fused_computation.14 | loop fusion | flops 2359296 | bytes 1218048 | tf_op jit(solution)/shard_map/jit(_where)/select_n | solution.py:79
  35.8 2.3 collective-permute-start.8
  39.4 10.2 %project.1 = (bf16[3,1536,512]{2,1,0:T(8,128)(2,1)}, bf16[1536,512]{1,0:T(8,128)(2,1)}, bf16[3,512,512]{2,1,0:T(8,128)(2,1)}, bf16[512,512]{1,0:T(8,128)(2,1)}, bf16[4,96,384]{2,1,0:T(8,128)(2,1)}) custom-call(s32[21]{0:T(128)} %concatenate.29.scalars.refs_0_, bf16[1536,512]{1,0:T(8,128)(2,1)} %tokens_ref.5, f32[1,512]{1,0:T(1,128)} %bitcast.34, ...), custom_call_target="tpu_custom_call" | custom-call | flops 2415919104 | bytes 9437184 | tf_op jit(solution)/shard_map/project/pallas_call | solution.py:866
  49.5 3.6 %collective-permute-start.12 = (bf16[4,96,384]{2,1,0:T(8,128)(2,1)}, bf16[4,96,384]{2,1,0:T(8,128)(2,1)S(1)}, u32[]{:S(2)}, u32[]{:S(2)}) collective-permute-start(bf16[4,96,384]{2,1,0:T(8,128)(2,1)} %get-tuple-element.84), channel_id=1, source_target_pairs={{0,1},{2,3},{4,5},{6,7},{8,9},{10,11},{12,13},{14,15},{16,17},{18,... | collective-permute-start | bytes 884744 | tf_op jit(solution)/shard_map/ppermute | solution.py:786
  54.9 2.7 %collective-permute-start.10 = (bf16[2,256,512]{2,1,0:T(8,128)(2,1)S(1)}, bf16[2,256,512]{2,1,0:T(8,128)(2,1)S(1)}, u32[]{:S(2)}, u32[]{:S(2)}) collective-permute-start(bf16[2,256,512]{2,1,0:T(8,128)(2,1)S(1)} %get-tuple-element.174), channel_id=1, source_target_pairs={{0,1},{1,0},{2,3},{3,2},{4,5},{5,4},{6,7},{7,6},{8,9},{9,8},{10,11... | collective-permute-start | bytes 1572872 | tf_op jit(solution)/shard_map/ppermute | solution.py:760
  58.9 1.7 collective-permute-done.12.refs_2_.message_ref
  61.3 17.5 %forward.2 = (bf16[1536,512]{1,0:T(8,128)(2,1)}, f32[1536,512]{1,0:T(8,128)}, f32[1536,512]{1,0:T(8,128)}, f32[1536,512]{1,0:T(8,128)}, f32[1536,512]{1,0:T(8,12...) custom-call(s32[21]{0:T(128)} %concatenate.29.scalars.refs_0_, ...), custom_call_target="tpu_custom_call" | custom-call | flops 4718592000 | bytes 23592960 | tf_op jit(solution)/shard_map/forward/pallas_call | solution.py:908
  78.9 3.4 %collective-permute-done.10 = bf16[2,256,512]{2,1,0:T(8,128)(2,1)S(1)} collective-permute-done((bf16[2,256,512]{2,1,0:T(8,128)(2,1)S(1)}, bf16[2,256,512]{2,1,0:T(8,128)(2,1)S(1)}, u32[]{:S(2)}, u32[]{:S(2)}) %collective-permute-start.10) | collective-permute-done | bytes 524320 | tf_op jit(solution)/shard_map/ppermute | solution.py:760
  82.5 9.1 %forward.3 = (bf16[1536,512]{1,0:T(8,128)(2,1)}, f32[1536,512]{1,0:T(8,128)}, f32[1536,512]{1,0:T(8,128)}, f32[1536,512]{1,0:T(8,128)}, f32[1536,512]{1,0:T(8,12...) custom-call(s32[21]{0:T(128)} %concatenate.29.scalars.refs_0_, ...), custom_call_target="tpu_custom_call", output_to_operand_aliasing={{0}: (7, {}), {1}: (8, {}), {2}: (9, {}), {3}: (10, {}), {4... | custom-call | flops 1572864000 | bytes 7864320 | tf_op jit(solution)/shard_map/forward/pallas_call | solution.py:908
  92.9 26.1 %feed.1 = (bf16[1536,512]{1,0:T(8,128)(2,1)}, f32[1536,512]{1,0:T(8,128)}, bf16[1536,512]{1,0:T(8,128)(2,1)}, bf16[1536,512]{1,0:T(8,128)(2,1)}, bf16[1536,512]{...) custom-call(s32[21]{0:T(128)} %concatenate.29.scalars.refs_0_, ...), custom_call_target="tpu_custom_call" | custom-call | flops 12884901888 | bytes 25165824 | tf_op jit(solution)/shard_map/feed/pallas_call | solution.py:938
  119.0 7.7 %prologue.1 = bf16[4,96,384]{2,1,0:T(8,128)(2,1)} custom-call(s32[21]{0:T(128)} %concatenate.29.scalars.refs_0_, bf16[3,1536,512]{2,1,0:T(8,128)(2,1)} %get-tuple-element.82.refs_1_.query_ref.key_ref.value_ref.qkv_ref, bf16[3,1536,512]{2,1,0:T(8,128)(2,1)} %get-tuple-element.82.refs_1_.query_ref.key_ref.value_ref.qkv_ref, ...), custom_call_target="tpu_custom_call" | custom-call | flops 393216000 | bytes 15728640 | tf_op jit(solution)/shard_map/prologue/pallas_call | solution.py:956
  126.7 8.4 %feed_grad.2 = bf16[2,1024,512]{2,1,0:T(8,128)(2,1)} custom-call(s32[21]{0:T(128)} %concatenate.29.scalars.refs_0_, bf16[1536,512]{1,0:T(8,128)(2,1)} %get-tuple-element.112.normed_ref, bf16[1536,512]{1,0:T(8,128)(2,1)} %cotangent_ref.5, bf16[1536,2048]{1,0:T(8,128)(2,1)} %get-tuple-element.113.active_ref, bf16[1536,2048]{1,0:T(8,128)(2,1)} %get-tuple-element.122.d_inner_ref), custom_call_target="tpu_custom_call" | custom-call | flops 3221225472 | bytes 9437184 | tf_op jit(solution)/shard_map/feed_grad/pallas_call | solution.py:988
  137.1 10.8 %feed_grad.3 = (f32[512,512]{1,0:T(8,128)}, f32[2,1024,512]{2,1,0:T(8,128)}) custom-call(s32[21]{0:T(128)} %concatenate.29.scalars.refs_0_, bf16[1536,512]{1,0:T(8,128)(2,1)} %get-tuple-element.112.normed_ref, bf16[1536,512]{1,0:T(8,128)(2,1)} %cotangent_ref.5, bf16[1536,2048]{1,0:T(8,128)(2,1)} %get-tuple-element.113.active_ref, ...), custom_call_target="tpu_custom_call" | custom-call | flops 3221225472 | bytes 9437184 | tf_op jit(solution)/shard_map/feed_grad/pallas_call | solution.py:988
  147.9 3.1 %fusion.17 = (bf16[2,1024,512]{2,1,0:T(8,128)(2,1)S(1)}, f32[2,1024,512]{2,1,0:T(8,128)S(1)}) fusion(f32[2,1024,512]{2,1,0:T(8,128)} %get-tuple-element.124, bf16[2,1024,512]{2,1,0:T(8,128)(2,1)S(1)} %collective-permute-done.14), kind=kLoop, calls=%fused_computation.69 | loop fusion | flops 3145728 | bytes 12582912 | tf_op jit(solution)/shard_map/convert.11
  152.7 6.7 %collective-permute-start.17 = (bf16[2,256,512]{2,1,0:T(8,128)(2,1)S(1)}, bf16[2,256,512]{2,1,0:T(8,128)(2,1)S(1)}, u32[]{:S(2)}, u32[]{:S(2)}) collective-permute-start(bf16[2,256,512]{2,1,0:T(8,128)(2,1)S(1)} %get-tuple-element.161), channel_id=1, source_target_pairs={{0,5},{1,4},{2,7},{3,6},{4,1},{5,0},{6,3},{7,2},{8,13},{9,12},{10,... | collective-permute-start | bytes 1572872 | tf_op jit(solution)/shard_map/ppermute | solution.py:760
  160.0 28.1 %backward.2 = (bf16[3,1536,512]{2,1,0:T(8,128)(2,1)}, f32[24,384]{1,0:T(8,128)}) custom-call(s32[21]{0:T(128)} %concatenate.29.scalars.refs_0_, bf16[3,1536,512]{2,1,0:T(8,128)(2,1)} %get-tuple-element.82.refs_1_.query_ref.key_ref.value_ref.qkv_ref, bf16[4,96,384]{2,1,0:T(8,128)(2,1)} %copy-done, bf16[1536,128]{1,0:T(8,128)(2,1)} %get-tuple-element.86.refs_3_.bias_ref, ...), custom_call_target="tpu_custom_call" | custom-call | flops 9437184000 | bytes 23592960 | tf_op jit(solution)/shard_map/backward/pallas_call | solution.py:1022
  189.2 2.9 %collective-permute-start.19 = (bf16[2,64,512]{2,1,0:T(8,128)(2,1)S(1)}, bf16[2,64,512]{2,1,0:T(8,128)(2,1)S(1)}, u32[]{:S(2)}, u32[]{:S(2)}) collective-permute-start(bf16[2,64,512]{2,1,0:T(8,128)(2,1)S(1)} %get-tuple-element.168), channel_id=1, source_target_pairs={{0,16},{1,17},{2,18},{3,19},{4,20},{5,21},{6,22},{7,23},{8,24},{9,... | collective-permute-start | bytes 393224 | tf_op jit(solution)/shard_map/ppermute | solution.py:760
  192.0 12.7 %backward.3 = (bf16[3,1536,512]{2,1,0:T(8,128)(2,1)}, f32[24,128]{1,0:T(8,128)}) custom-call(s32[21]{0:T(128)} %concatenate.29.scalars.refs_0_, bf16[3,1536,512]{2,1,0:T(8,128)(2,1)} %get-tuple-element.82.refs_1_.query_ref.key_ref.value_ref.qkv_ref, bf16[4,96,384]{2,1,0:T(8,128)(2,1)} %copy-done, ...), custom_call_target="tpu_custom_call", output_to_operand_aliasing={{0}: (15, {})} | custom-call | flops 3145728000 | bytes 7864320 | tf_op jit(solution)/shard_map/backward/pallas_call | solution.py:1022
  204.8 8.9 %weight_grad.1 = (f32[16,4,32,256]{3,2,1,0:T(8,128)}, bf16[16,4,32,256]{3,2,1,0:T(8,128)(2,1)}, f32[8,512]{1,0:T(8,128)}) custom-call(s32[21]{0:T(128)} %concatenate.29.scalars.refs_0_, bf16[1536,512]{1,0:T(8,128)(2,1)} %get-tuple-element.111.normed_ref, bf16[3,1536,512]{2,1,0:T(8,128)(2,1)} %get-tuple-element.140.d_qkv_ref, ...), custom_call_target="tpu_custom_call" | custom-call | flops 2415919104 | bytes 6291456 | tf_op jit(solution)/shard_map/weight_grad/pallas_call | solution.py:1069
  216.6 2.1 fusion.15
  222.4 2.1 collective-permute-start.24
  224.4 8.9 %input.1 = f32[1536,512]{1,0:T(8,128)} custom-call(s32[21]{0:T(128)} %concatenate.29.scalars.refs_0_, bf16[3,1536,512]{2,1,0:T(8,128)(2,1)} %get-tuple-element.140.d_qkv_ref, bf16[3,512,512]{2,1,0:T(8,128)(2,1)} %get-tuple-element.133.weight_ref, bf16[1536,512]{1,0:T(8,128)(2,1)} %tokens_ref.5, f32[1536,512]{1,0:T(8,128)} %get-tuple-element.141.d_hidden_ref, ...), custom_call_target="tpu_custom_call" | custom-call | flops 2415919104 | bytes 18874368 | tf_op jit(solution)/shard_map/input/pallas_call | solution.py:1096
  234.4 2.6 %collective-permute-done.25 = f32[1,1048]{1,0:T(1,128)S(1)} collective-permute-done((f32[1,1048]{1,0:T(1,128)S(1)}, f32[1,1048]{1,0:T(1,128)S(1)}, u32[]{:S(2)}, u32[]{:S(2)}) %collective-permute-start.25) | collective-permute-done | bytes 4224 | tf_op jit(solution)/shard_map/ppermute | solution.py:760
  237.8 4.0 %collective-permute-done.29 = f32[1,1048]{1,0:T(1,128)S(1)} collective-permute-done((f32[1,1048]{1,0:T(1,128)S(1)}, f32[1,1048]{1,0:T(1,128)S(1)}, u32[]{:S(2)}, u32[]{:S(2)}) %collective-permute-start.29) | collective-permute-done | bytes 4224 | tf_op jit(solution)/shard_map/ppermute | solution.py:760
  241.8 1.6 collective-permute-start.30
  246.0 2.5 %collective-permute-start.31 = (bf16[1,4,32,256]{3,2,1,0:T(8,128)(2,1)S(1)}, bf16[1,4,32,256]{3,2,1,0:T(8,128)(2,1)S(1)}, u32[]{:S(2)}, u32[]{:S(2)}) collective-permute-start(bf16[1,4,32,256]{3,2,1,0:T(8,128)(2,1)S(1)} %get-tuple-element.173), channel_id=1, source_target_pairs={{0,8},{1,9},{2,10},{3,11},{4,12},{5,13},{6,14},{7,15},{8,0},{9,1},... | collective-permute-start | bytes 196616 | tf_op jit(solution)/shard_map/ppermute | solution.py:760
  (138 shorter events, 36.8 us)
Async XLA Ops:
  1.5 14.3 %collective-permute-start.2 = (bf16[1,4,32,256]{3,2,1,0:T(8,128)(2,1)S(1)}, bf16[1,4,32,256]{3,2,1,0:T(8,128)(2,1)S(1)}, u32[]{:S(2)}, u32[]{:S(2)}) collective-permute-start(bf16[1,4,32,256]{3,2,1,0:T(8,128)(2,1)S(1)} %maximum_bitcast_fusion), channel_id=1, source_target_pairs={{0,24},{1,25},{2,26},{3,27},{4,28},{5,29},{6,30},{7,31},{8,16},{9,... | collective-permute-start | bytes 196616 | tf_op jit(solution)/shard_map/ppermute | solution.py:760
  6.6 9.2 %collective-permute-start.1 = (bf16[1,4,32,256]{3,2,1,0:T(8,128)(2,1)S(1)}, bf16[1,4,32,256]{3,2,1,0:T(8,128)(2,1)S(1)}, u32[]{:S(2)}, u32[]{:S(2)}) collective-permute-start(bf16[1,4,32,256]{3,2,1,0:T(8,128)(2,1)S(1)} %maximum_bitcast_fusion), channel_id=1, source_target_pairs={{0,16},{1,17},{2,18},{3,19},{4,20},{5,21},{6,22},{7,23},{8,24},{9,... | collective-permute-start | bytes 196616 | tf_op jit(solution)/shard_map/ppermute | solution.py:760
  6.6 9.2 %collective-permute-start = (bf16[1,4,32,256]{3,2,1,0:T(8,128)(2,1)S(1)}, bf16[1,4,32,256]{3,2,1,0:T(8,128)(2,1)S(1)}, u32[]{:S(2)}, u32[]{:S(2)}) collective-permute-start(bf16[1,4,32,256]{3,2,1,0:T(8,128)(2,1)S(1)} %maximum_bitcast_fusion), channel_id=1, source_target_pairs={{0,8},{1,9},{2,10},{3,11},{4,12},{5,13},{6,14},{7,15},{8,0},{9,1},... | collective-permute-start | bytes 196616 | tf_op jit(solution)/shard_map/ppermute | solution.py:760
  15.8 14.2 %collective-permute-start.5 = (bf16[4,4,32,256]{3,2,1,0:T(8,128)(2,1)S(1)}, bf16[4,4,32,256]{3,2,1,0:T(8,128)(2,1)S(1)}, u32[]{:S(2)}, u32[]{:S(2)}) collective-permute-start(bf16[4,4,32,256]{3,2,1,0:T(8,128)(2,1)S(1)} %pad_maximum_fusion), channel_id=1, source_target_pairs={{0,5},{1,4},{2,7},{3,6},{4,1},{5,0},{6,3},{7,2},{8,13},{9,12},{10,... | collective-permute-start | bytes 786440 | tf_op jit(solution)/shard_map/ppermute | solution.py:760
  18.5 11.5 %collective-permute-start.4 = (bf16[4,4,32,256]{3,2,1,0:T(8,128)(2,1)S(1)}, bf16[4,4,32,256]{3,2,1,0:T(8,128)(2,1)S(1)}, u32[]{:S(2)}, u32[]{:S(2)}) collective-permute-start(bf16[4,4,32,256]{3,2,1,0:T(8,128)(2,1)S(1)} %pad_maximum_fusion), channel_id=1, source_target_pairs={{0,1},{1,0},{2,3},{3,2},{4,5},{5,4},{6,7},{7,6},{8,9},{9,8},{10,11... | collective-permute-start | bytes 786440 | tf_op jit(solution)/shard_map/ppermute | solution.py:760
  19.0 10.9 %collective-permute-start.3 = (bf16[4,4,32,256]{3,2,1,0:T(8,128)(2,1)S(1)}, bf16[4,4,32,256]{3,2,1,0:T(8,128)(2,1)S(1)}, u32[]{:S(2)}, u32[]{:S(2)}) collective-permute-start(bf16[4,4,32,256]{3,2,1,0:T(8,128)(2,1)S(1)} %pad_maximum_fusion), channel_id=1, source_target_pairs={{0,4},{1,5},{2,6},{3,7},{4,0},{5,1},{6,2},{7,3},{8,12},{9,13},{10,... | collective-permute-start | bytes 786440 | tf_op jit(solution)/shard_map/ppermute | solution.py:760
  19.4 5.0 %collective-permute-start.6 = (bf16[2,64,512]{2,1,0:T(8,128)(2,1)S(1)}, bf16[2,64,512]{2,1,0:T(8,128)(2,1)S(1)}, u32[]{:S(2)}, u32[]{:S(2)}) collective-permute-start(bf16[2,64,512]{2,1,0:T(8,128)(2,1)S(1)} %pad_maximum_fusion.2), channel_id=1, source_target_pairs={{0,8},{1,9},{2,10},{3,11},{4,12},{5,13},{6,14},{7,15},{8,0},{9,1},... | collective-permute-start | bytes 393224 | tf_op jit(solution)/shard_map/ppermute | solution.py:760
  30.1 8.1 %collective-permute-start.7 = (bf16[16,4,32,256]{3,2,1,0:T(8,128)(2,1)S(1)}, bf16[16,4,32,256]{3,2,1,0:T(8,128)(2,1)S(1)}, u32[]{:S(2)}, u32[]{:S(2)}) collective-permute-start(bf16[16,4,32,256]{3,2,1,0:T(8,128)(2,1)S(1)} %constant_dynamic-update-slice_fusion.own_ref), channel_id=1, source_target_pairs={{0,2},{1,3},{2,0},{3,1},{4,6},{5,7},{6,4},{7,5},{8,10},{9,11},{10,... | collective-permute-start | bytes 3145736 | tf_op jit(solution)/shard_map/ppermute | solution.py:760
  35.8 18.1 %collective-permute-start.8 = (bf16[2,128,512]{2,1,0:T(8,128)(2,1)S(1)}, bf16[2,128,512]{2,1,0:T(8,128)(2,1)S(1)}, u32[]{:S(2)}, u32[]{:S(2)}) collective-permute-start(bf16[2,128,512]{2,1,0:T(8,128)(2,1)S(1)} %pad_maximum_fusion.1), channel_id=1, source_target_pairs={{0,16},{1,17},{2,18},{3,19},{4,20},{5,21},{6,22},{7,23},{8,24},{9,... | collective-permute-start | bytes 786440 | tf_op jit(solution)/shard_map/ppermute | solution.py:760
  49.5 11.1 %collective-permute-start.12 = (bf16[4,96,384]{2,1,0:T(8,128)(2,1)}, bf16[4,96,384]{2,1,0:T(8,128)(2,1)S(1)}, u32[]{:S(2)}, u32[]{:S(2)}) collective-permute-start(bf16[4,96,384]{2,1,0:T(8,128)(2,1)} %get-tuple-element.84), channel_id=1, source_target_pairs={{0,1},{2,3},{4,5},{6,7},{8,9},{10,11},{12,13},{14,15},{16,17},{18,... | collective-permute-start | bytes 884744 | tf_op jit(solution)/shard_map/ppermute | solution.py:786
  54.6 24.3 %collective-permute-start.11 = (bf16[2,256,512]{2,1,0:T(8,128)(2,1)S(1)}, bf16[2,256,512]{2,1,0:T(8,128)(2,1)S(1)}, u32[]{:S(2)}, u32[]{:S(2)}) collective-permute-start(bf16[2,256,512]{2,1,0:T(8,128)(2,1)S(1)} %get-tuple-element.174), channel_id=1, source_target_pairs={{0,5},{1,4},{2,7},{3,6},{4,1},{5,0},{6,3},{7,2},{8,13},{9,12},{10,... | collective-permute-start | bytes 1572872 | tf_op jit(solution)/shard_map/ppermute | solution.py:760
  54.9 27.4 %collective-permute-start.10 = (bf16[2,256,512]{2,1,0:T(8,128)(2,1)S(1)}, bf16[2,256,512]{2,1,0:T(8,128)(2,1)S(1)}, u32[]{:S(2)}, u32[]{:S(2)}) collective-permute-start(bf16[2,256,512]{2,1,0:T(8,128)(2,1)S(1)} %get-tuple-element.174), channel_id=1, source_target_pairs={{0,1},{1,0},{2,3},{3,2},{4,5},{5,4},{6,7},{7,6},{8,9},{9,8},{10,11... | collective-permute-start | bytes 1572872 | tf_op jit(solution)/shard_map/ppermute | solution.py:760
  57.6 24.7 %collective-permute-start.9 = (bf16[2,256,512]{2,1,0:T(8,128)(2,1)S(1)}, bf16[2,256,512]{2,1,0:T(8,128)(2,1)S(1)}, u32[]{:S(2)}, u32[]{:S(2)}) collective-permute-start(bf16[2,256,512]{2,1,0:T(8,128)(2,1)S(1)} %get-tuple-element.174), channel_id=1, source_target_pairs={{0,4},{1,5},{2,6},{3,7},{4,0},{5,1},{6,2},{7,3},{8,12},{9,13},{10,... | collective-permute-start | bytes 1572872 | tf_op jit(solution)/shard_map/ppermute | solution.py:760
  82.4 9.2 %collective-permute-start.13 = (bf16[2,1024,512]{2,1,0:T(8,128)(2,1)S(1)}, bf16[2,1024,512]{2,1,0:T(8,128)(2,1)S(1)}, u32[]{:S(2)}, u32[]{:S(2)}) collective-permute-start(bf16[2,1024,512]{2,1,0:T(8,128)(2,1)S(1)} %constant_dynamic-update-slice_fusion.9.own_ref), channel_id=1, source_target_pairs={{0,2},{1,3},{2,0},{3,1},{4,6},{5,7},{6,4},{7,5},{8,10},{9,11},{10,... | collective-permute-start | bytes 6291464 | tf_op jit(solution)/shard_map/ppermute | solution.py:760
  135.1 12.8 %collective-permute-start.14 = (bf16[2,1024,512]{2,1,0:T(8,128)(2,1)}, bf16[2,1024,512]{2,1,0:T(8,128)(2,1)S(1)}, u32[]{:S(2)}, u32[]{:S(2)}) collective-permute-start(bf16[2,1024,512]{2,1,0:T(8,128)(2,1)} %feed_grad.2), channel_id=1, source_target_pairs={{0,2},{1,3},{2,0},{3,1},{4,6},{5,7},{6,4},{7,5},{8,10},{9,11},{10,... | collective-permute-start | bytes 6291464 | tf_op jit(solution)/shard_map/ppermute | solution.py:760
  135.6 15.6 %collective-permute-start.21 = (bf16[4,96,384]{2,1,0:T(8,128)(2,1)S(1)}, bf16[4,96,384]{2,1,0:T(8,128)(2,1)S(1)}, u32[]{:S(2)}, u32[]{:S(2)}) collective-permute-start(bf16[4,96,384]{2,1,0:T(8,128)(2,1)S(1)} %copy-done.1), channel_id=1, source_target_pairs={{1,0},{3,2},{5,4},{7,6},{9,8},{11,10},{13,12},{15,14},{17,16},{19,... | collective-permute-start | bytes 884744 | tf_op jit(solution)/shard_map/ppermute | solution.py:786
  151.2 36.9 %collective-permute-start.15 = (bf16[2,256,512]{2,1,0:T(8,128)(2,1)S(1)}, bf16[2,256,512]{2,1,0:T(8,128)(2,1)S(1)}, u32[]{:S(2)}, u32[]{:S(2)}) collective-permute-start(bf16[2,256,512]{2,1,0:T(8,128)(2,1)S(1)} %get-tuple-element.160), channel_id=1, source_target_pairs={{0,4},{1,5},{2,6},{3,7},{4,0},{5,1},{6,2},{7,3},{8,12},{9,13},{10,... | collective-permute-start | bytes 1572872 | tf_op jit(solution)/shard_map/ppermute | solution.py:760
  152.7 35.4 %collective-permute-start.17 = (bf16[2,256,512]{2,1,0:T(8,128)(2,1)S(1)}, bf16[2,256,512]{2,1,0:T(8,128)(2,1)S(1)}, u32[]{:S(2)}, u32[]{:S(2)}) collective-permute-start(bf16[2,256,512]{2,1,0:T(8,128)(2,1)S(1)} %get-tuple-element.161), channel_id=1, source_target_pairs={{0,5},{1,4},{2,7},{3,6},{4,1},{5,0},{6,3},{7,2},{8,13},{9,12},{10,... | collective-permute-start | bytes 1572872 | tf_op jit(solution)/shard_map/ppermute | solution.py:760
  159.4 28.8 %collective-permute-start.16 = (bf16[2,256,512]{2,1,0:T(8,128)(2,1)S(1)}, bf16[2,256,512]{2,1,0:T(8,128)(2,1)S(1)}, u32[]{:S(2)}, u32[]{:S(2)}) collective-permute-start(bf16[2,256,512]{2,1,0:T(8,128)(2,1)S(1)} %get-tuple-element.162), channel_id=1, source_target_pairs={{0,1},{1,0},{2,3},{3,2},{4,5},{5,4},{6,7},{7,6},{8,9},{9,8},{10,11... | collective-permute-start | bytes 1572872 | tf_op jit(solution)/shard_map/ppermute | solution.py:760
  188.5 16.2 %collective-permute-start.18 = (bf16[2,64,512]{2,1,0:T(8,128)(2,1)S(1)}, bf16[2,64,512]{2,1,0:T(8,128)(2,1)S(1)}, u32[]{:S(2)}, u32[]{:S(2)}) collective-permute-start(bf16[2,64,512]{2,1,0:T(8,128)(2,1)S(1)} %get-tuple-element.166), channel_id=1, source_target_pairs={{0,8},{1,9},{2,10},{3,11},{4,12},{5,13},{6,14},{7,15},{8,0},{9,1},... | collective-permute-start | bytes 393224 | tf_op jit(solution)/shard_map/ppermute | solution.py:760
  188.8 15.9 %collective-permute-start.20 = (bf16[2,64,512]{2,1,0:T(8,128)(2,1)S(1)}, bf16[2,64,512]{2,1,0:T(8,128)(2,1)S(1)}, u32[]{:S(2)}, u32[]{:S(2)}) collective-permute-start(bf16[2,64,512]{2,1,0:T(8,128)(2,1)S(1)} %get-tuple-element.167), channel_id=1, source_target_pairs={{0,24},{1,25},{2,26},{3,27},{4,28},{5,29},{6,30},{7,31},{8,16},{9,... | collective-permute-start | bytes 393224 | tf_op jit(solution)/shard_map/ppermute | solution.py:760
  189.2 15.5 %collective-permute-start.19 = (bf16[2,64,512]{2,1,0:T(8,128)(2,1)S(1)}, bf16[2,64,512]{2,1,0:T(8,128)(2,1)S(1)}, u32[]{:S(2)}, u32[]{:S(2)}) collective-permute-start(bf16[2,64,512]{2,1,0:T(8,128)(2,1)S(1)} %get-tuple-element.168), channel_id=1, source_target_pairs={{0,16},{1,17},{2,18},{3,19},{4,20},{5,21},{6,22},{7,23},{8,24},{9,... | collective-permute-start | bytes 393224 | tf_op jit(solution)/shard_map/ppermute | solution.py:760
  214.8 7.5 %collective-permute-start.22 = (f32[1,1048]{1,0:T(1,128)S(1)}, f32[1,1048]{1,0:T(1,128)S(1)}, u32[]{:S(2)}, u32[]{:S(2)}) collective-permute-start(f32[1,1048]{1,0:T(1,128)S(1)} %broadcast_in_dim.149), channel_id=1, source_target_pairs={{0,2},{1,3},{2,0},{3,1},{4,6},{5,7},{6,4},{7,5},{8,10},{9,11},{10,... | collective-permute-start | bytes 12584 | tf_op jit(solution)/shard_map/ppermute | solution.py:760
  218.8 18.2 %collective-permute-start.28 = (bf16[4,4,32,256]{3,2,1,0:T(8,128)(2,1)S(1)}, bf16[4,4,32,256]{3,2,1,0:T(8,128)(2,1)S(1)}, u32[]{:S(2)}, u32[]{:S(2)}) collective-permute-start(bf16[4,4,32,256]{3,2,1,0:T(8,128)(2,1)S(1)} %get-tuple-element.163), channel_id=1, source_target_pairs={{0,5},{1,4},{2,7},{3,6},{4,1},{5,0},{6,3},{7,2},{8,13},{9,12},{10,... | collective-permute-start | bytes 786440 | tf_op jit(solution)/shard_map/ppermute | solution.py:760
  220.4 16.6 %collective-permute-start.27 = (bf16[4,4,32,256]{3,2,1,0:T(8,128)(2,1)S(1)}, bf16[4,4,32,256]{3,2,1,0:T(8,128)(2,1)S(1)}, u32[]{:S(2)}, u32[]{:S(2)}) collective-permute-start(bf16[4,4,32,256]{3,2,1,0:T(8,128)(2,1)S(1)} %get-tuple-element.164), channel_id=1, source_target_pairs={{0,1},{1,0},{2,3},{3,2},{4,5},{5,4},{6,7},{7,6},{8,9},{9,8},{10,11... | collective-permute-start | bytes 786440 | tf_op jit(solution)/shard_map/ppermute | solution.py:760
  221.0 16.1 %collective-permute-start.26 = (bf16[4,4,32,256]{3,2,1,0:T(8,128)(2,1)S(1)}, bf16[4,4,32,256]{3,2,1,0:T(8,128)(2,1)S(1)}, u32[]{:S(2)}, u32[]{:S(2)}) collective-permute-start(bf16[4,4,32,256]{3,2,1,0:T(8,128)(2,1)S(1)} %get-tuple-element.165), channel_id=1, source_target_pairs={{0,4},{1,5},{2,6},{3,7},{4,0},{5,1},{6,2},{7,3},{8,12},{9,13},{10,... | collective-permute-start | bytes 786440 | tf_op jit(solution)/shard_map/ppermute | solution.py:760
  222.4 11.0 %collective-permute-start.24 = (f32[1,1048]{1,0:T(1,128)S(1)}, f32[1,1048]{1,0:T(1,128)S(1)}, u32[]{:S(2)}, u32[]{:S(2)}) collective-permute-start(f32[1,1048]{1,0:T(1,128)S(1)} %reshape_add_fusion), channel_id=1, source_target_pairs={{0,1},{1,0},{2,3},{3,2},{4,5},{5,4},{6,7},{7,6},{8,9},{9,8},{10,11... | collective-permute-start | bytes 12584 | tf_op jit(solution)/shard_map/ppermute | solution.py:760
  237.2 4.6 %collective-permute-start.29 = (f32[1,1048]{1,0:T(1,128)S(1)}, f32[1,1048]{1,0:T(1,128)S(1)}, u32[]{:S(2)}, u32[]{:S(2)}) collective-permute-start(f32[1,1048]{1,0:T(1,128)S(1)} %add.111), channel_id=1, source_target_pairs={{0,16},{1,17},{2,18},{3,19},{4,20},{5,21},{6,22},{7,23},{8,24},{9,... | collective-permute-start | bytes 12584 | tf_op jit(solution)/shard_map/ppermute | solution.py:760
  241.8 6.8 %collective-permute-start.30 = (f32[1,1048]{1,0:T(1,128)S(1)}, f32[1,1048]{1,0:T(1,128)S(1)}, u32[]{:S(2)}, u32[]{:S(2)}) collective-permute-start(f32[1,1048]{1,0:T(1,128)S(1)} %add.115), channel_id=1, source_target_pairs={{0,8},{1,9},{2,10},{3,11},{4,12},{5,13},{6,14},{7,15},{8,0},{9,1},... | collective-permute-start | bytes 12584 | tf_op jit(solution)/shard_map/ppermute | solution.py:760
  244.2 6.2 %collective-permute-start.33 = (bf16[1,4,32,256]{3,2,1,0:T(8,128)(2,1)S(1)}, bf16[1,4,32,256]{3,2,1,0:T(8,128)(2,1)S(1)}, u32[]{:S(2)}, u32[]{:S(2)}) collective-permute-start(bf16[1,4,32,256]{3,2,1,0:T(8,128)(2,1)S(1)} %get-tuple-element.171), channel_id=1, source_target_pairs={{0,24},{1,25},{2,26},{3,27},{4,28},{5,29},{6,30},{7,31},{8,16},{9,... | collective-permute-start | bytes 196616 | tf_op jit(solution)/shard_map/ppermute | solution.py:760
  244.5 6.6 %collective-permute-start.32 = (bf16[1,4,32,256]{3,2,1,0:T(8,128)(2,1)S(1)}, bf16[1,4,32,256]{3,2,1,0:T(8,128)(2,1)S(1)}, u32[]{:S(2)}, u32[]{:S(2)}) collective-permute-start(bf16[1,4,32,256]{3,2,1,0:T(8,128)(2,1)S(1)} %get-tuple-element.172), channel_id=1, source_target_pairs={{0,16},{1,17},{2,18},{3,19},{4,20},{5,21},{6,22},{7,23},{8,24},{9,... | collective-permute-start | bytes 196616 | tf_op jit(solution)/shard_map/ppermute | solution.py:760
  246.0 5.1 %collective-permute-start.31 = (bf16[1,4,32,256]{3,2,1,0:T(8,128)(2,1)S(1)}, bf16[1,4,32,256]{3,2,1,0:T(8,128)(2,1)S(1)}, u32[]{:S(2)}, u32[]{:S(2)}) collective-permute-start(bf16[1,4,32,256]{3,2,1,0:T(8,128)(2,1)S(1)} %get-tuple-element.173), channel_id=1, source_target_pairs={{0,8},{1,9},{2,10},{3,11},{4,12},{5,13},{6,14},{7,15},{8,0},{9,1},... | collective-permute-start | bytes 196616 | tf_op jit(solution)/shard_map/ppermute | solution.py:760
  (15 other events, 122.6 us)

commit v9 on v8

--- a/solution.py
+++ b/solution.py
@@ -344,12 +344,10 @@
     invl_ref,
     invd_ref,
     back_ref,
-    adjoint,
 ):
     rows = query_ref.shape[1]
     step_rows = rows // 3
     b0, b1, b2 = (blend_ref[pl.ds(f, 1), :] for f in range(3))
-    adjoint[...] = jnp.zeros(adjoint.shape, F32)
 
     tails = message_ref[0, pl.ds(HEAD_DIM, TAIL), :]
     key = jnp.concatenate([tails[:, :PAIR], key_ref[0]], axis=0)
@@ -363,45 +361,36 @@
     scale = b0 * invl_ref[...]
     rows_q = (query.astype(F32) * (scale * HEAD_DIM**-0.5)).astype(BF16)
     rows_g = (grad_f * scale).astype(BF16)
-    weights, shifted = near_back(
-        near_scores(query, split_heads(key)),
-        mm(grad, split_heads(value), NT),
-        bias,
-        spread(grad_f * near_ref[...]),
-    )
+    scores = near_scores(query, split_heads(key))
+    grad_pair = mm(grad, split_heads(value), NT)
+    spread_near = spread(grad_f * near_ref[...])
+    heads = same_head().astype(F32).astype(BF16)
+    heads = jnp.concatenate([heads, heads], axis=0)
+
+    total = jnp.zeros((PAIR, 3 * PAIR), F32)
+    for step in range(3):
+        here = pl.ds(step * step_rows, step_rows)
+        row = iota((step_rows, PAIR), 0) + step * step_rows
+        start = start_ref[here, :]
+        all_grad = grad_ref[here, :]
+        product = all_grad.astype(F32) * far1_ref[here, :]
+        high = product.astype(BF16)
+        low = (product - high.astype(F32)).astype(BF16)
+        along = mm(jnp.concatenate([high, low], axis=1), heads).astype(BF16)
+        query_f = query_ref[0, here, :].astype(F32)
+        live = start < 0
+        scaled = jnp.where(live, lift(query_f) * (b1 * invd_ref[here, :]), 0.0)
+        bent = jnp.where(live, jnp.tanh(query_f) * (b2 / (row - start + 1).astype(F32)), 0.0)
+        from_lift = mm(scaled.astype(BF16), jnp.concatenate([all_grad, along], axis=1), TN)
+        from_bend = mm(bent.astype(BF16), all_grad, TN)
+        total = total + jnp.concatenate([from_lift, from_bend], axis=1)
+
+    weights, shifted = near_back(scores, grad_pair, bias, spread_near)
     d_key = fold(mm(shifted, rows_q, TN))
     back_ref[0, pl.ds(HEAD_DIM, TAIL), :] = jnp.concatenate(
         [d_key[:TAIL], fold(mm(weights, rows_g, TN))[:TAIL], jnp.zeros((TAIL, PAIR), F32)], axis=1
     ).astype(BF16)
-    heads = same_head().astype(F32).astype(BF16)
-    heads = jnp.concatenate([heads, heads], axis=0)
-
-    for step in range(3):
-        at = step * step_rows
-
-        @pl.when(scalars[scalars.shape[0] + CARRIED] > at)
-        def _():
-            here = pl.ds(at, step_rows)
-            row = iota((step_rows, PAIR), 0) + at
-            start = start_ref[here, :]
-            grad = grad_ref[here, :]
-            grad_f = grad.astype(F32)
-            product = grad_f * far1_ref[here, :]
-            high = product.astype(BF16)
-            low = (product - high.astype(F32)).astype(BF16)
-            along = mm(jnp.concatenate([high, low], axis=1), heads).astype(BF16)
-            query_f = query_ref[0, here, :].astype(F32)
-            live = start < 0
-            scaled = jnp.where(live, lift(query_f) * (b1 * invd_ref[here, :]), 0.0)
-            bent = jnp.where(
-                live, jnp.tanh(query_f) * (b2 / (row - start + 1).astype(F32)), 0.0
-            )
-            adjoint[:, : 2 * PAIR] += mm(
-                scaled.astype(BF16), jnp.concatenate([grad, along], axis=1), TN
-            )
-            adjoint[:, 2 * PAIR :] += mm(bent.astype(BF16), grad, TN)
-
-    back_ref[0, pl.ds(0, HEAD_DIM), :] = fold_state(adjoint[...])
+    back_ref[0, pl.ds(0, HEAD_DIM), :] = fold_state(total)
 
 
 def key_side(adjoint_low, lift_k, bend_k, value):
@@ -810,16 +799,6 @@
     groups = phases()
     flips = all_flips()
 
-    shards = jnp.concatenate([qkv_weight, out_weight.T[None]], axis=0)[None]
-    feed = jnp.stack([in_weight, down_weight])
-    shards = widen(shards, groups[0], 0)
-    feed, _ = lax.optimization_barrier((feed, shards))
-    feed = widen(feed, groups[0][:1], 1)
-    for group in groups[1:-1]:
-        shards = widen(shards, group, 0)
-    shards, feed = lax.optimization_barrier((shards, feed))
-    others = peer(shards, groups[-1], 1)
-
     item_lengths = lengths[0]
     slots = item_lengths.shape[0]
     ends = jnp.sum(
@@ -845,10 +824,20 @@
             lax.axis_index("head").astype(jnp.int32)[None],
         ]
     )
-    start_wide = jnp.broadcast_to(start[:, None], (rows, PAIR))
+    shards = jnp.concatenate([qkv_weight, out_weight.T[None]], axis=0)[None]
+    feed = jnp.stack([in_weight, down_weight])
+    shards = widen(shards, groups[0], 0)
+    feed, late, _ = lax.optimization_barrier((feed, start, shards))
+    start_wide = jnp.broadcast_to(late[:, None], (rows, PAIR))
     row_wide = jnp.broadcast_to(local[:, None], (rows, PAIR))
     bias, far, tally = masks(row_wide, start_wide, row_wide // ROWS * ROWS - TAIL)
     tables = (bias.astype(BF16), far.astype(BF16), tally)
+    feed = widen(feed, groups[0][:1], 1)
+    for group in groups[1:-1]:
+        shards = widen(shards, group, 0)
+    shards, feed, start_wide, tables = lax.optimization_barrier((shards, feed, start_wide, tables))
+    others = peer(shards, groups[-1], 1)
+
     keep_all = (start[rows - 1] < 0).astype(F32)
     blend_wide = jnp.repeat(blend, HEAD_DIM, axis=1)
 
@@ -862,7 +851,6 @@
     def whole_spec(shape):
         return pl.BlockSpec(shape, lambda p, s: (0,) * len(shape))
 
-    others, start_wide, tables = lax.optimization_barrier((others, start_wide, tables))
     qkv, normed_one, qkv_all, out_all, closing = call(
         functools.partial(project_kernel, flips=flips),
         [
@@ -970,7 +958,7 @@
         ],
         spec["message"],
         message_shape,
-        [state_scratch],
+        [],
         pairs,
         "prologue",
         500 * big,

time: 254 us -> 248 us (0.976)
  waiting for transfers between devices: 23.4 us -> 18.2 us
    ppermute x32, waiting for transfers between devices: 21.6 us -> 16.4 us  [peer(): return lax.ppermute(array, ('dp', 'head'), pairs)]
  transfers between devices with their start and end apart: 34 -> 34, of which waited for: 10 -> 11; matrix products, arithmetic and copies ran while one was open for 10% -> 10% of each run, Pallas kernels for 39% -> 39%
where the time goes in v9:
time: 248 us
  Pallas kernels  150 us (60%)
  starting transfers between devices  45.4 us (18%)
  waiting for transfers between devices  18.2 us (7%)
  other arithmetic  17.1 us (7%)
  local copies, waits for them, and re-layouts  14.9 us (6%)
    pallas_call x2, Pallas kernels, per_device(): call(backward_kernel, [spec['qkv'], spec['message']] + [spec['start']] *...  40.8 us
    ppermute x32, starting transfers between devices, peer(): return lax.ppermute(array, ('dp', 'head'), pairs)  40.3 us
    pallas_call x2, Pallas kernels, per_device(): call(functools.partial(resume, forward_kernel, 7, len(results)), [spec['q...  26.6 us
    pallas_call x1, Pallas kernels, per_device(): call(feed_kernel, [row_spec] * 3 + [whole_spec((width, width)), whole_spe...  26.1 us
    pallas_call x2, Pallas kernels, feed_grad(): call(feed_grad_kernel, [whole_rows] * 2 + [columns] * 2 + more_in_specs,...  19.2 us
    ppermute x32, waiting for transfers between devices, peer(): return lax.ppermute(array, ('dp', 'head'), pairs)  16.4 us
    pallas_call x1, Pallas kernels, per_device(): call(functools.partial(project_kernel, flips=flips), [pl.BlockSpec((part,...  10.2 us
    pallas_call x1, Pallas kernels, per_device(): call(prologue_kernel, [spec['query'], pl.BlockSpec((1, ROWS, PAIR), lambd...  9.66 us
  transfers between devices with their start and end apart: 34, of which 11 were waited for; matrix products, arithmetic and copies ran while one was open for 10% of the time, Pallas kernels for 39%

profile of v9, /device:TPU:0, one launch (start us, length us, event | category | flops | bytes accessed | tf_op | source)
XLA Modules:
  0.0 247.6 jit_solution(456097568903182641)
XLA Ops:
  1.5 5.1 %collective-permute-start.2 = (bf16[1,4,32,256]{3,2,1,0:T(8,128)(2,1)S(1)}, bf16[1,4,32,256]{3,2,1,0:T(8,128)(2,1)S(1)}, u32[]{:S(2)}, u32[]{:S(2)}) collective-permute-start(bf16[1,4,32,256]{3,2,1,0:T(8,128)(2,1)S(1)} %maximum_bitcast_fusion), channel_id=1, source_target_pairs={{0,24},{1,25},{2,26},{3,27},{4,28},{5,29},{6,30},{7,31},{8,16},{9,... | collective-permute-start | bytes 196616 | tf_op jit(solution)/shard_map/ppermute | solution.py:749
  12.3 2.5 %collective-permute-start.5 = (bf16[4,4,32,256]{3,2,1,0:T(8,128)(2,1)S(1)}, bf16[4,4,32,256]{3,2,1,0:T(8,128)(2,1)S(1)}, u32[]{:S(2)}, u32[]{:S(2)}) collective-permute-start(bf16[4,4,32,256]{3,2,1,0:T(8,128)(2,1)S(1)} %pad_maximum_fusion), channel_id=1, source_target_pairs={{0,5},{1,4},{2,7},{3,6},{4,1},{5,0},{6,3},{7,2},{8,13},{9,12},{10,... | collective-permute-start | bytes 786440 | tf_op jit(solution)/shard_map/ppermute | solution.py:749
  16.9 2.4 convert_convert_fusion.refs_4_.far_ref
  19.3 3.3 %fusion.6 = (f32[1536,128]{1,0:T(8,128)}, bf16[1536,128]{1,0:T(8,128)(2,1)}) fusion(f32[1536]{0:T(1024)S(1)} %get-tuple-element.181, f32[1536]{0:T(1024)S(1)} %get-tuple-element.180, s32[1536]{0:T(1024)S(1)} %get-tuple-element.184, s32[1536]{0:T(1024)S(1)} %get-tuple-element.185, s32[1536]{0:T(1024)S(1)} %get-tuple-element.80, ...), kind=kLoop, calls=%fused_computation.14 | loop fusion | flops 2359296 | bytes 1218048 | tf_op jit(solution)/shard_map/jit(_where)/select_n | solution.py:79
  22.6 4.1 %collective-permute-done.3 = bf16[4,4,32,256]{3,2,1,0:T(8,128)(2,1)S(1)} collective-permute-done((bf16[4,4,32,256]{3,2,1,0:T(8,128)(2,1)S(1)}, bf16[4,4,32,256]{3,2,1,0:T(8,128)(2,1)S(1)}, u32[]{:S(2)}, u32[]{:S(2)}) %collective-permute-start.3) | collective-permute-done | bytes 262176 | tf_op jit(solution)/shard_map/ppermute | solution.py:749
  30.4 1.9 concatenate.29.scalars.refs_0_
  34.6 10.2 %project.1 = (bf16[3,1536,512]{2,1,0:T(8,128)(2,1)}, bf16[1536,512]{1,0:T(8,128)(2,1)}, bf16[3,512,512]{2,1,0:T(8,128)(2,1)}, bf16[512,512]{1,0:T(8,128)(2,1)}, bf16[4,96,384]{2,1,0:T(8,128)(2,1)}) custom-call(s32[21]{0:T(128)} %concatenate.29.scalars.refs_0_, bf16[1536,512]{1,0:T(8,128)(2,1)} %tokens_ref.5, f32[1,512]{1,0:T(1,128)} %bitcast.34, ...), custom_call_target="tpu_custom_call" | custom-call | flops 2415919104 | bytes 9437184 | tf_op jit(solution)/shard_map/project/pallas_call | solution.py:854
  44.7 3.6 %collective-permute-start.12 = (bf16[4,96,384]{2,1,0:T(8,128)(2,1)}, bf16[4,96,384]{2,1,0:T(8,128)(2,1)S(1)}, u32[]{:S(2)}, u32[]{:S(2)}) collective-permute-start(bf16[4,96,384]{2,1,0:T(8,128)(2,1)} %get-tuple-element.84), channel_id=1, source_target_pairs={{0,1},{2,3},{4,5},{6,7},{8,9},{10,11},{12,13},{14,15},{16,17},{18,... | collective-permute-start | bytes 884744 | tf_op jit(solution)/shard_map/ppermute | solution.py:775
  50.5 2.3 collective-permute-start.10
  54.1 1.7 collective-permute-done.12.refs_2_.message_ref
  56.5 17.5 %forward.2 = (bf16[1536,512]{1,0:T(8,128)(2,1)}, f32[1536,512]{1,0:T(8,128)}, f32[1536,512]{1,0:T(8,128)}, f32[1536,512]{1,0:T(8,128)}, f32[1536,512]{1,0:T(8,12...) custom-call(s32[21]{0:T(128)} %concatenate.29.scalars.refs_0_, ...), custom_call_target="tpu_custom_call" | custom-call | flops 4718592000 | bytes 23592960 | tf_op jit(solution)/shard_map/forward/pallas_call | solution.py:896
  74.1 3.4 %collective-permute-done.10 = bf16[2,256,512]{2,1,0:T(8,128)(2,1)S(1)} collective-permute-done((bf16[2,256,512]{2,1,0:T(8,128)(2,1)S(1)}, bf16[2,256,512]{2,1,0:T(8,128)(2,1)S(1)}, u32[]{:S(2)}, u32[]{:S(2)}) %collective-permute-start.10) | collective-permute-done | bytes 524320 | tf_op jit(solution)/shard_map/ppermute | solution.py:749
  77.7 9.1 %forward.3 = (bf16[1536,512]{1,0:T(8,128)(2,1)}, f32[1536,512]{1,0:T(8,128)}, f32[1536,512]{1,0:T(8,128)}, f32[1536,512]{1,0:T(8,128)}, f32[1536,512]{1,0:T(8,12...) custom-call(s32[21]{0:T(128)} %concatenate.29.scalars.refs_0_, ...), custom_call_target="tpu_custom_call", output_to_operand_aliasing={{0}: (7, {}), {1}: (8, {}), {2}: (9, {}), {3}: (10, {}), {4... | custom-call | flops 1572864000 | bytes 7864320 | tf_op jit(solution)/shard_map/forward/pallas_call | solution.py:896
  88.2 26.1 %feed.1 = (bf16[1536,512]{1,0:T(8,128)(2,1)}, f32[1536,512]{1,0:T(8,128)}, bf16[1536,512]{1,0:T(8,128)(2,1)}, bf16[1536,512]{1,0:T(8,128)(2,1)}, bf16[1536,512]{...) custom-call(s32[21]{0:T(128)} %concatenate.29.scalars.refs_0_, ...), custom_call_target="tpu_custom_call" | custom-call | flops 12884901888 | bytes 25165824 | tf_op jit(solution)/shard_map/feed/pallas_call | solution.py:926
  114.3 9.7 %prologue.1 = bf16[4,96,384]{2,1,0:T(8,128)(2,1)} custom-call(s32[21]{0:T(128)} %concatenate.29.scalars.refs_0_, bf16[3,1536,512]{2,1,0:T(8,128)(2,1)} %get-tuple-element.82.refs_1_.query_ref.key_ref.value_ref.qkv_ref, bf16[3,1536,512]{2,1,0:T(8,128)(2,1)} %get-tuple-element.82.refs_1_.query_ref.key_ref.value_ref.qkv_ref, ...), custom_call_target="tpu_custom_call" | custom-call | flops 393216000 | bytes 15728640 | tf_op jit(solution)/shard_map/prologue/pallas_call | solution.py:944
  123.9 8.4 %feed_grad.2 = bf16[2,1024,512]{2,1,0:T(8,128)(2,1)} custom-call(s32[21]{0:T(128)} %concatenate.29.scalars.refs_0_, bf16[1536,512]{1,0:T(8,128)(2,1)} %get-tuple-element.112.normed_ref, bf16[1536,512]{1,0:T(8,128)(2,1)} %cotangent_ref.5, bf16[1536,2048]{1,0:T(8,128)(2,1)} %get-tuple-element.113.active_ref, bf16[1536,2048]{1,0:T(8,128)(2,1)} %get-tuple-element.122.d_inner_ref), custom_call_target="tpu_custom_call" | custom-call | flops 3221225472 | bytes 9437184 | tf_op jit(solution)/shard_map/feed_grad/pallas_call | solution.py:976
  134.3 10.8 %feed_grad.3 = (f32[512,512]{1,0:T(8,128)}, f32[2,1024,512]{2,1,0:T(8,128)}) custom-call(s32[21]{0:T(128)} %concatenate.29.scalars.refs_0_, bf16[1536,512]{1,0:T(8,128)(2,1)} %get-tuple-element.112.normed_ref, bf16[1536,512]{1,0:T(8,128)(2,1)} %cotangent_ref.5, bf16[1536,2048]{1,0:T(8,128)(2,1)} %get-tuple-element.113.active_ref, ...), custom_call_target="tpu_custom_call" | custom-call | flops 3221225472 | bytes 9437184 | tf_op jit(solution)/shard_map/feed_grad/pallas_call | solution.py:976
  145.1 3.1 %fusion.17 = (bf16[2,1024,512]{2,1,0:T(8,128)(2,1)S(1)}, f32[2,1024,512]{2,1,0:T(8,128)S(1)}) fusion(f32[2,1024,512]{2,1,0:T(8,128)} %get-tuple-element.124, bf16[2,1024,512]{2,1,0:T(8,128)(2,1)S(1)} %collective-permute-done.14), kind=kLoop, calls=%fused_computation.69 | loop fusion | flops 3145728 | bytes 12582912 | tf_op jit(solution)/shard_map/convert.11
  149.9 2.7 %collective-permute-start.17 = (bf16[2,256,512]{2,1,0:T(8,128)(2,1)S(1)}, bf16[2,256,512]{2,1,0:T(8,128)(2,1)S(1)}, u32[]{:S(2)}, u32[]{:S(2)}) collective-permute-start(bf16[2,256,512]{2,1,0:T(8,128)(2,1)S(1)} %get-tuple-element.161), channel_id=1, source_target_pairs={{0,5},{1,4},{2,7},{3,6},{4,1},{5,0},{6,3},{7,2},{8,13},{9,12},{10,... | collective-permute-start | bytes 1572872 | tf_op jit(solution)/shard_map/ppermute | solution.py:749
  153.1 28.1 %backward.2 = (bf16[3,1536,512]{2,1,0:T(8,128)(2,1)}, f32[24,384]{1,0:T(8,128)}) custom-call(s32[21]{0:T(128)} %concatenate.29.scalars.refs_0_, bf16[3,1536,512]{2,1,0:T(8,128)(2,1)} %get-tuple-element.82.refs_1_.query_ref.key_ref.value_ref.qkv_ref, bf16[4,96,384]{2,1,0:T(8,128)(2,1)} %copy-done, bf16[1536,128]{1,0:T(8,128)(2,1)} %get-tuple-element.86.refs_3_.bias_ref, ...), custom_call_target="tpu_custom_call" | custom-call | flops 9437184000 | bytes 23592960 | tf_op jit(solution)/shard_map/backward/pallas_call | solution.py:1010
  181.7 1.8 collective-permute-start.18
  185.2 12.7 %backward.3 = (bf16[3,1536,512]{2,1,0:T(8,128)(2,1)}, f32[24,128]{1,0:T(8,128)}) custom-call(s32[21]{0:T(128)} %concatenate.29.scalars.refs_0_, bf16[3,1536,512]{2,1,0:T(8,128)(2,1)} %get-tuple-element.82.refs_1_.query_ref.key_ref.value_ref.qkv_ref, bf16[4,96,384]{2,1,0:T(8,128)(2,1)} %copy-done, ...), custom_call_target="tpu_custom_call", output_to_operand_aliasing={{0}: (15, {})} | custom-call | flops 3145728000 | bytes 7864320 | tf_op jit(solution)/shard_map/backward/pallas_call | solution.py:1010
  198.0 8.9 %weight_grad.1 = (f32[16,4,32,256]{3,2,1,0:T(8,128)}, bf16[16,4,32,256]{3,2,1,0:T(8,128)(2,1)}, f32[8,512]{1,0:T(8,128)}) custom-call(s32[21]{0:T(128)} %concatenate.29.scalars.refs_0_, bf16[1536,512]{1,0:T(8,128)(2,1)} %get-tuple-element.111.normed_ref, bf16[3,1536,512]{2,1,0:T(8,128)(2,1)} %get-tuple-element.140.d_qkv_ref, ...), custom_call_target="tpu_custom_call" | custom-call | flops 2415919104 | bytes 6291456 | tf_op jit(solution)/shard_map/weight_grad/pallas_call | solution.py:1057
  209.8 2.1 fusion.15
  212.0 3.0 %collective-permute-start.28 = (bf16[4,4,32,256]{3,2,1,0:T(8,128)(2,1)S(1)}, bf16[4,4,32,256]{3,2,1,0:T(8,128)(2,1)S(1)}, u32[]{:S(2)}, u32[]{:S(2)}) collective-permute-start(bf16[4,4,32,256]{3,2,1,0:T(8,128)(2,1)S(1)} %get-tuple-element.163), channel_id=1, source_target_pairs={{0,5},{1,4},{2,7},{3,6},{4,1},{5,0},{6,3},{7,2},{8,13},{9,12},{10,... | collective-permute-start | bytes 786440 | tf_op jit(solution)/shard_map/ppermute | solution.py:749
  215.6 2.0 collective-permute-start.24
  217.6 8.9 %input.1 = f32[1536,512]{1,0:T(8,128)} custom-call(s32[21]{0:T(128)} %concatenate.29.scalars.refs_0_, bf16[3,1536,512]{2,1,0:T(8,128)(2,1)} %get-tuple-element.140.d_qkv_ref, bf16[3,512,512]{2,1,0:T(8,128)(2,1)} %get-tuple-element.133.weight_ref, bf16[1536,512]{1,0:T(8,128)(2,1)} %tokens_ref.5, f32[1536,512]{1,0:T(8,128)} %get-tuple-element.141.d_hidden_ref, ...), custom_call_target="tpu_custom_call" | custom-call | flops 2415919104 | bytes 18874368 | tf_op jit(solution)/shard_map/input/pallas_call | solution.py:1084
  228.0 2.6 %collective-permute-done.25 = f32[1,1048]{1,0:T(1,128)S(1)} collective-permute-done((f32[1,1048]{1,0:T(1,128)S(1)}, f32[1,1048]{1,0:T(1,128)S(1)}, u32[]{:S(2)}, u32[]{:S(2)}) %collective-permute-start.25) | collective-permute-done | bytes 4224 | tf_op jit(solution)/shard_map/ppermute | solution.py:749
  230.9 2.6 %collective-permute-start.29 = (f32[1,1048]{1,0:T(1,128)S(1)}, f32[1,1048]{1,0:T(1,128)S(1)}, u32[]{:S(2)}, u32[]{:S(2)}) collective-permute-start(f32[1,1048]{1,0:T(1,128)S(1)} %add.108), channel_id=1, source_target_pairs={{0,16},{1,17},{2,18},{3,19},{4,20},{5,21},{6,22},{7,23},{8,24},{9,... | collective-permute-start | bytes 12584 | tf_op jit(solution)/shard_map/ppermute | solution.py:749
  233.4 2.0 collective-permute-done.29
  235.5 2.6 %collective-permute-start.30 = (f32[1,1048]{1,0:T(1,128)S(1)}, f32[1,1048]{1,0:T(1,128)S(1)}, u32[]{:S(2)}, u32[]{:S(2)}) collective-permute-start(f32[1,1048]{1,0:T(1,128)S(1)} %add.112), channel_id=1, source_target_pairs={{0,8},{1,9},{2,10},{3,11},{4,12},{5,13},{6,14},{7,15},{8,0},{9,1},... | collective-permute-start | bytes 12584 | tf_op jit(solution)/shard_map/ppermute | solution.py:749
  240.3 2.9 %collective-permute-start.31 = (bf16[1,4,32,256]{3,2,1,0:T(8,128)(2,1)S(1)}, bf16[1,4,32,256]{3,2,1,0:T(8,128)(2,1)S(1)}, u32[]{:S(2)}, u32[]{:S(2)}) collective-permute-start(bf16[1,4,32,256]{3,2,1,0:T(8,128)(2,1)S(1)} %get-tuple-element.173), channel_id=1, source_target_pairs={{0,8},{1,9},{2,10},{3,11},{4,12},{5,13},{6,14},{7,15},{8,0},{9,1},... | collective-permute-start | bytes 196616 | tf_op jit(solution)/shard_map/ppermute | solution.py:749
  (138 shorter events, 37.9 us)
Async XLA Ops:
  1.5 10.2 %collective-permute-start.2 = (bf16[1,4,32,256]{3,2,1,0:T(8,128)(2,1)S(1)}, bf16[1,4,32,256]{3,2,1,0:T(8,128)(2,1)S(1)}, u32[]{:S(2)}, u32[]{:S(2)}) collective-permute-start(bf16[1,4,32,256]{3,2,1,0:T(8,128)(2,1)S(1)} %maximum_bitcast_fusion), channel_id=1, source_target_pairs={{0,24},{1,25},{2,26},{3,27},{4,28},{5,29},{6,30},{7,31},{8,16},{9,... | collective-permute-start | bytes 196616 | tf_op jit(solution)/shard_map/ppermute | solution.py:749
  6.6 5.6 %collective-permute-start.1 = (bf16[1,4,32,256]{3,2,1,0:T(8,128)(2,1)S(1)}, bf16[1,4,32,256]{3,2,1,0:T(8,128)(2,1)S(1)}, u32[]{:S(2)}, u32[]{:S(2)}) collective-permute-start(bf16[1,4,32,256]{3,2,1,0:T(8,128)(2,1)S(1)} %maximum_bitcast_fusion), channel_id=1, source_target_pairs={{0,16},{1,17},{2,18},{3,19},{4,20},{5,21},{6,22},{7,23},{8,24},{9,... | collective-permute-start | bytes 196616 | tf_op jit(solution)/shard_map/ppermute | solution.py:749
  6.6 5.6 %collective-permute-start = (bf16[1,4,32,256]{3,2,1,0:T(8,128)(2,1)S(1)}, bf16[1,4,32,256]{3,2,1,0:T(8,128)(2,1)S(1)}, u32[]{:S(2)}, u32[]{:S(2)}) collective-permute-start(bf16[1,4,32,256]{3,2,1,0:T(8,128)(2,1)S(1)} %maximum_bitcast_fusion), channel_id=1, source_target_pairs={{0,8},{1,9},{2,10},{3,11},{4,12},{5,13},{6,14},{7,15},{8,0},{9,1},... | collective-permute-start | bytes 196616 | tf_op jit(solution)/shard_map/ppermute | solution.py:749
  12.3 14.7 %collective-permute-start.5 = (bf16[4,4,32,256]{3,2,1,0:T(8,128)(2,1)S(1)}, bf16[4,4,32,256]{3,2,1,0:T(8,128)(2,1)S(1)}, u32[]{:S(2)}, u32[]{:S(2)}) collective-permute-start(bf16[4,4,32,256]{3,2,1,0:T(8,128)(2,1)S(1)} %pad_maximum_fusion), channel_id=1, source_target_pairs={{0,5},{1,4},{2,7},{3,6},{4,1},{5,0},{6,3},{7,2},{8,13},{9,12},{10,... | collective-permute-start | bytes 786440 | tf_op jit(solution)/shard_map/ppermute | solution.py:749
  14.8 12.2 %collective-permute-start.4 = (bf16[4,4,32,256]{3,2,1,0:T(8,128)(2,1)S(1)}, bf16[4,4,32,256]{3,2,1,0:T(8,128)(2,1)S(1)}, u32[]{:S(2)}, u32[]{:S(2)}) collective-permute-start(bf16[4,4,32,256]{3,2,1,0:T(8,128)(2,1)S(1)} %pad_maximum_fusion), channel_id=1, source_target_pairs={{0,1},{1,0},{2,3},{3,2},{4,5},{5,4},{6,7},{7,6},{8,9},{9,8},{10,11... | collective-permute-start | bytes 786440 | tf_op jit(solution)/shard_map/ppermute | solution.py:749
  15.3 11.4 %collective-permute-start.3 = (bf16[4,4,32,256]{3,2,1,0:T(8,128)(2,1)S(1)}, bf16[4,4,32,256]{3,2,1,0:T(8,128)(2,1)S(1)}, u32[]{:S(2)}, u32[]{:S(2)}) collective-permute-start(bf16[4,4,32,256]{3,2,1,0:T(8,128)(2,1)S(1)} %pad_maximum_fusion), channel_id=1, source_target_pairs={{0,4},{1,5},{2,6},{3,7},{4,0},{5,1},{6,2},{7,3},{8,12},{9,13},{10,... | collective-permute-start | bytes 786440 | tf_op jit(solution)/shard_map/ppermute | solution.py:749
  15.8 6.8 %collective-permute-start.6 = (bf16[2,64,512]{2,1,0:T(8,128)(2,1)S(1)}, bf16[2,64,512]{2,1,0:T(8,128)(2,1)S(1)}, u32[]{:S(2)}, u32[]{:S(2)}) collective-permute-start(bf16[2,64,512]{2,1,0:T(8,128)(2,1)S(1)} %pad_maximum_fusion.2), channel_id=1, source_target_pairs={{0,8},{1,9},{2,10},{3,11},{4,12},{5,13},{6,14},{7,15},{8,0},{9,1},... | collective-permute-start | bytes 393224 | tf_op jit(solution)/shard_map/ppermute | solution.py:749
  28.2 5.4 %collective-permute-start.7 = (bf16[16,4,32,256]{3,2,1,0:T(8,128)(2,1)S(1)}, bf16[16,4,32,256]{3,2,1,0:T(8,128)(2,1)S(1)}, u32[]{:S(2)}, u32[]{:S(2)}) collective-permute-start(bf16[16,4,32,256]{3,2,1,0:T(8,128)(2,1)S(1)} %constant_dynamic-update-slice_fusion.own_ref), channel_id=1, source_target_pairs={{0,2},{1,3},{2,0},{3,1},{4,6},{5,7},{6,4},{7,5},{8,10},{9,11},{10,... | collective-permute-start | bytes 3145736 | tf_op jit(solution)/shard_map/ppermute | solution.py:749
  32.3 16.8 %collective-permute-start.8 = (bf16[2,128,512]{2,1,0:T(8,128)(2,1)S(1)}, bf16[2,128,512]{2,1,0:T(8,128)(2,1)S(1)}, u32[]{:S(2)}, u32[]{:S(2)}) collective-permute-start(bf16[2,128,512]{2,1,0:T(8,128)(2,1)S(1)} %pad_maximum_fusion.1), channel_id=1, source_target_pairs={{0,16},{1,17},{2,18},{3,19},{4,20},{5,21},{6,22},{7,23},{8,24},{9,... | collective-permute-start | bytes 786440 | tf_op jit(solution)/shard_map/ppermute | solution.py:749
  44.7 11.1 %collective-permute-start.12 = (bf16[4,96,384]{2,1,0:T(8,128)(2,1)}, bf16[4,96,384]{2,1,0:T(8,128)(2,1)S(1)}, u32[]{:S(2)}, u32[]{:S(2)}) collective-permute-start(bf16[4,96,384]{2,1,0:T(8,128)(2,1)} %get-tuple-element.84), channel_id=1, source_target_pairs={{0,1},{2,3},{4,5},{6,7},{8,9},{10,11},{12,13},{14,15},{16,17},{18,... | collective-permute-start | bytes 884744 | tf_op jit(solution)/shard_map/ppermute | solution.py:775
  49.8 24.2 %collective-permute-start.11 = (bf16[2,256,512]{2,1,0:T(8,128)(2,1)S(1)}, bf16[2,256,512]{2,1,0:T(8,128)(2,1)S(1)}, u32[]{:S(2)}, u32[]{:S(2)}) collective-permute-start(bf16[2,256,512]{2,1,0:T(8,128)(2,1)S(1)} %get-tuple-element.174), channel_id=1, source_target_pairs={{0,5},{1,4},{2,7},{3,6},{4,1},{5,0},{6,3},{7,2},{8,13},{9,12},{10,... | collective-permute-start | bytes 1572872 | tf_op jit(solution)/shard_map/ppermute | solution.py:749
  50.5 27.0 %collective-permute-start.10 = (bf16[2,256,512]{2,1,0:T(8,128)(2,1)S(1)}, bf16[2,256,512]{2,1,0:T(8,128)(2,1)S(1)}, u32[]{:S(2)}, u32[]{:S(2)}) collective-permute-start(bf16[2,256,512]{2,1,0:T(8,128)(2,1)S(1)} %get-tuple-element.174), channel_id=1, source_target_pairs={{0,1},{1,0},{2,3},{3,2},{4,5},{5,4},{6,7},{7,6},{8,9},{9,8},{10,11... | collective-permute-start | bytes 1572872 | tf_op jit(solution)/shard_map/ppermute | solution.py:749
  52.8 24.7 %collective-permute-start.9 = (bf16[2,256,512]{2,1,0:T(8,128)(2,1)S(1)}, bf16[2,256,512]{2,1,0:T(8,128)(2,1)S(1)}, u32[]{:S(2)}, u32[]{:S(2)}) collective-permute-start(bf16[2,256,512]{2,1,0:T(8,128)(2,1)S(1)} %get-tuple-element.174), channel_id=1, source_target_pairs={{0,4},{1,5},{2,6},{3,7},{4,0},{5,1},{6,2},{7,3},{8,12},{9,13},{10,... | collective-permute-start | bytes 1572872 | tf_op jit(solution)/shard_map/ppermute | solution.py:749
  77.6 9.2 %collective-permute-start.13 = (bf16[2,1024,512]{2,1,0:T(8,128)(2,1)S(1)}, bf16[2,1024,512]{2,1,0:T(8,128)(2,1)S(1)}, u32[]{:S(2)}, u32[]{:S(2)}) collective-permute-start(bf16[2,1024,512]{2,1,0:T(8,128)(2,1)S(1)} %constant_dynamic-update-slice_fusion.9.own_ref), channel_id=1, source_target_pairs={{0,2},{1,3},{2,0},{3,1},{4,6},{5,7},{6,4},{7,5},{8,10},{9,11},{10,... | collective-permute-start | bytes 6291464 | tf_op jit(solution)/shard_map/ppermute | solution.py:749
  132.3 12.8 %collective-permute-start.14 = (bf16[2,1024,512]{2,1,0:T(8,128)(2,1)}, bf16[2,1024,512]{2,1,0:T(8,128)(2,1)S(1)}, u32[]{:S(2)}, u32[]{:S(2)}) collective-permute-start(bf16[2,1024,512]{2,1,0:T(8,128)(2,1)} %feed_grad.2), channel_id=1, source_target_pairs={{0,2},{1,3},{2,0},{3,1},{4,6},{5,7},{6,4},{7,5},{8,10},{9,11},{10,... | collective-permute-start | bytes 6291464 | tf_op jit(solution)/shard_map/ppermute | solution.py:749
  132.8 15.6 %collective-permute-start.21 = (bf16[4,96,384]{2,1,0:T(8,128)(2,1)S(1)}, bf16[4,96,384]{2,1,0:T(8,128)(2,1)S(1)}, u32[]{:S(2)}, u32[]{:S(2)}) collective-permute-start(bf16[4,96,384]{2,1,0:T(8,128)(2,1)S(1)} %copy-done.1), channel_id=1, source_target_pairs={{1,0},{3,2},{5,4},{7,6},{9,8},{11,10},{13,12},{15,14},{17,16},{19,... | collective-permute-start | bytes 884744 | tf_op jit(solution)/shard_map/ppermute | solution.py:775
  148.4 32.9 %collective-permute-start.15 = (bf16[2,256,512]{2,1,0:T(8,128)(2,1)S(1)}, bf16[2,256,512]{2,1,0:T(8,128)(2,1)S(1)}, u32[]{:S(2)}, u32[]{:S(2)}) collective-permute-start(bf16[2,256,512]{2,1,0:T(8,128)(2,1)S(1)} %get-tuple-element.160), channel_id=1, source_target_pairs={{0,4},{1,5},{2,6},{3,7},{4,0},{5,1},{6,2},{7,3},{8,12},{9,13},{10,... | collective-permute-start | bytes 1572872 | tf_op jit(solution)/shard_map/ppermute | solution.py:749
  149.9 31.4 %collective-permute-start.17 = (bf16[2,256,512]{2,1,0:T(8,128)(2,1)S(1)}, bf16[2,256,512]{2,1,0:T(8,128)(2,1)S(1)}, u32[]{:S(2)}, u32[]{:S(2)}) collective-permute-start(bf16[2,256,512]{2,1,0:T(8,128)(2,1)S(1)} %get-tuple-element.161), channel_id=1, source_target_pairs={{0,5},{1,4},{2,7},{3,6},{4,1},{5,0},{6,3},{7,2},{8,13},{9,12},{10,... | collective-permute-start | bytes 1572872 | tf_op jit(solution)/shard_map/ppermute | solution.py:749
  152.5 28.8 %collective-permute-start.16 = (bf16[2,256,512]{2,1,0:T(8,128)(2,1)S(1)}, bf16[2,256,512]{2,1,0:T(8,128)(2,1)S(1)}, u32[]{:S(2)}, u32[]{:S(2)}) collective-permute-start(bf16[2,256,512]{2,1,0:T(8,128)(2,1)S(1)} %get-tuple-element.162), channel_id=1, source_target_pairs={{0,1},{1,0},{2,3},{3,2},{4,5},{5,4},{6,7},{7,6},{8,9},{9,8},{10,11... | collective-permute-start | bytes 1572872 | tf_op jit(solution)/shard_map/ppermute | solution.py:749
  181.7 16.2 %collective-permute-start.18 = (bf16[2,64,512]{2,1,0:T(8,128)(2,1)S(1)}, bf16[2,64,512]{2,1,0:T(8,128)(2,1)S(1)}, u32[]{:S(2)}, u32[]{:S(2)}) collective-permute-start(bf16[2,64,512]{2,1,0:T(8,128)(2,1)S(1)} %get-tuple-element.166), channel_id=1, source_target_pairs={{0,8},{1,9},{2,10},{3,11},{4,12},{5,13},{6,14},{7,15},{8,0},{9,1},... | collective-permute-start | bytes 393224 | tf_op jit(solution)/shard_map/ppermute | solution.py:749
  183.5 14.4 %collective-permute-start.20 = (bf16[2,64,512]{2,1,0:T(8,128)(2,1)S(1)}, bf16[2,64,512]{2,1,0:T(8,128)(2,1)S(1)}, u32[]{:S(2)}, u32[]{:S(2)}) collective-permute-start(bf16[2,64,512]{2,1,0:T(8,128)(2,1)S(1)} %get-tuple-element.167), channel_id=1, source_target_pairs={{0,24},{1,25},{2,26},{3,27},{4,28},{5,29},{6,30},{7,31},{8,16},{9,... | collective-permute-start | bytes 393224 | tf_op jit(solution)/shard_map/ppermute | solution.py:749
  184.8 13.1 %collective-permute-start.19 = (bf16[2,64,512]{2,1,0:T(8,128)(2,1)S(1)}, bf16[2,64,512]{2,1,0:T(8,128)(2,1)S(1)}, u32[]{:S(2)}, u32[]{:S(2)}) collective-permute-start(bf16[2,64,512]{2,1,0:T(8,128)(2,1)S(1)} %get-tuple-element.168), channel_id=1, source_target_pairs={{0,16},{1,17},{2,18},{3,19},{4,20},{5,21},{6,22},{7,23},{8,24},{9,... | collective-permute-start | bytes 393224 | tf_op jit(solution)/shard_map/ppermute | solution.py:749
  208.0 7.6 %collective-permute-start.22 = (f32[1,1048]{1,0:T(1,128)S(1)}, f32[1,1048]{1,0:T(1,128)S(1)}, u32[]{:S(2)}, u32[]{:S(2)}) collective-permute-start(f32[1,1048]{1,0:T(1,128)S(1)} %broadcast_in_dim.149), channel_id=1, source_target_pairs={{0,2},{1,3},{2,0},{3,1},{4,6},{5,7},{6,4},{7,5},{8,10},{9,11},{10,... | collective-permute-start | bytes 12584 | tf_op jit(solution)/shard_map/ppermute | solution.py:749
  212.0 18.7 %collective-permute-start.28 = (bf16[4,4,32,256]{3,2,1,0:T(8,128)(2,1)S(1)}, bf16[4,4,32,256]{3,2,1,0:T(8,128)(2,1)S(1)}, u32[]{:S(2)}, u32[]{:S(2)}) collective-permute-start(bf16[4,4,32,256]{3,2,1,0:T(8,128)(2,1)S(1)} %get-tuple-element.163), channel_id=1, source_target_pairs={{0,5},{1,4},{2,7},{3,6},{4,1},{5,0},{6,3},{7,2},{8,13},{9,12},{10,... | collective-permute-start | bytes 786440 | tf_op jit(solution)/shard_map/ppermute | solution.py:749
  214.9 15.7 %collective-permute-start.27 = (bf16[4,4,32,256]{3,2,1,0:T(8,128)(2,1)S(1)}, bf16[4,4,32,256]{3,2,1,0:T(8,128)(2,1)S(1)}, u32[]{:S(2)}, u32[]{:S(2)}) collective-permute-start(bf16[4,4,32,256]{3,2,1,0:T(8,128)(2,1)S(1)} %get-tuple-element.164), channel_id=1, source_target_pairs={{0,1},{1,0},{2,3},{3,2},{4,5},{5,4},{6,7},{7,6},{8,9},{9,8},{10,11... | collective-permute-start | bytes 786440 | tf_op jit(solution)/shard_map/ppermute | solution.py:749
  214.9 15.7 %collective-permute-start.26 = (bf16[4,4,32,256]{3,2,1,0:T(8,128)(2,1)S(1)}, bf16[4,4,32,256]{3,2,1,0:T(8,128)(2,1)S(1)}, u32[]{:S(2)}, u32[]{:S(2)}) collective-permute-start(bf16[4,4,32,256]{3,2,1,0:T(8,128)(2,1)S(1)} %get-tuple-element.165), channel_id=1, source_target_pairs={{0,4},{1,5},{2,6},{3,7},{4,0},{5,1},{6,2},{7,3},{8,12},{9,13},{10,... | collective-permute-start | bytes 786440 | tf_op jit(solution)/shard_map/ppermute | solution.py:749
  215.6 11.4 %collective-permute-start.24 = (f32[1,1048]{1,0:T(1,128)S(1)}, f32[1,1048]{1,0:T(1,128)S(1)}, u32[]{:S(2)}, u32[]{:S(2)}) collective-permute-start(f32[1,1048]{1,0:T(1,128)S(1)} %reshape_add_fusion), channel_id=1, source_target_pairs={{0,1},{1,0},{2,3},{3,2},{4,5},{5,4},{6,7},{7,6},{8,9},{9,8},{10,11... | collective-permute-start | bytes 12584 | tf_op jit(solution)/shard_map/ppermute | solution.py:749
  230.9 4.6 %collective-permute-start.29 = (f32[1,1048]{1,0:T(1,128)S(1)}, f32[1,1048]{1,0:T(1,128)S(1)}, u32[]{:S(2)}, u32[]{:S(2)}) collective-permute-start(f32[1,1048]{1,0:T(1,128)S(1)} %add.108), channel_id=1, source_target_pairs={{0,16},{1,17},{2,18},{3,19},{4,20},{5,21},{6,22},{7,23},{8,24},{9,... | collective-permute-start | bytes 12584 | tf_op jit(solution)/shard_map/ppermute | solution.py:749
  235.5 7.8 %collective-permute-start.30 = (f32[1,1048]{1,0:T(1,128)S(1)}, f32[1,1048]{1,0:T(1,128)S(1)}, u32[]{:S(2)}, u32[]{:S(2)}) collective-permute-start(f32[1,1048]{1,0:T(1,128)S(1)} %add.112), channel_id=1, source_target_pairs={{0,8},{1,9},{2,10},{3,11},{4,12},{5,13},{6,14},{7,15},{8,0},{9,1},... | collective-permute-start | bytes 12584 | tf_op jit(solution)/shard_map/ppermute | solution.py:749
  238.8 6.1 %collective-permute-start.33 = (bf16[1,4,32,256]{3,2,1,0:T(8,128)(2,1)S(1)}, bf16[1,4,32,256]{3,2,1,0:T(8,128)(2,1)S(1)}, u32[]{:S(2)}, u32[]{:S(2)}) collective-permute-start(bf16[1,4,32,256]{3,2,1,0:T(8,128)(2,1)S(1)} %get-tuple-element.171), channel_id=1, source_target_pairs={{0,24},{1,25},{2,26},{3,27},{4,28},{5,29},{6,30},{7,31},{8,16},{9,... | collective-permute-start | bytes 196616 | tf_op jit(solution)/shard_map/ppermute | solution.py:749
  240.1 6.2 %collective-permute-start.32 = (bf16[1,4,32,256]{3,2,1,0:T(8,128)(2,1)S(1)}, bf16[1,4,32,256]{3,2,1,0:T(8,128)(2,1)S(1)}, u32[]{:S(2)}, u32[]{:S(2)}) collective-permute-start(bf16[1,4,32,256]{3,2,1,0:T(8,128)(2,1)S(1)} %get-tuple-element.172), channel_id=1, source_target_pairs={{0,16},{1,17},{2,18},{3,19},{4,20},{5,21},{6,22},{7,23},{8,24},{9,... | collective-permute-start | bytes 196616 | tf_op jit(solution)/shard_map/ppermute | solution.py:749
  240.3 6.0 %collective-permute-start.31 = (bf16[1,4,32,256]{3,2,1,0:T(8,128)(2,1)S(1)}, bf16[1,4,32,256]{3,2,1,0:T(8,128)(2,1)S(1)}, u32[]{:S(2)}, u32[]{:S(2)}) collective-permute-start(bf16[1,4,32,256]{3,2,1,0:T(8,128)(2,1)S(1)} %get-tuple-element.173), channel_id=1, source_target_pairs={{0,8},{1,9},{2,10},{3,11},{4,12},{5,13},{6,14},{7,15},{8,0},{9,1},... | collective-permute-start | bytes 196616 | tf_op jit(solution)/shard_map/ppermute | solution.py:749
  (15 other events, 115.6 us)

commit v10 on v9

--- a/solution.py
+++ b/solution.py
@@ -322,7 +322,7 @@
             finish()
         return carry
 
-    lax.fori_loop(0, rows // ROWS // 2, body, 0, unroll=2)
+    lax.fori_loop(0, rows // ROWS // 2, body, 0, unroll=4)
 
 
 def near_back(scores, grad_pair, bias, spread_near):
@@ -558,7 +558,7 @@
             finish()
         return carry
 
-    lax.fori_loop(0, steps // 2, body, 0, unroll=2)
+    lax.fori_loop(0, steps // 2, body, 0, unroll=4)
 
 
 def feed_kernel(
@@ -1103,9 +1103,11 @@
     total_sums = total_sums + peer(total_sums, [hops[2]], 1)
     for group in reversed(groups[:-2]):
         parts = jnp.split(share, 1 << len(group), axis=0)
-        gives = [part.astype(BF16) for part in parts[1:]]
-        total_sums, _ = lax.optimization_barrier((total_sums, gives))
-        share = narrow(parts[0], gives, group)
+        arrived = [
+            peer(part.astype(BF16), group, combo) for combo, part in enumerate(parts[1:], 1)
+        ]
+        total_sums, _ = lax.optimization_barrier((total_sums, arrived[0]))
+        share = parts[0] + sum(part.astype(F32) for part in arrived)
     for pair in hops[3:]:
         total_sums = total_sums + peer(total_sums, [pair], 1)
     total_sums = total_sums[0]

time: 248 us -> 247 us (level)
  starting transfers between devices: 45.4 us -> 41.9 us
  waiting for transfers between devices: 18.2 us -> 21.6 us
    ppermute x32, waiting for transfers between devices: 16.4 us -> 19.8 us  [peer(): return lax.ppermute(array, ('dp', 'head'), pairs)]
    ppermute x32, starting transfers between devices: 40.3 us -> 37.1 us  [peer(): return lax.ppermute(array, ('dp', 'head'), pairs)]
  transfers between devices with their start and end apart: 34 -> 34, of which waited for: 11 -> 10; matrix products, arithmetic and copies ran while one was open for 10% -> 10% of each run, Pallas kernels for 39% -> 39%
where the time goes in v10:
time: 247 us; the launch traced here: 246 us
  Pallas kernels  149 us (60%)
  starting transfers between devices  41.9 us (17%)
  waiting for transfers between devices  21.6 us (9%)
  other arithmetic  17.1 us (7%)
  local copies, waits for them, and re-layouts  14.9 us (6%)
    pallas_call x2, Pallas kernels, per_device(): call(backward_kernel, [spec['qkv'], spec['message']] + [spec['start']] *...  40.1 us
    ppermute x32, starting transfers between devices, peer(): return lax.ppermute(array, ('dp', 'head'), pairs)  37.1 us
    pallas_call x1, Pallas kernels, per_device(): call(feed_kernel, [row_spec] * 3 + [whole_spec((width, width)), whole_spe...  26.1 us
    pallas_call x2, Pallas kernels, per_device(): call(functools.partial(resume, forward_kernel, 7, len(results)), [spec['q...  25.6 us
    ppermute x32, waiting for transfers between devices, peer(): return lax.ppermute(array, ('dp', 'head'), pairs)  19.8 us
    pallas_call x2, Pallas kernels, feed_grad(): call(feed_grad_kernel, [whole_rows] * 2 + [columns] * 2 + more_in_specs,...  19.4 us
    pallas_call x1, Pallas kernels, per_device(): call(functools.partial(project_kernel, flips=flips), [pl.BlockSpec((part,...  10.2 us
    pallas_call x1, Pallas kernels, per_device(): call(prologue_kernel, [spec['query'], pl.BlockSpec((1, ROWS, PAIR), lambd...  9.66 us
  transfers between devices with their start and end apart: 34, of which 10 were waited for; matrix products, arithmetic and copies ran while one was open for 10% of the time, Pallas kernels for 39%

profile of v10, /device:TPU:0, one launch (start us, length us, event | category | flops | bytes accessed | tf_op | source)
XLA Modules:
  0.0 246.0 jit_solution(5545543415192099015)
XLA Ops:
  1.5 5.1 %collective-permute-start.2 = (bf16[1,4,32,256]{3,2,1,0:T(8,128)(2,1)S(1)}, bf16[1,4,32,256]{3,2,1,0:T(8,128)(2,1)S(1)}, u32[]{:S(2)}, u32[]{:S(2)}) collective-permute-start(bf16[1,4,32,256]{3,2,1,0:T(8,128)(2,1)S(1)} %maximum_bitcast_fusion), channel_id=1, source_target_pairs={{0,24},{1,25},{2,26},{3,27},{4,28},{5,29},{6,30},{7,31},{8,16},{9,... | collective-permute-start | bytes 196616 | tf_op jit(solution)/shard_map/ppermute | solution.py:749
  12.3 2.5 %collective-permute-start.5 = (bf16[4,4,32,256]{3,2,1,0:T(8,128)(2,1)S(1)}, bf16[4,4,32,256]{3,2,1,0:T(8,128)(2,1)S(1)}, u32[]{:S(2)}, u32[]{:S(2)}) collective-permute-start(bf16[4,4,32,256]{3,2,1,0:T(8,128)(2,1)S(1)} %pad_maximum_fusion), channel_id=1, source_target_pairs={{0,5},{1,4},{2,7},{3,6},{4,1},{5,0},{6,3},{7,2},{8,13},{9,12},{10,... | collective-permute-start | bytes 786440 | tf_op jit(solution)/shard_map/ppermute | solution.py:749
  16.9 2.4 convert_convert_fusion.refs_4_.far_ref
  19.3 3.3 %fusion.6 = (f32[1536,128]{1,0:T(8,128)}, bf16[1536,128]{1,0:T(8,128)(2,1)}) fusion(f32[1536]{0:T(1024)S(1)} %get-tuple-element.181, f32[1536]{0:T(1024)S(1)} %get-tuple-element.180, s32[1536]{0:T(1024)S(1)} %get-tuple-element.184, s32[1536]{0:T(1024)S(1)} %get-tuple-element.185, s32[1536]{0:T(1024)S(1)} %get-tuple-element.80, ...), kind=kLoop, calls=%fused_computation.14 | loop fusion | flops 2359296 | bytes 1218048 | tf_op jit(solution)/shard_map/jit(_where)/select_n | solution.py:79
  22.6 4.1 %collective-permute-done.3 = bf16[4,4,32,256]{3,2,1,0:T(8,128)(2,1)S(1)} collective-permute-done((bf16[4,4,32,256]{3,2,1,0:T(8,128)(2,1)S(1)}, bf16[4,4,32,256]{3,2,1,0:T(8,128)(2,1)S(1)}, u32[]{:S(2)}, u32[]{:S(2)}) %collective-permute-start.3) | collective-permute-done | bytes 262176 | tf_op jit(solution)/shard_map/ppermute | solution.py:749
  30.4 1.9 concatenate.29.scalars.refs_0_
  34.6 10.2 %project.1 = (bf16[3,1536,512]{2,1,0:T(8,128)(2,1)}, bf16[1536,512]{1,0:T(8,128)(2,1)}, bf16[3,512,512]{2,1,0:T(8,128)(2,1)}, bf16[512,512]{1,0:T(8,128)(2,1)}, bf16[4,96,384]{2,1,0:T(8,128)(2,1)}) custom-call(s32[21]{0:T(128)} %concatenate.29.scalars.refs_0_, bf16[1536,512]{1,0:T(8,128)(2,1)} %tokens_ref.5, f32[1,512]{1,0:T(1,128)} %bitcast.34, ...), custom_call_target="tpu_custom_call" | custom-call | flops 2415919104 | bytes 9437184 | tf_op jit(solution)/shard_map/project/pallas_call | solution.py:854
  44.7 3.6 %collective-permute-start.12 = (bf16[4,96,384]{2,1,0:T(8,128)(2,1)}, bf16[4,96,384]{2,1,0:T(8,128)(2,1)S(1)}, u32[]{:S(2)}, u32[]{:S(2)}) collective-permute-start(bf16[4,96,384]{2,1,0:T(8,128)(2,1)} %get-tuple-element.84), channel_id=1, source_target_pairs={{0,1},{2,3},{4,5},{6,7},{8,9},{10,11},{12,13},{14,15},{16,17},{18,... | collective-permute-start | bytes 884744 | tf_op jit(solution)/shard_map/ppermute | solution.py:775
  50.5 2.3 collective-permute-start.10
  54.1 1.7 collective-permute-done.12.refs_2_.message_ref
  56.5 16.7 %forward.2 = (bf16[1536,512]{1,0:T(8,128)(2,1)}, f32[1536,512]{1,0:T(8,128)}, f32[1536,512]{1,0:T(8,128)}, f32[1536,512]{1,0:T(8,128)}, f32[1536,512]{1,0:T(8,12...) custom-call(s32[21]{0:T(128)} %concatenate.29.scalars.refs_0_, ...), custom_call_target="tpu_custom_call" | custom-call | flops 4718592000 | bytes 23592960 | tf_op jit(solution)/shard_map/forward/pallas_call | solution.py:896
  73.3 4.2 %collective-permute-done.10 = bf16[2,256,512]{2,1,0:T(8,128)(2,1)S(1)} collective-permute-done((bf16[2,256,512]{2,1,0:T(8,128)(2,1)S(1)}, bf16[2,256,512]{2,1,0:T(8,128)(2,1)S(1)}, u32[]{:S(2)}, u32[]{:S(2)}) %collective-permute-start.10) | collective-permute-done | bytes 524320 | tf_op jit(solution)/shard_map/ppermute | solution.py:749
  77.7 8.8 %forward.3 = (bf16[1536,512]{1,0:T(8,128)(2,1)}, f32[1536,512]{1,0:T(8,128)}, f32[1536,512]{1,0:T(8,128)}, f32[1536,512]{1,0:T(8,128)}, f32[1536,512]{1,0:T(8,12...) custom-call(s32[21]{0:T(128)} %concatenate.29.scalars.refs_0_, ...), custom_call_target="tpu_custom_call", output_to_operand_aliasing={{0}: (7, {}), {1}: (8, {}), {2}: (9, {}), {3}: (10, {}), {4... | custom-call | flops 1572864000 | bytes 7864320 | tf_op jit(solution)/shard_map/forward/pallas_call | solution.py:896
  87.9 26.1 %feed.1 = (bf16[1536,512]{1,0:T(8,128)(2,1)}, f32[1536,512]{1,0:T(8,128)}, bf16[1536,512]{1,0:T(8,128)(2,1)}, bf16[1536,512]{1,0:T(8,128)(2,1)}, bf16[1536,512]{...) custom-call(s32[21]{0:T(128)} %concatenate.29.scalars.refs_0_, ...), custom_call_target="tpu_custom_call" | custom-call | flops 12884901888 | bytes 25165824 | tf_op jit(solution)/shard_map/feed/pallas_call | solution.py:926
  114.0 9.7 %prologue.1 = bf16[4,96,384]{2,1,0:T(8,128)(2,1)} custom-call(s32[21]{0:T(128)} %concatenate.29.scalars.refs_0_, bf16[3,1536,512]{2,1,0:T(8,128)(2,1)} %get-tuple-element.82.refs_1_.query_ref.key_ref.value_ref.qkv_ref, bf16[3,1536,512]{2,1,0:T(8,128)(2,1)} %get-tuple-element.82.refs_1_.query_ref.key_ref.value_ref.qkv_ref, ...), custom_call_target="tpu_custom_call" | custom-call | flops 393216000 | bytes 15728640 | tf_op jit(solution)/shard_map/prologue/pallas_call | solution.py:944
  123.6 8.6 %feed_grad.2 = bf16[2,1024,512]{2,1,0:T(8,128)(2,1)} custom-call(s32[21]{0:T(128)} %concatenate.29.scalars.refs_0_, bf16[1536,512]{1,0:T(8,128)(2,1)} %get-tuple-element.112.normed_ref, bf16[1536,512]{1,0:T(8,128)(2,1)} %cotangent_ref.5, bf16[1536,2048]{1,0:T(8,128)(2,1)} %get-tuple-element.113.active_ref, bf16[1536,2048]{1,0:T(8,128)(2,1)} %get-tuple-element.122.d_inner_ref), custom_call_target="tpu_custom_call" | custom-call | flops 3221225472 | bytes 9437184 | tf_op jit(solution)/shard_map/feed_grad/pallas_call | solution.py:976
  134.0 10.8 %feed_grad.3 = (f32[512,512]{1,0:T(8,128)}, f32[2,1024,512]{2,1,0:T(8,128)}) custom-call(s32[21]{0:T(128)} %concatenate.29.scalars.refs_0_, bf16[1536,512]{1,0:T(8,128)(2,1)} %get-tuple-element.112.normed_ref, bf16[1536,512]{1,0:T(8,128)(2,1)} %cotangent_ref.5, bf16[1536,2048]{1,0:T(8,128)(2,1)} %get-tuple-element.113.active_ref, ...), custom_call_target="tpu_custom_call" | custom-call | flops 3221225472 | bytes 9437184 | tf_op jit(solution)/shard_map/feed_grad/pallas_call | solution.py:976
  144.8 3.1 %fusion.17 = (bf16[2,1024,512]{2,1,0:T(8,128)(2,1)S(1)}, f32[2,1024,512]{2,1,0:T(8,128)S(1)}) fusion(f32[2,1024,512]{2,1,0:T(8,128)} %get-tuple-element.124, bf16[2,1024,512]{2,1,0:T(8,128)(2,1)S(1)} %collective-permute-done.14), kind=kLoop, calls=%fused_computation.69 | loop fusion | flops 3145728 | bytes 12582912 | tf_op jit(solution)/shard_map/convert.11
  149.6 2.7 %collective-permute-start.17 = (bf16[2,256,512]{2,1,0:T(8,128)(2,1)S(1)}, bf16[2,256,512]{2,1,0:T(8,128)(2,1)S(1)}, u32[]{:S(2)}, u32[]{:S(2)}) collective-permute-start(bf16[2,256,512]{2,1,0:T(8,128)(2,1)S(1)} %get-tuple-element.161), channel_id=1, source_target_pairs={{0,5},{1,4},{2,7},{3,6},{4,1},{5,0},{6,3},{7,2},{8,13},{9,12},{10,... | collective-permute-start | bytes 1572872 | tf_op jit(solution)/shard_map/ppermute | solution.py:749
  152.9 27.7 %backward.2 = (bf16[3,1536,512]{2,1,0:T(8,128)(2,1)}, f32[24,384]{1,0:T(8,128)}) custom-call(s32[21]{0:T(128)} %concatenate.29.scalars.refs_0_, bf16[3,1536,512]{2,1,0:T(8,128)(2,1)} %get-tuple-element.82.refs_1_.query_ref.key_ref.value_ref.qkv_ref, bf16[4,96,384]{2,1,0:T(8,128)(2,1)} %copy-done, bf16[1536,128]{1,0:T(8,128)(2,1)} %get-tuple-element.86.refs_3_.bias_ref, ...), custom_call_target="tpu_custom_call" | custom-call | flops 9437184000 | bytes 23592960 | tf_op jit(solution)/shard_map/backward/pallas_call | solution.py:1010
  180.9 1.8 collective-permute-start.18
  184.5 12.5 %backward.3 = (bf16[3,1536,512]{2,1,0:T(8,128)(2,1)}, f32[24,128]{1,0:T(8,128)}) custom-call(s32[21]{0:T(128)} %concatenate.29.scalars.refs_0_, bf16[3,1536,512]{2,1,0:T(8,128)(2,1)} %get-tuple-element.82.refs_1_.query_ref.key_ref.value_ref.qkv_ref, bf16[4,96,384]{2,1,0:T(8,128)(2,1)} %copy-done, ...), custom_call_target="tpu_custom_call", output_to_operand_aliasing={{0}: (15, {})} | custom-call | flops 3145728000 | bytes 7864320 | tf_op jit(solution)/shard_map/backward/pallas_call | solution.py:1010
  197.1 8.9 %weight_grad.1 = (f32[16,4,32,256]{3,2,1,0:T(8,128)}, bf16[16,4,32,256]{3,2,1,0:T(8,128)(2,1)}, f32[8,512]{1,0:T(8,128)}) custom-call(s32[21]{0:T(128)} %concatenate.29.scalars.refs_0_, bf16[1536,512]{1,0:T(8,128)(2,1)} %get-tuple-element.111.normed_ref, bf16[3,1536,512]{2,1,0:T(8,128)(2,1)} %get-tuple-element.140.d_qkv_ref, ...), custom_call_target="tpu_custom_call" | custom-call | flops 2415919104 | bytes 6291456 | tf_op jit(solution)/shard_map/weight_grad/pallas_call | solution.py:1057
  208.9 2.1 fusion.15
  211.0 3.0 %collective-permute-start.28 = (bf16[4,4,32,256]{3,2,1,0:T(8,128)(2,1)S(1)}, bf16[4,4,32,256]{3,2,1,0:T(8,128)(2,1)S(1)}, u32[]{:S(2)}, u32[]{:S(2)}) collective-permute-start(bf16[4,4,32,256]{3,2,1,0:T(8,128)(2,1)S(1)} %get-tuple-element.163), channel_id=1, source_target_pairs={{0,5},{1,4},{2,7},{3,6},{4,1},{5,0},{6,3},{7,2},{8,13},{9,12},{10,... | collective-permute-start | bytes 786440 | tf_op jit(solution)/shard_map/ppermute | solution.py:749
  214.7 2.0 collective-permute-start.24
  216.7 8.9 %input.1 = f32[1536,512]{1,0:T(8,128)} custom-call(s32[21]{0:T(128)} %concatenate.29.scalars.refs_0_, bf16[3,1536,512]{2,1,0:T(8,128)(2,1)} %get-tuple-element.140.d_qkv_ref, bf16[3,512,512]{2,1,0:T(8,128)(2,1)} %get-tuple-element.133.weight_ref, bf16[1536,512]{1,0:T(8,128)(2,1)} %tokens_ref.5, f32[1536,512]{1,0:T(8,128)} %get-tuple-element.141.d_hidden_ref, ...), custom_call_target="tpu_custom_call" | custom-call | flops 2415919104 | bytes 18874368 | tf_op jit(solution)/shard_map/input/pallas_call | solution.py:1084
  227.3 2.6 %collective-permute-start.32 = (bf16[1,4,32,256]{3,2,1,0:T(8,128)(2,1)S(1)}, bf16[1,4,32,256]{3,2,1,0:T(8,128)(2,1)S(1)}, u32[]{:S(2)}, u32[]{:S(2)}) collective-permute-start(bf16[1,4,32,256]{3,2,1,0:T(8,128)(2,1)S(1)} %get-tuple-element.171), channel_id=1, source_target_pairs={{0,16},{1,17},{2,18},{3,19},{4,20},{5,21},{6,22},{7,23},{8,24},{9,... | collective-permute-start | bytes 196616 | tf_op jit(solution)/shard_map/ppermute | solution.py:749
  229.8 2.5 %collective-permute-start.33 = (bf16[1,4,32,256]{3,2,1,0:T(8,128)(2,1)S(1)}, bf16[1,4,32,256]{3,2,1,0:T(8,128)(2,1)S(1)}, u32[]{:S(2)}, u32[]{:S(2)}) collective-permute-start(bf16[1,4,32,256]{3,2,1,0:T(8,128)(2,1)S(1)} %get-tuple-element.172), channel_id=1, source_target_pairs={{0,24},{1,25},{2,26},{3,27},{4,28},{5,29},{6,30},{7,31},{8,16},{9,... | collective-permute-start | bytes 196616 | tf_op jit(solution)/shard_map/ppermute | solution.py:749
  233.1 3.5 %collective-permute-done.29 = bf16[1,4,32,256]{3,2,1,0:T(8,128)(2,1)S(1)} collective-permute-done((bf16[1,4,32,256]{3,2,1,0:T(8,128)(2,1)S(1)}, bf16[1,4,32,256]{3,2,1,0:T(8,128)(2,1)S(1)}, u32[]{:S(2)}, u32[]{:S(2)}) %collective-permute-start.29) | collective-permute-done | bytes 65568 | tf_op jit(solution)/shard_map/ppermute | solution.py:749
  237.9 3.3 %collective-permute-done.30 = f32[1,1048]{1,0:T(1,128)S(1)} collective-permute-done((f32[1,1048]{1,0:T(1,128)S(1)}, f32[1,1048]{1,0:T(1,128)S(1)}, u32[]{:S(2)}, u32[]{:S(2)}) %collective-permute-start.30) | collective-permute-done | bytes 4224 | tf_op jit(solution)/shard_map/ppermute | solution.py:749
  242.5 2.3 collective-permute-done.31
  (138 shorter events, 35.7 us)
Async XLA Ops:
  1.5 10.2 %collective-permute-start.2 = (bf16[1,4,32,256]{3,2,1,0:T(8,128)(2,1)S(1)}, bf16[1,4,32,256]{3,2,1,0:T(8,128)(2,1)S(1)}, u32[]{:S(2)}, u32[]{:S(2)}) collective-permute-start(bf16[1,4,32,256]{3,2,1,0:T(8,128)(2,1)S(1)} %maximum_bitcast_fusion), channel_id=1, source_target_pairs={{0,24},{1,25},{2,26},{3,27},{4,28},{5,29},{6,30},{7,31},{8,16},{9,... | collective-permute-start | bytes 196616 | tf_op jit(solution)/shard_map/ppermute | solution.py:749
  6.6 5.6 %collective-permute-start.1 = (bf16[1,4,32,256]{3,2,1,0:T(8,128)(2,1)S(1)}, bf16[1,4,32,256]{3,2,1,0:T(8,128)(2,1)S(1)}, u32[]{:S(2)}, u32[]{:S(2)}) collective-permute-start(bf16[1,4,32,256]{3,2,1,0:T(8,128)(2,1)S(1)} %maximum_bitcast_fusion), channel_id=1, source_target_pairs={{0,16},{1,17},{2,18},{3,19},{4,20},{5,21},{6,22},{7,23},{8,24},{9,... | collective-permute-start | bytes 196616 | tf_op jit(solution)/shard_map/ppermute | solution.py:749
  6.6 5.6 %collective-permute-start = (bf16[1,4,32,256]{3,2,1,0:T(8,128)(2,1)S(1)}, bf16[1,4,32,256]{3,2,1,0:T(8,128)(2,1)S(1)}, u32[]{:S(2)}, u32[]{:S(2)}) collective-permute-start(bf16[1,4,32,256]{3,2,1,0:T(8,128)(2,1)S(1)} %maximum_bitcast_fusion), channel_id=1, source_target_pairs={{0,8},{1,9},{2,10},{3,11},{4,12},{5,13},{6,14},{7,15},{8,0},{9,1},... | collective-permute-start | bytes 196616 | tf_op jit(solution)/shard_map/ppermute | solution.py:749
  12.3 14.7 %collective-permute-start.5 = (bf16[4,4,32,256]{3,2,1,0:T(8,128)(2,1)S(1)}, bf16[4,4,32,256]{3,2,1,0:T(8,128)(2,1)S(1)}, u32[]{:S(2)}, u32[]{:S(2)}) collective-permute-start(bf16[4,4,32,256]{3,2,1,0:T(8,128)(2,1)S(1)} %pad_maximum_fusion), channel_id=1, source_target_pairs={{0,5},{1,4},{2,7},{3,6},{4,1},{5,0},{6,3},{7,2},{8,13},{9,12},{10,... | collective-permute-start | bytes 786440 | tf_op jit(solution)/shard_map/ppermute | solution.py:749
  14.8 12.2 %collective-permute-start.4 = (bf16[4,4,32,256]{3,2,1,0:T(8,128)(2,1)S(1)}, bf16[4,4,32,256]{3,2,1,0:T(8,128)(2,1)S(1)}, u32[]{:S(2)}, u32[]{:S(2)}) collective-permute-start(bf16[4,4,32,256]{3,2,1,0:T(8,128)(2,1)S(1)} %pad_maximum_fusion), channel_id=1, source_target_pairs={{0,1},{1,0},{2,3},{3,2},{4,5},{5,4},{6,7},{7,6},{8,9},{9,8},{10,11... | collective-permute-start | bytes 786440 | tf_op jit(solution)/shard_map/ppermute | solution.py:749
  15.3 11.4 %collective-permute-start.3 = (bf16[4,4,32,256]{3,2,1,0:T(8,128)(2,1)S(1)}, bf16[4,4,32,256]{3,2,1,0:T(8,128)(2,1)S(1)}, u32[]{:S(2)}, u32[]{:S(2)}) collective-permute-start(bf16[4,4,32,256]{3,2,1,0:T(8,128)(2,1)S(1)} %pad_maximum_fusion), channel_id=1, source_target_pairs={{0,4},{1,5},{2,6},{3,7},{4,0},{5,1},{6,2},{7,3},{8,12},{9,13},{10,... | collective-permute-start | bytes 786440 | tf_op jit(solution)/shard_map/ppermute | solution.py:749
  15.8 6.8 %collective-permute-start.6 = (bf16[2,64,512]{2,1,0:T(8,128)(2,1)S(1)}, bf16[2,64,512]{2,1,0:T(8,128)(2,1)S(1)}, u32[]{:S(2)}, u32[]{:S(2)}) collective-permute-start(bf16[2,64,512]{2,1,0:T(8,128)(2,1)S(1)} %pad_maximum_fusion.2), channel_id=1, source_target_pairs={{0,8},{1,9},{2,10},{3,11},{4,12},{5,13},{6,14},{7,15},{8,0},{9,1},... | collective-permute-start | bytes 393224 | tf_op jit(solution)/shard_map/ppermute | solution.py:749
  28.2 5.4 %collective-permute-start.7 = (bf16[16,4,32,256]{3,2,1,0:T(8,128)(2,1)S(1)}, bf16[16,4,32,256]{3,2,1,0:T(8,128)(2,1)S(1)}, u32[]{:S(2)}, u32[]{:S(2)}) collective-permute-start(bf16[16,4,32,256]{3,2,1,0:T(8,128)(2,1)S(1)} %constant_dynamic-update-slice_fusion.own_ref), channel_id=1, source_target_pairs={{0,2},{1,3},{2,0},{3,1},{4,6},{5,7},{6,4},{7,5},{8,10},{9,11},{10,... | collective-permute-start | bytes 3145736 | tf_op jit(solution)/shard_map/ppermute | solution.py:749
  32.3 16.8 %collective-permute-start.8 = (bf16[2,128,512]{2,1,0:T(8,128)(2,1)S(1)}, bf16[2,128,512]{2,1,0:T(8,128)(2,1)S(1)}, u32[]{:S(2)}, u32[]{:S(2)}) collective-permute-start(bf16[2,128,512]{2,1,0:T(8,128)(2,1)S(1)} %pad_maximum_fusion.1), channel_id=1, source_target_pairs={{0,16},{1,17},{2,18},{3,19},{4,20},{5,21},{6,22},{7,23},{8,24},{9,... | collective-permute-start | bytes 786440 | tf_op jit(solution)/shard_map/ppermute | solution.py:749
  44.7 11.1 %collective-permute-start.12 = (bf16[4,96,384]{2,1,0:T(8,128)(2,1)}, bf16[4,96,384]{2,1,0:T(8,128)(2,1)S(1)}, u32[]{:S(2)}, u32[]{:S(2)}) collective-permute-start(bf16[4,96,384]{2,1,0:T(8,128)(2,1)} %get-tuple-element.84), channel_id=1, source_target_pairs={{0,1},{2,3},{4,5},{6,7},{8,9},{10,11},{12,13},{14,15},{16,17},{18,... | collective-permute-start | bytes 884744 | tf_op jit(solution)/shard_map/ppermute | solution.py:775
  49.8 23.5 %collective-permute-start.11 = (bf16[2,256,512]{2,1,0:T(8,128)(2,1)S(1)}, bf16[2,256,512]{2,1,0:T(8,128)(2,1)S(1)}, u32[]{:S(2)}, u32[]{:S(2)}) collective-permute-start(bf16[2,256,512]{2,1,0:T(8,128)(2,1)S(1)} %get-tuple-element.174), channel_id=1, source_target_pairs={{0,5},{1,4},{2,7},{3,6},{4,1},{5,0},{6,3},{7,2},{8,13},{9,12},{10,... | collective-permute-start | bytes 1572872 | tf_op jit(solution)/shard_map/ppermute | solution.py:749
  50.5 27.0 %collective-permute-start.10 = (bf16[2,256,512]{2,1,0:T(8,128)(2,1)S(1)}, bf16[2,256,512]{2,1,0:T(8,128)(2,1)S(1)}, u32[]{:S(2)}, u32[]{:S(2)}) collective-permute-start(bf16[2,256,512]{2,1,0:T(8,128)(2,1)S(1)} %get-tuple-element.174), channel_id=1, source_target_pairs={{0,1},{1,0},{2,3},{3,2},{4,5},{5,4},{6,7},{7,6},{8,9},{9,8},{10,11... | collective-permute-start | bytes 1572872 | tf_op jit(solution)/shard_map/ppermute | solution.py:749
  52.8 24.7 %collective-permute-start.9 = (bf16[2,256,512]{2,1,0:T(8,128)(2,1)S(1)}, bf16[2,256,512]{2,1,0:T(8,128)(2,1)S(1)}, u32[]{:S(2)}, u32[]{:S(2)}) collective-permute-start(bf16[2,256,512]{2,1,0:T(8,128)(2,1)S(1)} %get-tuple-element.174), channel_id=1, source_target_pairs={{0,4},{1,5},{2,6},{3,7},{4,0},{5,1},{6,2},{7,3},{8,12},{9,13},{10,... | collective-permute-start | bytes 1572872 | tf_op jit(solution)/shard_map/ppermute | solution.py:749
  77.6 8.9 %collective-permute-start.13 = (bf16[2,1024,512]{2,1,0:T(8,128)(2,1)S(1)}, bf16[2,1024,512]{2,1,0:T(8,128)(2,1)S(1)}, u32[]{:S(2)}, u32[]{:S(2)}) collective-permute-start(bf16[2,1024,512]{2,1,0:T(8,128)(2,1)S(1)} %constant_dynamic-update-slice_fusion.9.own_ref), channel_id=1, source_target_pairs={{0,2},{1,3},{2,0},{3,1},{4,6},{5,7},{6,4},{7,5},{8,10},{9,11},{10,... | collective-permute-start | bytes 6291464 | tf_op jit(solution)/shard_map/ppermute | solution.py:749
  132.2 12.6 %collective-permute-start.14 = (bf16[2,1024,512]{2,1,0:T(8,128)(2,1)}, bf16[2,1024,512]{2,1,0:T(8,128)(2,1)S(1)}, u32[]{:S(2)}, u32[]{:S(2)}) collective-permute-start(bf16[2,1024,512]{2,1,0:T(8,128)(2,1)} %feed_grad.2), channel_id=1, source_target_pairs={{0,2},{1,3},{2,0},{3,1},{4,6},{5,7},{6,4},{7,5},{8,10},{9,11},{10,... | collective-permute-start | bytes 6291464 | tf_op jit(solution)/shard_map/ppermute | solution.py:749
  132.7 15.3 %collective-permute-start.21 = (bf16[4,96,384]{2,1,0:T(8,128)(2,1)S(1)}, bf16[4,96,384]{2,1,0:T(8,128)(2,1)S(1)}, u32[]{:S(2)}, u32[]{:S(2)}) collective-permute-start(bf16[4,96,384]{2,1,0:T(8,128)(2,1)S(1)} %copy-done.1), channel_id=1, source_target_pairs={{1,0},{3,2},{5,4},{7,6},{9,8},{11,10},{13,12},{15,14},{17,16},{19,... | collective-permute-start | bytes 884744 | tf_op jit(solution)/shard_map/ppermute | solution.py:775
  148.1 32.5 %collective-permute-start.15 = (bf16[2,256,512]{2,1,0:T(8,128)(2,1)S(1)}, bf16[2,256,512]{2,1,0:T(8,128)(2,1)S(1)}, u32[]{:S(2)}, u32[]{:S(2)}) collective-permute-start(bf16[2,256,512]{2,1,0:T(8,128)(2,1)S(1)} %get-tuple-element.160), channel_id=1, source_target_pairs={{0,4},{1,5},{2,6},{3,7},{4,0},{5,1},{6,2},{7,3},{8,12},{9,13},{10,... | collective-permute-start | bytes 1572872 | tf_op jit(solution)/shard_map/ppermute | solution.py:749
  149.6 31.0 %collective-permute-start.17 = (bf16[2,256,512]{2,1,0:T(8,128)(2,1)S(1)}, bf16[2,256,512]{2,1,0:T(8,128)(2,1)S(1)}, u32[]{:S(2)}, u32[]{:S(2)}) collective-permute-start(bf16[2,256,512]{2,1,0:T(8,128)(2,1)S(1)} %get-tuple-element.161), channel_id=1, source_target_pairs={{0,5},{1,4},{2,7},{3,6},{4,1},{5,0},{6,3},{7,2},{8,13},{9,12},{10,... | collective-permute-start | bytes 1572872 | tf_op jit(solution)/shard_map/ppermute | solution.py:749
  152.3 28.3 %collective-permute-start.16 = (bf16[2,256,512]{2,1,0:T(8,128)(2,1)S(1)}, bf16[2,256,512]{2,1,0:T(8,128)(2,1)S(1)}, u32[]{:S(2)}, u32[]{:S(2)}) collective-permute-start(bf16[2,256,512]{2,1,0:T(8,128)(2,1)S(1)} %get-tuple-element.162), channel_id=1, source_target_pairs={{0,1},{1,0},{2,3},{3,2},{4,5},{5,4},{6,7},{7,6},{8,9},{9,8},{10,11... | collective-permute-start | bytes 1572872 | tf_op jit(solution)/shard_map/ppermute | solution.py:749
  180.9 16.0 %collective-permute-start.18 = (bf16[2,64,512]{2,1,0:T(8,128)(2,1)S(1)}, bf16[2,64,512]{2,1,0:T(8,128)(2,1)S(1)}, u32[]{:S(2)}, u32[]{:S(2)}) collective-permute-start(bf16[2,64,512]{2,1,0:T(8,128)(2,1)S(1)} %get-tuple-element.166), channel_id=1, source_target_pairs={{0,8},{1,9},{2,10},{3,11},{4,12},{5,13},{6,14},{7,15},{8,0},{9,1},... | collective-permute-start | bytes 393224 | tf_op jit(solution)/shard_map/ppermute | solution.py:749
  182.7 14.2 %collective-permute-start.20 = (bf16[2,64,512]{2,1,0:T(8,128)(2,1)S(1)}, bf16[2,64,512]{2,1,0:T(8,128)(2,1)S(1)}, u32[]{:S(2)}, u32[]{:S(2)}) collective-permute-start(bf16[2,64,512]{2,1,0:T(8,128)(2,1)S(1)} %get-tuple-element.167), channel_id=1, source_target_pairs={{0,24},{1,25},{2,26},{3,27},{4,28},{5,29},{6,30},{7,31},{8,16},{9,... | collective-permute-start | bytes 393224 | tf_op jit(solution)/shard_map/ppermute | solution.py:749
  184.0 12.9 %collective-permute-start.19 = (bf16[2,64,512]{2,1,0:T(8,128)(2,1)S(1)}, bf16[2,64,512]{2,1,0:T(8,128)(2,1)S(1)}, u32[]{:S(2)}, u32[]{:S(2)}) collective-permute-start(bf16[2,64,512]{2,1,0:T(8,128)(2,1)S(1)} %get-tuple-element.168), channel_id=1, source_target_pairs={{0,16},{1,17},{2,18},{3,19},{4,20},{5,21},{6,22},{7,23},{8,24},{9,... | collective-permute-start | bytes 393224 | tf_op jit(solution)/shard_map/ppermute | solution.py:749
  207.1 7.6 %collective-permute-start.22 = (f32[1,1048]{1,0:T(1,128)S(1)}, f32[1,1048]{1,0:T(1,128)S(1)}, u32[]{:S(2)}, u32[]{:S(2)}) collective-permute-start(f32[1,1048]{1,0:T(1,128)S(1)} %broadcast_in_dim.149), channel_id=1, source_target_pairs={{0,2},{1,3},{2,0},{3,1},{4,6},{5,7},{6,4},{7,5},{8,10},{9,11},{10,... | collective-permute-start | bytes 12584 | tf_op jit(solution)/shard_map/ppermute | solution.py:749
  211.0 16.0 %collective-permute-start.28 = (bf16[4,4,32,256]{3,2,1,0:T(8,128)(2,1)S(1)}, bf16[4,4,32,256]{3,2,1,0:T(8,128)(2,1)S(1)}, u32[]{:S(2)}, u32[]{:S(2)}) collective-permute-start(bf16[4,4,32,256]{3,2,1,0:T(8,128)(2,1)S(1)} %get-tuple-element.163), channel_id=1, source_target_pairs={{0,5},{1,4},{2,7},{3,6},{4,1},{5,0},{6,3},{7,2},{8,13},{9,12},{10,... | collective-permute-start | bytes 786440 | tf_op jit(solution)/shard_map/ppermute | solution.py:749
  214.0 13.1 %collective-permute-start.27 = (bf16[4,4,32,256]{3,2,1,0:T(8,128)(2,1)S(1)}, bf16[4,4,32,256]{3,2,1,0:T(8,128)(2,1)S(1)}, u32[]{:S(2)}, u32[]{:S(2)}) collective-permute-start(bf16[4,4,32,256]{3,2,1,0:T(8,128)(2,1)S(1)} %get-tuple-element.164), channel_id=1, source_target_pairs={{0,1},{1,0},{2,3},{3,2},{4,5},{5,4},{6,7},{7,6},{8,9},{9,8},{10,11... | collective-permute-start | bytes 786440 | tf_op jit(solution)/shard_map/ppermute | solution.py:749
  214.0 13.1 %collective-permute-start.26 = (bf16[4,4,32,256]{3,2,1,0:T(8,128)(2,1)S(1)}, bf16[4,4,32,256]{3,2,1,0:T(8,128)(2,1)S(1)}, u32[]{:S(2)}, u32[]{:S(2)}) collective-permute-start(bf16[4,4,32,256]{3,2,1,0:T(8,128)(2,1)S(1)} %get-tuple-element.165), channel_id=1, source_target_pairs={{0,4},{1,5},{2,6},{3,7},{4,0},{5,1},{6,2},{7,3},{8,12},{9,13},{10,... | collective-permute-start | bytes 786440 | tf_op jit(solution)/shard_map/ppermute | solution.py:749
  214.7 11.4 %collective-permute-start.24 = (f32[1,1048]{1,0:T(1,128)S(1)}, f32[1,1048]{1,0:T(1,128)S(1)}, u32[]{:S(2)}, u32[]{:S(2)}) collective-permute-start(f32[1,1048]{1,0:T(1,128)S(1)} %reshape_add_fusion), channel_id=1, source_target_pairs={{0,1},{1,0},{2,3},{3,2},{4,5},{5,4},{6,7},{7,6},{8,9},{9,8},{10,11... | collective-permute-start | bytes 12584 | tf_op jit(solution)/shard_map/ppermute | solution.py:749
  226.1 7.0 %collective-permute-start.25 = (f32[1,1048]{1,0:T(1,128)S(1)}, f32[1,1048]{1,0:T(1,128)S(1)}, u32[]{:S(2)}, u32[]{:S(2)}) collective-permute-start(f32[1,1048]{1,0:T(1,128)S(1)} %add.107), channel_id=1, source_target_pairs={{0,4},{1,5},{2,6},{3,7},{4,0},{5,1},{6,2},{7,3},{8,12},{9,13},{10,... | collective-permute-start | bytes 12584 | tf_op jit(solution)/shard_map/ppermute | solution.py:749
  227.3 9.9 %collective-permute-start.32 = (bf16[1,4,32,256]{3,2,1,0:T(8,128)(2,1)S(1)}, bf16[1,4,32,256]{3,2,1,0:T(8,128)(2,1)S(1)}, u32[]{:S(2)}, u32[]{:S(2)}) collective-permute-start(bf16[1,4,32,256]{3,2,1,0:T(8,128)(2,1)S(1)} %get-tuple-element.171), channel_id=1, source_target_pairs={{0,16},{1,17},{2,18},{3,19},{4,20},{5,21},{6,22},{7,23},{8,24},{9,... | collective-permute-start | bytes 196616 | tf_op jit(solution)/shard_map/ppermute | solution.py:749
  229.8 7.3 %collective-permute-start.33 = (bf16[1,4,32,256]{3,2,1,0:T(8,128)(2,1)S(1)}, bf16[1,4,32,256]{3,2,1,0:T(8,128)(2,1)S(1)}, u32[]{:S(2)}, u32[]{:S(2)}) collective-permute-start(bf16[1,4,32,256]{3,2,1,0:T(8,128)(2,1)S(1)} %get-tuple-element.172), channel_id=1, source_target_pairs={{0,24},{1,25},{2,26},{3,27},{4,28},{5,29},{6,30},{7,31},{8,16},{9,... | collective-permute-start | bytes 196616 | tf_op jit(solution)/shard_map/ppermute | solution.py:749
  232.3 4.3 %collective-permute-start.29 = (bf16[1,4,32,256]{3,2,1,0:T(8,128)(2,1)S(1)}, bf16[1,4,32,256]{3,2,1,0:T(8,128)(2,1)S(1)}, u32[]{:S(2)}, u32[]{:S(2)}) collective-permute-start(bf16[1,4,32,256]{3,2,1,0:T(8,128)(2,1)S(1)} %get-tuple-element.173), channel_id=1, source_target_pairs={{0,8},{1,9},{2,10},{3,11},{4,12},{5,13},{6,14},{7,15},{8,0},{9,1},... | collective-permute-start | bytes 196616 | tf_op jit(solution)/shard_map/ppermute | solution.py:749
  236.6 4.5 %collective-permute-start.30 = (f32[1,1048]{1,0:T(1,128)S(1)}, f32[1,1048]{1,0:T(1,128)S(1)}, u32[]{:S(2)}, u32[]{:S(2)}) collective-permute-start(f32[1,1048]{1,0:T(1,128)S(1)} %add.108), channel_id=1, source_target_pairs={{0,16},{1,17},{2,18},{3,19},{4,20},{5,21},{6,22},{7,23},{8,24},{9,... | collective-permute-start | bytes 12584 | tf_op jit(solution)/shard_map/ppermute | solution.py:749
  (15 other events, 115.6 us)

commit v11 on v10

--- a/solution.py
+++ b/solution.py
@@ -1108,8 +1108,10 @@
         ]
         total_sums, _ = lax.optimization_barrier((total_sums, arrived[0]))
         share = parts[0] + sum(part.astype(F32) for part in arrived)
-    for pair in hops[3:]:
-        total_sums = total_sums + peer(total_sums, [pair], 1)
+    for place in range(3, len(hops), 2):
+        group = hops[place : place + 2]
+        arrived = [peer(total_sums, group, combo) for combo in range(1, 1 << len(group))]
+        total_sums = total_sums + sum(arrived)
     total_sums = total_sums[0]
     gain_one, gain_two = total_sums[:width], total_sums[width : 2 * width]
     blend_sum = total_sums[2 * width :].reshape(blend.shape)

time: 247 us -> 245 us (level)
  waiting for transfers between devices: 21.6 us -> 16.9 us
  starting transfers between devices: 41.9 us -> 45 us
    ppermute x32 -> x33, waiting for transfers between devices: 19.8 us -> 15.2 us  [peer(): return lax.ppermute(array, ('dp', 'head'), pairs)]
    ppermute x32 -> x33, starting transfers between devices: 37.1 us -> 40.2 us  [peer(): return lax.ppermute(array, ('dp', 'head'), pairs)]
  transfers between devices with their start and end apart: 34 -> 35, of which waited for: 10 -> 9; matrix products, arithmetic and copies ran while one was open for 10% -> 10% of each run, Pallas kernels for 39% -> 39%
where the time goes in v11:
time: 245 us; the launch traced here: 244 us
  Pallas kernels  149 us (61%)
  starting transfers between devices  45 us (18%)
  other arithmetic  17.1 us (7%)
  waiting for transfers between devices  16.9 us (7%)
  local copies, waits for them, and re-layouts  14.8 us (6%)
    ppermute x33, starting transfers between devices, peer(): return lax.ppermute(array, ('dp', 'head'), pairs)  40.2 us
    pallas_call x2, Pallas kernels, per_device(): call(backward_kernel, [spec['qkv'], spec['message']] + [spec['start']] *...  40.1 us
    pallas_call x1, Pallas kernels, per_device(): call(feed_kernel, [row_spec] * 3 + [whole_spec((width, width)), whole_spe...  26.1 us
    pallas_call x2, Pallas kernels, per_device(): call(functools.partial(resume, forward_kernel, 7, len(results)), [spec['q...  25.6 us
    pallas_call x2, Pallas kernels, feed_grad(): call(feed_grad_kernel, [whole_rows] * 2 + [columns] * 2 + more_in_specs,...  19.3 us
    ppermute x33, waiting for transfers between devices, peer(): return lax.ppermute(array, ('dp', 'head'), pairs)  15.2 us
    pallas_call x1, Pallas kernels, per_device(): call(functools.partial(project_kernel, flips=flips), [pl.BlockSpec((part,...  10.2 us
    pallas_call x1, Pallas kernels, per_device(): call(prologue_kernel, [spec['query'], pl.BlockSpec((1, ROWS, PAIR), lambd...  9.67 us
  transfers between devices with their start and end apart: 35, of which 9 were waited for; matrix products, arithmetic and copies ran while one was open for 10% of the time, Pallas kernels for 39%

profile of v11, /device:TPU:0, one launch (start us, length us, event | category | flops | bytes accessed | tf_op | source)
XLA Modules:
  0.0 244.3 jit_solution(7984404356312189924)
XLA Ops:
  1.5 5.1 %collective-permute-start.2 = (bf16[1,4,32,256]{3,2,1,0:T(8,128)(2,1)S(1)}, bf16[1,4,32,256]{3,2,1,0:T(8,128)(2,1)S(1)}, u32[]{:S(2)}, u32[]{:S(2)}) collective-permute-start(bf16[1,4,32,256]{3,2,1,0:T(8,128)(2,1)S(1)} %maximum_bitcast_fusion), channel_id=1, source_target_pairs={{0,24},{1,25},{2,26},{3,27},{4,28},{5,29},{6,30},{7,31},{8,16},{9,... | collective-permute-start | bytes 196616 | tf_op jit(solution)/shard_map/ppermute | solution.py:749
  12.3 2.5 %collective-permute-start.5 = (bf16[4,4,32,256]{3,2,1,0:T(8,128)(2,1)S(1)}, bf16[4,4,32,256]{3,2,1,0:T(8,128)(2,1)S(1)}, u32[]{:S(2)}, u32[]{:S(2)}) collective-permute-start(bf16[4,4,32,256]{3,2,1,0:T(8,128)(2,1)S(1)} %pad_maximum_fusion), channel_id=1, source_target_pairs={{0,5},{1,4},{2,7},{3,6},{4,1},{5,0},{6,3},{7,2},{8,13},{9,12},{10,... | collective-permute-start | bytes 786440 | tf_op jit(solution)/shard_map/ppermute | solution.py:749
  16.9 2.4 convert_convert_fusion.refs_4_.far_ref
  19.3 3.3 %fusion.6 = (f32[1536,128]{1,0:T(8,128)}, bf16[1536,128]{1,0:T(8,128)(2,1)}) fusion(f32[1536]{0:T(1024)S(1)} %get-tuple-element.181, f32[1536]{0:T(1024)S(1)} %get-tuple-element.180, s32[1536]{0:T(1024)S(1)} %get-tuple-element.184, s32[1536]{0:T(1024)S(1)} %get-tuple-element.185, s32[1536]{0:T(1024)S(1)} %get-tuple-element.80, ...), kind=kLoop, calls=%fused_computation.14 | loop fusion | flops 2359296 | bytes 1218048 | tf_op jit(solution)/shard_map/jit(_where)/select_n | solution.py:79
  22.6 4.1 %collective-permute-done.3 = bf16[4,4,32,256]{3,2,1,0:T(8,128)(2,1)S(1)} collective-permute-done((bf16[4,4,32,256]{3,2,1,0:T(8,128)(2,1)S(1)}, bf16[4,4,32,256]{3,2,1,0:T(8,128)(2,1)S(1)}, u32[]{:S(2)}, u32[]{:S(2)}) %collective-permute-start.3) | collective-permute-done | bytes 262176 | tf_op jit(solution)/shard_map/ppermute | solution.py:749
  30.4 1.9 concatenate.29.scalars.refs_0_
  34.6 10.2 %project.1 = (bf16[3,1536,512]{2,1,0:T(8,128)(2,1)}, bf16[1536,512]{1,0:T(8,128)(2,1)}, bf16[3,512,512]{2,1,0:T(8,128)(2,1)}, bf16[512,512]{1,0:T(8,128)(2,1)}, bf16[4,96,384]{2,1,0:T(8,128)(2,1)}) custom-call(s32[21]{0:T(128)} %concatenate.29.scalars.refs_0_, bf16[1536,512]{1,0:T(8,128)(2,1)} %tokens_ref.5, f32[1,512]{1,0:T(1,128)} %bitcast.34, ...), custom_call_target="tpu_custom_call" | custom-call | flops 2415919104 | bytes 9437184 | tf_op jit(solution)/shard_map/project/pallas_call | solution.py:854
  44.7 3.6 %collective-permute-start.12 = (bf16[4,96,384]{2,1,0:T(8,128)(2,1)}, bf16[4,96,384]{2,1,0:T(8,128)(2,1)S(1)}, u32[]{:S(2)}, u32[]{:S(2)}) collective-permute-start(bf16[4,96,384]{2,1,0:T(8,128)(2,1)} %get-tuple-element.84), channel_id=1, source_target_pairs={{0,1},{2,3},{4,5},{6,7},{8,9},{10,11},{12,13},{14,15},{16,17},{18,... | collective-permute-start | bytes 884744 | tf_op jit(solution)/shard_map/ppermute | solution.py:775
  50.5 2.3 collective-permute-start.10
  54.0 1.8 collective-permute-done.12.refs_2_.message_ref
  56.5 16.7 %forward.2 = (bf16[1536,512]{1,0:T(8,128)(2,1)}, f32[1536,512]{1,0:T(8,128)}, f32[1536,512]{1,0:T(8,128)}, f32[1536,512]{1,0:T(8,128)}, f32[1536,512]{1,0:T(8,12...) custom-call(s32[21]{0:T(128)} %concatenate.29.scalars.refs_0_, ...), custom_call_target="tpu_custom_call" | custom-call | flops 4718592000 | bytes 23592960 | tf_op jit(solution)/shard_map/forward/pallas_call | solution.py:896
  73.3 4.2 %collective-permute-done.10 = bf16[2,256,512]{2,1,0:T(8,128)(2,1)S(1)} collective-permute-done((bf16[2,256,512]{2,1,0:T(8,128)(2,1)S(1)}, bf16[2,256,512]{2,1,0:T(8,128)(2,1)S(1)}, u32[]{:S(2)}, u32[]{:S(2)}) %collective-permute-start.10) | collective-permute-done | bytes 524320 | tf_op jit(solution)/shard_map/ppermute | solution.py:749
  77.7 8.8 %forward.3 = (bf16[1536,512]{1,0:T(8,128)(2,1)}, f32[1536,512]{1,0:T(8,128)}, f32[1536,512]{1,0:T(8,128)}, f32[1536,512]{1,0:T(8,128)}, f32[1536,512]{1,0:T(8,12...) custom-call(s32[21]{0:T(128)} %concatenate.29.scalars.refs_0_, ...), custom_call_target="tpu_custom_call", output_to_operand_aliasing={{0}: (7, {}), {1}: (8, {}), {2}: (9, {}), {3}: (10, {}), {4... | custom-call | flops 1572864000 | bytes 7864320 | tf_op jit(solution)/shard_map/forward/pallas_call | solution.py:896
  87.9 26.1 %feed.1 = (bf16[1536,512]{1,0:T(8,128)(2,1)}, f32[1536,512]{1,0:T(8,128)}, bf16[1536,512]{1,0:T(8,128)(2,1)}, bf16[1536,512]{1,0:T(8,128)(2,1)}, bf16[1536,512]{...) custom-call(s32[21]{0:T(128)} %concatenate.29.scalars.refs_0_, ...), custom_call_target="tpu_custom_call" | custom-call | flops 12884901888 | bytes 25165824 | tf_op jit(solution)/shard_map/feed/pallas_call | solution.py:926
  113.9 9.7 %prologue.1 = bf16[4,96,384]{2,1,0:T(8,128)(2,1)} custom-call(s32[21]{0:T(128)} %concatenate.29.scalars.refs_0_, bf16[3,1536,512]{2,1,0:T(8,128)(2,1)} %get-tuple-element.82.refs_1_.query_ref.key_ref.value_ref.qkv_ref, bf16[3,1536,512]{2,1,0:T(8,128)(2,1)} %get-tuple-element.82.refs_1_.query_ref.key_ref.value_ref.qkv_ref, ...), custom_call_target="tpu_custom_call" | custom-call | flops 393216000 | bytes 15728640 | tf_op jit(solution)/shard_map/prologue/pallas_call | solution.py:944
  123.6 8.6 %feed_grad.2 = bf16[2,1024,512]{2,1,0:T(8,128)(2,1)} custom-call(s32[21]{0:T(128)} %concatenate.29.scalars.refs_0_, bf16[1536,512]{1,0:T(8,128)(2,1)} %get-tuple-element.112.normed_ref, bf16[1536,512]{1,0:T(8,128)(2,1)} %cotangent_ref.5, bf16[1536,2048]{1,0:T(8,128)(2,1)} %get-tuple-element.113.active_ref, bf16[1536,2048]{1,0:T(8,128)(2,1)} %get-tuple-element.122.d_inner_ref), custom_call_target="tpu_custom_call" | custom-call | flops 3221225472 | bytes 9437184 | tf_op jit(solution)/shard_map/feed_grad/pallas_call | solution.py:976
  133.9 10.8 %feed_grad.3 = (f32[512,512]{1,0:T(8,128)}, f32[2,1024,512]{2,1,0:T(8,128)}) custom-call(s32[21]{0:T(128)} %concatenate.29.scalars.refs_0_, bf16[1536,512]{1,0:T(8,128)(2,1)} %get-tuple-element.112.normed_ref, bf16[1536,512]{1,0:T(8,128)(2,1)} %cotangent_ref.5, bf16[1536,2048]{1,0:T(8,128)(2,1)} %get-tuple-element.113.active_ref, ...), custom_call_target="tpu_custom_call" | custom-call | flops 3221225472 | bytes 9437184 | tf_op jit(solution)/shard_map/feed_grad/pallas_call | solution.py:976
  144.7 3.1 %fusion.17 = (bf16[2,1024,512]{2,1,0:T(8,128)(2,1)S(1)}, f32[2,1024,512]{2,1,0:T(8,128)S(1)}) fusion(f32[2,1024,512]{2,1,0:T(8,128)} %get-tuple-element.124, bf16[2,1024,512]{2,1,0:T(8,128)(2,1)S(1)} %collective-permute-done.14), kind=kLoop, calls=%fused_computation.70 | loop fusion | flops 3145728 | bytes 12582912 | tf_op jit(solution)/shard_map/convert.11
  149.5 2.7 %collective-permute-start.17 = (bf16[2,256,512]{2,1,0:T(8,128)(2,1)S(1)}, bf16[2,256,512]{2,1,0:T(8,128)(2,1)S(1)}, u32[]{:S(2)}, u32[]{:S(2)}) collective-permute-start(bf16[2,256,512]{2,1,0:T(8,128)(2,1)S(1)} %get-tuple-element.161), channel_id=1, source_target_pairs={{0,5},{1,4},{2,7},{3,6},{4,1},{5,0},{6,3},{7,2},{8,13},{9,12},{10,... | collective-permute-start | bytes 1572872 | tf_op jit(solution)/shard_map/ppermute | solution.py:749
  152.8 27.7 %backward.2 = (bf16[3,1536,512]{2,1,0:T(8,128)(2,1)}, f32[24,384]{1,0:T(8,128)}) custom-call(s32[21]{0:T(128)} %concatenate.29.scalars.refs_0_, bf16[3,1536,512]{2,1,0:T(8,128)(2,1)} %get-tuple-element.82.refs_1_.query_ref.key_ref.value_ref.qkv_ref, bf16[4,96,384]{2,1,0:T(8,128)(2,1)} %copy-done, bf16[1536,128]{1,0:T(8,128)(2,1)} %get-tuple-element.86.refs_3_.bias_ref, ...), custom_call_target="tpu_custom_call" | custom-call | flops 9437184000 | bytes 23592960 | tf_op jit(solution)/shard_map/backward/pallas_call | solution.py:1010
  180.8 1.8 collective-permute-start.18
  184.4 12.5 %backward.3 = (bf16[3,1536,512]{2,1,0:T(8,128)(2,1)}, f32[24,128]{1,0:T(8,128)}) custom-call(s32[21]{0:T(128)} %concatenate.29.scalars.refs_0_, bf16[3,1536,512]{2,1,0:T(8,128)(2,1)} %get-tuple-element.82.refs_1_.query_ref.key_ref.value_ref.qkv_ref, bf16[4,96,384]{2,1,0:T(8,128)(2,1)} %copy-done, ...), custom_call_target="tpu_custom_call", output_to_operand_aliasing={{0}: (15, {})} | custom-call | flops 3145728000 | bytes 7864320 | tf_op jit(solution)/shard_map/backward/pallas_call | solution.py:1010
  197.0 8.9 %weight_grad.1 = (f32[16,4,32,256]{3,2,1,0:T(8,128)}, bf16[16,4,32,256]{3,2,1,0:T(8,128)(2,1)}, f32[8,512]{1,0:T(8,128)}) custom-call(s32[21]{0:T(128)} %concatenate.29.scalars.refs_0_, bf16[1536,512]{1,0:T(8,128)(2,1)} %get-tuple-element.111.normed_ref, bf16[3,1536,512]{2,1,0:T(8,128)(2,1)} %get-tuple-element.140.d_qkv_ref, ...), custom_call_target="tpu_custom_call" | custom-call | flops 2415919104 | bytes 6291456 | tf_op jit(solution)/shard_map/weight_grad/pallas_call | solution.py:1057
  208.8 2.1 fusion.15
  210.9 3.0 %collective-permute-start.28 = (bf16[4,4,32,256]{3,2,1,0:T(8,128)(2,1)S(1)}, bf16[4,4,32,256]{3,2,1,0:T(8,128)(2,1)S(1)}, u32[]{:S(2)}, u32[]{:S(2)}) collective-permute-start(bf16[4,4,32,256]{3,2,1,0:T(8,128)(2,1)S(1)} %get-tuple-element.163), channel_id=1, source_target_pairs={{0,5},{1,4},{2,7},{3,6},{4,1},{5,0},{6,3},{7,2},{8,13},{9,12},{10,... | collective-permute-start | bytes 786440 | tf_op jit(solution)/shard_map/ppermute | solution.py:749
  214.6 2.0 collective-permute-start.24
  216.6 8.9 %input.1 = f32[1536,512]{1,0:T(8,128)} custom-call(s32[21]{0:T(128)} %concatenate.29.scalars.refs_0_, bf16[3,1536,512]{2,1,0:T(8,128)(2,1)} %get-tuple-element.140.d_qkv_ref, bf16[3,512,512]{2,1,0:T(8,128)(2,1)} %get-tuple-element.133.weight_ref, bf16[1536,512]{1,0:T(8,128)(2,1)} %tokens_ref.5, f32[1536,512]{1,0:T(8,128)} %get-tuple-element.141.d_hidden_ref, ...), custom_call_target="tpu_custom_call" | custom-call | flops 2415919104 | bytes 18874368 | tf_op jit(solution)/shard_map/input/pallas_call | solution.py:1084
  227.2 2.6 %collective-permute-start.33 = (bf16[1,4,32,256]{3,2,1,0:T(8,128)(2,1)S(1)}, bf16[1,4,32,256]{3,2,1,0:T(8,128)(2,1)S(1)}, u32[]{:S(2)}, u32[]{:S(2)}) collective-permute-start(bf16[1,4,32,256]{3,2,1,0:T(8,128)(2,1)S(1)} %get-tuple-element.171), channel_id=1, source_target_pairs={{0,16},{1,17},{2,18},{3,19},{4,20},{5,21},{6,22},{7,23},{8,24},{9,... | collective-permute-start | bytes 196616 | tf_op jit(solution)/shard_map/ppermute | solution.py:749
  229.8 2.5 %collective-permute-start.34 = (bf16[1,4,32,256]{3,2,1,0:T(8,128)(2,1)S(1)}, bf16[1,4,32,256]{3,2,1,0:T(8,128)(2,1)S(1)}, u32[]{:S(2)}, u32[]{:S(2)}) collective-permute-start(bf16[1,4,32,256]{3,2,1,0:T(8,128)(2,1)S(1)} %get-tuple-element.172), channel_id=1, source_target_pairs={{0,24},{1,25},{2,26},{3,27},{4,28},{5,29},{6,30},{7,31},{8,16},{9,... | collective-permute-start | bytes 196616 | tf_op jit(solution)/shard_map/ppermute | solution.py:749
  233.0 3.5 %collective-permute-done.29 = bf16[1,4,32,256]{3,2,1,0:T(8,128)(2,1)S(1)} collective-permute-done((bf16[1,4,32,256]{3,2,1,0:T(8,128)(2,1)S(1)}, bf16[1,4,32,256]{3,2,1,0:T(8,128)(2,1)S(1)}, u32[]{:S(2)}, u32[]{:S(2)}) %collective-permute-start.29) | collective-permute-done | bytes 65568 | tf_op jit(solution)/shard_map/ppermute | solution.py:749
  236.5 2.0 collective-permute-start.32
  238.6 2.4 collective-permute-start.30
  (139 shorter events, 35.2 us)
Async XLA Ops:
  1.5 10.2 %collective-permute-start.2 = (bf16[1,4,32,256]{3,2,1,0:T(8,128)(2,1)S(1)}, bf16[1,4,32,256]{3,2,1,0:T(8,128)(2,1)S(1)}, u32[]{:S(2)}, u32[]{:S(2)}) collective-permute-start(bf16[1,4,32,256]{3,2,1,0:T(8,128)(2,1)S(1)} %maximum_bitcast_fusion), channel_id=1, source_target_pairs={{0,24},{1,25},{2,26},{3,27},{4,28},{5,29},{6,30},{7,31},{8,16},{9,... | collective-permute-start | bytes 196616 | tf_op jit(solution)/shard_map/ppermute | solution.py:749
  6.6 5.6 %collective-permute-start.1 = (bf16[1,4,32,256]{3,2,1,0:T(8,128)(2,1)S(1)}, bf16[1,4,32,256]{3,2,1,0:T(8,128)(2,1)S(1)}, u32[]{:S(2)}, u32[]{:S(2)}) collective-permute-start(bf16[1,4,32,256]{3,2,1,0:T(8,128)(2,1)S(1)} %maximum_bitcast_fusion), channel_id=1, source_target_pairs={{0,16},{1,17},{2,18},{3,19},{4,20},{5,21},{6,22},{7,23},{8,24},{9,... | collective-permute-start | bytes 196616 | tf_op jit(solution)/shard_map/ppermute | solution.py:749
  6.6 5.6 %collective-permute-start = (bf16[1,4,32,256]{3,2,1,0:T(8,128)(2,1)S(1)}, bf16[1,4,32,256]{3,2,1,0:T(8,128)(2,1)S(1)}, u32[]{:S(2)}, u32[]{:S(2)}) collective-permute-start(bf16[1,4,32,256]{3,2,1,0:T(8,128)(2,1)S(1)} %maximum_bitcast_fusion), channel_id=1, source_target_pairs={{0,8},{1,9},{2,10},{3,11},{4,12},{5,13},{6,14},{7,15},{8,0},{9,1},... | collective-permute-start | bytes 196616 | tf_op jit(solution)/shard_map/ppermute | solution.py:749
  12.3 14.7 %collective-permute-start.5 = (bf16[4,4,32,256]{3,2,1,0:T(8,128)(2,1)S(1)}, bf16[4,4,32,256]{3,2,1,0:T(8,128)(2,1)S(1)}, u32[]{:S(2)}, u32[]{:S(2)}) collective-permute-start(bf16[4,4,32,256]{3,2,1,0:T(8,128)(2,1)S(1)} %pad_maximum_fusion), channel_id=1, source_target_pairs={{0,5},{1,4},{2,7},{3,6},{4,1},{5,0},{6,3},{7,2},{8,13},{9,12},{10,... | collective-permute-start | bytes 786440 | tf_op jit(solution)/shard_map/ppermute | solution.py:749
  14.8 12.2 %collective-permute-start.4 = (bf16[4,4,32,256]{3,2,1,0:T(8,128)(2,1)S(1)}, bf16[4,4,32,256]{3,2,1,0:T(8,128)(2,1)S(1)}, u32[]{:S(2)}, u32[]{:S(2)}) collective-permute-start(bf16[4,4,32,256]{3,2,1,0:T(8,128)(2,1)S(1)} %pad_maximum_fusion), channel_id=1, source_target_pairs={{0,1},{1,0},{2,3},{3,2},{4,5},{5,4},{6,7},{7,6},{8,9},{9,8},{10,11... | collective-permute-start | bytes 786440 | tf_op jit(solution)/shard_map/ppermute | solution.py:749
  15.3 11.4 %collective-permute-start.3 = (bf16[4,4,32,256]{3,2,1,0:T(8,128)(2,1)S(1)}, bf16[4,4,32,256]{3,2,1,0:T(8,128)(2,1)S(1)}, u32[]{:S(2)}, u32[]{:S(2)}) collective-permute-start(bf16[4,4,32,256]{3,2,1,0:T(8,128)(2,1)S(1)} %pad_maximum_fusion), channel_id=1, source_target_pairs={{0,4},{1,5},{2,6},{3,7},{4,0},{5,1},{6,2},{7,3},{8,12},{9,13},{10,... | collective-permute-start | bytes 786440 | tf_op jit(solution)/shard_map/ppermute | solution.py:749
  15.8 6.8 %collective-permute-start.6 = (bf16[2,64,512]{2,1,0:T(8,128)(2,1)S(1)}, bf16[2,64,512]{2,1,0:T(8,128)(2,1)S(1)}, u32[]{:S(2)}, u32[]{:S(2)}) collective-permute-start(bf16[2,64,512]{2,1,0:T(8,128)(2,1)S(1)} %pad_maximum_fusion.2), channel_id=1, source_target_pairs={{0,8},{1,9},{2,10},{3,11},{4,12},{5,13},{6,14},{7,15},{8,0},{9,1},... | collective-permute-start | bytes 393224 | tf_op jit(solution)/shard_map/ppermute | solution.py:749
  28.2 5.4 %collective-permute-start.7 = (bf16[16,4,32,256]{3,2,1,0:T(8,128)(2,1)S(1)}, bf16[16,4,32,256]{3,2,1,0:T(8,128)(2,1)S(1)}, u32[]{:S(2)}, u32[]{:S(2)}) collective-permute-start(bf16[16,4,32,256]{3,2,1,0:T(8,128)(2,1)S(1)} %constant_dynamic-update-slice_fusion.own_ref), channel_id=1, source_target_pairs={{0,2},{1,3},{2,0},{3,1},{4,6},{5,7},{6,4},{7,5},{8,10},{9,11},{10,... | collective-permute-start | bytes 3145736 | tf_op jit(solution)/shard_map/ppermute | solution.py:749
  32.2 16.8 %collective-permute-start.8 = (bf16[2,128,512]{2,1,0:T(8,128)(2,1)S(1)}, bf16[2,128,512]{2,1,0:T(8,128)(2,1)S(1)}, u32[]{:S(2)}, u32[]{:S(2)}) collective-permute-start(bf16[2,128,512]{2,1,0:T(8,128)(2,1)S(1)} %pad_maximum_fusion.1), channel_id=1, source_target_pairs={{0,16},{1,17},{2,18},{3,19},{4,20},{5,21},{6,22},{7,23},{8,24},{9,... | collective-permute-start | bytes 786440 | tf_op jit(solution)/shard_map/ppermute | solution.py:749
  44.7 11.1 %collective-permute-start.12 = (bf16[4,96,384]{2,1,0:T(8,128)(2,1)}, bf16[4,96,384]{2,1,0:T(8,128)(2,1)S(1)}, u32[]{:S(2)}, u32[]{:S(2)}) collective-permute-start(bf16[4,96,384]{2,1,0:T(8,128)(2,1)} %get-tuple-element.84), channel_id=1, source_target_pairs={{0,1},{2,3},{4,5},{6,7},{8,9},{10,11},{12,13},{14,15},{16,17},{18,... | collective-permute-start | bytes 884744 | tf_op jit(solution)/shard_map/ppermute | solution.py:775
  49.8 23.5 %collective-permute-start.11 = (bf16[2,256,512]{2,1,0:T(8,128)(2,1)S(1)}, bf16[2,256,512]{2,1,0:T(8,128)(2,1)S(1)}, u32[]{:S(2)}, u32[]{:S(2)}) collective-permute-start(bf16[2,256,512]{2,1,0:T(8,128)(2,1)S(1)} %get-tuple-element.174), channel_id=1, source_target_pairs={{0,5},{1,4},{2,7},{3,6},{4,1},{5,0},{6,3},{7,2},{8,13},{9,12},{10,... | collective-permute-start | bytes 1572872 | tf_op jit(solution)/shard_map/ppermute | solution.py:749
  50.5 27.0 %collective-permute-start.10 = (bf16[2,256,512]{2,1,0:T(8,128)(2,1)S(1)}, bf16[2,256,512]{2,1,0:T(8,128)(2,1)S(1)}, u32[]{:S(2)}, u32[]{:S(2)}) collective-permute-start(bf16[2,256,512]{2,1,0:T(8,128)(2,1)S(1)} %get-tuple-element.174), channel_id=1, source_target_pairs={{0,1},{1,0},{2,3},{3,2},{4,5},{5,4},{6,7},{7,6},{8,9},{9,8},{10,11... | collective-permute-start | bytes 1572872 | tf_op jit(solution)/shard_map/ppermute | solution.py:749
  52.7 24.8 %collective-permute-start.9 = (bf16[2,256,512]{2,1,0:T(8,128)(2,1)S(1)}, bf16[2,256,512]{2,1,0:T(8,128)(2,1)S(1)}, u32[]{:S(2)}, u32[]{:S(2)}) collective-permute-start(bf16[2,256,512]{2,1,0:T(8,128)(2,1)S(1)} %get-tuple-element.174), channel_id=1, source_target_pairs={{0,4},{1,5},{2,6},{3,7},{4,0},{5,1},{6,2},{7,3},{8,12},{9,13},{10,... | collective-permute-start | bytes 1572872 | tf_op jit(solution)/shard_map/ppermute | solution.py:749
  77.6 8.9 %collective-permute-start.13 = (bf16[2,1024,512]{2,1,0:T(8,128)(2,1)S(1)}, bf16[2,1024,512]{2,1,0:T(8,128)(2,1)S(1)}, u32[]{:S(2)}, u32[]{:S(2)}) collective-permute-start(bf16[2,1024,512]{2,1,0:T(8,128)(2,1)S(1)} %constant_dynamic-update-slice_fusion.9.own_ref), channel_id=1, source_target_pairs={{0,2},{1,3},{2,0},{3,1},{4,6},{5,7},{6,4},{7,5},{8,10},{9,11},{10,... | collective-permute-start | bytes 6291464 | tf_op jit(solution)/shard_map/ppermute | solution.py:749
  132.2 12.6 %collective-permute-start.14 = (bf16[2,1024,512]{2,1,0:T(8,128)(2,1)}, bf16[2,1024,512]{2,1,0:T(8,128)(2,1)S(1)}, u32[]{:S(2)}, u32[]{:S(2)}) collective-permute-start(bf16[2,1024,512]{2,1,0:T(8,128)(2,1)} %feed_grad.2), channel_id=1, source_target_pairs={{0,2},{1,3},{2,0},{3,1},{4,6},{5,7},{6,4},{7,5},{8,10},{9,11},{10,... | collective-permute-start | bytes 6291464 | tf_op jit(solution)/shard_map/ppermute | solution.py:749
  132.7 15.3 %collective-permute-start.21 = (bf16[4,96,384]{2,1,0:T(8,128)(2,1)S(1)}, bf16[4,96,384]{2,1,0:T(8,128)(2,1)S(1)}, u32[]{:S(2)}, u32[]{:S(2)}) collective-permute-start(bf16[4,96,384]{2,1,0:T(8,128)(2,1)S(1)} %copy-done.1), channel_id=1, source_target_pairs={{1,0},{3,2},{5,4},{7,6},{9,8},{11,10},{13,12},{15,14},{17,16},{19,... | collective-permute-start | bytes 884744 | tf_op jit(solution)/shard_map/ppermute | solution.py:775
  148.0 32.5 %collective-permute-start.15 = (bf16[2,256,512]{2,1,0:T(8,128)(2,1)S(1)}, bf16[2,256,512]{2,1,0:T(8,128)(2,1)S(1)}, u32[]{:S(2)}, u32[]{:S(2)}) collective-permute-start(bf16[2,256,512]{2,1,0:T(8,128)(2,1)S(1)} %get-tuple-element.160), channel_id=1, source_target_pairs={{0,4},{1,5},{2,6},{3,7},{4,0},{5,1},{6,2},{7,3},{8,12},{9,13},{10,... | collective-permute-start | bytes 1572872 | tf_op jit(solution)/shard_map/ppermute | solution.py:749
  149.5 31.0 %collective-permute-start.17 = (bf16[2,256,512]{2,1,0:T(8,128)(2,1)S(1)}, bf16[2,256,512]{2,1,0:T(8,128)(2,1)S(1)}, u32[]{:S(2)}, u32[]{:S(2)}) collective-permute-start(bf16[2,256,512]{2,1,0:T(8,128)(2,1)S(1)} %get-tuple-element.161), channel_id=1, source_target_pairs={{0,5},{1,4},{2,7},{3,6},{4,1},{5,0},{6,3},{7,2},{8,13},{9,12},{10,... | collective-permute-start | bytes 1572872 | tf_op jit(solution)/shard_map/ppermute | solution.py:749
  152.2 28.3 %collective-permute-start.16 = (bf16[2,256,512]{2,1,0:T(8,128)(2,1)S(1)}, bf16[2,256,512]{2,1,0:T(8,128)(2,1)S(1)}, u32[]{:S(2)}, u32[]{:S(2)}) collective-permute-start(bf16[2,256,512]{2,1,0:T(8,128)(2,1)S(1)} %get-tuple-element.162), channel_id=1, source_target_pairs={{0,1},{1,0},{2,3},{3,2},{4,5},{5,4},{6,7},{7,6},{8,9},{9,8},{10,11... | collective-permute-start | bytes 1572872 | tf_op jit(solution)/shard_map/ppermute | solution.py:749
  180.8 16.0 %collective-permute-start.18 = (bf16[2,64,512]{2,1,0:T(8,128)(2,1)S(1)}, bf16[2,64,512]{2,1,0:T(8,128)(2,1)S(1)}, u32[]{:S(2)}, u32[]{:S(2)}) collective-permute-start(bf16[2,64,512]{2,1,0:T(8,128)(2,1)S(1)} %get-tuple-element.166), channel_id=1, source_target_pairs={{0,8},{1,9},{2,10},{3,11},{4,12},{5,13},{6,14},{7,15},{8,0},{9,1},... | collective-permute-start | bytes 393224 | tf_op jit(solution)/shard_map/ppermute | solution.py:749
  182.7 14.2 %collective-permute-start.20 = (bf16[2,64,512]{2,1,0:T(8,128)(2,1)S(1)}, bf16[2,64,512]{2,1,0:T(8,128)(2,1)S(1)}, u32[]{:S(2)}, u32[]{:S(2)}) collective-permute-start(bf16[2,64,512]{2,1,0:T(8,128)(2,1)S(1)} %get-tuple-element.167), channel_id=1, source_target_pairs={{0,24},{1,25},{2,26},{3,27},{4,28},{5,29},{6,30},{7,31},{8,16},{9,... | collective-permute-start | bytes 393224 | tf_op jit(solution)/shard_map/ppermute | solution.py:749
  184.0 12.9 %collective-permute-start.19 = (bf16[2,64,512]{2,1,0:T(8,128)(2,1)S(1)}, bf16[2,64,512]{2,1,0:T(8,128)(2,1)S(1)}, u32[]{:S(2)}, u32[]{:S(2)}) collective-permute-start(bf16[2,64,512]{2,1,0:T(8,128)(2,1)S(1)} %get-tuple-element.168), channel_id=1, source_target_pairs={{0,16},{1,17},{2,18},{3,19},{4,20},{5,21},{6,22},{7,23},{8,24},{9,... | collective-permute-start | bytes 393224 | tf_op jit(solution)/shard_map/ppermute | solution.py:749
  207.0 7.6 %collective-permute-start.22 = (f32[1,1048]{1,0:T(1,128)S(1)}, f32[1,1048]{1,0:T(1,128)S(1)}, u32[]{:S(2)}, u32[]{:S(2)}) collective-permute-start(f32[1,1048]{1,0:T(1,128)S(1)} %broadcast_in_dim.149), channel_id=1, source_target_pairs={{0,2},{1,3},{2,0},{3,1},{4,6},{5,7},{6,4},{7,5},{8,10},{9,11},{10,... | collective-permute-start | bytes 12584 | tf_op jit(solution)/shard_map/ppermute | solution.py:749
  210.9 16.1 %collective-permute-start.28 = (bf16[4,4,32,256]{3,2,1,0:T(8,128)(2,1)S(1)}, bf16[4,4,32,256]{3,2,1,0:T(8,128)(2,1)S(1)}, u32[]{:S(2)}, u32[]{:S(2)}) collective-permute-start(bf16[4,4,32,256]{3,2,1,0:T(8,128)(2,1)S(1)} %get-tuple-element.163), channel_id=1, source_target_pairs={{0,5},{1,4},{2,7},{3,6},{4,1},{5,0},{6,3},{7,2},{8,13},{9,12},{10,... | collective-permute-start | bytes 786440 | tf_op jit(solution)/shard_map/ppermute | solution.py:749
  213.9 13.1 %collective-permute-start.27 = (bf16[4,4,32,256]{3,2,1,0:T(8,128)(2,1)S(1)}, bf16[4,4,32,256]{3,2,1,0:T(8,128)(2,1)S(1)}, u32[]{:S(2)}, u32[]{:S(2)}) collective-permute-start(bf16[4,4,32,256]{3,2,1,0:T(8,128)(2,1)S(1)} %get-tuple-element.164), channel_id=1, source_target_pairs={{0,1},{1,0},{2,3},{3,2},{4,5},{5,4},{6,7},{7,6},{8,9},{9,8},{10,11... | collective-permute-start | bytes 786440 | tf_op jit(solution)/shard_map/ppermute | solution.py:749
  213.9 13.1 %collective-permute-start.26 = (bf16[4,4,32,256]{3,2,1,0:T(8,128)(2,1)S(1)}, bf16[4,4,32,256]{3,2,1,0:T(8,128)(2,1)S(1)}, u32[]{:S(2)}, u32[]{:S(2)}) collective-permute-start(bf16[4,4,32,256]{3,2,1,0:T(8,128)(2,1)S(1)} %get-tuple-element.165), channel_id=1, source_target_pairs={{0,4},{1,5},{2,6},{3,7},{4,0},{5,1},{6,2},{7,3},{8,12},{9,13},{10,... | collective-permute-start | bytes 786440 | tf_op jit(solution)/shard_map/ppermute | solution.py:749
  214.6 11.4 %collective-permute-start.24 = (f32[1,1048]{1,0:T(1,128)S(1)}, f32[1,1048]{1,0:T(1,128)S(1)}, u32[]{:S(2)}, u32[]{:S(2)}) collective-permute-start(f32[1,1048]{1,0:T(1,128)S(1)} %reshape_add_fusion), channel_id=1, source_target_pairs={{0,1},{1,0},{2,3},{3,2},{4,5},{5,4},{6,7},{7,6},{8,9},{9,8},{10,11... | collective-permute-start | bytes 12584 | tf_op jit(solution)/shard_map/ppermute | solution.py:749
  226.0 7.0 %collective-permute-start.25 = (f32[1,1048]{1,0:T(1,128)S(1)}, f32[1,1048]{1,0:T(1,128)S(1)}, u32[]{:S(2)}, u32[]{:S(2)}) collective-permute-start(f32[1,1048]{1,0:T(1,128)S(1)} %add.110), channel_id=1, source_target_pairs={{0,4},{1,5},{2,6},{3,7},{4,0},{5,1},{6,2},{7,3},{8,12},{9,13},{10,... | collective-permute-start | bytes 12584 | tf_op jit(solution)/shard_map/ppermute | solution.py:749
  227.2 13.7 %collective-permute-start.33 = (bf16[1,4,32,256]{3,2,1,0:T(8,128)(2,1)S(1)}, bf16[1,4,32,256]{3,2,1,0:T(8,128)(2,1)S(1)}, u32[]{:S(2)}, u32[]{:S(2)}) collective-permute-start(bf16[1,4,32,256]{3,2,1,0:T(8,128)(2,1)S(1)} %get-tuple-element.171), channel_id=1, source_target_pairs={{0,16},{1,17},{2,18},{3,19},{4,20},{5,21},{6,22},{7,23},{8,24},{9,... | collective-permute-start | bytes 196616 | tf_op jit(solution)/shard_map/ppermute | solution.py:749
  229.8 11.2 %collective-permute-start.34 = (bf16[1,4,32,256]{3,2,1,0:T(8,128)(2,1)S(1)}, bf16[1,4,32,256]{3,2,1,0:T(8,128)(2,1)S(1)}, u32[]{:S(2)}, u32[]{:S(2)}) collective-permute-start(bf16[1,4,32,256]{3,2,1,0:T(8,128)(2,1)S(1)} %get-tuple-element.172), channel_id=1, source_target_pairs={{0,24},{1,25},{2,26},{3,27},{4,28},{5,29},{6,30},{7,31},{8,16},{9,... | collective-permute-start | bytes 196616 | tf_op jit(solution)/shard_map/ppermute | solution.py:749
  236.5 5.7 %collective-permute-start.32 = (f32[1,1048]{1,0:T(1,128)S(1)}, f32[1,1048]{1,0:T(1,128)S(1)}, u32[]{:S(2)}, u32[]{:S(2)}) collective-permute-start(f32[1,1048]{1,0:T(1,128)S(1)} %add.111), channel_id=1, source_target_pairs={{0,24},{1,25},{2,26},{3,27},{4,28},{5,29},{6,30},{7,31},{8,16},{9,... | collective-permute-start | bytes 12584 | tf_op jit(solution)/shard_map/ppermute | solution.py:749
  238.6 4.5 %collective-permute-start.30 = (f32[1,1048]{1,0:T(1,128)S(1)}, f32[1,1048]{1,0:T(1,128)S(1)}, u32[]{:S(2)}, u32[]{:S(2)}) collective-permute-start(f32[1,1048]{1,0:T(1,128)S(1)} %add.111), channel_id=1, source_target_pairs={{0,16},{1,17},{2,18},{3,19},{4,20},{5,21},{6,22},{7,23},{8,24},{9,... | collective-permute-start | bytes 12584 | tf_op jit(solution)/shard_map/ppermute | solution.py:749
  (16 other events, 119.8 us)
